TPU v7x, 32 devices: a whole 2x2x4 slice. The times are simulated.
32 devices in a mesh: fsdp: 4 (over x, core), ctx: 2 (over y), tp: 4 (over z).
Axes of the slice: x: 2, y: 2, z: 4, core: 2. Of those that a mesh axis runs over, the one named last changes fastest.
Arguments:
- states: bfloat16 [4, 1024, 2048], P('fsdp', 'ctx'), may hold values from -6 to 6
- teacher: bfloat16 [4, 1024, 2048], P('fsdp', 'ctx'), may hold values from -6 to 6
- lengths: int32 [4], P('fsdp'), may hold values from 513 to 1024, as said below
- routes: int32 [4, 1024, 8], P('fsdp', 'ctx'), may hold values from 0 to 31, all different within a row; in each aligned block of 512 rows (0 to 511, 512 to 1023, ..., all dimensions but the last counted through in order) at most 160 rows name the same one
- gate_weights: float32 [4, 1024, 8], P('fsdp', 'ctx'), may hold values from 0.05 to 0.2
- w_qkv: bfloat16 [2048, 3, 2048], P(('fsdp', 'ctx'), None, 'tp'), may hold values from -0.125 to 0.125
- w_out: bfloat16 [2048, 2048], P('tp', ('fsdp', 'ctx')), may hold values from -3 to 3
- norm_gains: bfloat16 [2, 2048], P(None, ('fsdp', 'ctx')), may hold values from 0.5 to 1.5
- qk_gains: bfloat16 [2, 128], P(None, ('fsdp', 'ctx')), may hold values from 0.099609375 to 1.8984375
- w_gate_up: bfloat16 [32, 2048, 2, 1024], P(('fsdp', 'ctx'), None, None, 'tp'), may hold values from -0.125 to 0.125
- w_down: bfloat16 [32, 1024, 2048], P(('fsdp', 'ctx'), 'tp'), may hold values from -0.75 to 0.75
Outputs:
- activations: bfloat16 [4, 1024, 2048], P('fsdp', 'ctx')
- loss_value: float32 [], replicated
- valid_count: float32 [], replicated
- grad_states: float32 [4, 1024, 2048], P('fsdp', 'ctx')
- grad_qkv: float32 [2048, 3, 2048], P(('fsdp', 'ctx'), None, 'tp')
- grad_out: float32 [2048, 2048], P('tp', ('fsdp', 'ctx'))
- grad_norm_gains: float32 [2, 2048], P(None, ('fsdp', 'ctx'))
- grad_qk_gains: float32 [2, 128], P(None, ('fsdp', 'ctx'))
- grad_gate_up: float32 [32, 2048, 2, 1024], P(('fsdp', 'ctx'), None, None, 'tp')
- grad_down: float32 [32, 1024, 2048], P(('fsdp', 'ctx'), 'tp')
Inputs may be any that keep to these rules, and one draw needn't show every extreme that they name: `lengths`: every sequence has at least 513 valid slots, and some sequence has exactly 1024. `routes`: each slot names 8 different experts; among the 512 slots of one sequence on one index of ctx (aligned blocks of the flattened slots) no expert is named more than 160 times, a bound that some block reaches.
All inputs are finite; a program needn't handle non-finite values.
Results may differ from a plain program's by a relative error of at most 0.015.
Values may be sent and summed in bfloat16 or wider, within the bound.
No kernel may reach another device: no remote copies, remote signals or barrier semaphores. Data moves between devices by JAX's collectives and lax.ppermute only.
A program may use at most 320 MiB of HBM per device.

v0:
```python
import jax
import jax.numpy as jnp
from jax import lax
from jax.sharding import PartitionSpec as P

norm_eps = 1e-05
rope_base = 10000.0
loss_scale = 4096.0
masked_score = -1e30


def rms_norm(values, gain_vec):
    return (
        values * lax.rsqrt(jnp.mean(values * values, axis=-1, keepdims=True) + norm_eps) * gain_vec
    )


def norm_back(grad_normed, values, gain_vec):
    inverse = lax.rsqrt(jnp.mean(values * values, axis=-1, keepdims=True) + norm_eps)
    scaled = values * inverse
    grad_scaled = grad_normed * gain_vec
    grad_values = inverse * (
        grad_scaled - scaled * jnp.mean(grad_scaled * scaled, axis=-1, keepdims=True)
    )
    return (grad_values, jnp.sum(grad_normed * scaled, axis=0))


def rotate(values, position):
    half_dim = values.shape[-1] // 2
    frequency = rope_base ** (-2.0 * jnp.arange(half_dim, dtype=jnp.float32) / values.shape[-1])
    angles = position.astype(jnp.float32)[:, None] * frequency[None, :]
    cosine = jnp.cos(angles)[:, None, :]
    sine_part = jnp.sin(angles)[:, None, :]
    first_half = values[..., :half_dim]
    second_half = values[..., half_dim:]
    return jnp.concatenate(
        [
            first_half * cosine - second_half * sine_part,
            second_half * cosine + first_half * sine_part,
        ],
        axis=-1,
    )


def prepare(projected, qk_float, position):
    queries = rotate(rms_norm(projected[:, 0], qk_float[0]), position)
    key_states = rotate(rms_norm(projected[:, 1], qk_float[1]), position)
    return (queries, key_states, projected[:, 2])


def dispatch(route_rows, gate_rows, capacity, experts):
    flat_routes = route_rows.reshape(-1)
    matches = (flat_routes[:, None] == jnp.arange(experts, dtype=jnp.int32)[None, :]).astype(
        jnp.int32
    )
    ranking = jnp.sum((jnp.cumsum(matches, axis=0) - 1) * matches, axis=1)
    source = jnp.arange(flat_routes.shape[0], dtype=jnp.int32) // route_rows.shape[-1]
    slot_rows = jnp.zeros((experts, capacity), jnp.int32).at[flat_routes, ranking].set(source)
    slot_gate = (
        jnp.zeros((experts, capacity), jnp.float32)
        .at[flat_routes, ranking]
        .set(gate_rows.reshape(-1))
    )
    return (slot_rows, slot_gate)


def fold_local(pieces, update, initial, shard_experts):

    def one_turn(step_index, running):
        begin_row = step_index * shard_experts
        portion = tuple(
            (lax.dynamic_slice_in_dim(piece, begin_row, shard_experts, 0) for piece in pieces)
        )
        return update(running, portion, begin_row)

    return lax.fori_loop(0, pieces[0].shape[0] // shard_experts, one_turn, initial)


def attend_sequence(query_seq, kv_seq, valid_seq, query_rows, score_scale):
    blocks = query_seq.shape[0] // query_rows

    def attend_block(query_block):
        scores = (
            jnp.einsum(
                "qhd,khd->hqk", query_block, kv_seq[:, 0], preferred_element_type=jnp.float32
            )
            * score_scale
        )
        scores = jnp.where(valid_seq[None, None, :], scores, masked_score)
        peak_score = jnp.max(scores, axis=-1, keepdims=True)
        exponent = jnp.exp(scores - peak_score)
        row_total = jnp.sum(exponent, axis=-1, keepdims=True)
        probability = (exponent / row_total).astype(jnp.bfloat16)
        output = jnp.einsum(
            "hqk,khd->qhd", probability, kv_seq[:, 1], preferred_element_type=jnp.float32
        )
        return (output, (peak_score + jnp.log(row_total))[..., 0])

    return lax.map(
        attend_block, query_seq.reshape(blocks, query_rows, query_seq.shape[1], query_seq.shape[2])
    )


def back_sequence(query_seq, kv_seq, valid_seq, log_seq, grad_seq, query_rows, score_scale):
    blocks = query_seq.shape[0] // query_rows

    def back_block(accumulated, packed):
        query_block, log_block, grad_block = packed
        scores = (
            jnp.einsum(
                "qhd,khd->hqk", query_block, kv_seq[:, 0], preferred_element_type=jnp.float32
            )
            * score_scale
        )
        scores = jnp.where(valid_seq[None, None, :], scores, masked_score)
        probability = jnp.exp(scores - log_block[..., None])
        grad_prob = jnp.einsum(
            "qhd,khd->hqk", grad_block, kv_seq[:, 1], preferred_element_type=jnp.float32
        )
        grad_scores = (
            probability * (grad_prob - jnp.sum(probability * grad_prob, axis=-1, keepdims=True))
        ).astype(jnp.bfloat16)
        grad_query = (
            jnp.einsum(
                "hqk,khd->qhd", grad_scores, kv_seq[:, 0], preferred_element_type=jnp.float32
            )
            * score_scale
        )
        grad_key = (
            jnp.einsum("hqk,qhd->khd", grad_scores, query_block, preferred_element_type=jnp.float32)
            * score_scale
        )
        grad_value = jnp.einsum(
            "hqk,qhd->khd",
            probability.astype(jnp.bfloat16),
            grad_block,
            preferred_element_type=jnp.float32,
        )
        return (accumulated + jnp.stack([grad_key, grad_value], axis=1), grad_query)

    initial = jnp.zeros((kv_seq.shape[0], 2, query_seq.shape[1], query_seq.shape[2]), jnp.float32)
    shaped_query = query_seq.reshape(blocks, query_rows, query_seq.shape[1], query_seq.shape[2])
    shaped_grad = grad_seq.reshape(blocks, query_rows, query_seq.shape[1], query_seq.shape[2])
    accumulated, grad_query = lax.scan(back_block, initial, (shaped_query, log_seq, shaped_grad))
    return (grad_query.reshape(query_seq.shape), accumulated)


def per_device(
    states,
    teacher,
    lengths,
    routes,
    gate_weights,
    w_qkv,
    w_out,
    norm_gains,
    qk_gains,
    w_gate_up,
    w_down,
):
    seq_count, slot_count, model_width = states.shape
    top_count = routes.shape[-1]
    full_len = slot_count * lax.axis_size("ctx")
    tokens = seq_count * slot_count
    shard_experts = w_gate_up.shape[0]
    experts = shard_experts * lax.axis_size(("fsdp", "ctx"))
    capacity = seq_count * (5 * slot_count * top_count // (4 * experts))
    position = lax.axis_index("ctx") * slot_count + jnp.arange(slot_count, dtype=jnp.int32)
    row_valid = (position[None, :] < lengths[:, None]).reshape(tokens)
    key_valid = jnp.arange(full_len, dtype=jnp.int32)[None, :] < lengths[:, None]
    tok_position = jnp.tile(position, seq_count)
    full_qkv, full_out, full_norm, full_qk = (
        lax.all_gather(w_qkv, ("fsdp", "ctx"), axis=0, tiled=True),
        lax.all_gather(w_out, ("fsdp", "ctx"), axis=1, tiled=True),
        lax.all_gather(norm_gains, ("fsdp", "ctx"), axis=1, tiled=True),
        lax.all_gather(qk_gains, ("fsdp", "ctx"), axis=1, tiled=True),
    )
    gain_attn = full_norm[0].astype(jnp.float32)
    gain_ffn = full_norm[1].astype(jnp.float32)
    qk_float = full_qk.astype(jnp.float32)
    head_dim = full_qk.shape[1]
    heads_local = full_qkv.shape[2] // head_dim
    score_scale = head_dim ** (-0.5)
    query_rows = min(512, slot_count)
    flat_states = states.astype(jnp.float32).reshape(tokens, model_width)
    normed = rms_norm(flat_states, gain_attn).astype(jnp.bfloat16)
    projected = jnp.einsum(
        "nd,dkh->nkh", normed, full_qkv, preferred_element_type=jnp.float32
    ).reshape(tokens, 3, heads_local, head_dim)

    def prepare_local(projected_in, gains_in):
        return prepare(projected_in, gains_in, tok_position)

    (queries, key_states, values), prepare_back = jax.vjp(prepare_local, projected, qk_float)
    query_low = queries.astype(jnp.bfloat16).reshape(seq_count, slot_count, heads_local, head_dim)
    key_value = (
        jnp.stack([key_states, values], axis=1)
        .astype(jnp.bfloat16)
        .reshape(seq_count, slot_count, 2, heads_local, head_dim)
    )
    gathered = lax.all_gather(key_value, "ctx", axis=1, tiled=True)

    def attend_one(packed):
        return attend_sequence(packed[0], packed[1], packed[2], query_rows, score_scale)

    attended, log_total = lax.map(attend_one, (query_low, gathered, key_valid))
    attended_low = attended.reshape(tokens, heads_local * head_dim).astype(jnp.bfloat16)
    branch = lax.psum(jnp.dot(attended_low, full_out, preferred_element_type=jnp.float32), "tp")
    middle = flat_states + branch
    normed_ffn = rms_norm(middle, gain_ffn).astype(jnp.bfloat16)
    slot_rows, slot_gate = dispatch(
        routes.reshape(tokens, top_count),
        gate_weights.reshape(tokens, top_count),
        capacity,
        experts,
    )
    hidden_local = w_gate_up.shape[3]

    def expert_forward(running, portion, expert_start):
        expert_total, keep_gate_up = running
        part_gate_up, part_down = portion
        count_here = part_gate_up.shape[0]
        slot_index = lax.dynamic_slice_in_dim(slot_rows, expert_start, count_here, 0)
        slot_weight = lax.dynamic_slice_in_dim(slot_gate, expert_start, count_here, 0)
        expert_in = jnp.take(normed_ffn, slot_index, axis=0)
        gate_up = jnp.einsum(
            "ecd,edkf->eckf", expert_in, part_gate_up, preferred_element_type=jnp.float32
        )
        hidden = (jax.nn.silu(gate_up[:, :, 0]) * gate_up[:, :, 1]).astype(jnp.bfloat16)
        expert_out = jnp.einsum(
            "ecf,efd->ecd", hidden, part_down, preferred_element_type=jnp.float32
        )
        weighted = (expert_out * slot_weight[:, :, None]).reshape(-1, model_width)
        expert_total = expert_total.at[slot_index.reshape(-1)].add(weighted)
        keep_gate_up = lax.dynamic_update_slice_in_dim(keep_gate_up, gate_up, expert_start, 0)
        return (expert_total, keep_gate_up)

    forward_init = (
        jnp.zeros((tokens, model_width), jnp.float32),
        jnp.zeros((experts, capacity, 2, hidden_local), jnp.float32),
    )
    expert_part, gate_up_keep = fold_local(
        (
            lax.all_gather(w_gate_up, ("fsdp", "ctx"), axis=0, tiled=True),
            lax.all_gather(w_down, ("fsdp", "ctx"), axis=0, tiled=True),
        ),
        expert_forward,
        forward_init,
        shard_experts,
    )
    mixture = lax.psum(expert_part, "tp")
    final_state = middle + mixture
    activations = final_state.astype(jnp.bfloat16).reshape(seq_count, slot_count, model_width)
    difference = final_state - teacher.astype(jnp.float32).reshape(tokens, model_width)
    valid_float = row_valid.astype(jnp.float32)
    local_loss = jnp.sum(valid_float * jnp.sum(difference * difference, axis=-1))
    total_loss, valid_count = lax.psum((local_loss, jnp.sum(valid_float)), ("fsdp", "ctx"))
    loss_value = total_loss / valid_count
    grad_final = 2.0 * loss_scale / valid_count * valid_float[:, None] * difference

    def expert_backward(running, portion, expert_start):
        grad_total, keep_grad = running
        part_gate_up, part_down = portion
        count_here = part_gate_up.shape[0]
        slot_index = lax.dynamic_slice_in_dim(slot_rows, expert_start, count_here, 0)
        slot_weight = lax.dynamic_slice_in_dim(slot_gate, expert_start, count_here, 0)
        grad_out_rows = (slot_weight[:, :, None] * jnp.take(grad_final, slot_index, axis=0)).astype(
            jnp.bfloat16
        )
        gate_up = lax.dynamic_slice_in_dim(gate_up_keep, expert_start, count_here, 0)
        gate_part = gate_up[:, :, 0]
        up_part = gate_up[:, :, 1]
        gate_sigmoid = jax.nn.sigmoid(gate_part)
        grad_hidden = jnp.einsum(
            "ecd,efd->ecf", grad_out_rows, part_down, preferred_element_type=jnp.float32
        )
        grad_gate = grad_hidden * up_part * gate_sigmoid * (1.0 + gate_part * (1.0 - gate_sigmoid))
        grad_up = grad_hidden * gate_part * gate_sigmoid
        grad_rows = jnp.stack([grad_gate, grad_up], axis=2).astype(jnp.bfloat16)
        grad_in = jnp.einsum(
            "eckf,edkf->ecd", grad_rows, part_gate_up, preferred_element_type=jnp.float32
        )
        grad_total = grad_total.at[slot_index.reshape(-1)].add(grad_in.reshape(-1, model_width))
        keep_grad = lax.dynamic_update_slice_in_dim(keep_grad, grad_rows, expert_start, 0)
        return (grad_total, keep_grad)

    backward_init = (
        jnp.zeros((tokens, model_width), jnp.float32),
        jnp.zeros((experts, capacity, 2, hidden_local), jnp.bfloat16),
    )
    grad_ffn_part, grad_keep = fold_local(
        (
            lax.all_gather(w_gate_up, ("fsdp", "ctx"), axis=0, tiled=True),
            lax.all_gather(w_down, ("fsdp", "ctx"), axis=0, tiled=True),
        ),
        expert_backward,
        backward_init,
        shard_experts,
    )
    grad_ffn = lax.psum(grad_ffn_part, "tp")
    grad_middle_norm, grad_gain_ffn = norm_back(grad_ffn, middle, gain_ffn)
    grad_middle = grad_final + grad_middle_norm
    slot_index = slot_rows
    expert_in = jnp.take(normed_ffn, slot_index, axis=0)
    grad_rows = grad_keep
    grad_gate_up = lax.psum_scatter(
        jnp.einsum(
            "ecd,eckf->edkf", expert_in, grad_rows, preferred_element_type=jnp.float32
        ).astype(jnp.bfloat16),
        ("fsdp", "ctx"),
        scatter_dimension=0,
        tiled=True,
    ).astype(jnp.float32)
    slot_index = slot_rows
    slot_weight = slot_gate
    gate_up = gate_up_keep
    hidden = (jax.nn.silu(gate_up[:, :, 0]) * gate_up[:, :, 1]).astype(jnp.bfloat16)
    grad_out_rows = (slot_weight[:, :, None] * jnp.take(grad_final, slot_index, axis=0)).astype(
        jnp.bfloat16
    )
    grad_down = lax.psum_scatter(
        jnp.einsum(
            "ecf,ecd->efd", hidden, grad_out_rows, preferred_element_type=jnp.float32
        ).astype(jnp.bfloat16),
        ("fsdp", "ctx"),
        scatter_dimension=0,
        tiled=True,
    ).astype(jnp.float32)
    grad_branch = grad_middle.astype(jnp.bfloat16)
    grad_attended = jnp.einsum(
        "nd,fd->nf", grad_branch, full_out, preferred_element_type=jnp.float32
    ).astype(jnp.bfloat16)
    grad_w_out = jnp.einsum(
        "nf,nd->fd", attended_low, grad_branch, preferred_element_type=jnp.float32
    )

    def back_one(packed):
        return back_sequence(
            packed[0], packed[1], packed[2], packed[3], packed[4], query_rows, score_scale
        )

    grad_query, grad_key_value = lax.map(
        back_one,
        (
            query_low,
            gathered,
            key_valid,
            log_total,
            grad_attended.reshape(seq_count, slot_count, heads_local, head_dim),
        ),
    )
    own_kv = lax.psum_scatter(
        grad_key_value.astype(jnp.bfloat16), "ctx", scatter_dimension=1, tiled=True
    ).astype(jnp.float32)
    grad_projected, grad_qk_part = prepare_back(
        (
            grad_query.reshape(tokens, heads_local, head_dim),
            own_kv[:, :, 0].reshape(tokens, heads_local, head_dim),
            own_kv[:, :, 1].reshape(tokens, heads_local, head_dim),
        )
    )
    grad_proj_low = grad_projected.astype(jnp.bfloat16).reshape(tokens, 3, heads_local * head_dim)
    grad_normed_part = jnp.einsum(
        "nkh,dkh->nd", grad_proj_low, full_qkv, preferred_element_type=jnp.float32
    )
    grad_normed, grad_qk = (
        lax.psum(grad_normed_part.astype(jnp.bfloat16), "tp").astype(jnp.float32),
        lax.psum(grad_qk_part.astype(jnp.bfloat16), "tp").astype(jnp.float32),
    )
    grad_w_qkv = jnp.einsum(
        "nd,nkh->dkh", normed, grad_proj_low, preferred_element_type=jnp.float32
    )
    grad_states_norm, grad_gain_attn = norm_back(grad_normed, flat_states, gain_attn)
    grad_states = (grad_middle + grad_states_norm).reshape(seq_count, slot_count, model_width)
    grad_gains = jnp.stack([grad_gain_attn, grad_gain_ffn], axis=0)
    out_qkv, out_w_out, out_gains, out_qk = (
        lax.psum_scatter(
            grad_w_qkv.astype(jnp.bfloat16), ("fsdp", "ctx"), scatter_dimension=0, tiled=True
        ).astype(jnp.float32),
        lax.psum_scatter(
            grad_w_out.astype(jnp.bfloat16), ("fsdp", "ctx"), scatter_dimension=1, tiled=True
        ).astype(jnp.float32),
        lax.psum_scatter(
            grad_gains.astype(jnp.bfloat16), ("fsdp", "ctx"), scatter_dimension=1, tiled=True
        ).astype(jnp.float32),
        lax.psum_scatter(
            grad_qk.astype(jnp.bfloat16), ("fsdp", "ctx"), scatter_dimension=1, tiled=True
        ).astype(jnp.float32),
    )
    return (
        activations,
        loss_value,
        valid_count,
        grad_states,
        out_qkv,
        out_w_out,
        out_gains,
        out_qk,
        grad_gate_up,
        grad_down,
    )


def solution(mesh):
    placed = (
        P("fsdp", "ctx", None),
        P("fsdp", "ctx", None),
        P("fsdp"),
        P("fsdp", "ctx", None),
        P("fsdp", "ctx", None),
        P(("fsdp", "ctx"), None, "tp"),
        P("tp", ("fsdp", "ctx")),
        P(None, ("fsdp", "ctx")),
        P(None, ("fsdp", "ctx")),
        P(("fsdp", "ctx"), None, None, "tp"),
        P(("fsdp", "ctx"), "tp", None),
    )
    return jax.shard_map(
        per_device,
        mesh=mesh,
        in_specs=placed,
        out_specs=(
            P("fsdp", "ctx", None),
            P(),
            P(),
            P("fsdp", "ctx", None),
            P(("fsdp", "ctx"), None, "tp"),
            P("tp", ("fsdp", "ctx")),
            P(None, ("fsdp", "ctx")),
            P(None, ("fsdp", "ctx")),
            P(("fsdp", "ctx"), None, None, "tp"),
            P(("fsdp", "ctx"), "tp", None),
        ),
        check_vma=False,
    )
```

profile of v0, /device:TPU:0, one launch (start us, length us, event | category | flops | bytes accessed | tf_op | source)
XLA Modules:
  0.0 2688.7 jit_solution(10310771875583334511)
XLA Ops:
  37.2 21.0 all-gather.7.cloned.1.call-done
  77.1 31.9 %all-gather.9.cloned.1.call-done = bf16[1,1024,2,4,128]{1,4,3,2,0:T(8,128)(2,1)} async-done(((bf16[1,512,2,4,128]{1,4,3,2,0:T(8,128)(2,1)}), bf16[1,1024,2,4,128]{1,4,3,2,0:T(8,128)(2,1)}) %all-gather.9.cloned.1.call-update) | async-done | bytes 2097168 | tf_op jit(solution)/shard_map/all_gather | solution.py:201
  118.3 20.8 all-gather.11.cloned.1.call-done
  196.6 102.6 %all-reduce.14.cloned.1.call-done = f32[512,2048]{1,0:T(8,128)} async-done(((f32[512,2048]{1,0:T(8,128)}), f32[512,2048]{1,0:T(8,128)}) %all-reduce.14.cloned.1.call-update) | async-done | bytes 4194320 | tf_op jit(solution)/shard_map/psum | solution.py:208
  304.3 156.5 %all-gather.15.cloned.1.call-done = bf16[32,256,2048]{2,1,0:T(8,128)(2,1)} async-done(((bf16[4,256,2048]{2,1,0:T(8,128)(2,1)}), bf16[32,256,2048]{2,1,0:T(8,128)(2,1)}) %all-gather.15.cloned.1.call-update) | async-done | bytes 33554448 | tf_op jit(solution)/shard_map/all_gather | solution.py:245
  460.9 305.3 %all-gather.13.cloned.1.call-done = bf16[32,2048,2,256]{3,1,2,0:T(8,128)(2,1)} async-done(((bf16[4,2048,2,256]{3,1,2,0:T(8,128)(2,1)}), bf16[32,2048,2,256]{3,1,2,0:T(8,128)(2,1)}) %all-gather.13.cloned.1.call-update) | async-done | bytes 67108880 | tf_op jit(solution)/shard_map/all_gather | solution.py:244
  774.1 284.2 %while.29 = (s32[]{:T(128)}, f32[512,2048]{1,0:T(8,128)}, f32[32,160,2,256]{3,1,2,0:T(8,128)}, s32[32,160]{1,0:T(8,128)S(1)}, bf16[512,2048]{1,0:T(8,128)(2,1)S(...) while((s32[]{:T(128)}, f32[512,2048]{1,0:T(8,128)}, ...), condition=%wide.region_14.15_spmd, body=%wide.region_12.14_spmd.sunk | while | flops 2018189824 | bytes 45398448 | solution.py:76
  791.1 18.8 scatter_fusion
  826.6 18.8 scatter_fusion
  862.1 18.8 scatter_fusion
  933.1 18.8 scatter_fusion
  968.5 18.8 scatter_fusion
  1004.0 18.8 scatter_fusion
  1039.5 18.8 scatter_fusion
  1083.3 130.2 %all-reduce.16.cloned.1.call-done = f32[512,2048]{1,0:T(8,128)} async-done(((f32[512,2048]{1,0:T(8,128)}), f32[512,2048]{1,0:T(8,128)}) %all-reduce.16.cloned.1.call-update) | async-done | bytes 4194320 | tf_op jit(solution)/shard_map/psum | solution.py:251
  1226.5 347.3 %while.30 = (s32[]{:T(128)}, f32[512,2048]{1,0:T(8,128)}, bf16[32,160,2,256]{3,1,2,0:T(8,128)(2,1)}, s32[32,160]{1,0:T(8,128)S(1)}, f32[32,160]{1,0:T(8,128)S(1)...) while((s32[]{:T(128)}, f32[512,2048]{1,0:T(8,128)}, ...), condition=%wide.region_23.24_spmd, body=%wide.region_21.23_spmd.sunk | while | flops 2021302784 | bytes 53263308 | solution.py:76
  1251.2 18.8 scatter_fusion.1
  1294.6 18.8 scatter_fusion.1
  1338.0 18.8 scatter_fusion.1
  1381.3 18.8 scatter_fusion.1
  1424.7 18.8 scatter_fusion.1
  1468.1 18.8 scatter_fusion.1
  1554.9 18.8 scatter_fusion.1
  1574.5 153.5 %all-reduce.18.cloned.1.call-done = f32[512,2048]{1,0:T(8,128)} async-done(((f32[512,2048]{1,0:T(8,128)}), f32[512,2048]{1,0:T(8,128)}) %all-reduce.18.cloned.1.call-update) | async-done | bytes 4194320 | tf_op jit(solution)/shard_map/psum | solution.py:300
  1760.1 26.4 reduce-scatter.12.cloned.1.call-done
  1804.5 80.7 %all-reduce.20.cloned.1.call-done = bf16[512,2048]{1,0:T(8,128)(2,1)} async-done(((bf16[512,2048]{1,0:T(8,128)(2,1)}), bf16[512,2048]{1,0:T(8,128)(2,1)}) %all-reduce.20.cloned.1.call-update) | async-done | bytes 2097168 | tf_op jit(solution)/shard_map/psum | solution.py:367
  1897.3 41.6 %gather_fusion.3 = f32[5120,2048]{1,0:T(8,128)} fusion(f32[512,2048]{1,0:T(8,128)} %get-tuple-element.787, s32[5120]{0:T(1024)S(1)} %broadcast_clamp_fusion), kind=kCustom, calls=%fused_computation.3 | custom fusion | bytes 83906560 | tf_op jit(solution)/shard_map/jit(_take)/gather | solution.py:318
  1938.9 30.5 %fusion.43 = bf16[32,256,2048]{2,1,0:T(8,128)(2,1)} fusion(f32[32,160,2048]{2,1,0:T(8,128)} %bitcast.265, f32[32,160]{1,0:T(8,128)S(1)} %copy-done.27, pred[32,160]{1,0:T(8,128)(4,1)S(1)} %compare_and_fusion.2, f32[32,160,2,256]{3,1,2,0:T(8,128)} %get-tuple-element.471), kind=kOutput, calls=%fused_computation.73 | convolution fusion | flops 5424807936 | bytes 86008832 | tf_op jit(solution)/shard_map/ecf,ecd->efd/dot_general | solution.py:322
  1971.0 26.0 gather_fusion.2
  1997.0 38.9 %convolution_convert_fusion = bf16[32,2048,2,256]{3,1,2,0:T(8,128)(2,1)} fusion(bf16[32,160,2,256]{3,1,2,0:T(8,128)(2,1)} %get-tuple-element.406, bf16[32,160,2048]{2,1,0:T(8,128)(2,1)} %bitcast.269, pred[32,160]{1,0:T(8,128)(4,1)S(1)} %compare_and_fusion.2), kind=kOutput, calls=%fused_computation.65 | convolution fusion | flops 10781458432 | bytes 93328384 | tf_op jit(solution)/shard_map/ecd,eckf->edkf/dot_general | solution.py:307
  2075.1 200.9 %reduce-scatter.20.cloned.1.call-done = bf16[4,256,2048]{2,1,0:T(8,128)(2,1)} async-done(((bf16[32,256,2048]{2,1,0:T(8,128)(2,1)}), bf16[4,256,2048]{2,1,0:T(8,128)(2,1)}) %reduce-scatter.20.cloned.1.call-update) | async-done | bytes 4194320 | tf_op jit(solution)/shard_map/reduce_scatter | solution.py:321
  2282.7 380.6 %reduce-scatter.18.cloned.1.call-done = bf16[4,2048,2,256]{3,1,2,0:T(8,128)(2,1)} async-done(((bf16[32,2048,2,256]{3,1,2,0:T(8,128)(2,1)}), bf16[4,2048,2,256]{3,1,2,0:T(8,128)(2,1)}) %reduce-scatter.18.cloned.1.call-update) | async-done | bytes 8388624 | tf_op jit(solution)/shard_map/reduce_scatter | solution.py:306
  (449 shorter events, 657.8 us)
Async XLA Ops:
  7.2 51.0 %all-gather.7.cloned.1.call-start = ((), (), s32[]{:S(2)}) async-start(), calls=%async_computation.7 | async-start | bytes 7077888 | tf_op jit(solution)/shard_map/all_gather | solution.py:173
  7.9 101.1 %all-gather.9.cloned.1.call-start = ((), (), s32[]{:S(2)}) async-start(), calls=%async_computation.8 | async-start | bytes 3145728 | tf_op jit(solution)/shard_map/all_gather | solution.py:201
  34.5 38.8 %copy-start.58 = (f32[128]{0:T(128)}, f32[128]{0:T(128)S(1)}, u32[]{:S(2)}) copy-start(f32[128]{0:T(128)S(1)} %get-tuple-element.563) | copy-start | bytes 1540
  34.5 38.8 %copy-start.60 = (f32[128]{0:T(128)}, f32[128]{0:T(128)S(1)}, u32[]{:S(2)}) copy-start(f32[128]{0:T(128)S(1)} %get-tuple-element.564) | copy-start | bytes 1540
  37.1 36.4 %copy-start.22 = (f32[512,64]{0,1:T(8,128)}, f32[512,64]{0,1:T(8,128)S(1)}, u32[]{:S(2)}) copy-start(f32[512,64]{0,1:T(8,128)S(1)} %get-tuple-element.561) | copy-start | bytes 393220
  37.2 264.8 %copy-start.30 = (f32[1,2048]{1,0:T(1,128)}, f32[1,2048]{1,0:T(1,128)S(1)}, u32[]{:S(2)}) copy-start(f32[1,2048]{1,0:T(1,128)S(1)} %get-tuple-element.559) | copy-start | bytes 24580
  74.5 37.2 %copy-start.17 = (bf16[512,4,64]{0,2,1:T(8,128)(2,1)}, bf16[512,4,64]{0,2,1:T(8,128)(2,1)S(1)}, u32[]{:S(2)}) copy-start(bf16[512,4,64]{0,2,1:T(8,128)(2,1)S(1)} %get-tuple-element.551) | copy-start | bytes 786436
  74.5 37.2 %copy-start.19 = (bf16[512,4,64]{0,2,1:T(8,128)(2,1)}, bf16[512,4,64]{0,2,1:T(8,128)(2,1)S(1)}, u32[]{:S(2)}) copy-start(bf16[512,4,64]{0,2,1:T(8,128)(2,1)S(1)} %get-tuple-element.552) | copy-start | bytes 786436
  75.7 63.4 %all-gather.11.cloned.1.call-start = ((), (), s32[]{:S(2)}) async-start(), calls=%async_computation.9 | async-start | bytes 2359296 | tf_op jit(solution)/shard_map/all_gather | solution.py:174
  76.4 222.7 %all-reduce.14.cloned.1.call-start = ((), (), s32[]{:S(2)}) async-start(), calls=%async_computation.10 | async-start | bytes 8388608 | tf_op jit(solution)/shard_map/psum | solution.py:208
  77.1 36.7 %copy-start.52 = (pred[1024]{0:T(1024)(128)(4,1)}, pred[1024]{0:T(1024)(128)(4,1)S(1)}, u32[]{:S(2)}) copy-start(pred[1024]{0:T(1024)(128)(4,1)S(1)} %iota_compare_fusion.2) | copy-start | bytes 3076
  144.0 316.8 %all-gather.15.cloned.1.call-start = ((), (), s32[]{:S(2)}) async-start(), calls=%async_computation.12 | async-start | bytes 37748736 | tf_op jit(solution)/shard_map/all_gather | solution.py:245
  144.6 621.6 %all-gather.13.cloned.1.call-start = ((), (), s32[]{:S(2)}) async-start(), calls=%async_computation.11 | async-start | bytes 75497472 | tf_op jit(solution)/shard_map/all_gather | solution.py:244
  152.6 1060.9 %all-reduce.16.cloned.1.call-start = ((), (), s32[]{:S(2)}) async-start(), calls=%async_computation.13 | async-start | bytes 8388608 | tf_op jit(solution)/shard_map/psum | solution.py:251
  302.0 466.8 %copy-start.45 = (f32[512]{0:T(512)}, f32[512]{0:T(512)S(1)}, u32[]{:S(2)}) copy-start(f32[512]{0:T(512)S(1)} %add_rsqrt_fusion) | copy-start | bytes 6148
  1058.3 669.6 %all-reduce.18.cloned.1.call-start = ((), (), s32[]{:S(2)}) async-start(), calls=%async_computation.14 | async-start | bytes 8388608 | tf_op jit(solution)/shard_map/psum | solution.py:300
  1573.7 161.7 %copy-start.26 = (f32[32,160]{1,0:T(8,128)}, f32[32,160]{1,0:T(8,128)S(1)}, u32[]{:S(2)}) copy-start(f32[32,160]{1,0:T(8,128)S(1)} %get-tuple-element.829) | copy-start | bytes 61444
  1573.7 154.2 %copy-start.13 = (bf16[1,512,2048]{2,1,0:T(8,128)(2,1)S(1)}, bf16[1,512,2048]{2,1,0:T(8,128)(2,1)}, u32[]{:S(2)}) copy-start(bf16[1,512,2048]{2,1,0:T(8,128)(2,1)} %param.16) | copy-start | bytes 6291460
  1573.8 154.2 %copy-start.31 = (f32[1,2048]{1,0:T(1,128)S(1)}, f32[1,2048]{1,0:T(1,128)}, u32[]{:S(2)}) copy-start(f32[1,2048]{1,0:T(1,128)} %copy-done.30) | copy-start | bytes 24580
  1573.8 154.2 %copy-start.46 = (f32[512]{0:T(512)S(1)}, f32[512]{0:T(512)}, u32[]{:S(2)}) copy-start(f32[512]{0:T(512)} %copy-done.45) | copy-start | bytes 6148
  1573.8 212.7 %reduce-scatter.12.cloned.1.call-start = ((), (), s32[]{:S(2)}) async-start(), calls=%async_computation.15 | async-start | bytes 3145728 | tf_op jit(solution)/shard_map/reduce_scatter | solution.py:352
  1755.5 129.7 %all-reduce.20.cloned.1.call-start = ((), (), s32[]{:S(2)}) async-start(), calls=%async_computation.16 | async-start | bytes 4194304 | tf_op jit(solution)/shard_map/psum | solution.py:367
  1798.6 86.7 %copy-start.8 = (bf16[1,512,2048]{2,1,0:T(8,128)(2,1)S(1)}, bf16[1,512,2048]{2,1,0:T(8,128)(2,1)}, u32[]{:S(2)}) copy-start(bf16[1,512,2048]{2,1,0:T(8,128)(2,1)} %param.15) | copy-start | bytes 6291460
  1798.6 86.7 %copy-start.37 = (f32[1,2048]{1,0:T(1,128)S(1)}, f32[1,2048]{1,0:T(1,128)}, u32[]{:S(2)}) copy-start(f32[1,2048]{1,0:T(1,128)} %copy-done.36) | copy-start | bytes 24580
  1798.6 86.6 %copy-start.50 = (f32[512]{0:T(512)S(1)}, f32[512]{0:T(512)}, u32[]{:S(2)}) copy-start(f32[512]{0:T(512)} %copy-done.49) | copy-start | bytes 6148
  1798.6 254.2 %reduce-scatter.16.cloned.1.call-start = ((), (), s32[]{:S(2)}) async-start(), calls=%async_computation.18 | async-start | bytes 2359296 | tf_op jit(solution)/shard_map/reduce_scatter | solution.py:380
  1803.6 251.0 %reduce-scatter.24.cloned.1.call-start = ((), (), s32[]{:S(2)}) async-start(), calls=%async_computation.22 | async-start | bytes 36864
  1804.5 266.7 %reduce-scatter.22.cloned.1.call-start = ((), (), s32[]{:S(2)}) async-start(), calls=%async_computation.21 | async-start | bytes 589824
  1889.9 182.8 %reduce-scatter.14.cloned.1.call-start = ((), (), s32[]{:S(2)}) async-start(), calls=%async_computation.17 | async-start | bytes 7077888 | tf_op jit(solution)/shard_map/reduce_scatter | solution.py:377
  1897.1 378.9 %reduce-scatter.20.cloned.1.call-start = ((), (), s32[]{:S(2)}) async-start(), calls=%async_computation.20 | async-start | bytes 37748736 | tf_op jit(solution)/shard_map/reduce_scatter | solution.py:321
  1897.3 41.6 %copy-start.27 = (f32[32,160]{1,0:T(8,128)S(1)}, f32[32,160]{1,0:T(8,128)}, u32[]{:S(2)}) copy-start(f32[32,160]{1,0:T(8,128)} %copy-done.26) | copy-start | bytes 61444
  1969.4 693.8 %reduce-scatter.18.cloned.1.call-start = ((), (), s32[]{:S(2)}) async-start(), calls=%async_computation.19 | async-start | bytes 75497472 | tf_op jit(solution)/shard_map/reduce_scatter | solution.py:306
  (52 other events, 471.3 us)
Sparse Core Ops, SparseCore 0:
  9.9 48.2 all-gather.6
  75.8 33.1 all-gather.8
  110.9 28.1 all-gather.10
  144.1 154.9 all-reduce.13
  301.0 159.7 all-gather.14
  463.3 302.8 all-gather.12
  1058.5 154.9 all-reduce.15
  1573.9 153.9 all-reduce.17
  1755.6 30.8 reduce-scatter.11
  1798.7 86.4 all-reduce.19
  1888.9 40.1 reduce-scatter.15
  1932.0 31.2 reduce-scatter.23
  1966.6 34.1 reduce-scatter.21
  2004.6 62.2 reduce-scatter.13
  2070.7 205.2 reduce-scatter.19
  2279.4 383.7 reduce-scatter.17
where the time goes:
time: 2700 us; the launch traced here: 2690 us
  waiting for transfers between devices  1610 us (60%)
  other arithmetic  378 us (14%)
  matrix products  331 us (12%)
  local copies, waits for them, and re-layouts  283 us (10%)
  blocking collectives  63.8 us (2%)
    reduce_scatter x1, waiting for transfers between devices, per_device(): lax.psum_scatter(jnp.einsum('ecd,eckf->edkf', expert_in, grad_rows, prefe...  381 us
    all_gather x1, waiting for transfers between devices, per_device(): lax.all_gather(w_gate_up, ('fsdp', 'ctx'), axis=0, tiled=True)  305 us
    reduce_scatter x1, waiting for transfers between devices, per_device(): lax.psum_scatter(jnp.einsum('ecf,ecd->efd', hidden, grad_out_rows, prefer...  201 us
    all_gather x1, waiting for transfers between devices, per_device(): lax.all_gather(w_down, ('fsdp', 'ctx'), axis=0, tiled=True)  157 us
    psum x1, waiting for transfers between devices, per_device(): grad_ffn = lax.psum(grad_ffn_part, 'tp')  153 us
    scatter-add x8, other arithmetic, expert_forward(): expert_total = expert_total.at[slot_index.reshape(-1)].add(weighted)  151 us
    scatter-add x8, other arithmetic, expert_backward(): grad_total.at[slot_index.reshape(-1)].add(grad_in.reshape(-1, model_width))  151 us
    psum x1, waiting for transfers between devices, per_device(): mixture = lax.psum(expert_part, 'tp')  130 us
  transfers between devices with their start and end apart: 16, of which 12 were waited for; matrix products, arithmetic and copies ran while one was open for 9% of the time, Pallas kernels for 0%

commit v1 on v0

v1 whole, which is shorter than its diff:
```python
import jax
import jax.numpy as jnp
from jax import lax
from jax.experimental import pallas as pl
from jax.experimental.pallas import tpu as pltpu
from jax.sharding import PartitionSpec as P

norm_eps = 1e-05
rope_base = 10000.0
loss_scale = 4096.0
masked_score = -1e30
plane = ("fsdp", "ctx")
everywhere = ("fsdp", "ctx", "tp")
low = jnp.bfloat16
wide = jnp.float32


def rms_norm(values, gain_vec):
    return (
        values * lax.rsqrt(jnp.mean(values * values, axis=-1, keepdims=True) + norm_eps) * gain_vec
    )


def norm_back(grad_normed, values, gain_vec):
    inverse = lax.rsqrt(jnp.mean(values * values, axis=-1, keepdims=True) + norm_eps)
    scaled = values * inverse
    grad_scaled = grad_normed * gain_vec
    grad_values = inverse * (
        grad_scaled - scaled * jnp.mean(grad_scaled * scaled, axis=-1, keepdims=True)
    )
    return (grad_values, jnp.sum(grad_normed * scaled, axis=0))


def rotate(values, position):
    half_dim = values.shape[-1] // 2
    frequency = rope_base ** (-2.0 * jnp.arange(half_dim, dtype=wide) / values.shape[-1])
    angles = position.astype(wide)[:, None] * frequency[None, :]
    cosine = jnp.cos(angles)[:, None, :]
    sine_part = jnp.sin(angles)[:, None, :]
    first_half = values[..., :half_dim]
    second_half = values[..., half_dim:]
    return jnp.concatenate(
        [
            first_half * cosine - second_half * sine_part,
            second_half * cosine + first_half * sine_part,
        ],
        axis=-1,
    )


def prepare(projected, qk_float, position):
    queries = rotate(rms_norm(projected[:, 0], qk_float[0]), position)
    key_states = rotate(rms_norm(projected[:, 1], qk_float[1]), position)
    return (queries, key_states, projected[:, 2])


def attend_sequence(query_seq, kv_seq, valid_seq, score_scale):
    scores = (
        jnp.einsum("qhd,khd->hqk", query_seq, kv_seq[:, 0], preferred_element_type=wide)
        * score_scale
    )
    scores = jnp.where(valid_seq[None, None, :], scores, masked_score)
    peak_score = jnp.max(scores, axis=-1, keepdims=True)
    exponent = jnp.exp(scores - peak_score)
    row_total = jnp.sum(exponent, axis=-1, keepdims=True)
    probability = (exponent / row_total).astype(low)
    output = jnp.einsum("hqk,khd->qhd", probability, kv_seq[:, 1], preferred_element_type=wide)
    return (output, (peak_score + jnp.log(row_total))[..., 0])


def back_sequence(query_seq, kv_seq, valid_seq, log_seq, grad_seq, score_scale):
    scores = (
        jnp.einsum("qhd,khd->hqk", query_seq, kv_seq[:, 0], preferred_element_type=wide)
        * score_scale
    )
    scores = jnp.where(valid_seq[None, None, :], scores, masked_score)
    probability = jnp.exp(scores - log_seq[..., None])
    grad_prob = jnp.einsum("qhd,khd->hqk", grad_seq, kv_seq[:, 1], preferred_element_type=wide)
    grad_scores = (
        probability * (grad_prob - jnp.sum(probability * grad_prob, axis=-1, keepdims=True))
    ).astype(low)
    grad_query = (
        jnp.einsum("hqk,khd->qhd", grad_scores, kv_seq[:, 0], preferred_element_type=wide)
        * score_scale
    )
    grad_key = (
        jnp.einsum("hqk,qhd->khd", grad_scores, query_seq, preferred_element_type=wide)
        * score_scale
    )
    grad_value = jnp.einsum(
        "hqk,qhd->khd", probability.astype(low), grad_seq, preferred_element_type=wide
    )
    return (grad_query, jnp.stack([grad_key, grad_value], axis=1))


def route_tables(route_rows, gate_rows, experts):
    slots = route_rows.shape[0]
    hit = route_rows[None, :, :] == jnp.arange(experts, dtype=jnp.int32)[:, None, None]
    named = jnp.sum(hit.astype(wide), axis=-1)
    gates = jnp.sum(jnp.where(hit, gate_rows[None, :, :], 0.0), axis=-1)
    order = jnp.arange(slots, dtype=jnp.int32)
    before = (order[:, None] < order[None, :]).astype(low)
    rank = jnp.dot(named.astype(low), before, preferred_element_type=wide)
    return jnp.stack([jnp.where(named > 0.0, rank, -1.0), gates], axis=1)


def pick_rows(table_ref, block, capacity, slots):
    rank = table_ref[block, 0, 0:1, :].astype(jnp.int32)
    gate = table_ref[block, 0, 1:2, :]
    match = lax.broadcasted_iota(jnp.int32, (capacity, slots), 0) == rank
    chosen = jnp.where(match, 1.0, 0.0).astype(low)
    weight = jnp.sum(jnp.where(match, gate, 0.0), axis=1, keepdims=True)
    return (chosen, weight)


def spread_rows(place_ref, block, experts, capacity, slots):
    column = lax.broadcasted_iota(jnp.int32, (slots, experts * capacity), 1)
    match = column == place_ref[block, :, 0:1]
    for expert in range(1, experts):
        match = match | (column == place_ref[block, :, expert : expert + 1])
    return jnp.where(match, 1.0, 0.0).astype(low)


def nt_dot(left, right):
    return lax.dot_general(left, right, (((1,), (1,)), ((), ())), preferred_element_type=wide)


def tiles_of(width, most=512):
    step = min(width, most)
    return [slice(begin, begin + step) for begin in range(0, width, step)]


def combine_blocks(place_ref, rows_ref, out_ref, blocks, experts, capacity, slots, width):
    for block in range(blocks):
        matrix = spread_rows(place_ref, block, experts, capacity, slots)
        for cut in tiles_of(width):
            out_ref[block * slots : (block + 1) * slots, cut] = jnp.dot(
                matrix, rows_ref[block, :, cut], preferred_element_type=wide
            ).astype(low)


def forward_body(
    x_ref, table_ref, place_ref, up_ref, down_ref, out_ref, rows_ref, gate_up_ref, hidden_ref, y_ref
):
    expert = pl.program_id(1)
    experts = pl.num_programs(1)
    blocks, capacity, width = rows_ref.shape[1:]
    slots = x_ref.shape[0] // blocks
    half = down_ref.shape[1]
    weights = []
    for block in range(blocks):
        chosen, weight = pick_rows(table_ref, block, capacity, slots)
        weights.append(weight)
        for cut in tiles_of(width):
            rows_ref[0, block, :, cut] = jnp.dot(
                chosen,
                x_ref[block * slots : (block + 1) * slots, cut],
                preferred_element_type=wide,
            ).astype(low)
    rows = rows_ref[0].reshape(blocks * capacity, width)
    gate_up = jnp.dot(rows, up_ref[0], preferred_element_type=wide)
    gate_up_ref[0] = gate_up.reshape(blocks, capacity, 2 * half)
    gate_part = gate_up[:, :half]
    up_part = gate_up[:, half:]
    weight = jnp.concatenate(weights, axis=0)
    hidden = (gate_part * jax.nn.sigmoid(gate_part) * up_part * weight).astype(low)
    hidden_ref[0] = hidden.reshape(blocks, capacity, half)
    begin = pl.multiple_of(expert * capacity, 16)
    for cut in tiles_of(width):
        y_ref[:, pl.ds(begin, capacity), cut] = (
            jnp.dot(hidden, down_ref[0, :, cut], preferred_element_type=wide)
            .astype(low)
            .reshape(blocks, capacity, -1)
        )
    total = y_ref.shape[1] // capacity

    @pl.when(expert == experts - 1)
    def _():
        combine_blocks(place_ref, y_ref, out_ref, blocks, total, capacity, slots, width)


def backward_body(
    x_ref, table_ref, place_ref, up_ref, down_ref, gate_up_ref, out_ref, rows_ref, grad_ref, y_ref
):
    expert = pl.program_id(1)
    experts = pl.num_programs(1)
    blocks, capacity, width = rows_ref.shape[1:]
    slots = x_ref.shape[0] // blocks
    half = down_ref.shape[1]
    weights = []
    for block in range(blocks):
        chosen, weight = pick_rows(table_ref, block, capacity, slots)
        weights.append(weight)
        for cut in tiles_of(width):
            rows_ref[0, block, :, cut] = jnp.dot(
                chosen,
                x_ref[block * slots : (block + 1) * slots, cut],
                preferred_element_type=wide,
            ).astype(low)
    rows = rows_ref[0].reshape(blocks * capacity, width)
    weight = jnp.concatenate(weights, axis=0)
    grad_hidden = nt_dot(rows, down_ref[0]) * weight
    gate_up = gate_up_ref[0].reshape(blocks * capacity, 2 * half)
    gate_part = gate_up[:, :half]
    up_part = gate_up[:, half:]
    sigmoid = jax.nn.sigmoid(gate_part)
    grad_gate = grad_hidden * up_part * sigmoid * (1.0 + gate_part * (1.0 - sigmoid))
    grad_up = grad_hidden * gate_part * sigmoid
    grad_rows = jnp.concatenate([grad_gate, grad_up], axis=1).astype(low)
    grad_ref[0] = grad_rows.reshape(blocks, capacity, 2 * half)
    begin = pl.multiple_of(expert * capacity, 16)
    for cut in tiles_of(width):
        y_ref[:, pl.ds(begin, capacity), cut] = (
            nt_dot(grad_rows, up_ref[0, cut, :]).astype(low).reshape(blocks, capacity, -1)
        )
    total = y_ref.shape[1] // capacity

    @pl.when(expert == experts - 1)
    def _():
        combine_blocks(place_ref, y_ref, out_ref, blocks, total, capacity, slots, width)


def expert_call(body, x, table, place, w_up, w_down, gate_up, capacity, group):
    blocks, experts, _, slots = table.shape
    width = x.shape[1]
    double, half = w_up.shape[2], w_down.shape[1]
    backward = gate_up is not None
    row_spec = lambda last: pl.BlockSpec((1, group, capacity, last), lambda c, e: (e, c, 0, 0))
    row_shape = lambda last, kind: jax.ShapeDtypeStruct((experts, blocks, capacity, last), kind)
    in_specs = [
        pl.BlockSpec((group * slots, width), lambda c, e: (c, 0)),
        pl.BlockSpec((group, 1, 2, slots), lambda c, e: (c, e, 0, 0)),
        pl.BlockSpec((group, slots, experts), lambda c, e: (c, 0, 0)),
        pl.BlockSpec((1, width, double), lambda c, e: (e, 0, 0)),
        pl.BlockSpec((1, half, width), lambda c, e: (e, 0, 0)),
    ]
    operands = [x, table, place, w_up, w_down]
    out_specs = [pl.BlockSpec((group * slots, width), lambda c, e: (c, 0)), row_spec(width)]
    out_shape = [jax.ShapeDtypeStruct(x.shape, low), row_shape(width, low)]
    if backward:
        in_specs.append(row_spec(double))
        operands.append(gate_up)
        out_specs.append(row_spec(double))
        out_shape.append(row_shape(double, low))
    else:
        out_specs += [row_spec(double), row_spec(half)]
        out_shape += [row_shape(double, wide), row_shape(half, low)]
    rows = experts * blocks * capacity
    return pl.pallas_call(
        body,
        grid=(blocks // group, experts),
        in_specs=in_specs,
        out_specs=out_specs,
        out_shape=out_shape,
        scratch_shapes=[pltpu.VMEM((group, experts * capacity, width), low)],
        compiler_params=pltpu.CompilerParams(
            dimension_semantics=("arbitrary", "arbitrary"), vmem_limit_bytes=60 << 20
        ),
        cost_estimate=pl.CostEstimate(
            flops=2 * rows * width * (2 * slots + double + half),
            bytes_accessed=2 * x.size * 2 + rows * (2 * width + 6 * double),
            transcendentals=rows * half,
        ),
    )(*operands)


def per_device(
    states,
    teacher,
    lengths,
    routes,
    gate_weights,
    w_qkv,
    w_out,
    norm_gains,
    qk_gains,
    w_gate_up,
    w_down,
):
    seq_count, slot_count, width = states.shape
    top_count = routes.shape[-1]
    ctx_size = lax.axis_size("ctx")
    tp_size = lax.axis_size("tp")
    shards = lax.axis_size(plane)
    ctx_index = lax.axis_index("ctx")
    tp_index = lax.axis_index("tp")
    plane_index = lax.axis_index(plane)
    tokens = seq_count * slot_count
    part = tokens // tp_size
    shard_experts = w_gate_up.shape[0]
    hidden_local = w_gate_up.shape[3]
    experts = shard_experts * shards
    capacity = 5 * tokens * top_count // (4 * experts)
    own_slots = jnp.arange(slot_count, dtype=jnp.int32)
    position = ctx_index * slot_count + own_slots
    tok_position = jnp.tile(position, seq_count)
    row_valid = (position[None, :] < lengths[:, None]).reshape(tokens).astype(wide)
    mirror = [(i, (i + 1) % ctx_size) for i in range(ctx_size)]

    gain_cols, head_cols = norm_gains.shape[1], qk_gains.shape[1]
    small = jnp.concatenate(
        [
            norm_gains.astype(wide).reshape(-1),
            qk_gains.astype(wide).reshape(-1),
            jnp.sum(lengths).astype(wide)[None],
        ]
    )
    small_all = lax.all_gather(small, plane, axis=0)
    gain_rows = small_all[:, : 2 * gain_cols].reshape(shards, 2, gain_cols)
    full_gains = jnp.swapaxes(gain_rows, 0, 1).reshape(2, shards * gain_cols)
    head_rows = small_all[:, 2 * gain_cols : 2 * (gain_cols + head_cols)]
    qk_float = jnp.swapaxes(head_rows.reshape(shards, 2, head_cols), 0, 1).reshape(
        2, shards * head_cols
    )
    valid_count = jnp.sum(small_all[:, -1]) / ctx_size
    gain_attn, gain_ffn = full_gains[0], full_gains[1]
    head_dim = qk_float.shape[1]
    heads_local = w_qkv.shape[2] // head_dim
    score_scale = head_dim ** (-0.5)

    tables = route_tables(
        routes.reshape(tokens, top_count), gate_weights.reshape(tokens, top_count), experts
    )
    table = lax.all_to_all(tables, plane, split_axis=0, concat_axis=0, tiled=True).reshape(
        shards, shard_experts, 2, tokens
    )
    rank = table[:, :, 0].astype(jnp.int32)
    offset = (jnp.arange(shard_experts, dtype=jnp.int32) * capacity)[None, :, None]
    place = jnp.swapaxes(jnp.where(rank >= 0, rank + offset, -1), 1, 2)
    w_up = w_gate_up.reshape(shard_experts, width, 2 * hidden_local)

    full_qkv = lax.all_gather(w_qkv, plane, axis=0, tiled=True)
    full_out = lax.all_gather(
        lax.all_gather(w_out, "tp", axis=0, tiled=True), plane, axis=1, tiled=True
    )
    flat_states = states.astype(wide).reshape(tokens, width)
    normed = rms_norm(flat_states, gain_attn).astype(low)
    projected = jnp.einsum(
        "nd,dkh->nkh", normed, full_qkv, preferred_element_type=wide
    ).reshape(tokens, 3, heads_local, head_dim)

    def prepare_local(projected_in, gains_in):
        return prepare(projected_in, gains_in, tok_position)

    (queries, key_states, values), prepare_back = jax.vjp(prepare_local, projected, qk_float)
    query_low = queries.astype(low).reshape(seq_count, slot_count, heads_local, head_dim)
    key_value = (
        jnp.stack([key_states, values], axis=1)
        .astype(low)
        .reshape(seq_count, slot_count, 2, heads_local, head_dim)
    )
    other_kv = lax.ppermute(key_value, "ctx", mirror)
    gathered = jnp.concatenate([key_value, other_kv], axis=1)
    other_position = (1 - ctx_index) * slot_count + own_slots
    key_position = jnp.concatenate([position, other_position])
    key_valid = key_position[None, :] < lengths[:, None]
    pieces = [
        attend_sequence(query_low[i], gathered[i], key_valid[i], score_scale)
        for i in range(seq_count)
    ]
    attended_low = (
        jnp.stack([p[0] for p in pieces]).astype(low).reshape(tokens, heads_local * head_dim)
    )
    attended_all = lax.all_gather(attended_low, "tp", axis=1, tiled=True)
    middle = flat_states + jnp.dot(attended_all, full_out, preferred_element_type=wide)
    normed_ffn = rms_norm(middle, gain_ffn).astype(low)

    x_all = lax.all_gather(normed_ffn, plane, axis=0, tiled=True)
    partial_out, rows_in, gate_up, hidden = expert_call(
        forward_body, x_all, table, place, w_up, w_down, None, capacity, 2
    )
    begin = tp_index * part
    own = lambda a: lax.dynamic_slice_in_dim(a, begin, part, 0)
    mixture = lax.psum_scatter(
        lax.psum_scatter(partial_out, plane, scatter_dimension=0, tiled=True),
        "tp",
        scatter_dimension=0,
        tiled=True,
    ).astype(wide)
    middle_own = own(middle)
    final_own = middle_own + mixture
    difference = final_own - own(teacher.reshape(tokens, width)).astype(wide)
    valid_own = own(row_valid)
    local_loss = jnp.sum(valid_own * jnp.sum(difference * difference, axis=-1))
    grad_final = 2.0 * loss_scale / valid_count * valid_own[:, None] * difference
    activations = lax.all_gather(final_own.astype(low), "tp", axis=0, tiled=True).reshape(
        seq_count, slot_count, width
    )

    grad_block = lax.all_gather(grad_final.astype(low), "tp", axis=0, tiled=True)
    grad_all = lax.all_gather(grad_block, plane, axis=0, tiled=True)
    partial_in, rows_out, grad_rows = expert_call(
        backward_body, grad_all, table, place, w_up, w_down, gate_up, capacity, 2
    )
    grad_ffn = lax.psum_scatter(
        lax.psum_scatter(partial_in, plane, scatter_dimension=0, tiled=True),
        "tp",
        scatter_dimension=0,
        tiled=True,
    ).astype(wide)
    grad_gate_up = jnp.einsum(
        "ebcd,ebcf->edf", rows_in, grad_rows, preferred_element_type=wide
    ).reshape(shard_experts, width, 2, hidden_local)
    grad_down = jnp.einsum("ebcf,ebcd->efd", hidden, rows_out, preferred_element_type=wide)

    grad_middle_norm, grad_gain_ffn = norm_back(grad_ffn, middle_own, gain_ffn)
    grad_middle = grad_final + grad_middle_norm
    grad_branch = grad_middle.astype(low)

    grad_attended = lax.all_to_all(
        nt_dot(grad_branch, full_out).astype(low), "tp", split_axis=1, concat_axis=0, tiled=True
    )
    branch_block = lax.all_gather(grad_branch, "tp", axis=0, tiled=True)
    grad_w_out = jnp.einsum("nf,nd->fd", attended_low, branch_block, preferred_element_type=wide)
    grad_heads = grad_attended.reshape(seq_count, slot_count, heads_local, head_dim)
    backs = [
        back_sequence(
            query_low[i], gathered[i], key_valid[i], pieces[i][1], grad_heads[i], score_scale
        )
        for i in range(seq_count)
    ]
    grad_query = jnp.stack([b[0] for b in backs])
    grad_kv = jnp.stack([b[1] for b in backs])
    sent_kv = grad_kv[:, slot_count:].astype(low)
    own_kv = grad_kv[:, :slot_count] + lax.ppermute(sent_kv, "ctx", mirror).astype(wide)
    grad_projected, grad_qk = prepare_back(
        (
            grad_query.reshape(tokens, heads_local, head_dim),
            own_kv[:, :, 0].reshape(tokens, heads_local, head_dim),
            own_kv[:, :, 1].reshape(tokens, heads_local, head_dim),
        )
    )
    grad_proj_low = grad_projected.astype(low).reshape(tokens, 3, heads_local * head_dim)
    grad_normed = lax.psum_scatter(
        jnp.einsum("nkh,dkh->nd", grad_proj_low, full_qkv, preferred_element_type=wide).astype(low),
        "tp",
        scatter_dimension=0,
        tiled=True,
    ).astype(wide)
    grad_w_qkv = jnp.einsum("nd,nkh->dkh", normed, grad_proj_low, preferred_element_type=wide)
    grad_states_norm, grad_gain_attn = norm_back(grad_normed, own(flat_states), gain_attn)
    grad_states = (
        lax.all_gather((grad_middle + grad_states_norm).astype(low), "tp", axis=0, tiled=True)
        .astype(wide)
        .reshape(seq_count, slot_count, width)
    )
    sums = lax.psum(
        jnp.concatenate(
            [grad_gain_attn, grad_gain_ffn, grad_qk.reshape(-1), local_loss[None]]
        ),
        everywhere,
    )
    out_gains = lax.dynamic_slice_in_dim(
        sums[: 2 * width].reshape(2, width), plane_index * gain_cols, gain_cols, 1
    )
    out_qk = lax.dynamic_slice_in_dim(
        sums[2 * width : 2 * (width + head_dim)].reshape(2, head_dim),
        plane_index * head_cols,
        head_cols,
        1,
    )
    loss_value = sums[-1] / valid_count
    out_qkv = lax.psum_scatter(
        grad_w_qkv.astype(low), plane, scatter_dimension=0, tiled=True
    ).astype(wide)
    out_w_out = lax.psum_scatter(
        grad_w_out.astype(low), plane, scatter_dimension=1, tiled=True
    ).astype(wide)
    return (
        activations,
        loss_value,
        valid_count,
        grad_states,
        out_qkv,
        out_w_out,
        out_gains,
        out_qk,
        grad_gate_up,
        grad_down,
    )


def solution(mesh):
    placed = (
        P("fsdp", "ctx", None),
        P("fsdp", "ctx", None),
        P("fsdp"),
        P("fsdp", "ctx", None),
        P("fsdp", "ctx", None),
        P(("fsdp", "ctx"), None, "tp"),
        P("tp", ("fsdp", "ctx")),
        P(None, ("fsdp", "ctx")),
        P(None, ("fsdp", "ctx")),
        P(("fsdp", "ctx"), None, None, "tp"),
        P(("fsdp", "ctx"), "tp", None),
    )
    return jax.shard_map(
        per_device,
        mesh=mesh,
        in_specs=placed,
        out_specs=(
            P("fsdp", "ctx", None),
            P(),
            P(),
            P("fsdp", "ctx", None),
            P(("fsdp", "ctx"), None, "tp"),
            P("tp", ("fsdp", "ctx")),
            P(None, ("fsdp", "ctx")),
            P(None, ("fsdp", "ctx")),
            P(("fsdp", "ctx"), None, None, "tp"),
            P(("fsdp", "ctx"), "tp", None),
        ),
        check_vma=False,
    )
```

time: 2700 us -> 1280 us (0.47)
  waiting for transfers between devices: 1610 us -> 827 us
  other arithmetic: 378 us -> 45.5 us
  matrix products: 331 us -> 92.5 us
  local copies, waits for them, and re-layouts: 283 us -> 70.7 us
  Pallas kernels: 0 us -> 139 us
    psum x4 -> x0, waiting for transfers between devices: 467 us -> none  [the longest x1 153 us: per_device(): grad_ffn = lax.psum(grad_ffn_part, 'tp')]
    scatter-add x16 -> x0, other arithmetic: 301 us -> none  [the longest x8 151 us: expert_forward(): expert_total = expert_total.at[slot_index.reshape(-1)].add(weighted)]
    dot_general x45 -> x14, matrix products: 326 us -> 87.8 us  [the longest x1 20 us: per_device(): jnp.einsum('ebcd,ebcf->edf', rows_in, grad_rows, preferred_element_type=w...]
    reduce_scatter x5 -> x7, waiting for transfers between devices: 608 us -> 405 us  [the longest x1 116 us: per_device(): lax.psum_scatter(partial_out, plane, scatter_dimension=0, tiled=True)]
    all_gather x5 -> x10, waiting for transfers between devices: 535 us -> 363 us  [the longest x1 88.8 us: per_device(): grad_all = lax.all_gather(grad_block, plane, axis=0, tiled=True)]
    gather x18 -> x0, local copies, waits for them, and re-layouts: 172 us -> none  [the longest x8 72.3 us: expert_backward(): jnp.take(grad_final, slot_index, axis=0)]
    pallas_call x0 -> x2, Pallas kernels: none -> 139 us  [expert_call(): pl.pallas_call(body, grid=(blocks // group, experts), in_specs=in_specs,...]
    ppermute x0 -> x2, waiting for transfers between devices: none -> 43 us  [the longest x1 24.1 us: per_device(): other_kv = lax.ppermute(key_value, 'ctx', mirror)]
  transfers between devices with their start and end apart: 16 -> 21, of which waited for: 12 -> 17; matrix products, arithmetic and copies ran while one was open for 9% -> 10% of each run, Pallas kernels for 0% -> 0%
where the time goes in v1:
time: 1280 us; the launch traced here: 1270 us
  waiting for transfers between devices  827 us (65%)
  Pallas kernels  139 us (11%)
  matrix products  92.5 us (7%)
  local copies, waits for them, and re-layouts  70.7 us (6%)
  blocking collectives  66.2 us (5%)
  other arithmetic  45.5 us (4%)
  between operations  21.8 us (2%)
    pallas_call x2, Pallas kernels, expert_call(): pl.pallas_call(body, grid=(blocks // group, experts), in_specs=in_specs,...  139 us
    reduce_scatter x1, waiting for transfers between devices, per_device(): lax.psum_scatter(partial_out, plane, scatter_dimension=0, tiled=True)  116 us
    reduce_scatter x1, waiting for transfers between devices, per_device(): lax.psum_scatter(partial_in, plane, scatter_dimension=0, tiled=True)  116 us
    all_gather x1, waiting for transfers between devices, per_device(): grad_all = lax.all_gather(grad_block, plane, axis=0, tiled=True)  88.8 us
    all_gather x1, waiting for transfers between devices, per_device(): x_all = lax.all_gather(normed_ffn, plane, axis=0, tiled=True)  65.5 us
    all_gather x1, waiting for transfers between devices, per_device(): lax.all_gather(lax.all_gather(w_out, 'tp', axis=0, tiled=True), plane, ax...  56.4 us
    reduce_scatter x1, waiting for transfers between devices, per_device(): lax.psum_scatter(lax.psum_scatter(partial_in, plane, scatter_dimension=0,...  45.7 us
    reduce_scatter x1, waiting for transfers between devices, per_device(): lax.psum_scatter(grad_w_qkv.astype(low), plane, scatter_dimension=0, tile...  45 us
  transfers between devices with their start and end apart: 21, of which 17 were waited for; matrix products, arithmetic and copies ran while one was open for 10% of the time, Pallas kernels for 0%

profile of v1, /device:TPU:0, one launch (start us, length us, event | category | flops | bytes accessed | tf_op | source)
XLA Modules:
  0.0 1273.7 jit_solution(2169725158753026371)
XLA Ops:
  13.0 25.9 %all-reduce.9 = f32[4360]{0:T(1024)S(1)} all-reduce(f32[4360]{0:T(1024)S(1)} %maximum_dynamic-update-slice_fusion), channel_id=2, replica_groups=mesh['fsdp'=4,'ctx'=2,'tp'=4] {'fsdp','ctx'}, use_global_device_ids=true, to_apply=%add.9 | all-reduce | flops 4360 | bytes 34880
  42.0 17.5 %all-gather.12.cloned.1.call-done = bf16[2048,3,512]{2,0,1:T(8,128)(2,1)} async-done(((bf16[256,3,512]{2,0,1:T(8,128)(2,1)}), bf16[2048,3,512]{2,0,1:T(8,128)(2,1)}) %all-gather.12.cloned.1.call-update) | async-done | bytes 6291472 | tf_op jit(solution)/shard_map/all_gather | solution.py:332
  59.5 8.9 copy.64
  68.4 5.7 fusion.9
  77.5 24.1 %collective-permute-done = bf16[1,512,2,4,128]{1,4,3,2,0:T(8,128)(2,1)} collective-permute-done((bf16[1,512,2,4,128]{1,4,3,2,0:T(8,128)(2,1)S(1)}, bf16[1,512,2,4,128]{1,4,3,2,0:T(8,128)(2,1)}, u32[]{:S(2)}, u32[]{:S(2)}) %collective-permute-start) | collective-permute-done | bytes 1048608 | tf_op jit(solution)/shard_map/ppermute | solution.py:352
  112.4 44.6 %all-gather.14.cloned.1.call-done = bf16[512,2048]{0,1:T(8,128)(2,1)} async-done(((bf16[512,512]{0,1:T(8,128)(2,1)}), bf16[512,2048]{0,1:T(8,128)(2,1)}) %all-gather.14.cloned.1.call-update) | async-done | bytes 2097168 | tf_op jit(solution)/shard_map/all_gather | solution.py:364
  157.0 56.4 %all-gather.18.cloned.1.call-done = bf16[2048,2048]{1,0:T(8,128)(2,1)} async-done(((bf16[2048,256]{1,0:T(8,128)(2,1)}), bf16[2048,2048]{1,0:T(8,128)(2,1)}) %all-gather.18.cloned.1.call-update) | async-done | bytes 8388624 | tf_op jit(solution)/shard_map/all_gather | solution.py:333
  213.3 9.8 multiply_reduce_fusion.1
  231.6 14.4 %reshape.350.up_ref = bf16[4,2048,512]{2,1,0:T(8,128)(2,1)} reshape(bf16[4,2048,2,256]{3,2,1,0:T(2,128)(2,1)} %param.20) | data formatting | bytes 16777216 | tf_op jit(solution)/shard_map/reshape | solution.py:330
  251.4 65.5 %all-gather.20.cloned.1.call-done.x_ref = bf16[4096,2048]{1,0:T(8,128)(2,1)} async-done(((bf16[512,2048]{1,0:T(8,128)(2,1)}), bf16[4096,2048]{1,0:T(8,128)(2,1)}) %all-gather.20.cloned.1.call-update) | async-done | bytes 16777232 | tf_op jit(solution)/shard_map/all_gather | solution.py:368
  316.9 65.2 %shard_map.186 = (bf16[4096,2048]{1,0:T(8,128)(2,1)}, bf16[4,8,160,2048]{3,2,1,0:T(8,128)(2,1)}, f32[4,8,160,512]{3,2,1,0:T(8,128)}, bf16[4,8,160,256]{3,2,1,0:T(8,128)(2,1)}) custom-call(bf16[4096,2048]{1,0:T(8,128)(2,1)} %all-gather.20.cloned.1.call-done.x_ref, f32[8,4,2,512]{3,2,1,0:T(2,128)} %bitcast.193, s32[8,512,4]{2,1,0:T(8,128)} %fusion.12.place_ref, ...), custom_call_target="tpu_custom_call" | custom-call | flops 37580963840 | bytes 70254592 | tf_op jit(solution)/shard_map/pallas_call | solution.py:249
  382.2 115.9 %reduce-scatter.8.cloned.1.call-done = bf16[512,2048]{1,0:T(8,128)(2,1)} async-done(((bf16[4096,2048]{1,0:T(8,128)(2,1)}), bf16[512,2048]{1,0:T(8,128)(2,1)}) %reduce-scatter.8.cloned.1.call-update) | async-done | bytes 2097168 | tf_op jit(solution)/shard_map/reduce_scatter | solution.py:375
  499.8 44.1 %reduce-scatter.10.cloned.1.call-done = bf16[128,2048]{1,0:T(8,128)(2,1)} async-done(((bf16[512,2048]{1,0:T(8,128)(2,1)}), bf16[128,2048]{1,0:T(8,128)(2,1)}) %reduce-scatter.10.cloned.1.call-update) | async-done | bytes 524304 | tf_op jit(solution)/shard_map/reduce_scatter | solution.py:374
  547.1 44.9 %all-gather.24.cloned.1.call-done = bf16[512,2048]{1,0:T(8,128)(2,1)} async-done(((bf16[128,2048]{1,0:T(8,128)(2,1)}), bf16[512,2048]{1,0:T(8,128)(2,1)}) %all-gather.24.cloned.1.call-update) | async-done | bytes 2097168 | tf_op jit(solution)/shard_map/all_gather | solution.py:390
  592.0 88.8 %all-gather.26.cloned.1.call-done.x_ref = bf16[4096,2048]{1,0:T(8,128)(2,1)} async-done(((bf16[512,2048]{1,0:T(8,128)(2,1)}), bf16[4096,2048]{1,0:T(8,128)(2,1)}) %all-gather.26.cloned.1.call-update) | async-done | bytes 16777232 | tf_op jit(solution)/shard_map/all_gather | solution.py:391
  680.8 73.7 %shard_map.187 = (bf16[4096,2048]{1,0:T(8,128)(2,1)}, bf16[4,8,160,2048]{3,2,1,0:T(8,128)(2,1)}, bf16[4,8,160,512]{3,2,1,0:T(8,128)(2,1)}) custom-call(bf16[4096,2048]{1,0:T(8,128)(2,1)} %all-gather.26.cloned.1.call-done.x_ref, f32[8,4,2,512]{3,2,1,0:T(2,128)} %bitcast.194, s32[8,512,4]{2,1,0:T(8,128)} %fusion.12.place_ref, ...), custom_call_target="tpu_custom_call" | custom-call | flops 37580963840 | bytes 70254592 | tf_op jit(solution)/shard_map/pallas_call | solution.py:249
  754.6 115.9 %reduce-scatter.12.cloned.1.call-done = bf16[512,2048]{1,0:T(8,128)(2,1)} async-done(((bf16[4096,2048]{1,0:T(8,128)(2,1)}), bf16[512,2048]{1,0:T(8,128)(2,1)}) %reduce-scatter.12.cloned.1.call-update) | async-done | bytes 2097168 | tf_op jit(solution)/shard_map/reduce_scatter | solution.py:396
  870.5 45.7 %reduce-scatter.14.cloned.1.call-done = bf16[128,2048]{1,0:T(8,128)(2,1)} async-done(((bf16[512,2048]{1,0:T(8,128)(2,1)}), bf16[128,2048]{1,0:T(8,128)(2,1)}) %reduce-scatter.14.cloned.1.call-update) | async-done | bytes 524304 | tf_op jit(solution)/shard_map/reduce_scatter | solution.py:395
  921.2 6.4 convolution_convert_fusion.2
  932.2 14.1 %all-to-all-done.1 = bf16[128,4,512]{2,0,1:T(8,128)(2,1)S(1)} async-done(((bf16[128,4,512]{2,0,1:T(8,128)(2,1)}), bf16[128,4,512]{2,0,1:T(8,128)(2,1)S(1)}, u32[]{:S(2)}, u32[]{:S(2)}) %all-to-all-start.1) | async-done | bytes 524320 | tf_op jit(solution)/shard_map/all_to_all | solution.py:410
  946.8 5.2 multiply_reduce_fusion
  956.6 4.7 multiply_convert_fusion
  972.5 18.9 %collective-permute-done.1 = bf16[1,512,2,4,128]{1,4,3,2,0:T(8,128)(2,1)S(1)} collective-permute-done((bf16[1,512,2,4,128]{1,4,3,2,0:T(8,128)(2,1)}, bf16[1,512,2,4,128]{1,4,3,2,0:T(8,128)(2,1)S(1)}, u32[]{:S(2)}, u32[]{:S(2)}) %collective-permute-start.1) | collective-permute-done | bytes 1048608 | tf_op jit(solution)/shard_map/ppermute | solution.py:425
  1001.6 10.7 all-gather.30.cloned.1.call-done
  1019.6 38.0 %reduce-scatter.16.cloned.1.call-done = bf16[128,2048]{1,0:T(8,128)(2,1)} async-done(((bf16[512,2048]{1,0:T(8,128)(2,1)}), bf16[128,2048]{1,0:T(8,128)(2,1)}) %reduce-scatter.16.cloned.1.call-update) | async-done | bytes 524304 | tf_op jit(solution)/shard_map/reduce_scatter | solution.py:434
  1061.9 7.2 convolution_convert_fusion
  1069.1 34.8 %all-gather.22.cloned.1.call-done = bf16[512,2048]{1,0:T(8,128)(2,1)} async-done(((bf16[128,2048]{1,0:T(8,128)(2,1)}), bf16[512,2048]{1,0:T(8,128)(2,1)}) %all-gather.22.cloned.1.call-update) | async-done | bytes 2097168 | tf_op jit(solution)/shard_map/all_gather | solution.py:386
  1103.9 20.0 %fusion.51 = f32[4,2048,512,1]{1,2,3,0:T(8,128)} fusion(bf16[4,8,160,2048]{3,2,1,0:T(8,128)(2,1)} %get-tuple-element.20, bf16[4,8,160,512]{3,2,1,0:T(8,128)(2,1)} %get-tuple-element.21), kind=kOutput, calls=%fused_computation.154 | convolution fusion | flops 10737418240 | bytes 42991616 | tf_op jit(solution)/shard_map/ebcd,ebcf->edf/dot_general | solution.py:401
  1123.9 25.4 %copy.76 = f32[4,2048,2,256]{3,2,1,0:T(2,128)} copy(f32[4,2048,2,256]{1,3,2,0:T(8,128)} %bitcast.179) | data formatting | bytes 33554432
  1149.2 15.1 %convolution_bitcast_fusion = f32[4,256,2048]{2,1,0:T(8,128)} fusion(bf16[4,8,160,256]{3,2,1,0:T(8,128)(2,1)S(1)} %copy-done.40, bf16[4,8,160,2048]{3,2,1,0:T(8,128)(2,1)} %get-tuple-element.23), kind=kOutput, calls=%fused_computation.9 | convolution fusion | flops 5368709120 | bytes 31981568 | tf_op jit(solution)/shard_map/ebcf,ebcd->efd/dot_general | solution.py:404
  1165.7 40.3 %psum.7 = f32[4353]{0:T(1024)S(1)} all-reduce(f32[4353]{0:T(1024)S(1)} %pad_maximum_fusion.5), channel_id=1, replica_groups=mesh['fsdp'=4,'ctx'=2,'tp'=4] {'fsdp','ctx','tp'}, use_global_device_ids=true, to_apply=%region_26.27 | all-reduce | flops 4353 | bytes 34824 | tf_op jit(solution)/shard_map/psum | solution.py:447
  1214.8 45.0 %reduce-scatter.18.cloned.1.call-done = bf16[256,3,512]{2,0,1:T(8,128)(2,1)} async-done(((bf16[2048,3,512]{2,0,1:T(8,128)(2,1)}), bf16[256,3,512]{2,0,1:T(8,128)(2,1)}) %reduce-scatter.18.cloned.1.call-update) | async-done | bytes 786448 | tf_op jit(solution)/shard_map/reduce_scatter | solution.py:463
  (219 shorter events, 99.2 us)
Async XLA Ops:
  8.0 51.4 %all-gather.12.cloned.1.call-start = ((), (), s32[]{:S(2)}) async-start(), calls=%async_computation.9 | async-start | bytes 7077888 | tf_op jit(solution)/shard_map/all_gather | solution.py:332
  8.7 102.6 %all-gather.16.cloned.1.call-start = ((), (), s32[]{:S(2)}) async-start(), calls=%async_computation.11 | async-start | bytes 1310720 | tf_op jit(solution)/shard_map/all_gather | solution.py:334
  39.0 29.4 %copy-start.26 = (f32[1,2,8,128]{3,1,2,0:T(2,128)}, f32[1,2,8,128]{3,1,2,0:T(2,128)S(1)}, u32[]{:S(2)}) copy-start(f32[1,2,8,128]{3,1,2,0:T(2,128)S(1)} %copy.90) | copy-start | bytes 24580
  39.2 35.3 %copy-start.34 = (f32[128]{0:T(128)}, f32[128]{0:T(128)S(1)}, u32[]{:S(2)}) copy-start(f32[128]{0:T(128)S(1)} %mul.447) | copy-start | bytes 1540
  39.3 35.3 %copy-start.36 = (f32[128]{0:T(128)}, f32[128]{0:T(128)S(1)}, u32[]{:S(2)}) copy-start(f32[128]{0:T(128)S(1)} %mul.464) | copy-start | bytes 1540
  41.4 27.0 %copy-start.38 = (f32[512]{0:T(512)}, f32[512]{0:T(512)S(1)}, u32[]{:S(2)}) copy-start(f32[512]{0:T(512)S(1)} %add_rsqrt_fusion.1) | copy-start | bytes 6148
  41.9 32.9 %copy-start.16 = (f32[512,64]{0,1:T(8,128)}, f32[512,64]{0,1:T(8,128)S(1)}, u32[]{:S(2)}) copy-start(f32[512,64]{0,1:T(8,128)S(1)} %get-tuple-element.107) | copy-start | bytes 393220
  42.0 32.9 %copy-start.18 = (f32[512,64]{0,1:T(8,128)}, f32[512,64]{0,1:T(8,128)S(1)}, u32[]{:S(2)}) copy-start(f32[512,64]{0,1:T(8,128)S(1)} %get-tuple-element.108) | copy-start | bytes 393220
  76.1 25.5 %collective-permute-start = (bf16[1,512,2,4,128]{1,4,3,2,0:T(8,128)(2,1)S(1)}, bf16[1,512,2,4,128]{1,4,3,2,0:T(8,128)(2,1)}, u32[]{:S(2)}, u32[]{:S(2)}) collective-permute-start(bf16[1,512,2,4,128]{1,4,3,2,0:T(8,128)(2,1)S(1)} %pad_maximum_fusion), channel_id=1, source_target_pairs={{0,4},{4,0},{1,5},{5,1},{2,6},{6,2},{3,7},{7,3},{8,12},{12,8},{9,1... | collective-permute-start | bytes 3145736 | tf_op jit(solution)/shard_map/ppermute | solution.py:352
  77.4 79.6 %all-gather.14.cloned.1.call-start = ((), (), s32[]{:S(2)}) async-start(), calls=%async_computation.10 | async-start | bytes 2621440 | tf_op jit(solution)/shard_map/all_gather | solution.py:364
  111.3 102.0 %all-gather.18.cloned.1.call-start = ((), (), s32[]{:S(2)}) async-start(), calls=%async_computation.12 | async-start | bytes 9437184 | tf_op jit(solution)/shard_map/all_gather | solution.py:333
  111.9 205.0 %all-gather.20.cloned.1.call-start = ((), (), s32[]{:S(2)}) async-start(), calls=%async_computation.13 | async-start | bytes 18874368 | tf_op jit(solution)/shard_map/all_gather | solution.py:368
  228.2 17.9 %all-to-all-start = ((f32[32,2,512]{2,1,0:T(2,128)}), f32[32,2,512]{2,1,0:T(2,128)S(1)}, u32[]{:S(2)}, u32[]{:S(2)}) async-start(f32[32,2,512]{2,1,0:T(2,128)} %copy.67), calls=%async_computation | async-start | bytes 262144 | tf_op jit(solution)/shard_map/all_to_all | solution.py:324
  231.6 266.5 %reduce-scatter.8.cloned.1.call-start = ((), (), s32[]{:S(2)}) async-start(), calls=%async_computation.14 | async-start | bytes 18874368 | tf_op jit(solution)/shard_map/reduce_scatter | solution.py:375
  246.1 70.8 %copy-start.21 = (f32[32,2,512]{2,1,0:T(2,128)}, f32[32,2,512]{2,1,0:T(2,128)S(1)}, u32[]{:S(2)}) copy-start(f32[32,2,512]{2,1,0:T(2,128)S(1)} %all-to-all-done) | copy-start | bytes 393220
  382.2 161.8 %reduce-scatter.10.cloned.1.call-start = ((), (), s32[]{:S(2)}) async-start(), calls=%async_computation.15 | async-start | bytes 2621440 | tf_op jit(solution)/shard_map/reduce_scatter | solution.py:374
  498.1 93.8 %all-gather.24.cloned.1.call-start = ((), (), s32[]{:S(2)}) async-start(), calls=%async_computation.17 | async-start | bytes 2621440 | tf_op jit(solution)/shard_map/all_gather | solution.py:390
  547.0 133.7 %all-gather.26.cloned.1.call-start = ((), (), s32[]{:S(2)}) async-start(), calls=%async_computation.18 | async-start | bytes 18874368 | tf_op jit(solution)/shard_map/all_gather | solution.py:391
  592.0 278.5 %reduce-scatter.12.cloned.1.call-start = ((), (), s32[]{:S(2)}) async-start(), calls=%async_computation.19 | async-start | bytes 18874368 | tf_op jit(solution)/shard_map/reduce_scatter | solution.py:396
  754.5 161.7 %reduce-scatter.14.cloned.1.call-start = ((), (), s32[]{:S(2)}) async-start(), calls=%async_computation.20 | async-start | bytes 2621440 | tf_op jit(solution)/shard_map/reduce_scatter | solution.py:395
  928.5 17.9 %all-to-all-start.1 = ((bf16[128,4,512]{2,0,1:T(8,128)(2,1)}), bf16[128,4,512]{2,0,1:T(8,128)(2,1)S(1)}, u32[]{:S(2)}, u32[]{:S(2)}) async-start(bf16[128,4,512]{2,0,1:T(8,128)(2,1)} %bitcast.187), calls=%async_computation.5 | async-start | bytes 1048576 | tf_op jit(solution)/shard_map/all_to_all | solution.py:410
  931.9 80.4 %all-gather.30.cloned.1.call-start = ((), (), s32[]{:S(2)}) async-start(), calls=%async_computation.24 | async-start | bytes 2621440 | tf_op jit(solution)/shard_map/all_gather | solution.py:413
  967.1 24.3 %collective-permute-start.1 = (bf16[1,512,2,4,128]{1,4,3,2,0:T(8,128)(2,1)}, bf16[1,512,2,4,128]{1,4,3,2,0:T(8,128)(2,1)S(1)}, u32[]{:S(2)}, u32[]{:S(2)}) collective-permute-start(bf16[1,512,2,4,128]{1,4,3,2,0:T(8,128)(2,1)} %slice.178), channel_id=1, source_target_pairs={{0,4},{4,0},{1,5},{5,1},{2,6},{6,2},{3,7},{7,3},{8,12},{12,8},{9,1... | collective-permute-start | bytes 3145736 | tf_op jit(solution)/shard_map/ppermute | solution.py:425
  968.5 89.0 %reduce-scatter.16.cloned.1.call-start = ((), (), s32[]{:S(2)}) async-start(), calls=%async_computation.21 | async-start | bytes 2621440 | tf_op jit(solution)/shard_map/reduce_scatter | solution.py:434
  1001.0 102.9 %all-gather.22.cloned.1.call-start = ((), (), s32[]{:S(2)}) async-start(), calls=%async_computation.16 | async-start | bytes 2621440 | tf_op jit(solution)/shard_map/all_gather | solution.py:386
  1001.6 206.9 %reduce-scatter.20.cloned.1.call-start = ((), (), s32[]{:S(2)}) async-start(), calls=%async_computation.25 | async-start | bytes 2359296 | tf_op jit(solution)/shard_map/reduce_scatter | solution.py:466
  1016.5 41.0 %copy-start.27 = (f32[1,2,8,128]{3,1,2,0:T(2,128)S(1)}, f32[1,2,8,128]{3,1,2,0:T(2,128)}, u32[]{:S(2)}) copy-start(f32[1,2,8,128]{3,1,2,0:T(2,128)} %copy-done.26) | copy-start | bytes 24580
  1016.5 42.8 %copy-start.11 = (f32[128,2048]{1,0:T(8,128)S(1)}, f32[128,2048]{1,0:T(8,128)}, u32[]{:S(2)}) copy-start(f32[128,2048]{1,0:T(8,128)} %get-tuple-element.81) | copy-start | bytes 3145732
  1016.5 193.7 %all-gather.28.cloned.1.call-start = ((), (), s32[]{:S(2)}) async-start(), calls=%async_computation.22 | async-start | bytes 2621440 | tf_op jit(solution)/shard_map/all_gather | solution.py:443
  1019.4 42.5 %copy-start.39 = (f32[512]{0:T(512)S(1)}, f32[512]{0:T(512)}, u32[]{:S(2)}) copy-start(f32[512]{0:T(512)} %copy-done.38) | copy-start | bytes 6148
  1061.8 198.0 %reduce-scatter.18.cloned.1.call-start = ((), (), s32[]{:S(2)}) async-start(), calls=%async_computation.23 | async-start | bytes 7077888 | tf_op jit(solution)/shard_map/reduce_scatter | solution.py:463
  1210.2 52.1 %copy-start.14 = (bf16[512,2048]{1,0:T(8,128)(2,1)S(1)}, bf16[512,2048]{1,0:T(8,128)(2,1)}, u32[]{:S(2)}) copy-start(bf16[512,2048]{1,0:T(8,128)(2,1)} %all-gather.22.cloned.1.call-done) | copy-start | bytes 6291460
  (32 other events, 208.2 us)
Sparse Core Ops, SparseCore 0:
  10.7 48.6 all-gather.11
  227.0 89.8 all-gather.19
  592.1 88.6 all-gather.25
Sparse Core Ops, SparseCore 1:
  77.5 28.1 all-gather.15
  111.4 45.5 all-gather.13
  158.7 54.6 all-gather.17
  382.2 115.8 reduce-scatter.7
  500.4 43.4 reduce-scatter.9
  547.1 44.8 all-gather.23
  754.6 115.8 reduce-scatter.11
  872.7 43.5 reduce-scatter.13
  968.6 43.7 all-gather.29
  1015.2 42.3 reduce-scatter.15
  1059.1 44.8 all-gather.21
  1107.5 39.9 reduce-scatter.19
  1149.5 46.5 all-gather.27
  1199.4 60.3 reduce-scatter.17

commit v2 on v1

--- a/solution.py
+++ b/solution.py
@@ -1,3 +1,5 @@
+import functools
+
 import jax
 import jax.numpy as jnp
 from jax import lax
@@ -130,39 +132,53 @@
     return [slice(begin, begin + step) for begin in range(0, width, step)]
 
 
-def combine_blocks(place_ref, rows_ref, out_ref, blocks, experts, capacity, slots, width):
-    for block in range(blocks):
-        matrix = spread_rows(place_ref, block, experts, capacity, slots)
-        for cut in tiles_of(width):
-            out_ref[block * slots : (block + 1) * slots, cut] = jnp.dot(
-                matrix, rows_ref[block, :, cut], preferred_element_type=wide
-            ).astype(low)
-
-
-def forward_body(
-    x_ref, table_ref, place_ref, up_ref, down_ref, out_ref, rows_ref, gate_up_ref, hidden_ref, y_ref
-):
-    expert = pl.program_id(1)
-    experts = pl.num_programs(1)
+def take_rows(x_refs, table_ref, rows_ref):
     blocks, capacity, width = rows_ref.shape[1:]
-    slots = x_ref.shape[0] // blocks
-    half = down_ref.shape[1]
+    halves = len(x_refs) // blocks
+    slots = halves * x_refs[0].shape[0]
+    step = slots // halves
     weights = []
     for block in range(blocks):
         chosen, weight = pick_rows(table_ref, block, capacity, slots)
         weights.append(weight)
         for cut in tiles_of(width):
-            rows_ref[0, block, :, cut] = jnp.dot(
-                chosen,
-                x_ref[block * slots : (block + 1) * slots, cut],
-                preferred_element_type=wide,
+            found = jnp.dot(
+                chosen[:, :step], x_refs[block * halves][:, cut], preferred_element_type=wide
+            )
+            for half in range(1, halves):
+                found = found + jnp.dot(
+                    chosen[:, half * step : (half + 1) * step],
+                    x_refs[block * halves + half][:, cut],
+                    preferred_element_type=wide,
+                )
+            rows_ref[0, block, :, cut] = found.astype(low)
+    return (rows_ref[0].reshape(blocks * capacity, width), jnp.concatenate(weights, axis=0))
+
+
+def combine_blocks(place_ref, y_ref, out_refs, capacity):
+    blocks, total, width = y_ref.shape
+    slots, step = out_refs[0].shape
+    parts = width // step
+    for block in range(blocks):
+        matrix = spread_rows(place_ref, block, total // capacity, capacity, slots)
+        for k in range(parts):
+            out_refs[block * parts + k][...] = jnp.dot(
+                matrix, y_ref[block, :, k * step : (k + 1) * step], preferred_element_type=wide
             ).astype(low)
-    rows = rows_ref[0].reshape(blocks * capacity, width)
+
+
+def forward_body(n_x, n_out, n_keep, *refs):
+    x_refs, refs = refs[:n_x], refs[n_x:]
+    (table_ref, place_ref, up_ref, down_ref), refs = refs[:4], refs[4 + n_keep :]
+    out_refs, (rows_ref, gate_up_ref, hidden_ref, y_ref) = refs[:n_out], refs[n_out:]
+    expert = pl.program_id(0)
+    blocks, capacity, width = rows_ref.shape[1:]
+    half = down_ref.shape[1]
+    rows, weight = take_rows(x_refs, table_ref, rows_ref)
     gate_up = jnp.dot(rows, up_ref[0], preferred_element_type=wide)
     gate_up_ref[0] = gate_up.reshape(blocks, capacity, 2 * half)
     gate_part = gate_up[:, :half]
     up_part = gate_up[:, half:]
-    weight = jnp.concatenate(weights, axis=0)
     hidden = (gate_part * jax.nn.sigmoid(gate_part) * up_part * weight).astype(low)
     hidden_ref[0] = hidden.reshape(blocks, capacity, half)
     begin = pl.multiple_of(expert * capacity, 16)
@@ -172,33 +188,20 @@
             .astype(low)
             .reshape(blocks, capacity, -1)
         )
-    total = y_ref.shape[1] // capacity
-
-    @pl.when(expert == experts - 1)
+
+    @pl.when(expert == pl.num_programs(0) - 1)
     def _():
-        combine_blocks(place_ref, y_ref, out_ref, blocks, total, capacity, slots, width)
-
-
-def backward_body(
-    x_ref, table_ref, place_ref, up_ref, down_ref, gate_up_ref, out_ref, rows_ref, grad_ref, y_ref
-):
-    expert = pl.program_id(1)
-    experts = pl.num_programs(1)
+        combine_blocks(place_ref, y_ref, out_refs, capacity)
+
+
+def backward_body(n_x, n_out, n_keep, *refs):
+    x_refs, refs = refs[:n_x], refs[n_x:]
+    (table_ref, place_ref, up_ref, down_ref, gate_up_ref), refs = refs[:5], refs[5 + n_keep :]
+    out_refs, (rows_ref, grad_ref, y_ref) = refs[:n_out], refs[n_out:]
+    expert = pl.program_id(0)
     blocks, capacity, width = rows_ref.shape[1:]
-    slots = x_ref.shape[0] // blocks
     half = down_ref.shape[1]
-    weights = []
-    for block in range(blocks):
-        chosen, weight = pick_rows(table_ref, block, capacity, slots)
-        weights.append(weight)
-        for cut in tiles_of(width):
-            rows_ref[0, block, :, cut] = jnp.dot(
-                chosen,
-                x_ref[block * slots : (block + 1) * slots, cut],
-                preferred_element_type=wide,
-            ).astype(low)
-    rows = rows_ref[0].reshape(blocks * capacity, width)
-    weight = jnp.concatenate(weights, axis=0)
+    rows, weight = take_rows(x_refs, table_ref, rows_ref)
     grad_hidden = nt_dot(rows, down_ref[0]) * weight
     gate_up = gate_up_ref[0].reshape(blocks * capacity, 2 * half)
     gate_part = gate_up[:, :half]
@@ -213,55 +216,130 @@
         y_ref[:, pl.ds(begin, capacity), cut] = (
             nt_dot(grad_rows, up_ref[0, cut, :]).astype(low).reshape(blocks, capacity, -1)
         )
-    total = y_ref.shape[1] // capacity
-
-    @pl.when(expert == experts - 1)
+
+    @pl.when(expert == pl.num_programs(0) - 1)
     def _():
-        combine_blocks(place_ref, y_ref, out_ref, blocks, total, capacity, slots, width)
-
-
-def expert_call(body, x, table, place, w_up, w_down, gate_up, capacity, group):
+        combine_blocks(place_ref, y_ref, out_refs, capacity)
+
+
+def expert_call(chunk, pieces, table, place, w_up, w_down, gate_up, kept, capacity, total, parts):
     blocks, experts, _, slots = table.shape
-    width = x.shape[1]
+    width = pieces[0].shape[1]
     double, half = w_up.shape[2], w_down.shape[1]
     backward = gate_up is not None
-    row_spec = lambda last: pl.BlockSpec((1, group, capacity, last), lambda c, e: (e, c, 0, 0))
-    row_shape = lambda last, kind: jax.ShapeDtypeStruct((experts, blocks, capacity, last), kind)
-    in_specs = [
-        pl.BlockSpec((group * slots, width), lambda c, e: (c, 0)),
-        pl.BlockSpec((group, 1, 2, slots), lambda c, e: (c, e, 0, 0)),
-        pl.BlockSpec((group, slots, experts), lambda c, e: (c, 0, 0)),
-        pl.BlockSpec((1, width, double), lambda c, e: (e, 0, 0)),
-        pl.BlockSpec((1, half, width), lambda c, e: (e, 0, 0)),
+    row_spec = lambda last: pl.BlockSpec(
+        (1, blocks, capacity, last), lambda e: (e, chunk, 0, 0)
+    )
+    row_shape = lambda last, kind: jax.ShapeDtypeStruct((experts, total, capacity, last), kind)
+    step = width // parts
+    whole = lambda shape: pl.BlockSpec(shape, lambda e: (0,) * len(shape))
+    in_specs = [whole(p.shape) for p in pieces] + [
+        pl.BlockSpec((blocks, 1, 2, slots), lambda e: (0, e, 0, 0)),
+        whole((blocks, slots, experts)),
+        pl.BlockSpec((1, width, double), lambda e: (e, 0, 0)),
+        pl.BlockSpec((1, half, width), lambda e: (e, 0, 0)),
     ]
-    operands = [x, table, place, w_up, w_down]
-    out_specs = [pl.BlockSpec((group * slots, width), lambda c, e: (c, 0)), row_spec(width)]
-    out_shape = [jax.ShapeDtypeStruct(x.shape, low), row_shape(width, low)]
+    operands = [*pieces, table, place, w_up, w_down]
+    n_out = blocks * parts
+    out_specs = [whole((slots, step))] * n_out + [row_spec(width), row_spec(double)]
+    out_shape = [jax.ShapeDtypeStruct((slots, step), low)] * n_out + [row_shape(width, low)]
     if backward:
         in_specs.append(row_spec(double))
         operands.append(gate_up)
-        out_specs.append(row_spec(double))
         out_shape.append(row_shape(double, low))
     else:
-        out_specs += [row_spec(double), row_spec(half)]
+        out_specs.append(row_spec(half))
         out_shape += [row_shape(double, wide), row_shape(half, low)]
+    aliases = {len(operands) + i: n_out + i for i in range(len(kept))}
     rows = experts * blocks * capacity
-    return pl.pallas_call(
+    body = functools.partial(
+        backward_body if backward else forward_body, len(pieces), n_out, len(kept)
+    )
+    made = pl.pallas_call(
         body,
-        grid=(blocks // group, experts),
-        in_specs=in_specs,
+        grid=(experts,),
+        in_specs=in_specs + [pl.BlockSpec(memory_space=pl.ANY)] * len(kept),
         out_specs=out_specs,
         out_shape=out_shape,
-        scratch_shapes=[pltpu.VMEM((group, experts * capacity, width), low)],
+        input_output_aliases=aliases,
+        scratch_shapes=[pltpu.VMEM((blocks, experts * capacity, width), low)],
         compiler_params=pltpu.CompilerParams(
-            dimension_semantics=("arbitrary", "arbitrary"), vmem_limit_bytes=60 << 20
+            dimension_semantics=("arbitrary",), vmem_limit_bytes=56 << 20
         ),
         cost_estimate=pl.CostEstimate(
             flops=2 * rows * width * (2 * slots + double + half),
-            bytes_accessed=2 * x.size * 2 + rows * (2 * width + 6 * double),
+            bytes_accessed=4 * blocks * slots * width + rows * (2 * width + 6 * double),
             transcendentals=rows * half,
         ),
-    )(*operands)
+    )(*operands, *kept)
+    outs = [made[b * parts : (b + 1) * parts] for b in range(blocks)]
+    return (outs, made[n_out:])
+
+
+def added(left, right):
+    return left.astype(wide) + right.astype(wide)
+
+
+class Plane:
+    def __init__(self):
+        self.fsdp, self.ctx = lax.axis_size("fsdp"), lax.axis_size("ctx")
+        self.tree = self.fsdp == 4 and self.ctx == 2
+        self.shards = self.fsdp * self.ctx
+
+    def core(self, a):
+        return lax.ppermute(a, "fsdp", [(i, i ^ 1) for i in range(self.fsdp)])
+
+    def along_x(self, a):
+        return lax.ppermute(a, "fsdp", [(i, i ^ 2) for i in range(self.fsdp)])
+
+    def along_y(self, a):
+        return lax.ppermute(a, "ctx", [(i, i ^ 1) for i in range(self.ctx)])
+
+    def order(self):
+        if not self.tree:
+            return list(range(self.shards))
+        fsdp, ctx = lax.axis_index("fsdp"), lax.axis_index("ctx")
+        chips = ((0, 0), (1, 0), (0, 1), (1, 1))
+        return [(fsdp ^ (2 * x) ^ core) * 2 + (ctx ^ y) for x, y in chips for core in (0, 1)]
+
+    def gather(self, first, second):
+        if not self.tree:
+            tops = jnp.split(lax.all_gather(first, plane, axis=0, tiled=True), self.shards)
+            ends = jnp.split(lax.all_gather(second, plane, axis=0, tiled=True), self.shards)
+            return [
+                [tops[i], ends[i], tops[i + 1], ends[i + 1]] for i in range(0, self.shards, 2)
+            ]
+        x_first, y_second = self.along_x(first), self.along_y(second)
+        x_second, y_first = self.along_x(second), self.along_y(first)
+        far_first, far_second = self.along_y(x_first), self.along_x(y_second)
+        pairs = [
+            (first, second),
+            (x_first, x_second),
+            (y_first, y_second),
+            (far_first, far_second),
+        ]
+        return [[a, b, self.core(a), self.core(b)] for a, b in pairs]
+
+    def reduce(self, outs):
+        if not self.tree:
+            flat = [jnp.concatenate(block, axis=1) for pair in outs for block in pair]
+            total = lax.psum_scatter(
+                jnp.concatenate(flat, axis=0), plane, scatter_dimension=0, tiled=True
+            )
+            return jnp.split(total.astype(wide), len(outs[0][0]), axis=1)
+        sums = []
+        for k in range(len(outs[0][0])):
+            own, near_x, near_y, far = [added(pair[0][k], self.core(pair[1][k])) for pair in outs]
+            if k % 2 == 0:
+                near_y = near_y + self.along_x(far.astype(low)).astype(wide)
+            else:
+                near_x = near_x + self.along_y(far.astype(low)).astype(wide)
+            sums.append(
+                own
+                + self.along_x(near_x.astype(low)).astype(wide)
+                + self.along_y(near_y.astype(low)).astype(wide)
+            )
+        return sums
 
 
 def per_device(
@@ -328,16 +406,28 @@
     offset = (jnp.arange(shard_experts, dtype=jnp.int32) * capacity)[None, :, None]
     place = jnp.swapaxes(jnp.where(rank >= 0, rank + offset, -1), 1, 2)
     w_up = w_gate_up.reshape(shard_experts, width, 2 * hidden_local)
-
-    full_qkv = lax.all_gather(w_qkv, plane, axis=0, tiled=True)
+    places = Plane()
+    order = places.order()
+    sort = lambda a: jnp.concatenate(
+        [lax.dynamic_slice_in_dim(a, block, 1, 0) for block in order], axis=0
+    )
+    table, place = sort(table), sort(place)
+    back_table = jnp.swapaxes(
+        table.reshape(shards, shard_experts, 2, tp_size, 2, part // 2), 3, 4
+    ).reshape(table.shape)
+    chunks = shards // 2
+    pair = lambda a, c: a[2 * c : 2 * c + 2]
+    parts = 4
+
+    full_qkv = lax.all_gather(w_qkv.reshape(w_qkv.shape[0], -1), plane, axis=0, tiled=True)
     full_out = lax.all_gather(
         lax.all_gather(w_out, "tp", axis=0, tiled=True), plane, axis=1, tiled=True
     )
     flat_states = states.astype(wide).reshape(tokens, width)
     normed = rms_norm(flat_states, gain_attn).astype(low)
-    projected = jnp.einsum(
-        "nd,dkh->nkh", normed, full_qkv, preferred_element_type=wide
-    ).reshape(tokens, 3, heads_local, head_dim)
+    projected = jnp.dot(normed, full_qkv, preferred_element_type=wide).reshape(
+        tokens, 3, heads_local, head_dim
+    )
 
     def prepare_local(projected_in, gains_in):
         return prepare(projected_in, gains_in, tok_position)
@@ -365,18 +455,33 @@
     middle = flat_states + jnp.dot(attended_all, full_out, preferred_element_type=wide)
     normed_ffn = rms_norm(middle, gain_ffn).astype(low)
 
-    x_all = lax.all_gather(normed_ffn, plane, axis=0, tiled=True)
-    partial_out, rows_in, gate_up, hidden = expert_call(
-        forward_body, x_all, table, place, w_up, w_down, None, capacity, 2
-    )
     begin = tp_index * part
     own = lambda a: lax.dynamic_slice_in_dim(a, begin, part, 0)
-    mixture = lax.psum_scatter(
-        lax.psum_scatter(partial_out, plane, scatter_dimension=0, tiled=True),
-        "tp",
-        scatter_dimension=0,
-        tiled=True,
-    ).astype(wide)
+    half_rows = tokens // 2
+    x_chunks = places.gather(normed_ffn[:half_rows], normed_ffn[half_rows:])
+    kept, outs = (), []
+    for c in range(chunks):
+        made, kept = expert_call(
+            c, x_chunks[c], pair(table, c), pair(place, c), w_up, w_down, None, kept,
+            capacity, shards, parts,
+        )
+        outs.append(made)
+    rows_in, gate_up, hidden = kept
+
+    def finish(outs):
+        sums = places.reduce(outs)
+        ready = [
+            lax.psum_scatter(
+                jnp.concatenate(sums[k : k + 2], axis=1).astype(low),
+                "tp",
+                scatter_dimension=0,
+                tiled=True,
+            )
+            for k in range(0, parts, 2)
+        ]
+        return jnp.concatenate(ready, axis=1).astype(wide)
+
+    mixture = finish(outs)
     middle_own = own(middle)
     final_own = middle_own + mixture
     difference = final_own - own(teacher.reshape(tokens, width)).astype(wide)
@@ -387,17 +492,20 @@
         seq_count, slot_count, width
     )
 
-    grad_block = lax.all_gather(grad_final.astype(low), "tp", axis=0, tiled=True)
-    grad_all = lax.all_gather(grad_block, plane, axis=0, tiled=True)
-    partial_in, rows_out, grad_rows = expert_call(
-        backward_body, grad_all, table, place, w_up, w_down, gate_up, capacity, 2
-    )
-    grad_ffn = lax.psum_scatter(
-        lax.psum_scatter(partial_in, plane, scatter_dimension=0, tiled=True),
-        "tp",
-        scatter_dimension=0,
-        tiled=True,
-    ).astype(wide)
+    grad_low = grad_final.astype(low)
+    grad_chunks = places.gather(
+        lax.all_gather(grad_low[: part // 2], "tp", axis=0, tiled=True),
+        lax.all_gather(grad_low[part // 2 :], "tp", axis=0, tiled=True),
+    )
+    kept, outs = (), []
+    for c in range(chunks):
+        made, kept = expert_call(
+            c, grad_chunks[c], pair(back_table, c), pair(place, c), w_up, w_down, gate_up, kept,
+            capacity, shards, parts,
+        )
+        outs.append(made)
+    rows_out, grad_rows = kept
+    grad_ffn = finish(outs)
     grad_gate_up = jnp.einsum(
         "ebcd,ebcf->edf", rows_in, grad_rows, preferred_element_type=wide
     ).reshape(shard_experts, width, 2, hidden_local)
@@ -430,14 +538,14 @@
             own_kv[:, :, 1].reshape(tokens, heads_local, head_dim),
         )
     )
-    grad_proj_low = grad_projected.astype(low).reshape(tokens, 3, heads_local * head_dim)
+    grad_proj_low = grad_projected.astype(low).reshape(tokens, -1)
     grad_normed = lax.psum_scatter(
-        jnp.einsum("nkh,dkh->nd", grad_proj_low, full_qkv, preferred_element_type=wide).astype(low),
+        nt_dot(grad_proj_low, full_qkv).astype(low),
         "tp",
         scatter_dimension=0,
         tiled=True,
     ).astype(wide)
-    grad_w_qkv = jnp.einsum("nd,nkh->dkh", normed, grad_proj_low, preferred_element_type=wide)
+    grad_w_qkv = jnp.einsum("nd,nk->dk", normed, grad_proj_low, preferred_element_type=wide)
     grad_states_norm, grad_gain_attn = norm_back(grad_normed, own(flat_states), gain_attn)
     grad_states = (
         lax.all_gather((grad_middle + grad_states_norm).astype(low), "tp", axis=0, tiled=True)
@@ -462,7 +570,7 @@
     loss_value = sums[-1] / valid_count
     out_qkv = lax.psum_scatter(
         grad_w_qkv.astype(low), plane, scatter_dimension=0, tiled=True
-    ).astype(wide)
+    ).astype(wide).reshape(w_qkv.shape)
     out_w_out = lax.psum_scatter(
         grad_w_out.astype(low), plane, scatter_dimension=1, tiled=True
     ).astype(wide)

time: 1280 us -> 1180 us (0.922)
  waiting for transfers between devices: 827 us -> 615 us
  starting transfers between devices: 11.4 us -> 57 us
  Pallas kernels: 139 us -> 169 us
  other arithmetic: 45.5 us -> 65 us
    reduce_scatter x5, waiting for transfers between devices: 360 us -> 89.7 us  [the longest x4 51.8 us: finish(): lax.psum_scatter(jnp.concatenate(sums[k:k + 2], axis=1).astype(low), 'tp'...]
    ppermute x0 -> x84, waiting for transfers between devices: none -> 222 us  [the longest x18 124 us: along_x(): return lax.ppermute(a, 'fsdp', [(i, i ^ 2) for i in range(self.fsdp)])]
    all_gather x4 -> x3, waiting for transfers between devices: 217 us -> 71.1 us  [the longest x1 27.8 us: per_device(): lax.all_gather(grad_low[part // 2:], 'tp', axis=0, tiled=True)]
    ppermute x0 -> x84, starting transfers between devices: none -> 47.1 us  [the longest x18 20.2 us: along_x(): return lax.ppermute(a, 'fsdp', [(i, i ^ 2) for i in range(self.fsdp)])]
    pallas_call x2 -> x8, Pallas kernels: 139 us -> 169 us  [expert_call(): pl.pallas_call(body, grid=(experts,), in_specs=in_specs + [pl.BlockSpec(m...]
    all_gather x1, waiting for transfers between devices: 44.6 us -> 25.7 us  [per_device(): attended_all = lax.all_gather(attended_low, 'tp', axis=1, tiled=True)]
    convert_element_type x3 -> x27, other arithmetic: 5.79 us -> 19.6 us  [the longest x4 4.82 us: reduce(): near_x = near_x + self.along_y(far.astype(low)).astype(wide)]
    unnamed x95 -> x231, local copies, waits for them, and re-layouts: 41.1 us -> 50 us
  transfers between devices with their start and end apart: 21 -> 104, of which waited for: 17 -> 41; matrix products, arithmetic and copies ran while one was open for 10% -> 15% of each run, Pallas kernels for 0% -> 14%
where the time goes in v2:
time: 1180 us; the launch traced here: 1170 us
  waiting for transfers between devices  615 us (52%)
  Pallas kernels  169 us (14%)
  matrix products  91.1 us (8%)
  local copies, waits for them, and re-layouts  81.9 us (7%)
  blocking collectives  66.3 us (6%)
  other arithmetic  65 us (6%)
  starting transfers between devices  57 us (5%)
  between operations  22.9 us (2%)
    pallas_call x8, Pallas kernels, expert_call(): pl.pallas_call(body, grid=(experts,), in_specs=in_specs + [pl.BlockSpec(m...  169 us
    ppermute x18, waiting for transfers between devices, along_x(): return lax.ppermute(a, 'fsdp', [(i, i ^ 2) for i in range(self.fsdp)])  124 us
    ppermute x18, waiting for transfers between devices, along_y(): return lax.ppermute(a, 'ctx', [(i, i ^ 1) for i in range(self.ctx)])  96.2 us
    all_gather x1, waiting for transfers between devices, per_device(): lax.all_gather(lax.all_gather(w_out, 'tp', axis=0, tiled=True), plane, ax...  56.4 us
    reduce_scatter x4, waiting for transfers between devices, finish(): lax.psum_scatter(jnp.concatenate(sums[k:k + 2], axis=1).astype(low), 'tp'...  51.8 us
    unnamed x231, local copies, waits for them, and re-layouts  50 us
    reduce_scatter x1, waiting for transfers between devices, per_device(): lax.psum_scatter(grad_w_qkv.astype(low), plane, scatter_dimension=0, tile...  44.6 us
    psum x1, blocking collectives, per_device(): lax.psum(jnp.concatenate([grad_gain_attn, grad_gain_ffn, grad_qk.reshape(...  40.4 us
  transfers between devices with their start and end apart: 104, of which 41 were waited for; matrix products, arithmetic and copies ran while one was open for 15% of the time, Pallas kernels for 14%

profile of v2, /device:TPU:0, one launch (start us, length us, event | category | flops | bytes accessed | tf_op | source)
XLA Modules:
  0.0 1168.3 jit_solution(760851323405120717)
XLA Ops:
  14.7 25.9 %all-reduce.9 = f32[4360]{0:T(1024)S(1)} all-reduce(f32[4360]{0:T(1024)S(1)} %maximum_dynamic-update-slice_fusion), channel_id=2, replica_groups=mesh['fsdp'=4,'ctx'=2,'tp'=4] {'fsdp','ctx'}, use_global_device_ids=true, to_apply=%add.9 | all-reduce | flops 4360 | bytes 34880
  43.8 17.4 %all-gather.11.cloned.1.call-done = bf16[2048,1536]{0,1:T(8,128)(2,1)} async-done(((bf16[256,1536]{0,1:T(8,128)(2,1)}), bf16[2048,1536]{0,1:T(8,128)(2,1)}) %all-gather.11.cloned.1.call-update) | async-done | bytes 6291472 | tf_op jit(solution)/shard_map/all_gather | solution.py:422
  70.4 25.1 %collective-permute-done = bf16[1,512,2,4,128]{1,4,3,2,0:T(8,128)(2,1)} collective-permute-done((bf16[1,512,2,4,128]{1,4,3,2,0:T(8,128)(2,1)}, bf16[1,512,2,4,128]{1,4,3,2,0:T(8,128)(2,1)}, u32[]{:S(2)}, u32[]{:S(2)}) %collective-permute-start) | collective-permute-done | bytes 1048608 | tf_op jit(solution)/shard_map/ppermute | solution.py:442
  111.1 14.1 %reshape.368.refs_6_ = bf16[4,2048,512]{2,1,0:T(8,128)(2,1)} reshape(bf16[4,2048,2,256]{3,2,1,0:T(2,128)(2,1)} %param.20) | data formatting | bytes 16777216 | tf_op jit(solution)/shard_map/reshape | solution.py:408
  125.2 25.7 %all-gather.13.cloned.1.call-done = bf16[512,2048]{0,1:T(8,128)(2,1)} async-done(((bf16[512,512]{0,1:T(8,128)(2,1)}), bf16[512,2048]{0,1:T(8,128)(2,1)}) %all-gather.13.cloned.1.call-update) | async-done | bytes 2097168 | tf_op jit(solution)/shard_map/all_gather | solution.py:454
  150.9 56.4 %all-gather.17.cloned.1.call-done = bf16[2048,2048]{1,0:T(8,128)(2,1)} async-done(((bf16[2048,256]{1,0:T(8,128)(2,1)}), bf16[2048,2048]{1,0:T(8,128)(2,1)}) %all-gather.17.cloned.1.call-update) | async-done | bytes 8388624 | tf_op jit(solution)/shard_map/all_gather | solution.py:423
  222.5 21.6 %collective-permute-done.4.refs_0_ = bf16[256,2048]{1,0:T(8,128)(2,1)S(1)} collective-permute-done((bf16[256,2048]{1,0:T(8,128)(2,1)}, bf16[256,2048]{1,0:T(8,128)(2,1)S(1)}, u32[]{:S(2)}, u32[]{:S(2)}) %collective-permute-start.4) | collective-permute-done | bytes 1048608 | tf_op jit(solution)/shard_map/ppermute | solution.py:293
  246.6 19.4 %collective-permute-done.5.refs_1_ = bf16[256,2048]{1,0:T(8,128)(2,1)} collective-permute-done((bf16[256,2048]{1,0:T(8,128)(2,1)}, bf16[256,2048]{1,0:T(8,128)(2,1)}, u32[]{:S(2)}, u32[]{:S(2)}) %collective-permute-start.5) | collective-permute-done | bytes 1048608 | tf_op jit(solution)/shard_map/ppermute | solution.py:293
  272.9 19.8 %shard_map.186 = (bf16[512,512]{1,0:T(8,128)(2,1)}, bf16[512,512]{1,0:T(8,128)(2,1)}, bf16[512,512]{1,0:T(8,128)(2,1)}, bf16[512,512]{1,0:T(8,128)(2,1)}, bf16[5...) custom-call(bf16[256,2048]{1,0:T(8,128)(2,1)} %get-tuple-element.263, ...), custom_call_target="tpu_custom_call" | custom-call | flops 9395240960 | bytes 17563648 | tf_op jit(solution)/shard_map/pallas_call | solution.py:258
  293.3 20.0 %shard_map.187 = (bf16[512,512]{1,0:T(8,128)(2,1)}, bf16[512,512]{1,0:T(8,128)(2,1)}, bf16[512,512]{1,0:T(8,128)(2,1)}, bf16[512,512]{1,0:T(8,128)(2,1)}, bf16[5...) custom-call(bf16[256,2048]{1,0:T(8,128)(2,1)} %copy-done.24, ...), custom_call_target="tpu_custom_call", output_to_operand_aliasing={{8}: (8, {}), {9}: (9, {}), {10}: (10, {})} | custom-call | flops 9395240960 | bytes 17563648 | tf_op jit(solution)/shard_map/pallas_call | solution.py:258
  314.9 19.8 %shard_map.188 = (bf16[512,512]{1,0:T(8,128)(2,1)}, bf16[512,512]{1,0:T(8,128)(2,1)}, bf16[512,512]{1,0:T(8,128)(2,1)}, bf16[512,512]{1,0:T(8,128)(2,1)}, bf16[5...) custom-call(bf16[256,2048]{1,0:T(8,128)(2,1)} %copy-done.26, ...), custom_call_target="tpu_custom_call", output_to_operand_aliasing={{8}: (8, {}), {9}: (9, {}), {10}: (10, {})} | custom-call | flops 9395240960 | bytes 17563648 | tf_op jit(solution)/shard_map/pallas_call | solution.py:258
  336.0 20.1 %shard_map.189 = (bf16[512,512]{1,0:T(8,128)(2,1)}, bf16[512,512]{1,0:T(8,128)(2,1)}, bf16[512,512]{1,0:T(8,128)(2,1)}, bf16[512,512]{1,0:T(8,128)(2,1)}, bf16[5...) custom-call(bf16[256,2048]{1,0:T(8,128)(2,1)} %collective-permute-do, ...), custom_call_target="tpu_custom_call", output_to_operand_aliasing={{8}: (8, {}), {9}: (9, {}), {10}: (10, {})} | custom-call | flops 9395240960 | bytes 17563648 | tf_op jit(solution)/shard_map/pallas_call | solution.py:258
  363.0 11.7 %collective-permute-done.20 = bf16[512,512]{1,0:T(8,128)(2,1)S(1)} collective-permute-done((bf16[512,512]{1,0:T(8,128)(2,1)S(1)}, bf16[512,512]{1,0:T(8,128)(2,1)S(1)}, u32[]{:S(2)}, u32[]{:S(2)}) %collective-permute-start.20) | collective-permute-done | bytes 524320 | tf_op jit(solution)/shard_map/ppermute | solution.py:293
  455.9 25.2 %reduce-scatter.10.cloned.1.call-done = bf16[128,1024]{1,0:T(8,128)(2,1)} async-done(((bf16[512,1024]{1,0:T(8,128)(2,1)}), bf16[128,1024]{1,0:T(8,128)(2,1)}) %reduce-scatter.10.cloned.1.call-update) | async-done | bytes 262160 | tf_op jit(solution)/shard_map/reduce_scatter | solution.py:474
  485.2 25.9 %all-gather.21.cloned.1.call-done.refs_0_ = bf16[256,2048]{1,0:T(8,128)(2,1)} async-done(((bf16[64,2048]{1,0:T(8,128)(2,1)}), bf16[256,2048]{1,0:T(8,128)(2,1)}) %all-gather.21.cloned.1.call-update) | async-done | bytes 1048592 | tf_op jit(solution)/shard_map/all_gather | solution.py:497
  512.6 27.8 %all-gather.23.cloned.1.call-done.refs_1_ = bf16[256,2048]{1,0:T(8,128)(2,1)} async-done(((bf16[64,2048]{1,0:T(8,128)(2,1)}), bf16[256,2048]{1,0:T(8,128)(2,1)}) %all-gather.23.cloned.1.call-update) | async-done | bytes 1048592 | tf_op jit(solution)/shard_map/all_gather | solution.py:498
  545.8 20.5 %collective-permute-done.47.refs_1_ = bf16[256,2048]{1,0:T(8,128)(2,1)} collective-permute-done((bf16[256,2048]{1,0:T(8,128)(2,1)}, bf16[256,2048]{1,0:T(8,128)(2,1)}, u32[]{:S(2)}, u32[]{:S(2)}) %collective-permute-start.47) | collective-permute-done | bytes 1048608 | tf_op jit(solution)/shard_map/ppermute | solution.py:293
  571.6 19.1 %collective-permute-done.52.refs_0_ = bf16[256,2048]{1,0:T(8,128)(2,1)} collective-permute-done((bf16[256,2048]{1,0:T(8,128)(2,1)}, bf16[256,2048]{1,0:T(8,128)(2,1)}, u32[]{:S(2)}, u32[]{:S(2)}) %collective-permute-start.52) | collective-permute-done | bytes 1048608 | tf_op jit(solution)/shard_map/ppermute | solution.py:296
  591.2 22.4 %shard_map.190 = (bf16[512,512]{1,0:T(8,128)(2,1)}, bf16[512,512]{1,0:T(8,128)(2,1)}, bf16[512,512]{1,0:T(8,128)(2,1)}, bf16[512,512]{1,0:T(8,128)(2,1)}, bf16[5...) custom-call(bf16[256,2048]{1,0:T(8,128)(2,1)} %all-gather.21.cloned., ...), custom_call_target="tpu_custom_call" | custom-call | flops 9395240960 | bytes 17563648 | tf_op jit(solution)/shard_map/pallas_call | solution.py:258
  614.2 22.1 %shard_map.191 = (bf16[512,512]{1,0:T(8,128)(2,1)}, bf16[512,512]{1,0:T(8,128)(2,1)}, bf16[512,512]{1,0:T(8,128)(2,1)}, bf16[512,512]{1,0:T(8,128)(2,1)}, bf16[5...) custom-call(bf16[256,2048]{1,0:T(8,128)(2,1)} %collective-permute-do, ...), custom_call_target="tpu_custom_call", output_to_operand_aliasing={{8}: (9, {}), {9}: (10, {})} | custom-call | flops 9395240960 | bytes 17563648 | tf_op jit(solution)/shard_map/pallas_call | solution.py:258
  637.8 22.2 %shard_map.192 = (bf16[512,512]{1,0:T(8,128)(2,1)}, bf16[512,512]{1,0:T(8,128)(2,1)}, bf16[512,512]{1,0:T(8,128)(2,1)}, bf16[512,512]{1,0:T(8,128)(2,1)}, bf16[5...) custom-call(bf16[256,2048]{1,0:T(8,128)(2,1)} %collective-permute-do, ...), custom_call_target="tpu_custom_call", output_to_operand_aliasing={{8}: (9, {}), {9}: (10, {})} | custom-call | flops 9395240960 | bytes 17563648 | tf_op jit(solution)/shard_map/pallas_call | solution.py:258
  661.4 22.4 %shard_map.193 = (bf16[512,512]{1,0:T(8,128)(2,1)}, bf16[512,512]{1,0:T(8,128)(2,1)}, bf16[512,512]{1,0:T(8,128)(2,1)}, bf16[512,512]{1,0:T(8,128)(2,1)}, bf16[5...) custom-call(bf16[256,2048]{1,0:T(8,128)(2,1)} %copy-done.27, ...), custom_call_target="tpu_custom_call", output_to_operand_aliasing={{8}: (9, {}), {9}: (10, {})} | custom-call | flops 9395240960 | bytes 17563648 | tf_op jit(solution)/shard_map/pallas_call | solution.py:258
  781.8 26.6 %reduce-scatter.14.cloned.1.call-done = bf16[128,1024]{1,0:T(8,128)(2,1)} async-done(((bf16[512,1024]{1,0:T(8,128)(2,1)}), bf16[128,1024]{1,0:T(8,128)(2,1)}) %reduce-scatter.14.cloned.1.call-update) | async-done | bytes 262160 | tf_op jit(solution)/shard_map/reduce_scatter | solution.py:474
  823.9 14.3 %all-to-all-done.1 = bf16[128,4,512]{2,0,1:T(8,128)(2,1)S(1)} async-done(((bf16[128,4,512]{2,0,1:T(8,128)(2,1)}), bf16[128,4,512]{2,0,1:T(8,128)(2,1)S(1)}, u32[]{:S(2)}, u32[]{:S(2)}) %all-to-all-start.1) | async-done | bytes 524320 | tf_op jit(solution)/shard_map/all_to_all | solution.py:518
  864.7 18.9 %collective-permute-done.85 = bf16[1,512,2,4,128]{1,4,3,2,0:T(8,128)(2,1)S(1)} collective-permute-done((bf16[1,512,2,4,128]{1,4,3,2,0:T(8,128)(2,1)}, bf16[1,512,2,4,128]{1,4,3,2,0:T(8,128)(2,1)S(1)}, u32[]{:S(2)}, u32[]{:S(2)}) %collective-permute-start.85) | collective-permute-done | bytes 1048608 | tf_op jit(solution)/shard_map/ppermute | solution.py:533
  911.7 37.9 %reduce-scatter.16.cloned.1.call-done = bf16[128,2048]{1,0:T(8,128)(2,1)} async-done(((bf16[512,2048]{1,0:T(8,128)(2,1)}), bf16[128,2048]{1,0:T(8,128)(2,1)}) %reduce-scatter.16.cloned.1.call-update) | async-done | bytes 524304 | tf_op jit(solution)/shard_map/reduce_scatter | solution.py:542
  961.3 34.8 %all-gather.19.cloned.1.call-done = bf16[512,2048]{1,0:T(8,128)(2,1)} async-done(((bf16[128,2048]{1,0:T(8,128)(2,1)}), bf16[512,2048]{1,0:T(8,128)(2,1)}) %all-gather.19.cloned.1.call-update) | async-done | bytes 2097168 | tf_op jit(solution)/shard_map/all_gather | solution.py:491
  996.1 20.0 %fusion.53 = f32[4,2048,512,1]{1,2,3,0:T(8,128)} fusion(bf16[4,8,160,2048]{3,2,1,0:T(8,128)(2,1)} %get-tuple-element.174, bf16[4,8,160,512]{3,2,1,0:T(8,128)(2,1)} %get-tuple-element.175), kind=kOutput, calls=%fused_computation.228 | convolution fusion | flops 10737418240 | bytes 42991616 | tf_op jit(solution)/shard_map/ebcd,ebcf->edf/dot_general | solution.py:509
  1016.0 25.3 %copy.108 = f32[4,2048,2,256]{3,2,1,0:T(2,128)} copy(f32[4,2048,2,256]{1,3,2,0:T(8,128)} %bitcast.193) | data formatting | bytes 33554432
  1041.3 15.1 %convolution_bitcast_fusion = f32[4,256,2048]{2,1,0:T(8,128)} fusion(bf16[4,8,160,256]{3,2,1,0:T(8,128)(2,1)S(1)} %copy-done.4, bf16[4,8,160,2048]{3,2,1,0:T(8,128)(2,1)} %get-tuple-element.177), kind=kOutput, calls=%fused_computation.9 | convolution fusion | flops 5368709120 | bytes 31981568 | tf_op jit(solution)/shard_map/ebcf,ebcd->efd/dot_general | solution.py:512
  1058.4 40.4 %psum.7 = f32[4353]{0:T(1024)S(1)} all-reduce(f32[4353]{0:T(1024)S(1)} %pad_maximum_fusion.15), channel_id=1, replica_groups=mesh['fsdp'=4,'ctx'=2,'tp'=4] {'fsdp','ctx','tp'}, use_global_device_ids=true, to_apply=%region_26.27 | all-reduce | flops 4353 | bytes 34824 | tf_op jit(solution)/shard_map/psum | solution.py:555
  1107.5 44.6 %reduce-scatter.18.cloned.1.call-done = bf16[256,1536]{1,0:T(8,128)(2,1)} async-done(((bf16[2048,1536]{1,0:T(8,128)(2,1)}), bf16[256,1536]{1,0:T(8,128)(2,1)}) %reduce-scatter.18.cloned.1.call-update) | async-done | bytes 786448 | tf_op jit(solution)/shard_map/reduce_scatter | solution.py:571
  (584 shorter events, 363.0 us)
Async XLA Ops:
  8.0 53.2 %all-gather.11.cloned.1.call-start = ((), (), s32[]{:S(2)}) async-start(), calls=%async_computation.9 | async-start | bytes 7077888 | tf_op jit(solution)/shard_map/all_gather | solution.py:422
  10.5 94.8 %all-gather.15.cloned.1.call-start = ((), (), s32[]{:S(2)}) async-start(), calls=%async_computation.11 | async-start | bytes 1310720 | tf_op jit(solution)/shard_map/all_gather | solution.py:424
  70.3 80.6 %all-gather.13.cloned.1.call-start = ((), (), s32[]{:S(2)}) async-start(), calls=%async_computation.10 | async-start | bytes 2621440 | tf_op jit(solution)/shard_map/all_gather | solution.py:454
  105.2 102.0 %all-gather.17.cloned.1.call-start = ((), (), s32[]{:S(2)}) async-start(), calls=%async_computation.12 | async-start | bytes 9437184 | tf_op jit(solution)/shard_map/all_gather | solution.py:423
  107.1 112.3 %all-to-all-start = ((f32[32,2,512]{2,1,0:T(2,128)}), f32[32,2,512]{2,1,0:T(2,128)S(1)}, u32[]{:S(2)}, u32[]{:S(2)}) async-start(f32[32,2,512]{2,1,0:T(2,128)} %copy.92), calls=%async_computation | async-start | bytes 262144 | tf_op jit(solution)/shard_map/all_to_all | solution.py:402
  110.5 345.4 %reduce-scatter.8.cloned.1.call-start = ((), (), s32[]{:S(2)}) async-start(), calls=%async_computation.13 | async-start | bytes 1310720 | tf_op jit(solution)/shard_map/reduce_scatter | solution.py:474
  219.7 46.3 %collective-permute-start.5 = (bf16[256,2048]{1,0:T(8,128)(2,1)}, bf16[256,2048]{1,0:T(8,128)(2,1)}, u32[]{:S(2)}, u32[]{:S(2)}) collective-permute-start(bf16[256,2048]{1,0:T(8,128)(2,1)} %get-tuple-element.262.refs_1_), channel_id=1, source_target_pairs={{0,16},{8,24},{16,0},{24,8},{1,17},{9,25},{17,1},{25,9},{2,18},{10... | collective-permute-start | bytes 3145736 | tf_op jit(solution)/shard_map/ppermute | solution.py:293
  220.4 45.7 %collective-permute-start.11 = (bf16[256,2048]{1,0:T(8,128)(2,1)}, bf16[256,2048]{1,0:T(8,128)(2,1)S(1)}, u32[]{:S(2)}, u32[]{:S(2)}) collective-permute-start(bf16[256,2048]{1,0:T(8,128)(2,1)} %get-tuple-element.262.refs_1_), channel_id=1, source_target_pairs={{0,4},{4,0},{1,5},{5,1},{2,6},{6,2},{3,7},{7,3},{8,12},{12,8},{9,1... | collective-permute-start | bytes 3145736 | tf_op jit(solution)/shard_map/ppermute | solution.py:296
  220.7 51.6 %collective-permute-start.10 = (bf16[256,2048]{1,0:T(8,128)(2,1)}, bf16[256,2048]{1,0:T(8,128)(2,1)S(1)}, u32[]{:S(2)}, u32[]{:S(2)}) collective-permute-start(bf16[256,2048]{1,0:T(8,128)(2,1)} %get-tuple-element.263.refs_0_), channel_id=1, source_target_pairs={{0,4},{4,0},{1,5},{5,1},{2,6},{6,2},{3,7},{7,3},{8,12},{12,8},{9,1... | collective-permute-start | bytes 3145736 | tf_op jit(solution)/shard_map/ppermute | solution.py:296
  246.3 46.4 %collective-permute-start.15 = (bf16[256,2048]{1,0:T(8,128)(2,1)S(1)}, bf16[256,2048]{1,0:T(8,128)(2,1)}, u32[]{:S(2)}, u32[]{:S(2)}) collective-permute-start(bf16[256,2048]{1,0:T(8,128)(2,1)S(1)} %collective-permute-done.4.refs_0_), channel_id=1, source_target_pairs={{0,4},{4,0},{1,5},{5,1},{2,6},{6,2},{3,7},{7,3},{8,12},{12,8},{9,1... | collective-permute-start | bytes 3145736 | tf_op jit(solution)/shard_map/ppermute | solution.py:296
  402.9 78.2 %reduce-scatter.10.cloned.1.call-start = ((), (), s32[]{:S(2)}) async-start(), calls=%async_computation.14 | async-start | bytes 1310720 | tf_op jit(solution)/shard_map/reduce_scatter | solution.py:474
  453.9 57.3 %all-gather.21.cloned.1.call-start = ((), (), s32[]{:S(2)}) async-start(), calls=%async_computation.16 | async-start | bytes 1310720 | tf_op jit(solution)/shard_map/all_gather | solution.py:497
  484.6 55.8 %all-gather.23.cloned.1.call-start = ((), (), s32[]{:S(2)}) async-start(), calls=%async_computation.17 | async-start | bytes 1310720 | tf_op jit(solution)/shard_map/all_gather | solution.py:498
  485.2 296.6 %reduce-scatter.12.cloned.1.call-start = ((), (), s32[]{:S(2)}) async-start(), calls=%async_computation.18 | async-start | bytes 1310720 | tf_op jit(solution)/shard_map/reduce_scatter | solution.py:474
  543.4 47.3 %collective-permute-start.52 = (bf16[256,2048]{1,0:T(8,128)(2,1)}, bf16[256,2048]{1,0:T(8,128)(2,1)}, u32[]{:S(2)}, u32[]{:S(2)}) collective-permute-start(bf16[256,2048]{1,0:T(8,128)(2,1)} %all-gather.21.cloned.1.call-done.refs_0_), channel_id=1, source_target_pairs={{0,4},{4,0},{1,5},{5,1},{2,6},{6,2},{3,7},{7,3},{8,12},{12,8},{9,1... | collective-permute-start | bytes 3145736 | tf_op jit(solution)/shard_map/ppermute | solution.py:296
  543.9 46.8 %collective-permute-start.48 = (bf16[256,2048]{1,0:T(8,128)(2,1)}, bf16[256,2048]{1,0:T(8,128)(2,1)}, u32[]{:S(2)}, u32[]{:S(2)}) collective-permute-start(bf16[256,2048]{1,0:T(8,128)(2,1)} %collective-permute-done.46.refs_0_), channel_id=1, source_target_pairs={{0,8},{8,0},{16,24},{24,16},{1,9},{9,1},{17,25},{25,17},{2,10},{10... | collective-permute-start | bytes 3145736 | tf_op jit(solution)/shard_map/ppermute | solution.py:290
  544.7 68.9 %collective-permute-start.57 = (bf16[256,2048]{1,0:T(8,128)(2,1)}, bf16[256,2048]{1,0:T(8,128)(2,1)S(1)}, u32[]{:S(2)}, u32[]{:S(2)}) collective-permute-start(bf16[256,2048]{1,0:T(8,128)(2,1)} %collective-permute-done.46.refs_0_), channel_id=1, source_target_pairs={{0,4},{4,0},{1,5},{5,1},{2,6},{6,2},{3,7},{7,3},{8,12},{12,8},{9,1... | collective-permute-start | bytes 3145736 | tf_op jit(solution)/shard_map/ppermute | solution.py:296
  566.3 47.9 %collective-permute-start.49 = (bf16[256,2048]{1,0:T(8,128)(2,1)}, bf16[256,2048]{1,0:T(8,128)(2,1)}, u32[]{:S(2)}, u32[]{:S(2)}) collective-permute-start(bf16[256,2048]{1,0:T(8,128)(2,1)} %collective-permute-done.47.refs_1_), channel_id=1, source_target_pairs={{0,8},{8,0},{16,24},{24,16},{1,9},{9,1},{17,25},{25,17},{2,10},{10... | collective-permute-start | bytes 3145736 | tf_op jit(solution)/shard_map/ppermute | solution.py:290
  568.1 45.6 %collective-permute-start.58 = (bf16[256,2048]{1,0:T(8,128)(2,1)S(1)}, bf16[256,2048]{1,0:T(8,128)(2,1)}, u32[]{:S(2)}, u32[]{:S(2)}) collective-permute-start(bf16[256,2048]{1,0:T(8,128)(2,1)S(1)} %collective-permute-done.53.refs_1_), channel_id=1, source_target_pairs={{0,16},{8,24},{16,0},{24,8},{1,17},{9,25},{17,1},{25,9},{2,18},{10... | collective-permute-start | bytes 3145736 | tf_op jit(solution)/shard_map/ppermute | solution.py:293
  590.7 45.8 %collective-permute-start.55 = (bf16[256,2048]{1,0:T(8,128)(2,1)S(1)}, bf16[256,2048]{1,0:T(8,128)(2,1)S(1)}, u32[]{:S(2)}, u32[]{:S(2)}) collective-permute-start(bf16[256,2048]{1,0:T(8,128)(2,1)S(1)} %collective-permute-done.53.refs_1_), channel_id=1, source_target_pairs={{0,8},{8,0},{16,24},{24,16},{1,9},{9,1},{17,25},{25,17},{2,10},{10... | collective-permute-start | bytes 3145736 | tf_op jit(solution)/shard_map/ppermute | solution.py:290
  590.7 45.8 %collective-permute-start.54 = (bf16[256,2048]{1,0:T(8,128)(2,1)}, bf16[256,2048]{1,0:T(8,128)(2,1)S(1)}, u32[]{:S(2)}, u32[]{:S(2)}) collective-permute-start(bf16[256,2048]{1,0:T(8,128)(2,1)} %collective-permute-done.52.refs_0_), channel_id=1, source_target_pairs={{0,8},{8,0},{16,24},{24,16},{1,9},{9,1},{17,25},{25,17},{2,10},{10... | collective-permute-start | bytes 3145736 | tf_op jit(solution)/shard_map/ppermute | solution.py:290
  613.7 46.3 %collective-permute-start.59 = (bf16[256,2048]{1,0:T(8,128)(2,1)S(1)}, bf16[256,2048]{1,0:T(8,128)(2,1)S(1)}, u32[]{:S(2)}, u32[]{:S(2)}) collective-permute-start(bf16[256,2048]{1,0:T(8,128)(2,1)S(1)} %collective-permute-done.57.refs_0_), channel_id=1, source_target_pairs={{0,8},{8,0},{16,24},{24,16},{1,9},{9,1},{17,25},{25,17},{2,10},{10... | collective-permute-start | bytes 3145736 | tf_op jit(solution)/shard_map/ppermute | solution.py:290
  613.7 46.3 %collective-permute-start.60 = (bf16[256,2048]{1,0:T(8,128)(2,1)}, bf16[256,2048]{1,0:T(8,128)(2,1)S(1)}, u32[]{:S(2)}, u32[]{:S(2)}) collective-permute-start(bf16[256,2048]{1,0:T(8,128)(2,1)} %collective-permute-done.58.refs_1_), channel_id=1, source_target_pairs={{0,8},{8,0},{16,24},{24,16},{1,9},{9,1},{17,25},{25,17},{2,10},{10... | collective-permute-start | bytes 3145736 | tf_op jit(solution)/shard_map/ppermute | solution.py:290
  636.4 48.6 %collective-permute-start.50 = (bf16[512,512]{1,0:T(8,128)(2,1)}, bf16[512,512]{1,0:T(8,128)(2,1)S(1)}, u32[]{:S(2)}, u32[]{:S(2)}) collective-permute-start(bf16[512,512]{1,0:T(8,128)(2,1)} %get-tuple-element.141), channel_id=1, source_target_pairs={{0,8},{8,0},{16,24},{24,16},{1,9},{9,1},{17,25},{25,17},{2,10},{10... | collective-permute-start | bytes 1572872 | tf_op jit(solution)/shard_map/ppermute | solution.py:290
  717.6 45.8 %collective-permute-start.71 = (bf16[512,512]{1,0:T(8,128)(2,1)}, bf16[512,512]{1,0:T(8,128)(2,1)S(1)}, u32[]{:S(2)}, u32[]{:S(2)}) collective-permute-start(bf16[512,512]{1,0:T(8,128)(2,1)} %get-tuple-element.159), channel_id=1, source_target_pairs={{0,8},{8,0},{16,24},{24,16},{1,9},{9,1},{17,25},{25,17},{2,10},{10... | collective-permute-start | bytes 1572872 | tf_op jit(solution)/shard_map/ppermute | solution.py:290
  730.6 77.8 %reduce-scatter.14.cloned.1.call-start = ((), (), s32[]{:S(2)}) async-start(), calls=%async_computation.19 | async-start | bytes 1310720 | tf_op jit(solution)/shard_map/reduce_scatter | solution.py:474
  823.8 80.7 %all-gather.27.cloned.1.call-start = ((), (), s32[]{:S(2)}) async-start(), calls=%async_computation.23 | async-start | bytes 2621440 | tf_op jit(solution)/shard_map/all_gather | solution.py:521
  860.7 88.9 %reduce-scatter.16.cloned.1.call-start = ((), (), s32[]{:S(2)}) async-start(), calls=%async_computation.20 | async-start | bytes 2621440 | tf_op jit(solution)/shard_map/reduce_scatter | solution.py:542
  893.1 103.0 %all-gather.19.cloned.1.call-start = ((), (), s32[]{:S(2)}) async-start(), calls=%async_computation.15 | async-start | bytes 2621440 | tf_op jit(solution)/shard_map/all_gather | solution.py:491
  893.8 207.4 %reduce-scatter.20.cloned.1.call-start = ((), (), s32[]{:S(2)}) async-start(), calls=%async_computation.24 | async-start | bytes 2359296 | tf_op jit(solution)/shard_map/reduce_scatter | solution.py:574
  908.9 194.2 %all-gather.25.cloned.1.call-start = ((), (), s32[]{:S(2)}) async-start(), calls=%async_computation.21 | async-start | bytes 2621440 | tf_op jit(solution)/shard_map/all_gather | solution.py:551
  953.9 198.1 %reduce-scatter.18.cloned.1.call-start = ((), (), s32[]{:S(2)}) async-start(), calls=%async_computation.22 | async-start | bytes 7077888 | tf_op jit(solution)/shard_map/reduce_scatter | solution.py:571
  (179 other events, 3106.3 us)
Sparse Core Ops, SparseCore 0:
  11.3 49.8 all-gather.10
Sparse Core Ops, SparseCore 1:
  70.4 28.9 all-gather.14
  105.3 45.5 all-gather.12
  152.6 54.6 all-gather.16
  403.0 27.1 reduce-scatter.7
  453.9 27.1 reduce-scatter.9
  484.7 26.4 all-gather.20
  513.1 27.2 all-gather.22
  730.7 26.5 reduce-scatter.11
  781.9 26.5 reduce-scatter.13
  860.8 43.7 all-gather.26
  907.3 42.3 reduce-scatter.15
  951.3 44.8 all-gather.18
  999.6 39.9 reduce-scatter.19
  1041.7 46.5 all-gather.24
  1091.6 60.3 reduce-scatter.17

commit v3 on v2

--- a/solution.py
+++ b/solution.py
@@ -134,45 +134,54 @@
 
 def take_rows(x_refs, table_ref, rows_ref):
     blocks, capacity, width = rows_ref.shape[1:]
-    halves = len(x_refs) // blocks
-    slots = halves * x_refs[0].shape[0]
-    step = slots // halves
+    slots = table_ref.shape[3]
+    step, span = x_refs[0].shape
+    halves, splits = slots // step, width // span
     weights = []
     for block in range(blocks):
         chosen, weight = pick_rows(table_ref, block, capacity, slots)
         weights.append(weight)
         for cut in tiles_of(width):
-            found = jnp.dot(
-                chosen[:, :step], x_refs[block * halves][:, cut], preferred_element_type=wide
-            )
-            for half in range(1, halves):
-                found = found + jnp.dot(
+            split, begin = divmod(cut.start, span)
+            found = None
+            for half in range(halves):
+                x_ref = x_refs[(block * halves + half) * splits + split]
+                term = jnp.dot(
                     chosen[:, half * step : (half + 1) * step],
-                    x_refs[block * halves + half][:, cut],
+                    x_ref[:, begin : begin + cut.stop - cut.start],
                     preferred_element_type=wide,
                 )
+                found = term if found is None else found + term
             rows_ref[0, block, :, cut] = found.astype(low)
     return (rows_ref[0].reshape(blocks * capacity, width), jnp.concatenate(weights, axis=0))
 
 
-def combine_blocks(place_ref, y_ref, out_refs, capacity):
-    blocks, total, width = y_ref.shape
-    slots, step = out_refs[0].shape
-    parts = width // step
+def fill_spread(place_ref, spread_ref, capacity):
+    blocks, slots, total = spread_ref.shape
     for block in range(blocks):
-        matrix = spread_rows(place_ref, block, total // capacity, capacity, slots)
-        for k in range(parts):
-            out_refs[block * parts + k][...] = jnp.dot(
-                matrix, y_ref[block, :, k * step : (k + 1) * step], preferred_element_type=wide
+        spread_ref[block] = spread_rows(place_ref, block, total // capacity, capacity, slots)
+
+
+def combine_blocks(spread_ref, y_ref, out_refs):
+    for block, out_ref in enumerate(out_refs):
+        for cut in tiles_of(y_ref.shape[2]):
+            out_ref[:, cut] = jnp.dot(
+                spread_ref[block], y_ref[block, :, cut], preferred_element_type=wide
             ).astype(low)
 
 
 def forward_body(n_x, n_out, n_keep, *refs):
     x_refs, refs = refs[:n_x], refs[n_x:]
     (table_ref, place_ref, up_ref, down_ref), refs = refs[:4], refs[4 + n_keep :]
-    out_refs, (rows_ref, gate_up_ref, hidden_ref, y_ref) = refs[:n_out], refs[n_out:]
+    out_refs, (rows_ref, gate_up_ref, hidden_ref, y_ref, spread_ref) = refs[:n_out], refs[n_out:]
     expert = pl.program_id(0)
     blocks, capacity, width = rows_ref.shape[1:]
+    experts = y_ref.shape[1] // capacity
+
+    @pl.when(expert == 0)
+    def _():
+        fill_spread(place_ref, spread_ref, capacity)
+
     half = down_ref.shape[1]
     rows, weight = take_rows(x_refs, table_ref, rows_ref)
     gate_up = jnp.dot(rows, up_ref[0], preferred_element_type=wide)
@@ -189,17 +198,23 @@
             .reshape(blocks, capacity, -1)
         )
 
-    @pl.when(expert == pl.num_programs(0) - 1)
+    @pl.when(expert == experts - 1)
     def _():
-        combine_blocks(place_ref, y_ref, out_refs, capacity)
+        combine_blocks(spread_ref, y_ref, out_refs)
 
 
 def backward_body(n_x, n_out, n_keep, *refs):
     x_refs, refs = refs[:n_x], refs[n_x:]
     (table_ref, place_ref, up_ref, down_ref, gate_up_ref), refs = refs[:5], refs[5 + n_keep :]
-    out_refs, (rows_ref, grad_ref, y_ref) = refs[:n_out], refs[n_out:]
+    out_refs, (rows_ref, grad_ref, y_ref, spread_ref) = refs[:n_out], refs[n_out:]
     expert = pl.program_id(0)
     blocks, capacity, width = rows_ref.shape[1:]
+    experts = y_ref.shape[1] // capacity
+
+    @pl.when(expert == 0)
+    def _():
+        fill_spread(place_ref, spread_ref, capacity)
+
     half = down_ref.shape[1]
     rows, weight = take_rows(x_refs, table_ref, rows_ref)
     grad_hidden = nt_dot(rows, down_ref[0]) * weight
@@ -217,22 +232,22 @@
             nt_dot(grad_rows, up_ref[0, cut, :]).astype(low).reshape(blocks, capacity, -1)
         )
 
-    @pl.when(expert == pl.num_programs(0) - 1)
+    @pl.when(expert == experts - 1)
     def _():
-        combine_blocks(place_ref, y_ref, out_refs, capacity)
-
-
-def expert_call(chunk, pieces, table, place, w_up, w_down, gate_up, kept, capacity, total, parts):
+        combine_blocks(spread_ref, y_ref, out_refs)
+
+
+def expert_call(chunk, pieces, table, place, w_up, w_down, gate_up, kept, capacity, total):
     blocks, experts, _, slots = table.shape
-    width = pieces[0].shape[1]
+    width = w_up.shape[1]
     double, half = w_up.shape[2], w_down.shape[1]
     backward = gate_up is not None
+    once = pl.Buffered(1)
     row_spec = lambda last: pl.BlockSpec(
         (1, blocks, capacity, last), lambda e: (e, chunk, 0, 0)
     )
     row_shape = lambda last, kind: jax.ShapeDtypeStruct((experts, total, capacity, last), kind)
-    step = width // parts
-    whole = lambda shape: pl.BlockSpec(shape, lambda e: (0,) * len(shape))
+    whole = lambda shape: pl.BlockSpec(shape, lambda e: (0,) * len(shape), pipeline_mode=once)
     in_specs = [whole(p.shape) for p in pieces] + [
         pl.BlockSpec((blocks, 1, 2, slots), lambda e: (0, e, 0, 0)),
         whole((blocks, slots, experts)),
@@ -240,9 +255,9 @@
         pl.BlockSpec((1, half, width), lambda e: (e, 0, 0)),
     ]
     operands = [*pieces, table, place, w_up, w_down]
-    n_out = blocks * parts
-    out_specs = [whole((slots, step))] * n_out + [row_spec(width), row_spec(double)]
-    out_shape = [jax.ShapeDtypeStruct((slots, step), low)] * n_out + [row_shape(width, low)]
+    n_out = blocks
+    out_specs = [whole((slots, width))] * n_out + [row_spec(width), row_spec(double)]
+    out_shape = [jax.ShapeDtypeStruct((slots, width), low)] * n_out + [row_shape(width, low)]
     if backward:
         in_specs.append(row_spec(double))
         operands.append(gate_up)
@@ -262,9 +277,12 @@
         out_specs=out_specs,
         out_shape=out_shape,
         input_output_aliases=aliases,
-        scratch_shapes=[pltpu.VMEM((blocks, experts * capacity, width), low)],
+        scratch_shapes=[
+            pltpu.VMEM((blocks, experts * capacity, width), low),
+            pltpu.VMEM((blocks, slots, experts * capacity), low),
+        ],
         compiler_params=pltpu.CompilerParams(
-            dimension_semantics=("arbitrary",), vmem_limit_bytes=56 << 20
+            dimension_semantics=("arbitrary",), vmem_limit_bytes=48 << 20
         ),
         cost_estimate=pl.CostEstimate(
             flops=2 * rows * width * (2 * slots + double + half),
@@ -272,12 +290,39 @@
             transcendentals=rows * half,
         ),
     )(*operands, *kept)
-    outs = [made[b * parts : (b + 1) * parts] for b in range(blocks)]
-    return (outs, made[n_out:])
+    return (made[:n_out], made[n_out:])
 
 
 def added(left, right):
     return left.astype(wide) + right.astype(wide)
+
+
+def tie(values, *anchors):
+    return lax.optimization_barrier((values, anchors))[0]
+
+
+def sum_everywhere(values):
+    values = values[None]
+    for axis in everywhere:
+        size, step = lax.axis_size(axis), 1
+        while step < size:
+            pairs = [(i, i ^ step) for i in range(size)]
+            values = values + lax.ppermute(values, axis, pairs)
+            step *= 2
+    return values[0]
+
+
+def line_gather(shard):
+    size = lax.axis_size("tp")
+    if size > 4:
+        return lax.all_gather(shard, "tp", axis=0, tiled=True)
+    move = lambda d: lax.ppermute(
+        shard, "tp", [(i, i + d) for i in range(size) if 0 <= i + d < size]
+    )
+    near = [move(d) for d in range(size - 1, 0, -1)] + [shard] + [move(-d) for d in range(1, size)]
+    rows = shard.shape[0]
+    begin = (size - 1 - lax.axis_index("tp")) * rows
+    return lax.dynamic_slice_in_dim(jnp.concatenate(near, axis=0), begin, size * rows, 0)
 
 
 class Plane:
@@ -302,44 +347,107 @@
         chips = ((0, 0), (1, 0), (0, 1), (1, 1))
         return [(fsdp ^ (2 * x) ^ core) * 2 + (ctx ^ y) for x, y in chips for core in (0, 1)]
 
-    def gather(self, first, second):
+    def gather_whole(self, shard):
+        rows = shard.shape[0]
+        if not self.tree:
+            return lax.all_gather(shard, plane, axis=0, tiled=True)
+        halves = (shard[: rows // 2], shard[rows // 2 :]) if rows > 1 else (shard,)
+        x = [self.along_x(h) for h in halves]
+        y = [self.along_y(h) for h in halves]
+        far = [self.along_y(x[0])] + [self.along_x(h) for h in y[1:]]
+        whole = jnp.zeros((self.shards * rows, *shard.shape[1:]), shard.dtype)
+        order = self.order()
+        for c, pieces in enumerate((halves, x, y, far)):
+            for core in (0, 1):
+                begin = order[2 * c + core] * rows
+                for piece in pieces:
+                    found = self.core(piece) if core else piece
+                    whole = lax.dynamic_update_slice_in_dim(whole, found, begin, 0)
+                    begin = begin + piece.shape[0]
+        return whole
+
+    def reduce_whole(self, partial):
+        rows = partial.shape[0] // self.shards
+        if not self.tree:
+            return lax.psum_scatter(partial, plane, scatter_dimension=0, tiled=True).astype(wide)
+        blocks = [lax.dynamic_slice_in_dim(partial, i * rows, rows, 0) for i in self.order()]
+        pre = [added(blocks[2 * c], self.core(blocks[2 * c + 1])) for c in range(4)]
+        cuts = tiles_of(partial.shape[1], partial.shape[1] // 2)
+        return jnp.concatenate(
+            [self.total(k, *[p[:, cut] for p in pre]) for k, cut in enumerate(cuts)], axis=1
+        )
+
+    def total(self, k, own, near_x, near_y, far):
+        if k % 2 == 0:
+            near_y = near_y + self.along_x(far.astype(low)).astype(wide)
+        else:
+            near_x = near_x + self.along_y(far.astype(low)).astype(wide)
+        from_x, from_y = self.along_x(near_x.astype(low)), self.along_y(near_y.astype(low))
+        return own + from_x.astype(wide) + from_y.astype(wide)
+
+    def experts(self, first, second, call, parts, filler=list):
         if not self.tree:
             tops = jnp.split(lax.all_gather(first, plane, axis=0, tiled=True), self.shards)
             ends = jnp.split(lax.all_gather(second, plane, axis=0, tiled=True), self.shards)
-            return [
-                [tops[i], ends[i], tops[i + 1], ends[i + 1]] for i in range(0, self.shards, 2)
+            made = []
+            for i in range(0, self.shards, 2):
+                made += call(i // 2, [tops[i], ends[i], tops[i + 1], ends[i + 1]])
+            total = lax.psum_scatter(
+                jnp.concatenate(made, axis=0), plane, scatter_dimension=0, tiled=True
+            )
+            return jnp.split(total, parts // 2, axis=1)
+        cuts = tiles_of(first.shape[1], first.shape[1] // parts)
+        pre = lambda made, other: [added(made[0][:, cut], other[:, cut]) for cut in cuts]
+        middle = first.shape[1] // 2
+
+        def beyond(x_half, y_half):
+            return self.along_y(x_half[:, :middle]), self.along_x(y_half[:, middle:])
+
+        x_first, y_first = self.along_x(first), self.along_y(first)
+        far_first = beyond(x_first, y_first)
+        second = tie(second, x_first, y_first)
+        x_second, y_second = self.along_x(second), self.along_y(second)
+        own = call(0, [first, second, self.core(first), self.core(second)])
+        x_second, y_second = tie((x_second, y_second), own[0])
+        far_second = beyond(x_second, y_second)
+        near_x = call(1, [x_first, x_second, self.core(x_first), self.core(x_second)])
+        other_own, other_x = self.core(own[1]), self.core(near_x[1])
+        pieces = [y_first, y_second, self.core(y_first), self.core(y_second)]
+        near_y = call(2, tie(pieces, far_first, other_own))
+        other_y = self.core(near_y[1])
+        sum_x = pre(near_x, other_x)
+        early_x = [sum_x[k].astype(low) for k in range(0, parts, 2)]
+        pieces = [*far_first, *far_second]
+        pieces = tie(pieces + [self.core(piece) for piece in pieces], early_x)
+        sent_x = [self.along_x(a) for a in early_x]
+        far = tie(call(3, pieces), sent_x, other_y)
+        other_far = self.core(far[1])
+        sum_y = pre(near_y, other_y)
+        sent_y = [self.along_y(sum_y[k].astype(low)) for k in range(1, parts, 2)]
+        sum_own = pre(own, other_own)
+        sum_far = pre(far, other_far)
+        totals, fill = [], filler()
+
+        def send_far(k, before):
+            via_x, via_y = tie([sum_far[j].astype(low) for j in (k, k + 1)], before)
+            return self.along_x(via_x), self.along_y(via_y)
+
+        coming = send_far(0, ())
+        for k in range(0, parts, 2):
+            far_y, far_x = tie(coming, sent_y[k // 2], totals[-1:])
+            from_y = self.along_y((sum_y[k] + far_y.astype(wide)).astype(low))
+            from_x = self.along_x((sum_x[k + 1] + far_x.astype(wide)).astype(low))
+            if k + 2 < parts:
+                coming = send_far(k + 2, coming)
+                from_y, from_x = tie((from_y, from_x), coming)
+            elif fill:
+                from_y, from_x = tie((from_y, from_x), fill)
+            both = [
+                added(sum_own[k], sent_x[k // 2]) + from_y.astype(wide),
+                added(sum_own[k + 1], sent_y[k // 2]) + from_x.astype(wide),
             ]
-        x_first, y_second = self.along_x(first), self.along_y(second)
-        x_second, y_first = self.along_x(second), self.along_y(first)
-        far_first, far_second = self.along_y(x_first), self.along_x(y_second)
-        pairs = [
-            (first, second),
-            (x_first, x_second),
-            (y_first, y_second),
-            (far_first, far_second),
-        ]
-        return [[a, b, self.core(a), self.core(b)] for a, b in pairs]
-
-    def reduce(self, outs):
-        if not self.tree:
-            flat = [jnp.concatenate(block, axis=1) for pair in outs for block in pair]
-            total = lax.psum_scatter(
-                jnp.concatenate(flat, axis=0), plane, scatter_dimension=0, tiled=True
-            )
-            return jnp.split(total.astype(wide), len(outs[0][0]), axis=1)
-        sums = []
-        for k in range(len(outs[0][0])):
-            own, near_x, near_y, far = [added(pair[0][k], self.core(pair[1][k])) for pair in outs]
-            if k % 2 == 0:
-                near_y = near_y + self.along_x(far.astype(low)).astype(wide)
-            else:
-                near_x = near_x + self.along_y(far.astype(low)).astype(wide)
-            sums.append(
-                own
-                + self.along_x(near_x.astype(low)).astype(wide)
-                + self.along_y(near_y.astype(low)).astype(wide)
-            )
-        return sums
+            totals.append(jnp.concatenate(both, axis=1).astype(low))
+        return totals
 
 
 def per_device(
@@ -383,7 +491,8 @@
             jnp.sum(lengths).astype(wide)[None],
         ]
     )
-    small_all = lax.all_gather(small, plane, axis=0)
+    places = Plane()
+    small_all = places.gather_whole(small[None])
     gain_rows = small_all[:, : 2 * gain_cols].reshape(shards, 2, gain_cols)
     full_gains = jnp.swapaxes(gain_rows, 0, 1).reshape(2, shards * gain_cols)
     head_rows = small_all[:, 2 * gain_cols : 2 * (gain_cols + head_cols)]
@@ -406,23 +515,20 @@
     offset = (jnp.arange(shard_experts, dtype=jnp.int32) * capacity)[None, :, None]
     place = jnp.swapaxes(jnp.where(rank >= 0, rank + offset, -1), 1, 2)
     w_up = w_gate_up.reshape(shard_experts, width, 2 * hidden_local)
-    places = Plane()
     order = places.order()
     sort = lambda a: jnp.concatenate(
         [lax.dynamic_slice_in_dim(a, block, 1, 0) for block in order], axis=0
     )
     table, place = sort(table), sort(place)
-    back_table = jnp.swapaxes(
+    half_table = jnp.swapaxes(
         table.reshape(shards, shard_experts, 2, tp_size, 2, part // 2), 3, 4
     ).reshape(table.shape)
-    chunks = shards // 2
     pair = lambda a, c: a[2 * c : 2 * c + 2]
     parts = 4
 
     full_qkv = lax.all_gather(w_qkv.reshape(w_qkv.shape[0], -1), plane, axis=0, tiled=True)
-    full_out = lax.all_gather(
-        lax.all_gather(w_out, "tp", axis=0, tiled=True), plane, axis=1, tiled=True
-    )
+    rows_out = tie(line_gather(w_out), full_qkv[:1])
+    full_out = lax.all_gather(rows_out, plane, axis=1, tiled=True)
     flat_states = states.astype(wide).reshape(tokens, width)
     normed = rms_norm(flat_states, gain_attn).astype(low)
     projected = jnp.dot(normed, full_qkv, preferred_element_type=wide).reshape(
@@ -451,38 +557,37 @@
     attended_low = (
         jnp.stack([p[0] for p in pieces]).astype(low).reshape(tokens, heads_local * head_dim)
     )
-    attended_all = lax.all_gather(attended_low, "tp", axis=1, tiled=True)
-    middle = flat_states + jnp.dot(attended_all, full_out, preferred_element_type=wide)
-    normed_ffn = rms_norm(middle, gain_ffn).astype(low)
-
     begin = tp_index * part
     own = lambda a: lax.dynamic_slice_in_dim(a, begin, part, 0)
-    half_rows = tokens // 2
-    x_chunks = places.gather(normed_ffn[:half_rows], normed_ffn[half_rows:])
-    kept, outs = (), []
-    for c in range(chunks):
-        made, kept = expert_call(
-            c, x_chunks[c], pair(table, c), pair(place, c), w_up, w_down, None, kept,
-            capacity, shards, parts,
+    attended_own = lax.all_to_all(
+        attended_low, "tp", split_axis=0, concat_axis=1, tiled=True
+    )
+    states_own = own(flat_states)
+    middle_own = states_own + jnp.dot(attended_own, full_out, preferred_element_type=wide)
+    normed_own = rms_norm(middle_own, gain_ffn).astype(low)
+
+    both_halves = lambda a: [
+        lax.all_gather(half, "tp", axis=0, tiled=True) for half in (a[: part // 2], a[part // 2 :])
+    ]
+    saved = [()]
+
+    def forward(chunk, pieces):
+        made, saved[0] = expert_call(
+            chunk, pieces, pair(half_table, chunk), pair(place, chunk), w_up, w_down, None, saved[0],
+            capacity, shards,
         )
-        outs.append(made)
-    rows_in, gate_up, hidden = kept
-
-    def finish(outs):
-        sums = places.reduce(outs)
+        return made
+
+    def finish(sums):
         ready = [
-            lax.psum_scatter(
-                jnp.concatenate(sums[k : k + 2], axis=1).astype(low),
-                "tp",
-                scatter_dimension=0,
-                tiled=True,
-            )
-            for k in range(0, parts, 2)
+            lax.psum_scatter(total, "tp", scatter_dimension=0, tiled=True) for total in sums
         ]
         return jnp.concatenate(ready, axis=1).astype(wide)
 
-    mixture = finish(outs)
-    middle_own = own(middle)
+    mixture = finish(
+        places.experts(*both_halves(normed_own), forward, parts)
+    )
+    rows_in, gate_up, hidden = saved[0]
     final_own = middle_own + mixture
     difference = final_own - own(teacher.reshape(tokens, width)).astype(wide)
     valid_own = own(row_valid)
@@ -493,23 +598,34 @@
     )
 
     grad_low = grad_final.astype(low)
-    grad_chunks = places.gather(
-        lax.all_gather(grad_low[: part // 2], "tp", axis=0, tiled=True),
-        lax.all_gather(grad_low[part // 2 :], "tp", axis=0, tiled=True),
-    )
-    kept, outs = (), []
-    for c in range(chunks):
-        made, kept = expert_call(
-            c, grad_chunks[c], pair(back_table, c), pair(place, c), w_up, w_down, gate_up, kept,
-            capacity, shards, parts,
+    saved[0] = ()
+
+    def backward(chunk, pieces):
+        made, saved[0] = expert_call(
+            chunk, pieces, pair(half_table, chunk), pair(place, chunk), w_up, w_down, gate_up,
+            saved[0], capacity, shards,
         )
-        outs.append(made)
-    rows_out, grad_rows = kept
-    grad_ffn = finish(outs)
-    grad_gate_up = jnp.einsum(
-        "ebcd,ebcf->edf", rows_in, grad_rows, preferred_element_type=wide
-    ).reshape(shard_experts, width, 2, hidden_local)
-    grad_down = jnp.einsum("ebcf,ebcd->efd", hidden, rows_out, preferred_element_type=wide)
+        if chunk == 1:
+            made = tie(made, activations)
+        return made
+
+    def weight_grads():
+        rows_back, grad_rows = saved[0]
+        grad_up = jnp.einsum(
+            "ebcd,ebcf->edf", rows_in, grad_rows, preferred_element_type=wide
+        ).reshape(shard_experts, width, 2, hidden_local)
+        made.append(grad_up)
+        made.append(
+            jnp.einsum("ebcf,ebcd->efd", hidden, rows_back, preferred_element_type=wide)
+        )
+        return [made[1]]
+
+    made = []
+    sums = places.experts(*both_halves(grad_low), backward, parts, weight_grads)
+    if not made:
+        weight_grads()
+    grad_gate_up, grad_down = made
+    grad_ffn = tie(finish(sums), grad_gate_up, grad_down)
 
     grad_middle_norm, grad_gain_ffn = norm_back(grad_ffn, middle_own, gain_ffn)
     grad_middle = grad_final + grad_middle_norm
@@ -519,7 +635,7 @@
         nt_dot(grad_branch, full_out).astype(low), "tp", split_axis=1, concat_axis=0, tiled=True
     )
     branch_block = lax.all_gather(grad_branch, "tp", axis=0, tiled=True)
-    grad_w_out = jnp.einsum("nf,nd->fd", attended_low, branch_block, preferred_element_type=wide)
+    grad_w_out = jnp.einsum("nd,nf->df", branch_block, attended_low, preferred_element_type=wide)
     grad_heads = grad_attended.reshape(seq_count, slot_count, heads_local, head_dim)
     backs = [
         back_sequence(
@@ -546,17 +662,14 @@
         tiled=True,
     ).astype(wide)
     grad_w_qkv = jnp.einsum("nd,nk->dk", normed, grad_proj_low, preferred_element_type=wide)
-    grad_states_norm, grad_gain_attn = norm_back(grad_normed, own(flat_states), gain_attn)
+    grad_states_norm, grad_gain_attn = norm_back(grad_normed, states_own, gain_attn)
     grad_states = (
         lax.all_gather((grad_middle + grad_states_norm).astype(low), "tp", axis=0, tiled=True)
         .astype(wide)
         .reshape(seq_count, slot_count, width)
     )
-    sums = lax.psum(
-        jnp.concatenate(
-            [grad_gain_attn, grad_gain_ffn, grad_qk.reshape(-1), local_loss[None]]
-        ),
-        everywhere,
+    sums = sum_everywhere(
+        jnp.concatenate([grad_gain_attn, grad_gain_ffn, grad_qk.reshape(-1), local_loss[None]])
     )
     out_gains = lax.dynamic_slice_in_dim(
         sums[: 2 * width].reshape(2, width), plane_index * gain_cols, gain_cols, 1
@@ -568,12 +681,12 @@
         1,
     )
     loss_value = sums[-1] / valid_count
-    out_qkv = lax.psum_scatter(
-        grad_w_qkv.astype(low), plane, scatter_dimension=0, tiled=True
-    ).astype(wide).reshape(w_qkv.shape)
-    out_w_out = lax.psum_scatter(
-        grad_w_out.astype(low), plane, scatter_dimension=1, tiled=True
-    ).astype(wide)
+    weights_own = places.reduce_whole(
+        jnp.concatenate([grad_w_qkv.astype(low), grad_w_out.astype(low)], axis=1)
+    )
+    qkv_cols = grad_w_qkv.shape[1]
+    out_qkv = weights_own[:, :qkv_cols].reshape(w_qkv.shape)
+    out_w_out = weights_own[:, qkv_cols:].T
     return (
         activations,
         loss_value,

time: 1180 us -> 978 us (0.83)
  waiting for transfers between devices: 615 us -> 436 us
  blocking collectives: 66.3 us -> 0 us
  starting transfers between devices: 57 us -> 94.1 us
  other arithmetic: 65 us -> 82.5 us
    reduce_scatter x6 -> x4, waiting for transfers between devices: 96.4 us -> 30.2 us  [finish(): lax.psum_scatter(total, 'tp', scatter_dimension=0, tiled=True)]
    all_gather x5, waiting for transfers between devices: 136 us -> 79.7 us  [the longest x4 79.7 us: per_device(): lax.all_gather(half, 'tp', axis=0, tiled=True)]
    psum x1 -> x0, blocking collectives: 40.4 us -> none  [per_device(): lax.psum(jnp.concatenate([grad_gain_attn, grad_gain_ffn, grad_qk.reshape(...]
    all_gather x1, waiting for transfers between devices: 34.8 us -> 0.02 us  [per_device(): lax.all_gather(final_own.astype(low), 'tp', axis=0, tiled=True)]
    ppermute x18 -> x24, waiting for transfers between devices: 124 us -> 89.7 us  [along_x(): return lax.ppermute(a, 'fsdp', [(i, i ^ 2) for i in range(self.fsdp)])]
    ppermute x0 -> x11, waiting for transfers between devices: none -> 26.8 us  [the longest x6 21.9 us: line_gather(): lax.ppermute(shard, 'tp', [(i, i + d) for i in range(size) if 0 <= i + d...]
    unnamed x1 -> x0, blocking collectives: 25.9 us -> none
    ppermute x0 -> x11, starting transfers between devices: none -> 19.7 us  [the longest x6 14.6 us: line_gather(): lax.ppermute(shard, 'tp', [(i, i + d) for i in range(size) if 0 <= i + d...]
  transfers between devices with their start and end apart: 104 -> 115, of which waited for: 41 -> 57; matrix products, arithmetic and copies ran while one was open for 15% -> 19% of each run, Pallas kernels for 14% -> 17%
where the time goes in v3:
time: 978 us; the launch traced here: 967 us
  waiting for transfers between devices  436 us (45%)
  Pallas kernels  163 us (17%)
  starting transfers between devices  94.1 us (10%)
  matrix products  86.1 us (9%)
  local copies, waits for them, and re-layouts  85.4 us (9%)
  other arithmetic  82.5 us (8%)
  between operations  20.6 us (2%)
    pallas_call x8, Pallas kernels, expert_call(): pl.pallas_call(body, grid=(experts,), in_specs=in_specs + [pl.BlockSpec(m...  163 us
    ppermute x24, waiting for transfers between devices, along_x(): return lax.ppermute(a, 'fsdp', [(i, i ^ 2) for i in range(self.fsdp)])  89.7 us
    ppermute x25, waiting for transfers between devices, along_y(): return lax.ppermute(a, 'ctx', [(i, i ^ 1) for i in range(self.ctx)])  82.1 us
    all_gather x4, waiting for transfers between devices, per_device(): lax.all_gather(half, 'tp', axis=0, tiled=True)  79.7 us
    unnamed x211, local copies, waits for them, and re-layouts  48.3 us
    ppermute x1, waiting for transfers between devices, per_device(): other_kv = lax.ppermute(key_value, 'ctx', mirror)  39.5 us
    reduce_scatter x4, waiting for transfers between devices, finish(): lax.psum_scatter(total, 'tp', scatter_dimension=0, tiled=True)  30.2 us
    ppermute x25, starting transfers between devices, along_y(): return lax.ppermute(a, 'ctx', [(i, i ^ 1) for i in range(self.ctx)])  29 us
  transfers between devices with their start and end apart: 115, of which 57 were waited for; matrix products, arithmetic and copies ran while one was open for 19% of the time, Pallas kernels for 17%

profile of v3, /device:TPU:0, one launch (start us, length us, event | category | flops | bytes accessed | tf_op | source)
XLA Modules:
  0.0 966.9 jit_solution(479112244521736211)
XLA Ops:
  33.6 12.8 %collective-permute-done.12 = bf16[512,256]{1,0:T(8,128)(2,1)S(1)} collective-permute-done((bf16[512,256]{1,0:T(8,128)(2,1)S(1)}, bf16[512,256]{1,0:T(8,128)(2,1)S(1)}, u32[]{:S(2)}, u32[]{:S(2)}) %collective-permute-start.12) | collective-permute-done | bytes 262176 | tf_op jit(solution)/shard_map/ppermute | solution.py:319
  69.6 39.5 %collective-permute-done.7 = bf16[1,512,2,4,128]{1,4,3,2,0:T(8,128)(2,1)} collective-permute-done((bf16[1,512,2,4,128]{1,4,3,2,0:T(8,128)(2,1)}, bf16[1,512,2,4,128]{1,4,3,2,0:T(8,128)(2,1)}, u32[]{:S(2)}, u32[]{:S(2)}) %collective-permute-start.7) | collective-permute-done | bytes 1048608 | tf_op jit(solution)/shard_map/ppermute | solution.py:548
  126.6 10.2 %all-to-all-done = bf16[4,128,512]{1,2,0:T(8,128)(2,1)S(1)} async-done(((bf16[4,128,512]{1,2,0:T(8,128)(2,1)}), bf16[4,128,512]{1,2,0:T(8,128)(2,1)S(1)}, u32[]{:S(2)}, u32[]{:S(2)}) %all-to-all-start) | async-done | bytes 524320 | tf_op jit(solution)/shard_map/all_to_all | solution.py:562
  144.4 25.7 %all-gather.14.cloned.1.call-done.refs_0_ = bf16[256,2048]{1,0:T(8,128)(2,1)} async-done(((bf16[64,2048]{1,0:T(8,128)(2,1)}), bf16[256,2048]{1,0:T(8,128)(2,1)}) %all-gather.14.cloned.1.call-update) | async-done | bytes 1048592 | tf_op jit(solution)/shard_map/all_gather | solution.py:570
  177.7 14.1 %reshape.365.refs_6_.refs_10_ = bf16[4,2048,512]{2,1,0:T(8,128)(2,1)} reshape(bf16[4,2048,2,256]{3,2,1,0:T(2,128)(2,1)} %param.20) | data formatting | bytes 16777216 | tf_op jit(solution)/shard_map/reshape | solution.py:517
  205.9 18.9 %shard_map.186 = (bf16[512,2048]{1,0:T(8,128)(2,1)}, bf16[512,2048]{1,0:T(8,128)(2,1)}, bf16[4,8,160,2048]{3,2,1,0:T(8,128)(2,1)}, f32[4,8,160,512]{3,2,1,0:T(8,128)}, bf16[4,8,160,256]{3,2,1,0:T(8,128)(2,1)}) custom-call(bf16[256,2048]{1,0:T(8,128)(2,1)S(1)} %copy-done.4, bf16[256,2048]{1,0:T(8,128)(2,1)S(1)} %copy-done.5, ...), custom_call_target="tpu_custom_call" | custom-call | flops 9395240960 | bytes 17563648 | tf_op jit(solution)/shard_map/pallas_call | solution.py:273
  230.4 19.5 %shard_map.187 = (bf16[512,2048]{1,0:T(8,128)(2,1)}, bf16[512,2048]{1,0:T(8,128)(2,1)}, bf16[4,8,160,2048]{3,2,1,0:T(8,128)(2,1)}, f32[4,8,160,512]{3,2,1,0:T(8,128)}, bf16[4,8,160,256]{3,2,1,0:T(8,128)(2,1)}) custom-call(bf16[256,2048]{1,0:T(8,128)(2,1)S(1)} %collective-permute-done.14.refs_0_, ...), custom_call_target="tpu_custom_call", output_to_operand_aliasing={{2}: (8, {}), {3}: (9, {}), {4}: (10, {})} | custom-call | flops 9395240960 | bytes 17563648 | tf_op jit(solution)/shard_map/pallas_call | solution.py:273
  251.1 13.4 %collective-permute-done.28.refs_1_ = bf16[256,1024]{1,0:T(8,128)(2,1)} collective-permute-done((bf16[256,1024]{1,0:T(8,128)(2,1)S(1)}, bf16[256,1024]{1,0:T(8,128)(2,1)}, u32[]{:S(2)}, u32[]{:S(2)}) %collective-permute-start.28) | collective-permute-done | bytes 524320 | tf_op jit(solution)/shard_map/ppermute | solution.py:338
  264.5 19.7 %shard_map.188 = (bf16[512,2048]{1,0:T(8,128)(2,1)}, bf16[512,2048]{1,0:T(8,128)(2,1)}, bf16[4,8,160,2048]{3,2,1,0:T(8,128)(2,1)}, f32[4,8,160,512]{3,2,1,0:T(8,128)}, bf16[4,8,160,256]{3,2,1,0:T(8,128)(2,1)}) custom-call(bf16[256,2048]{1,0:T(8,128)(2,1)S(1)} %collective-permute-done.15.refs_0_, ...), custom_call_target="tpu_custom_call", output_to_operand_aliasing={{2}: (8, {}), {3}: (9, {}), {4}: (10, {})} | custom-call | flops 9395240960 | bytes 17563648 | tf_op jit(solution)/shard_map/pallas_call | solution.py:273
  288.6 11.1 %collective-permute-done.30.refs_2_ = bf16[256,1024]{1,0:T(8,128)(2,1)S(1)} collective-permute-done((bf16[256,1024]{1,0:T(8,128)(2,1)S(1)}, bf16[256,1024]{1,0:T(8,128)(2,1)S(1)}, u32[]{:S(2)}, u32[]{:S(2)}) %collective-permute-start.30) | collective-permute-done | bytes 524320 | tf_op jit(solution)/shard_map/ppermute | solution.py:341
  306.9 19.3 %shard_map.189 = (bf16[512,2048]{1,0:T(8,128)(2,1)}, bf16[512,2048]{1,0:T(8,128)(2,1)}, bf16[4,8,160,2048]{3,2,1,0:T(8,128)(2,1)}, f32[4,8,160,512]{3,2,1,0:T(8,128)}, bf16[4,8,160,256]{3,2,1,0:T(8,128)(2,1)}) custom-call(bf16[256,1024]{1,0:T(8,128)(2,1)S(1)} %collective-permute-done.27.refs_0_, ...), custom_call_target="tpu_custom_call", output_to_operand_aliasing={{2}: (12, {}), {3}: (13, {}), {4}: (14, {})} | custom-call | flops 9395240960 | bytes 17563648 | tf_op jit(solution)/shard_map/pallas_call | solution.py:273
  337.7 8.5 collective-permute-done.40
  364.0 9.2 collective-permute-done.42
  388.8 11.7 %collective-permute-done.45 = bf16[512,512]{1,0:T(8,128)(2,1)S(1)} collective-permute-done((bf16[512,512]{1,0:T(8,128)(2,1)S(1)}, bf16[512,512]{1,0:T(8,128)(2,1)S(1)}, u32[]{:S(2)}, u32[]{:S(2)}) %collective-permute-start.45) | collective-permute-done | bytes 524320 | tf_op jit(solution)/shard_map/ppermute | solution.py:341
  405.5 8.1 collective-permute-done.47
  420.4 24.0 %reduce-scatter.8.cloned.1.call-done = bf16[128,1024]{1,0:T(8,128)(2,1)} async-done(((bf16[512,1024]{1,0:T(8,128)(2,1)}), bf16[128,1024]{1,0:T(8,128)(2,1)}) %reduce-scatter.8.cloned.1.call-update) | async-done | bytes 262160 | tf_op jit(solution)/shard_map/reduce_scatter | solution.py:583
  448.3 25.9 %all-gather.20.cloned.1.call-done.refs_0_ = bf16[256,2048]{1,0:T(8,128)(2,1)} async-done(((bf16[64,2048]{1,0:T(8,128)(2,1)}), bf16[256,2048]{1,0:T(8,128)(2,1)}) %all-gather.20.cloned.1.call-update) | async-done | bytes 1048592 | tf_op jit(solution)/shard_map/all_gather | solution.py:570
  477.2 26.7 %all-gather.22.cloned.1.call-done.refs_1_ = bf16[256,2048]{1,0:T(8,128)(2,1)} async-done(((bf16[64,2048]{1,0:T(8,128)(2,1)}), bf16[256,2048]{1,0:T(8,128)(2,1)}) %all-gather.22.cloned.1.call-update) | async-done | bytes 1048592 | tf_op jit(solution)/shard_map/all_gather | solution.py:570
  509.4 21.4 %shard_map.190 = (bf16[512,2048]{1,0:T(8,128)(2,1)}, bf16[512,2048]{1,0:T(8,128)(2,1)}, bf16[4,8,160,2048]{3,2,1,0:T(8,128)(2,1)}, bf16[4,8,160,512]{3,2,1,0:T(8,128)(2,1)}) custom-call(bf16[256,2048]{1,0:T(8,128)(2,1)S(1)} %copy-done.6, bf16[256,2048]{1,0:T(8,128)(2,1)S(1)} %copy-done.7, bf16[256,2048]{1,0:T(8,128)(2,1)} %collective-permute-done.50.refs_2_, ...), custom_call_target="tpu_custom_call" | custom-call | flops 9395240960 | bytes 17563648 | tf_op jit(solution)/shard_map/pallas_call | solution.py:273
  535.5 21.0 %shard_map.191 = (bf16[512,2048]{1,0:T(8,128)(2,1)}, bf16[512,2048]{1,0:T(8,128)(2,1)}, bf16[4,8,160,2048]{3,2,1,0:T(8,128)(2,1)}, bf16[4,8,160,512]{3,2,1,0:T(8,128)(2,1)}) custom-call(bf16[256,2048]{1,0:T(8,128)(2,1)} %collective-permute-done.48.refs_0_, ...), custom_call_target="tpu_custom_call", output_to_operand_aliasing={{2}: (9, {}), {3}: (10, {})} | custom-call | flops 9395240960 | bytes 17563648 | tf_op jit(solution)/shard_map/pallas_call | solution.py:273
  557.9 13.2 %collective-permute-done.62.refs_1_ = bf16[256,1024]{1,0:T(8,128)(2,1)S(1)} collective-permute-done((bf16[256,1024]{1,0:T(8,128)(2,1)S(1)}, bf16[256,1024]{1,0:T(8,128)(2,1)S(1)}, u32[]{:S(2)}, u32[]{:S(2)}) %collective-permute-start.62) | collective-permute-done | bytes 524320 | tf_op jit(solution)/shard_map/ppermute | solution.py:338
  571.1 21.6 %shard_map.192 = (bf16[512,2048]{1,0:T(8,128)(2,1)}, bf16[512,2048]{1,0:T(8,128)(2,1)}, bf16[4,8,160,2048]{3,2,1,0:T(8,128)(2,1)}, bf16[4,8,160,512]{3,2,1,0:T(8,128)(2,1)}) custom-call(bf16[256,2048]{1,0:T(8,128)(2,1)S(1)} %collective-permute-done.49.refs_0_, ...), custom_call_target="tpu_custom_call", output_to_operand_aliasing={{2}: (9, {}), {3}: (10, {})} | custom-call | flops 9395240960 | bytes 17563648 | tf_op jit(solution)/shard_map/pallas_call | solution.py:273
  595.7 11.4 %collective-permute-done.64.refs_2_ = bf16[256,1024]{1,0:T(8,128)(2,1)S(1)} collective-permute-done((bf16[256,1024]{1,0:T(8,128)(2,1)S(1)}, bf16[256,1024]{1,0:T(8,128)(2,1)S(1)}, u32[]{:S(2)}, u32[]{:S(2)}) %collective-permute-start.64) | collective-permute-done | bytes 524320 | tf_op jit(solution)/shard_map/ppermute | solution.py:341
  612.4 21.2 %shard_map.193 = (bf16[512,2048]{1,0:T(8,128)(2,1)}, bf16[512,2048]{1,0:T(8,128)(2,1)}, bf16[4,8,160,2048]{3,2,1,0:T(8,128)(2,1)}, bf16[4,8,160,512]{3,2,1,0:T(8,128)(2,1)}) custom-call(bf16[256,1024]{1,0:T(8,128)(2,1)S(1)} %collective-permute-done.61.refs_0_, ...), custom_call_target="tpu_custom_call", output_to_operand_aliasing={{2}: (13, {}), {3}: (14, {})} | custom-call | flops 9395240960 | bytes 17563648 | tf_op jit(solution)/shard_map/pallas_call | solution.py:273
  667.8 8.8 collective-permute-done.76
  678.3 8.2 collective-permute-done.77
  704.8 15.5 %convolution_bitcast_fusion = f32[4,256,2048]{2,1,0:T(8,128)} fusion(bf16[4,8,160,256]{3,2,1,0:T(8,128)(2,1)S(1)} %copy-done.16, bf16[4,8,160,2048]{3,2,1,0:T(8,128)(2,1)} %get-tuple-element.194), kind=kOutput, calls=%fused_computation.25 | convolution fusion | flops 5368709120 | bytes 31981568 | tf_op jit(solution)/shard_map/ebcf,ebcd->efd/dot_general | solution.py:619
  723.3 19.3 %fusion.66 = f32[4,2048,512,1]{1,2,3,0:T(8,128)} fusion(bf16[4,8,160,2048]{3,2,1,0:T(8,128)(2,1)} %get-tuple-element.197, bf16[4,8,160,512]{3,2,1,0:T(8,128)(2,1)} %get-tuple-element.198), kind=kOutput, calls=%fused_computation.265 | convolution fusion | flops 10737418240 | bytes 42991616 | tf_op jit(solution)/shard_map/ebcd,ebcf->edf/dot_general | solution.py:614
  765.1 14.5 %all-to-all-done.2 = bf16[128,4,512]{2,0,1:T(8,128)(2,1)S(1)} async-done(((bf16[128,4,512]{2,0,1:T(8,128)(2,1)}), bf16[128,4,512]{2,0,1:T(8,128)(2,1)S(1)}, u32[]{:S(2)}, u32[]{:S(2)}) %all-to-all-start.2) | async-done | bytes 524320 | tf_op jit(solution)/shard_map/all_to_all | solution.py:634
  805.8 18.9 %collective-permute-done.82 = bf16[1,512,2,4,128]{1,4,3,2,0:T(8,128)(2,1)S(1)} collective-permute-done((bf16[1,512,2,4,128]{1,4,3,2,0:T(8,128)(2,1)}, bf16[1,512,2,4,128]{1,4,3,2,0:T(8,128)(2,1)S(1)}, u32[]{:S(2)}, u32[]{:S(2)}) %collective-permute-start.82) | collective-permute-done | bytes 1048608 | tf_op jit(solution)/shard_map/ppermute | solution.py:649
  869.6 22.0 %reduce-scatter.14.cloned.1.call-done = bf16[128,2048]{1,0:T(8,128)(2,1)} async-done(((bf16[512,2048]{1,0:T(8,128)(2,1)}), bf16[128,2048]{1,0:T(8,128)(2,1)}) %reduce-scatter.14.cloned.1.call-update) | async-done | bytes 524304 | tf_op jit(solution)/shard_map/reduce_scatter | solution.py:658
  912.2 25.0 %copy.104 = f32[4,2048,2,256]{3,2,1,0:T(2,128)} copy(f32[4,2048,2,256]{1,3,2,0:T(8,128)} %bitcast.200) | data formatting | bytes 33554432
  (599 shorter events, 386.1 us)
Async XLA Ops:
  7.2 52.8 %all-gather.10.cloned.1.call-start = ((), (), s32[]{:S(2)}) async-start(), calls=%async_computation.8 | async-start | bytes 7077888 | tf_op jit(solution)/shard_map/all_gather | solution.py:529
  9.6 127.2 %all-gather.12.cloned.1.call-start = ((), (), s32[]{:S(2)}) async-start(), calls=%async_computation.9 | async-start | bytes 9437184 | tf_op jit(solution)/shard_map/all_gather | solution.py:531
  69.2 39.9 %collective-permute-start.7 = (bf16[1,512,2,4,128]{1,4,3,2,0:T(8,128)(2,1)}, bf16[1,512,2,4,128]{1,4,3,2,0:T(8,128)(2,1)}, u32[]{:S(2)}, u32[]{:S(2)}) collective-permute-start(bf16[1,512,2,4,128]{1,4,3,2,0:T(8,128)(2,1)} %pad_maximum_fusion.1), channel_id=1, source_target_pairs={{0,4},{4,0},{1,5},{5,1},{2,6},{6,2},{3,7},{7,3},{8,12},{12,8},{9,1... | collective-permute-start | bytes 3145736 | tf_op jit(solution)/shard_map/ppermute | solution.py:548
  124.0 46.0 %all-gather.14.cloned.1.call-start = ((), (), s32[]{:S(2)}) async-start(), calls=%async_computation.10 | async-start | bytes 1310720 | tf_op jit(solution)/shard_map/all_gather | solution.py:570
  143.8 55.7 %all-gather.16.cloned.1.call-start = ((), (), s32[]{:S(2)}) async-start(), calls=%async_computation.11 | async-start | bytes 1310720 | tf_op jit(solution)/shard_map/all_gather | solution.py:570
  177.6 242.8 %reduce-scatter.6.cloned.1.call-start = ((), (), s32[]{:S(2)}) async-start(), calls=%async_computation.12 | async-start | bytes 1310720 | tf_op jit(solution)/shard_map/reduce_scatter | solution.py:583
  227.4 37.2 %collective-permute-start.18 = (bf16[512,2048]{1,0:T(8,128)(2,1)}, bf16[512,2048]{1,0:T(8,128)(2,1)}, u32[]{:S(2)}, u32[]{:S(2)}) collective-permute-start(bf16[512,2048]{1,0:T(8,128)(2,1)} %get-tuple-element.107), channel_id=1, source_target_pairs={{0,8},{8,0},{16,24},{24,16},{1,9},{9,1},{17,25},{25,17},{2,10},{10... | collective-permute-start | bytes 6291464 | tf_op jit(solution)/shard_map/ppermute | solution.py:335
  229.8 34.7 %collective-permute-start.25 = (bf16[256,2048]{1,0:T(8,128)(2,1)S(1)}, bf16[256,2048]{1,0:T(8,128)(2,1)}, u32[]{:S(2)}, u32[]{:S(2)}) collective-permute-start(bf16[256,2048]{1,0:T(8,128)(2,1)S(1)} %collective-permute-done.15.refs_0_), channel_id=1, source_target_pairs={{0,8},{8,0},{16,24},{24,16},{1,9},{9,1},{17,25},{25,17},{2,10},{10... | collective-permute-start | bytes 3145736 | tf_op jit(solution)/shard_map/ppermute | solution.py:335
  229.8 34.7 %collective-permute-start.26 = (bf16[256,2048]{1,0:T(8,128)(2,1)}, bf16[256,2048]{1,0:T(8,128)(2,1)}, u32[]{:S(2)}, u32[]{:S(2)}) collective-permute-start(bf16[256,2048]{1,0:T(8,128)(2,1)} %collective-permute-done.20.refs_1_), channel_id=1, source_target_pairs={{0,8},{8,0},{16,24},{24,16},{1,9},{9,1},{17,25},{25,17},{2,10},{10... | collective-permute-start | bytes 3145736 | tf_op jit(solution)/shard_map/ppermute | solution.py:335
  249.9 52.2 %collective-permute-start.23 = (bf16[512,2048]{1,0:T(8,128)(2,1)}, bf16[512,2048]{1,0:T(8,128)(2,1)}, u32[]{:S(2)}, u32[]{:S(2)}) collective-permute-start(bf16[512,2048]{1,0:T(8,128)(2,1)} %get-tuple-element.113), channel_id=1, source_target_pairs={{0,8},{8,0},{16,24},{24,16},{1,9},{9,1},{17,25},{25,17},{2,10},{10... | collective-permute-start | bytes 6291464 | tf_op jit(solution)/shard_map/ppermute | solution.py:335
  284.2 45.7 %collective-permute-start.29 = (bf16[512,2048]{1,0:T(8,128)(2,1)}, bf16[512,2048]{1,0:T(8,128)(2,1)}, u32[]{:S(2)}, u32[]{:S(2)}) collective-permute-start(bf16[512,2048]{1,0:T(8,128)(2,1)} %get-tuple-element.123), channel_id=1, source_target_pairs={{0,8},{8,0},{16,24},{24,16},{1,9},{9,1},{17,25},{25,17},{2,10},{10... | collective-permute-start | bytes 6291464 | tf_op jit(solution)/shard_map/ppermute | solution.py:335
  388.1 56.3 %reduce-scatter.8.cloned.1.call-start = ((), (), s32[]{:S(2)}) async-start(), calls=%async_computation.13 | async-start | bytes 1310720 | tf_op jit(solution)/shard_map/reduce_scatter | solution.py:583
  418.9 55.3 %all-gather.20.cloned.1.call-start = ((), (), s32[]{:S(2)}) async-start(), calls=%async_computation.15 | async-start | bytes 1310720 | tf_op jit(solution)/shard_map/all_gather | solution.py:570
  447.5 56.3 %all-gather.22.cloned.1.call-start = ((), (), s32[]{:S(2)}) async-start(), calls=%async_computation.16 | async-start | bytes 1310720 | tf_op jit(solution)/shard_map/all_gather | solution.py:570
  448.3 108.3 %all-gather.18.cloned.1.call-start = ((), (), s32[]{:S(2)}) async-start(), calls=%async_computation.14 | async-start | bytes 2621440 | tf_op jit(solution)/shard_map/all_gather | solution.py:596
  477.2 29.8 %collective-permute-start.50 = (bf16[256,2048]{1,0:T(8,128)(2,1)}, bf16[256,2048]{1,0:T(8,128)(2,1)}, u32[]{:S(2)}, u32[]{:S(2)}) collective-permute-start(bf16[256,2048]{1,0:T(8,128)(2,1)} %all-gather.20.cloned.1.call-done.refs_0_), channel_id=1, source_target_pairs={{0,8},{8,0},{16,24},{24,16},{1,9},{9,1},{17,25},{25,17},{2,10},{10... | collective-permute-start | bytes 3145736 | tf_op jit(solution)/shard_map/ppermute | solution.py:335
  503.9 238.8 %reduce-scatter.10.cloned.1.call-start = ((), (), s32[]{:S(2)}) async-start(), calls=%async_computation.17 | async-start | bytes 1310720 | tf_op jit(solution)/shard_map/reduce_scatter | solution.py:583
  531.5 39.6 %collective-permute-start.52 = (bf16[512,2048]{1,0:T(8,128)(2,1)}, bf16[512,2048]{1,0:T(8,128)(2,1)}, u32[]{:S(2)}, u32[]{:S(2)}) collective-permute-start(bf16[512,2048]{1,0:T(8,128)(2,1)} %get-tuple-element.152), channel_id=1, source_target_pairs={{0,8},{8,0},{16,24},{24,16},{1,9},{9,1},{17,25},{25,17},{2,10},{10... | collective-permute-start | bytes 6291464 | tf_op jit(solution)/shard_map/ppermute | solution.py:335
  534.9 36.1 %collective-permute-start.59 = (bf16[256,2048]{1,0:T(8,128)(2,1)S(1)}, bf16[256,2048]{1,0:T(8,128)(2,1)}, u32[]{:S(2)}, u32[]{:S(2)}) collective-permute-start(bf16[256,2048]{1,0:T(8,128)(2,1)S(1)} %collective-permute-done.49.refs_0_), channel_id=1, source_target_pairs={{0,8},{8,0},{16,24},{24,16},{1,9},{9,1},{17,25},{25,17},{2,10},{10... | collective-permute-start | bytes 3145736 | tf_op jit(solution)/shard_map/ppermute | solution.py:335
  535.0 36.1 %collective-permute-start.60 = (bf16[256,2048]{1,0:T(8,128)(2,1)}, bf16[256,2048]{1,0:T(8,128)(2,1)}, u32[]{:S(2)}, u32[]{:S(2)}) collective-permute-start(bf16[256,2048]{1,0:T(8,128)(2,1)} %collective-permute-done.54.refs_1_), channel_id=1, source_target_pairs={{0,8},{8,0},{16,24},{24,16},{1,9},{9,1},{17,25},{25,17},{2,10},{10... | collective-permute-start | bytes 3145736 | tf_op jit(solution)/shard_map/ppermute | solution.py:335
  556.5 52.7 %collective-permute-start.57 = (bf16[512,2048]{1,0:T(8,128)(2,1)}, bf16[512,2048]{1,0:T(8,128)(2,1)S(1)}, u32[]{:S(2)}, u32[]{:S(2)}) collective-permute-start(bf16[512,2048]{1,0:T(8,128)(2,1)} %get-tuple-element.159), channel_id=1, source_target_pairs={{0,8},{8,0},{16,24},{24,16},{1,9},{9,1},{17,25},{25,17},{2,10},{10... | collective-permute-start | bytes 6291464 | tf_op jit(solution)/shard_map/ppermute | solution.py:335
  592.7 42.8 %collective-permute-start.63 = (bf16[512,2048]{1,0:T(8,128)(2,1)}, bf16[512,2048]{1,0:T(8,128)(2,1)S(1)}, u32[]{:S(2)}, u32[]{:S(2)}) collective-permute-start(bf16[512,2048]{1,0:T(8,128)(2,1)} %get-tuple-element.168), channel_id=1, source_target_pairs={{0,8},{8,0},{16,24},{24,16},{1,9},{9,1},{17,25},{25,17},{2,10},{10... | collective-permute-start | bytes 6291464 | tf_op jit(solution)/shard_map/ppermute | solution.py:335
  667.0 32.2 %collective-permute-start.79 = (bf16[512,512]{1,0:T(8,128)(2,1)}, bf16[512,512]{1,0:T(8,128)(2,1)S(1)}, u32[]{:S(2)}, u32[]{:S(2)}) collective-permute-start(bf16[512,512]{1,0:T(8,128)(2,1)} %get-tuple-element.272), channel_id=1, source_target_pairs={{0,4},{4,0},{1,5},{5,1},{2,6},{6,2},{3,7},{7,3},{8,12},{12,8},{9,1... | collective-permute-start | bytes 1572872 | tf_op jit(solution)/shard_map/ppermute | solution.py:341
  692.7 56.2 %reduce-scatter.12.cloned.1.call-start = ((), (), s32[]{:S(2)}) async-start(), calls=%async_computation.18 | async-start | bytes 1310720 | tf_op jit(solution)/shard_map/reduce_scatter | solution.py:583
  765.0 81.1 %all-gather.26.cloned.1.call-start = ((), (), s32[]{:S(2)}) async-start(), calls=%async_computation.21 | async-start | bytes 2621440 | tf_op jit(solution)/shard_map/all_gather | solution.py:637
  801.9 89.7 %reduce-scatter.14.cloned.1.call-start = ((), (), s32[]{:S(2)}) async-start(), calls=%async_computation.19 | async-start | bytes 2621440 | tf_op jit(solution)/shard_map/reduce_scatter | solution.py:658
  835.4 116.6 %all-gather.24.cloned.1.call-start = ((), (), s32[]{:S(2)}) async-start(), calls=%async_computation.20 | async-start | bytes 2621440 | tf_op jit(solution)/shard_map/all_gather | solution.py:667
  866.6 38.1 %collective-permute-start.95 = (bf16[256,1024]{0,1:T(8,128)(2,1)}, bf16[256,1024]{0,1:T(8,128)(2,1)}, u32[]{:S(2)}, u32[]{:S(2)}) collective-permute-start(bf16[256,1024]{0,1:T(8,128)(2,1)} %get-tuple-element.310), channel_id=1, source_target_pairs={{0,4},{4,0},{1,5},{5,1},{2,6},{6,2},{3,7},{7,3},{8,12},{12,8},{9,1... | collective-permute-start | bytes 1572872 | tf_op jit(solution)/shard_map/ppermute | solution.py:341
  868.1 39.9 %collective-permute-start.93 = (bf16[256,1024]{0,1:T(8,128)(2,1)}, bf16[256,1024]{0,1:T(8,128)(2,1)}, u32[]{:S(2)}, u32[]{:S(2)}) collective-permute-start(bf16[256,1024]{0,1:T(8,128)(2,1)} %get-tuple-element.309), channel_id=1, source_target_pairs={{0,16},{8,24},{16,0},{24,8},{1,17},{9,25},{17,1},{25,9},{2,18},{10... | collective-permute-start | bytes 1572872 | tf_op jit(solution)/shard_map/ppermute | solution.py:338
  899.6 39.0 %collective-permute-start.90 = (bf16[256,1024]{0,1:T(8,128)(2,1)}, bf16[256,1024]{0,1:T(8,128)(2,1)S(1)}, u32[]{:S(2)}, u32[]{:S(2)}) collective-permute-start(bf16[256,1024]{0,1:T(8,128)(2,1)} %slice.713), channel_id=1, source_target_pairs={{0,16},{8,24},{16,0},{24,8},{1,17},{9,25},{17,1},{25,9},{2,18},{10... | collective-permute-start | bytes 1572872 | tf_op jit(solution)/shard_map/ppermute | solution.py:338
  903.3 35.4 %collective-permute-start.97 = (bf16[256,1024]{0,1:T(8,128)(2,1)}, bf16[256,1024]{0,1:T(8,128)(2,1)S(1)}, u32[]{:S(2)}, u32[]{:S(2)}) collective-permute-start(bf16[256,1024]{0,1:T(8,128)(2,1)} %slice.712), channel_id=1, source_target_pairs={{0,4},{4,0},{1,5},{5,1},{2,6},{6,2},{3,7},{7,3},{8,12},{12,8},{9,1... | collective-permute-start | bytes 1572872 | tf_op jit(solution)/shard_map/ppermute | solution.py:341
  906.7 31.9 %collective-permute-start.96 = (bf16[256,1024]{0,1:T(8,128)(2,1)}, bf16[256,1024]{0,1:T(8,128)(2,1)}, u32[]{:S(2)}, u32[]{:S(2)}) collective-permute-start(bf16[256,1024]{0,1:T(8,128)(2,1)} %fusion.33), channel_id=1, source_target_pairs={{0,16},{8,24},{16,0},{24,8},{1,17},{9,25},{17,1},{25,9},{2,18},{10... | collective-permute-start | bytes 1572872 | tf_op jit(solution)/shard_map/ppermute | solution.py:338
  (178 other events, 2408.4 us)
Sparse Core Ops, SparseCore 0:
  10.5 49.4 all-gather.9
  62.4 69.6 all-gather.11
  143.9 26.0 all-gather.13
  172.0 27.4 all-gather.15
  388.2 25.5 reduce-scatter.5
  419.0 25.3 reduce-scatter.7
  447.6 26.5 all-gather.19
  476.4 27.4 all-gather.21
  506.0 45.3 all-gather.17
  692.8 26.0 reduce-scatter.9
  723.4 25.4 reduce-scatter.11
  802.0 44.0 all-gather.25
  848.9 42.6 reduce-scatter.13
  896.0 45.2 all-gather.23

commit v4 on v3

--- a/solution.py
+++ b/solution.py
@@ -3,6 +3,7 @@
 import jax
 import jax.numpy as jnp
 from jax import lax
+from jax.experimental.layout import Layout, with_layout_constraint
 from jax.experimental import pallas as pl
 from jax.experimental.pallas import tpu as pltpu
 from jax.sharding import PartitionSpec as P
@@ -135,24 +136,18 @@
 def take_rows(x_refs, table_ref, rows_ref):
     blocks, capacity, width = rows_ref.shape[1:]
     slots = table_ref.shape[3]
-    step, span = x_refs[0].shape
-    halves, splits = slots // step, width // span
-    weights = []
+    weights, place = [], 0
     for block in range(blocks):
         chosen, weight = pick_rows(table_ref, block, capacity, slots)
         weights.append(weight)
-        for cut in tiles_of(width):
-            split, begin = divmod(cut.start, span)
-            found = None
-            for half in range(halves):
-                x_ref = x_refs[(block * halves + half) * splits + split]
-                term = jnp.dot(
-                    chosen[:, half * step : (half + 1) * step],
-                    x_ref[:, begin : begin + cut.stop - cut.start],
-                    preferred_element_type=wide,
-                )
-                found = term if found is None else found + term
-            rows_ref[0, block, :, cut] = found.astype(low)
+        done = 0
+        while done < width:
+            x_ref = x_refs[place]
+            for cut in tiles_of(x_ref.shape[1]):
+                rows_ref[0, block, :, done + cut.start : done + cut.stop] = jnp.dot(
+                    chosen, x_ref[:, cut], preferred_element_type=wide
+                ).astype(low)
+            done, place = done + x_ref.shape[1], place + 1
     return (rows_ref[0].reshape(blocks * capacity, width), jnp.concatenate(weights, axis=0))
 
 
@@ -237,14 +232,14 @@
         combine_blocks(spread_ref, y_ref, out_refs)
 
 
-def expert_call(chunk, pieces, table, place, w_up, w_down, gate_up, kept, capacity, total):
+def expert_call(begin, pieces, table, place, w_up, w_down, gate_up, kept, capacity, total):
     blocks, experts, _, slots = table.shape
     width = w_up.shape[1]
     double, half = w_up.shape[2], w_down.shape[1]
     backward = gate_up is not None
     once = pl.Buffered(1)
     row_spec = lambda last: pl.BlockSpec(
-        (1, blocks, capacity, last), lambda e: (e, chunk, 0, 0)
+        (1, blocks, capacity, last), lambda e: (e, begin // blocks, 0, 0)
     )
     row_shape = lambda last, kind: jax.ShapeDtypeStruct((experts, total, capacity, last), kind)
     whole = lambda shape: pl.BlockSpec(shape, lambda e: (0,) * len(shape), pipeline_mode=once)
@@ -282,7 +277,7 @@
             pltpu.VMEM((blocks, slots, experts * capacity), low),
         ],
         compiler_params=pltpu.CompilerParams(
-            dimension_semantics=("arbitrary",), vmem_limit_bytes=48 << 20
+            dimension_semantics=("arbitrary",), vmem_limit_bytes=56 << 20
         ),
         cost_estimate=pl.CostEstimate(
             flops=2 * rows * width * (2 * slots + double + half),
@@ -385,69 +380,66 @@
         from_x, from_y = self.along_x(near_x.astype(low)), self.along_y(near_y.astype(low))
         return own + from_x.astype(wide) + from_y.astype(wide)
 
-    def experts(self, first, second, call, parts, filler=list):
+    def experts(self, first, second, call, filler, ready=()):
         if not self.tree:
-            tops = jnp.split(lax.all_gather(first, plane, axis=0, tiled=True), self.shards)
-            ends = jnp.split(lax.all_gather(second, plane, axis=0, tiled=True), self.shards)
-            made = []
+            split = lambda a: jnp.split(lax.all_gather(a, plane, axis=0, tiled=True), self.shards)
+            halves, made = list(zip(split(first), split(second), strict=True)), []
             for i in range(0, self.shards, 2):
-                made += call(i // 2, [tops[i], ends[i], tops[i + 1], ends[i + 1]])
-            total = lax.psum_scatter(
+                made += call(i, [*halves[i], *halves[i + 1]])
+            return lax.psum_scatter(
                 jnp.concatenate(made, axis=0), plane, scatter_dimension=0, tiled=True
             )
-            return jnp.split(total, parts // 2, axis=1)
-        cuts = tiles_of(first.shape[1], first.shape[1] // parts)
-        pre = lambda made, other: [added(made[0][:, cut], other[:, cut]) for cut in cuts]
-        middle = first.shape[1] // 2
+        parts, step = 4, first.shape[1] // 2
+        middle = step
+        pre = lambda made, other: [
+            added(made[:, k * step : (k + 1) * step], other[:, k * step : (k + 1) * step])
+            for k in range(parts)
+        ]
+        narrow = lambda a: a.astype(low)
 
         def beyond(x_half, y_half):
             return self.along_y(x_half[:, :middle]), self.along_x(y_half[:, middle:])
 
         x_first, y_first = self.along_x(first), self.along_y(first)
+        second = tie(second, x_first, y_first, ready)
+        own_pieces = [first, second, self.core(first), self.core(second)]
         far_first = beyond(x_first, y_first)
-        second = tie(second, x_first, y_first)
         x_second, y_second = self.along_x(second), self.along_y(second)
-        own = call(0, [first, second, self.core(first), self.core(second)])
+        over_x, over_y = self.core(x_first), self.core(y_first)
+        own = tie(call(0, tie(own_pieces, over_x, over_y)), far_first)
         x_second, y_second = tie((x_second, y_second), own[0])
         far_second = beyond(x_second, y_second)
-        near_x = call(1, [x_first, x_second, self.core(x_first), self.core(x_second)])
+        far_pieces = [self.core(piece) for piece in far_first]
+        over_y = [over_y, self.core(y_second)]
+        near_x = call(2, [x_first, x_second, over_x, self.core(x_second)])
+        near_x = tie(near_x, far_second, far_pieces, over_y)
         other_own, other_x = self.core(own[1]), self.core(near_x[1])
-        pieces = [y_first, y_second, self.core(y_first), self.core(y_second)]
-        near_y = call(2, tie(pieces, far_first, other_own))
+        far_pieces += [self.core(piece) for piece in far_second]
+        near_y = tie(call(4, [y_first, y_second, *over_y]), other_own, other_x, far_pieces)
         other_y = self.core(near_y[1])
-        sum_x = pre(near_x, other_x)
-        early_x = [sum_x[k].astype(low) for k in range(0, parts, 2)]
-        pieces = [*far_first, *far_second]
-        pieces = tie(pieces + [self.core(piece) for piece in pieces], early_x)
+        sum_x, sum_y = pre(near_x[0], other_x), pre(near_y[0], other_y)
+        early_x = [narrow(sum_x[k]) for k in (0, 2)]
+        early_y = [narrow(sum_y[k]) for k in (1, 3)]
+        last = call(6, tie([*far_first, *far_second, *far_pieces], early_x, early_y))
         sent_x = [self.along_x(a) for a in early_x]
-        far = tie(call(3, pieces), sent_x, other_y)
-        other_far = self.core(far[1])
-        sum_y = pre(near_y, other_y)
-        sent_y = [self.along_y(sum_y[k].astype(low)) for k in range(1, parts, 2)]
-        sum_own = pre(own, other_own)
-        sum_far = pre(far, other_far)
-        totals, fill = [], filler()
-
-        def send_far(k, before):
-            via_x, via_y = tie([sum_far[j].astype(low) for j in (k, k + 1)], before)
-            return self.along_x(via_x), self.along_y(via_y)
-
-        coming = send_far(0, ())
-        for k in range(0, parts, 2):
-            far_y, far_x = tie(coming, sent_y[k // 2], totals[-1:])
-            from_y = self.along_y((sum_y[k] + far_y.astype(wide)).astype(low))
-            from_x = self.along_x((sum_x[k + 1] + far_x.astype(wide)).astype(low))
-            if k + 2 < parts:
-                coming = send_far(k + 2, coming)
-                from_y, from_x = tie((from_y, from_x), coming)
-            elif fill:
-                from_y, from_x = tie((from_y, from_x), fill)
-            both = [
-                added(sum_own[k], sent_x[k // 2]) + from_y.astype(wide),
-                added(sum_own[k + 1], sent_y[k // 2]) + from_x.astype(wide),
-            ]
-            totals.append(jnp.concatenate(both, axis=1).astype(low))
-        return totals
+        sent_y = [self.along_y(a) for a in early_y]
+        last = tie(last, sent_x, sent_y)
+        sum_far = pre(last[0], self.core(last[1]))
+        sum_own = pre(own[0], other_own)
+        fillers = iter(filler())
+        far = [(self.along_y if k % 2 else self.along_x)(narrow(sum_far[k])) for k in range(parts)]
+        far = tie(far, next(fillers))
+        near = [
+            self.along_x(narrow(added(sum_x[k], far[k])))
+            if k % 2
+            else self.along_y(narrow(added(sum_y[k], far[k])))
+            for k in range(parts)
+        ]
+        near = tie(near, next(fillers))
+        sent = [sent_x[0], sent_y[0], sent_x[1], sent_y[1]]
+        return jnp.concatenate(
+            [added(sum_own[k], sent[k]) + near[k].astype(wide) for k in range(parts)], axis=1
+        ).astype(low)
 
 
 def per_device(
@@ -520,13 +512,14 @@
         [lax.dynamic_slice_in_dim(a, block, 1, 0) for block in order], axis=0
     )
     table, place = sort(table), sort(place)
-    half_table = jnp.swapaxes(
-        table.reshape(shards, shard_experts, 2, tp_size, 2, part // 2), 3, 4
-    ).reshape(table.shape)
-    pair = lambda a, c: a[2 * c : 2 * c + 2]
-    parts = 4
-
-    full_qkv = lax.all_gather(w_qkv.reshape(w_qkv.shape[0], -1), plane, axis=0, tiled=True)
+    some = lambda a, begin, pieces: a[begin : begin + blocks_in(pieces)]
+
+    def blocks_in(pieces):
+        return sum(piece.shape[1] for piece in pieces) // width
+
+    full_qkv = lax.all_gather(
+        w_qkv.reshape(w_qkv.shape[0], -1), plane, axis=0, tiled=True
+    )
     rows_out = tie(line_gather(w_out), full_qkv[:1])
     full_out = lax.all_gather(rows_out, plane, axis=1, tiled=True)
     flat_states = states.astype(wide).reshape(tokens, width)
@@ -535,13 +528,14 @@
         tokens, 3, heads_local, head_dim
     )
 
-    def prepare_local(projected_in, gains_in):
-        return prepare(projected_in, gains_in, tok_position)
-
-    (queries, key_states, values), prepare_back = jax.vjp(prepare_local, projected, qk_float)
+    def prepare_query(projected_in, gain):
+        return rotate(rms_norm(projected_in, gain), tok_position)
+
+    queries, query_back = jax.vjp(prepare_query, projected[:, 0], qk_float[0])
+    key_states, key_back = jax.vjp(prepare_query, projected[:, 1], qk_float[1])
     query_low = queries.astype(low).reshape(seq_count, slot_count, heads_local, head_dim)
     key_value = (
-        jnp.stack([key_states, values], axis=1)
+        jnp.stack([key_states, projected[:, 2]], axis=1)
         .astype(low)
         .reshape(seq_count, slot_count, 2, heads_local, head_dim)
     )
@@ -566,66 +560,75 @@
     middle_own = states_own + jnp.dot(attended_own, full_out, preferred_element_type=wide)
     normed_own = rms_norm(middle_own, gain_ffn).astype(low)
 
-    both_halves = lambda a: [
-        lax.all_gather(half, "tp", axis=0, tiled=True) for half in (a[: part // 2], a[part // 2 :])
-    ]
+    middle_col = width // 2
+    cols = (slice(0, middle_col), slice(middle_col, width))
+
+    def spread(*halves):
+        return [lax.all_gather(half.astype(low), "tp", axis=0, tiled=True) for half in halves]
+
     saved = [()]
 
-    def forward(chunk, pieces):
+    def forward(begin, pieces):
         made, saved[0] = expert_call(
-            chunk, pieces, pair(half_table, chunk), pair(place, chunk), w_up, w_down, None, saved[0],
-            capacity, shards,
+            begin, pieces, some(table, begin, pieces), some(place, begin, pieces), w_up, w_down,
+            None, saved[0], capacity, shards,
         )
         return made
 
-    def finish(sums):
-        ready = [
-            lax.psum_scatter(total, "tp", scatter_dimension=0, tiled=True) for total in sums
-        ]
-        return jnp.concatenate(ready, axis=1).astype(wide)
-
-    mixture = finish(
-        places.experts(*both_halves(normed_own), forward, parts)
+    def finish(half):
+        return lax.psum_scatter(half, "tp", scatter_dimension=0, tiled=True).astype(wide)
+
+    teacher_own = own(teacher.reshape(tokens, width)).astype(wide)
+    valid_own = own(row_valid)
+    grad_scale = (2.0 * loss_scale / valid_count * valid_own)[:, None]
+    mixture = places.experts(
+        *spread(normed_own[:, cols[0]], normed_own[:, cols[1]]),
+        forward,
+        lambda: ((), ()),
+        (w_up, table, place),
     )
     rows_in, gate_up, hidden = saved[0]
-    final_own = middle_own + mixture
-    difference = final_own - own(teacher.reshape(tokens, width)).astype(wide)
-    valid_own = own(row_valid)
+    final_own = middle_own + finish(mixture)
+    difference = final_own - teacher_own
     local_loss = jnp.sum(valid_own * jnp.sum(difference * difference, axis=-1))
-    grad_final = 2.0 * loss_scale / valid_count * valid_own[:, None] * difference
+    grad_final = grad_scale * difference
+    spread_halves = spread(grad_final[:, cols[0]], grad_final[:, cols[1]])
     activations = lax.all_gather(final_own.astype(low), "tp", axis=0, tiled=True).reshape(
         seq_count, slot_count, width
     )
 
-    grad_low = grad_final.astype(low)
     saved[0] = ()
 
-    def backward(chunk, pieces):
+    def backward(begin, pieces):
         made, saved[0] = expert_call(
-            chunk, pieces, pair(half_table, chunk), pair(place, chunk), w_up, w_down, gate_up,
-            saved[0], capacity, shards,
+            begin, pieces, some(table, begin, pieces), some(place, begin, pieces), w_up, w_down,
+            gate_up, saved[0], capacity, shards,
         )
-        if chunk == 1:
+        if begin == 2:
             made = tie(made, activations)
         return made
 
     def weight_grads():
         rows_back, grad_rows = saved[0]
-        grad_up = jnp.einsum(
-            "ebcd,ebcf->edf", rows_in, grad_rows, preferred_element_type=wide
-        ).reshape(shard_experts, width, 2, hidden_local)
-        made.append(grad_up)
         made.append(
             jnp.einsum("ebcf,ebcd->efd", hidden, rows_back, preferred_element_type=wide)
         )
-        return [made[1]]
+        yield [made[0]]
+        grad_up = jnp.einsum("ebcd,ebcf->edf", rows_in, grad_rows, preferred_element_type=wide)
+        made.append(grad_up)
+        yield [grad_up]
 
     made = []
-    sums = places.experts(*both_halves(grad_low), backward, parts, weight_grads)
+    total_in = places.experts(*spread_halves, backward, weight_grads)
     if not made:
-        weight_grads()
-    grad_gate_up, grad_down = made
-    grad_ffn = tie(finish(sums), grad_gate_up, grad_down)
+        for _ in weight_grads():
+            pass
+    grad_down, grad_up = made
+    grad_gate_up = with_layout_constraint(
+        grad_up.reshape(shard_experts, width, 2, hidden_local),
+        Layout(major_to_minor=(0, 1, 2, 3)),
+    )
+    grad_ffn = tie(finish(total_in), grad_gate_up, grad_down)
 
     grad_middle_norm, grad_gain_ffn = norm_back(grad_ffn, middle_own, gain_ffn)
     grad_middle = grad_final + grad_middle_norm
@@ -647,14 +650,12 @@
     grad_kv = jnp.stack([b[1] for b in backs])
     sent_kv = grad_kv[:, slot_count:].astype(low)
     own_kv = grad_kv[:, :slot_count] + lax.ppermute(sent_kv, "ctx", mirror).astype(wide)
-    grad_projected, grad_qk = prepare_back(
-        (
-            grad_query.reshape(tokens, heads_local, head_dim),
-            own_kv[:, :, 0].reshape(tokens, heads_local, head_dim),
-            own_kv[:, :, 1].reshape(tokens, heads_local, head_dim),
-        )
-    )
-    grad_proj_low = grad_projected.astype(low).reshape(tokens, -1)
+    grad_q, grad_q_gain = query_back(grad_query.reshape(tokens, heads_local, head_dim))
+    grad_k, grad_k_gain = key_back(own_kv[:, :, 0].reshape(tokens, heads_local, head_dim))
+    grad_v = own_kv[:, :, 1].reshape(tokens, heads_local, head_dim)
+    flat = lambda a: a.astype(low).reshape(tokens, -1)
+    grad_proj_low = jnp.concatenate([flat(grad_q), flat(grad_k), flat(grad_v)], axis=1)
+    grad_qk = jnp.stack([grad_q_gain, grad_k_gain])
     grad_normed = lax.psum_scatter(
         nt_dot(grad_proj_low, full_qkv).astype(low),
         "tp",

time: 978 us -> 950 us (0.971)
  waiting for transfers between devices: 436 us -> 397 us
  Pallas kernels: 163 us -> 173 us
    ppermute x25, waiting for transfers between devices: 82.1 us -> 34.1 us  [along_y(): return lax.ppermute(a, 'ctx', [(i, i ^ 1) for i in range(self.ctx)])]
    unnamed x211 -> x185, local copies, waits for them, and re-layouts: 48.3 us -> 17.3 us
    ppermute x24, waiting for transfers between devices: 89.7 us -> 63.4 us  [along_x(): return lax.ppermute(a, 'fsdp', [(i, i ^ 2) for i in range(self.fsdp)])]
    reshape x2 -> x1, local copies, waits for them, and re-layouts: 0.32 us -> 25.1 us  [per_device(): grad_up.reshape(shard_experts, width, 2, hidden_local)]
    ppermute x5, waiting for transfers between devices: 4.91 us -> 17.5 us  [sum_everywhere(): values = values + lax.ppermute(values, axis, pairs)]
    all_gather x4, waiting for transfers between devices: 79.7 us -> 90.9 us  [spread(): lax.all_gather(half.astype(low), 'tp', axis=0, tiled=True)]
    reduce_scatter x4 -> x2, waiting for transfers between devices: 30.2 us -> 41.4 us  [finish(): lax.psum_scatter(half, 'tp', scatter_dimension=0, tiled=True).astype(wide)]
    pallas_call x8, Pallas kernels: 163 us -> 173 us  [expert_call(): pl.pallas_call(body, grid=(experts,), in_specs=in_specs + [pl.BlockSpec(m...]
  transfers between devices with their start and end apart: 115 -> 113, of which waited for: 57 -> 46; matrix products, arithmetic and copies ran while one was open for 19% -> 19% of each run, Pallas kernels for 17% -> 18%
where the time goes in v4:
time: 950 us; the launch traced here: 939 us
  waiting for transfers between devices  397 us (42%)
  Pallas kernels  173 us (18%)
  starting transfers between devices  96.9 us (10%)
  matrix products  88.8 us (9%)
  local copies, waits for them, and re-layouts  81.7 us (9%)
  other arithmetic  81 us (9%)
  between operations  20.6 us (2%)
    pallas_call x8, Pallas kernels, expert_call(): pl.pallas_call(body, grid=(experts,), in_specs=in_specs + [pl.BlockSpec(m...  173 us
    all_gather x4, waiting for transfers between devices, spread(): lax.all_gather(half.astype(low), 'tp', axis=0, tiled=True)  90.9 us
    ppermute x24, waiting for transfers between devices, along_x(): return lax.ppermute(a, 'fsdp', [(i, i ^ 2) for i in range(self.fsdp)])  63.4 us
    reduce_scatter x2, waiting for transfers between devices, finish(): lax.psum_scatter(half, 'tp', scatter_dimension=0, tiled=True).astype(wide)  41.4 us
    ppermute x1, waiting for transfers between devices, per_device(): other_kv = lax.ppermute(key_value, 'ctx', mirror)  39 us
    ppermute x25, waiting for transfers between devices, along_y(): return lax.ppermute(a, 'ctx', [(i, i ^ 1) for i in range(self.ctx)])  34.1 us
    ppermute x24, starting transfers between devices, along_x(): return lax.ppermute(a, 'fsdp', [(i, i ^ 2) for i in range(self.fsdp)])  27.6 us
    ppermute x25, starting transfers between devices, along_y(): return lax.ppermute(a, 'ctx', [(i, i ^ 1) for i in range(self.ctx)])  27.5 us
  transfers between devices with their start and end apart: 113, of which 46 were waited for; matrix products, arithmetic and copies ran while one was open for 19% of the time, Pallas kernels for 18%

profile of v4, /device:TPU:0, one launch (start us, length us, event | category | flops | bytes accessed | tf_op | source)
XLA Modules:
  0.0 938.9 jit_solution(16154428378960299050)
XLA Ops:
  33.9 12.7 %collective-permute-done.12 = bf16[512,256]{1,0:T(8,128)(2,1)S(1)} collective-permute-done((bf16[512,256]{1,0:T(8,128)(2,1)}, bf16[512,256]{1,0:T(8,128)(2,1)S(1)}, u32[]{:S(2)}, u32[]{:S(2)}) %collective-permute-start.12) | collective-permute-done | bytes 262176 | tf_op jit(solution)/shard_map/ppermute | solution.py:314
  69.1 39.0 %collective-permute-done.7 = bf16[1,512,2,4,128]{1,4,3,2,0:T(8,128)(2,1)} collective-permute-done((bf16[1,512,2,4,128]{1,4,3,2,0:T(8,128)(2,1)}, bf16[1,512,2,4,128]{1,4,3,2,0:T(8,128)(2,1)}, u32[]{:S(2)}, u32[]{:S(2)}) %collective-permute-start.7) | collective-permute-done | bytes 1048608 | tf_op jit(solution)/shard_map/ppermute | solution.py:542
  125.7 10.2 %all-to-all-done = bf16[4,128,512]{1,2,0:T(8,128)(2,1)S(1)} async-done(((bf16[4,128,512]{1,2,0:T(8,128)(2,1)}), bf16[4,128,512]{1,2,0:T(8,128)(2,1)S(1)}, u32[]{:S(2)}, u32[]{:S(2)}) %all-to-all-start) | async-done | bytes 524320 | tf_op jit(solution)/shard_map/all_to_all | solution.py:556
  142.6 25.6 %all-gather.14.cloned.1.call-done.refs_0_ = bf16[512,1024]{1,0:T(8,128)(2,1)} async-done(((bf16[128,1024]{1,0:T(8,128)(2,1)}), bf16[512,1024]{1,0:T(8,128)(2,1)}) %all-gather.14.cloned.1.call-update) | async-done | bytes 1048592 | tf_op jit(solution)/shard_map/all_gather | solution.py:567
  171.5 14.1 %reshape.348.refs_6_.refs_10_ = bf16[4,2048,512]{2,1,0:T(8,128)(2,1)} reshape(bf16[4,2048,2,256]{3,2,1,0:T(2,128)(2,1)} %param.20) | data formatting | bytes 16777216 | tf_op jit(solution)/shard_map/reshape | solution.py:509
  185.8 11.9 %all-gather.16.cloned.1.call-done.refs_1_ = bf16[512,1024]{1,0:T(8,128)(2,1)} async-done(((bf16[128,1024]{1,0:T(8,128)(2,1)}), bf16[512,1024]{1,0:T(8,128)(2,1)}) %all-gather.16.cloned.1.call-update) | async-done | bytes 1048592 | tf_op jit(solution)/shard_map/all_gather | solution.py:567
  214.0 20.3 %shard_map.186 = (bf16[512,2048]{1,0:T(8,128)(2,1)}, bf16[512,2048]{1,0:T(8,128)(2,1)}, bf16[4,8,160,2048]{3,2,1,0:T(8,128)(2,1)}, f32[4,8,160,512]{3,2,1,0:T(8,128)}, bf16[4,8,160,256]{3,2,1,0:T(8,128)(2,1)}) custom-call(bf16[512,1024]{1,0:T(8,128)(2,1)} %all-gather.14.cloned.1.call-done.refs_0_, bf16[512,1024]{1,0:T(8,128)(2,1)} %all-gather.16.cloned.1.call-done.refs_1_, ...), custom_call_target="tpu_custom_call" | custom-call | flops 9395240960 | bytes 17563648 | tf_op jit(solution)/shard_map/pallas_call | solution.py:268
  234.3 10.9 %collective-permute-done.20.refs_0_ = bf16[512,512]{1,0:T(8,128)(2,1)S(1)} collective-permute-done((bf16[512,512]{1,0:T(8,128)(2,1)S(1)}, bf16[512,512]{1,0:T(8,128)(2,1)S(1)}, u32[]{:S(2)}, u32[]{:S(2)}) %collective-permute-start.20) | collective-permute-done | bytes 524320 | tf_op jit(solution)/shard_map/ppermute | solution.py:336
  253.1 20.4 %shard_map.187 = (bf16[512,2048]{1,0:T(8,128)(2,1)}, bf16[512,2048]{1,0:T(8,128)(2,1)}, bf16[4,8,160,2048]{3,2,1,0:T(8,128)(2,1)}, f32[4,8,160,512]{3,2,1,0:T(8,128)}, bf16[4,8,160,256]{3,2,1,0:T(8,128)(2,1)}) custom-call(bf16[512,1024]{1,0:T(8,128)(2,1)} %copy-done.18, ...), custom_call_target="tpu_custom_call", output_to_operand_aliasing={{2}: (8, {}), {3}: (9, {}), {4}: (10, {})} | custom-call | flops 9395240960 | bytes 17563648 | tf_op jit(solution)/shard_map/pallas_call | solution.py:268
  276.3 20.5 %shard_map.188 = (bf16[512,2048]{1,0:T(8,128)(2,1)}, bf16[512,2048]{1,0:T(8,128)(2,1)}, bf16[4,8,160,2048]{3,2,1,0:T(8,128)(2,1)}, f32[4,8,160,512]{3,2,1,0:T(8,128)}, bf16[4,8,160,256]{3,2,1,0:T(8,128)(2,1)}) custom-call(bf16[512,1024]{1,0:T(8,128)(2,1)} %copy-done.17, ...), custom_call_target="tpu_custom_call", output_to_operand_aliasing={{2}: (8, {}), {3}: (9, {}), {4}: (10, {})} | custom-call | flops 9395240960 | bytes 17563648 | tf_op jit(solution)/shard_map/pallas_call | solution.py:268
  308.8 20.6 %shard_map.189 = (bf16[512,2048]{1,0:T(8,128)(2,1)}, bf16[512,2048]{1,0:T(8,128)(2,1)}, bf16[4,8,160,2048]{3,2,1,0:T(8,128)(2,1)}, f32[4,8,160,512]{3,2,1,0:T(8,128)}, bf16[4,8,160,256]{3,2,1,0:T(8,128)(2,1)}) custom-call(bf16[512,512]{1,0:T(8,128)(2,1)} %copy-done.45, ...), custom_call_target="tpu_custom_call", output_to_operand_aliasing={{2}: (12, {}), {3}: (13, {}), {4}: (14, {})} | custom-call | flops 9395240960 | bytes 17563648 | tf_op jit(solution)/shard_map/pallas_call | solution.py:268
  342.6 10.7 %collective-permute-done.40 = bf16[512,512]{1,0:T(8,128)(2,1)S(1)} collective-permute-done((bf16[512,512]{1,0:T(8,128)(2,1)S(1)}, bf16[512,512]{1,0:T(8,128)(2,1)S(1)}, u32[]{:S(2)}, u32[]{:S(2)}) %collective-permute-start.40) | collective-permute-done | bytes 524320 | tf_op jit(solution)/shard_map/ppermute | solution.py:333
  354.4 9.3 collective-permute-done.42
  372.2 9.0 collective-permute-done.45
  381.2 9.2 collective-permute-done.47
  398.0 41.4 %reduce-scatter.4.cloned.1.call-done = bf16[128,2048]{1,0:T(8,128)(2,1)} async-done(((bf16[512,2048]{1,0:T(8,128)(2,1)}), bf16[128,2048]{1,0:T(8,128)(2,1)}) %reduce-scatter.4.cloned.1.call-update) | async-done | bytes 524304 | tf_op jit(solution)/shard_map/reduce_scatter | solution.py:579
  443.3 26.6 %all-gather.20.cloned.1.call-done.refs_0_ = bf16[512,1024]{1,0:T(8,128)(2,1)} async-done(((bf16[128,1024]{1,0:T(8,128)(2,1)}), bf16[512,1024]{1,0:T(8,128)(2,1)}) %all-gather.20.cloned.1.call-update) | async-done | bytes 1048592 | tf_op jit(solution)/shard_map/all_gather | solution.py:567
  472.8 26.7 %all-gather.22.cloned.1.call-done.refs_1_ = bf16[512,1024]{1,0:T(8,128)(2,1)} async-done(((bf16[128,1024]{1,0:T(8,128)(2,1)}), bf16[512,1024]{1,0:T(8,128)(2,1)}) %all-gather.22.cloned.1.call-update) | async-done | bytes 1048592 | tf_op jit(solution)/shard_map/all_gather | solution.py:567
  507.1 23.0 %shard_map.190 = (bf16[512,2048]{1,0:T(8,128)(2,1)}, bf16[512,2048]{1,0:T(8,128)(2,1)}, bf16[4,8,160,2048]{3,2,1,0:T(8,128)(2,1)}, bf16[4,8,160,512]{3,2,1,0:T(8,128)(2,1)}) custom-call(bf16[512,1024]{1,0:T(8,128)(2,1)} %all-gather.20.cloned.1.call-done.refs_0_, bf16[512,1024]{1,0:T(8,128)(2,1)} %all-gather.22.cloned.1.call-done.refs_1_, ...), custom_call_target="tpu_custom_call" | custom-call | flops 9395240960 | bytes 17563648 | tf_op jit(solution)/shard_map/pallas_call | solution.py:268
  530.1 8.5 collective-permute-done.54.refs_0_
  543.9 23.0 %shard_map.191 = (bf16[512,2048]{1,0:T(8,128)(2,1)}, bf16[512,2048]{1,0:T(8,128)(2,1)}, bf16[4,8,160,2048]{3,2,1,0:T(8,128)(2,1)}, bf16[4,8,160,512]{3,2,1,0:T(8,128)(2,1)}) custom-call(bf16[512,1024]{1,0:T(8,128)(2,1)} %collective-permute-done.48.refs_0_, bf16[512,1024]{1,0:T(8,128)(2,1)} %copy-done.21, ...), custom_call_target="tpu_custom_call", output_to_operand_aliasing={{2}: (9, {}), {3}: (10, {})} | custom-call | flops 9395240960 | bytes 17563648 | tf_op jit(solution)/shard_map/pallas_call | solution.py:268
  568.1 22.8 %shard_map.192 = (bf16[512,2048]{1,0:T(8,128)(2,1)}, bf16[512,2048]{1,0:T(8,128)(2,1)}, bf16[4,8,160,2048]{3,2,1,0:T(8,128)(2,1)}, bf16[4,8,160,512]{3,2,1,0:T(8,128)(2,1)}) custom-call(bf16[512,1024]{1,0:T(8,128)(2,1)} %copy-done.19, bf16[512,1024]{1,0:T(8,128)(2,1)} %copy-done.20, ...), custom_call_target="tpu_custom_call", output_to_operand_aliasing={{2}: (9, {}), {3}: (10, {})} | custom-call | flops 9395240960 | bytes 17563648 | tf_op jit(solution)/shard_map/pallas_call | solution.py:268
  600.1 22.6 %shard_map.193 = (bf16[512,2048]{1,0:T(8,128)(2,1)}, bf16[512,2048]{1,0:T(8,128)(2,1)}, bf16[4,8,160,2048]{3,2,1,0:T(8,128)(2,1)}, bf16[4,8,160,512]{3,2,1,0:T(8,128)(2,1)}) custom-call(bf16[512,512]{1,0:T(8,128)(2,1)} %collective-permute-done.54.refs_0_, ...), custom_call_target="tpu_custom_call", output_to_operand_aliasing={{2}: (13, {}), {3}: (14, {})} | custom-call | flops 9395240960 | bytes 17563648 | tf_op jit(solution)/shard_map/pallas_call | solution.py:268
  634.3 15.3 %convolution_bitcast_fusion = f32[4,256,2048]{2,1,0:T(8,128)} fusion(bf16[4,8,160,256]{3,2,1,0:T(8,128)(2,1)S(1)} %copy-done.5, bf16[4,8,160,2048]{3,2,1,0:T(8,128)(2,1)} %get-tuple-element.200), kind=kOutput, calls=%fused_computation.25 | convolution fusion | flops 5368709120 | bytes 31981568 | tf_op jit(solution)/shard_map/ebcf,ebcd->efd/dot_general | solution.py:614
  662.8 10.1 %collective-permute-done.79 = bf16[512,512]{1,0:T(8,128)(2,1)S(1)} collective-permute-done((bf16[512,512]{1,0:T(8,128)(2,1)S(1)}, bf16[512,512]{1,0:T(8,128)(2,1)S(1)}, u32[]{:S(2)}, u32[]{:S(2)}) %collective-permute-start.79) | collective-permute-done | bytes 524320 | tf_op jit(solution)/shard_map/ppermute | solution.py:333
  672.9 9.2 collective-permute-done.81
  688.4 19.3 %fusion.75 = f32[4,2048,512,1]{1,2,3,0:T(8,128)} fusion(bf16[4,8,160,2048]{3,2,1,0:T(8,128)(2,1)} %get-tuple-element.205, bf16[4,8,160,512]{3,2,1,0:T(8,128)(2,1)} %get-tuple-element.206), kind=kOutput, calls=%fused_computation.272 | convolution fusion | flops 10737418240 | bytes 42991616 | tf_op jit(solution)/shard_map/ebcd,ebcf->edf/dot_general | solution.py:617
  707.6 25.1 %copy.112 = f32[4,2048,2,256]{3,2,1,0:T(2,128)} copy(f32[4,2048,2,256]{1,3,2,0:T(8,128)} %bitcast.199) | data formatting | bytes 33554432 | tf_op jit(solution)/shard_map/reshape | solution.py:628
  748.9 12.4 %all-to-all-done.2 = bf16[128,4,512]{2,0,1:T(8,128)(2,1)S(1)} async-done(((bf16[128,4,512]{2,0,1:T(8,128)(2,1)}), bf16[128,4,512]{2,0,1:T(8,128)(2,1)S(1)}, u32[]{:S(2)}, u32[]{:S(2)}) %all-to-all-start.2) | async-done | bytes 524320 | tf_op jit(solution)/shard_map/all_to_all | solution.py:637
  787.7 18.4 %collective-permute-done.82 = bf16[1,512,2,4,128]{1,4,3,2,0:T(8,128)(2,1)S(1)} collective-permute-done((bf16[1,512,2,4,128]{1,4,3,2,0:T(8,128)(2,1)}, bf16[1,512,2,4,128]{1,4,3,2,0:T(8,128)(2,1)S(1)}, u32[]{:S(2)}, u32[]{:S(2)}) %collective-permute-start.82) | collective-permute-done | bytes 1048608 | tf_op jit(solution)/shard_map/ppermute | solution.py:652
  851.7 21.7 %reduce-scatter.8.cloned.1.call-done = bf16[128,2048]{1,0:T(8,128)(2,1)} async-done(((bf16[512,2048]{1,0:T(8,128)(2,1)}), bf16[128,2048]{1,0:T(8,128)(2,1)}) %reduce-scatter.8.cloned.1.call-update) | async-done | bytes 524304 | tf_op jit(solution)/shard_map/reduce_scatter | solution.py:659
  894.3 12.4 %collective-permute-done.84 = f32[1,4353]{1,0:T(1,128)S(1)} collective-permute-done((f32[1,4353]{1,0:T(1,128)S(1)}, f32[1,4353]{1,0:T(1,128)S(1)}, u32[]{:S(2)}, u32[]{:S(2)}) %collective-permute-start.84) | collective-permute-done | bytes 17444 | tf_op jit(solution)/shard_map/ppermute | solution.py:305
  (556 shorter events, 335.4 us)
Async XLA Ops:
  7.2 52.8 %all-gather.10.cloned.1.call-start = ((), (), s32[]{:S(2)}) async-start(), calls=%async_computation.6 | async-start | bytes 7077888 | tf_op jit(solution)/shard_map/all_gather | solution.py:520
  9.6 126.4 %all-gather.12.cloned.1.call-start = ((), (), s32[]{:S(2)}) async-start(), calls=%async_computation.7 | async-start | bytes 9437184 | tf_op jit(solution)/shard_map/all_gather | solution.py:524
  68.8 39.4 %collective-permute-start.7 = (bf16[1,512,2,4,128]{1,4,3,2,0:T(8,128)(2,1)}, bf16[1,512,2,4,128]{1,4,3,2,0:T(8,128)(2,1)}, u32[]{:S(2)}, u32[]{:S(2)}) collective-permute-start(bf16[1,512,2,4,128]{1,4,3,2,0:T(8,128)(2,1)} %pad_maximum_fusion.4), channel_id=1, source_target_pairs={{0,4},{4,0},{1,5},{5,1},{2,6},{6,2},{3,7},{7,3},{8,12},{12,8},{9,1... | collective-permute-start | bytes 3145736 | tf_op jit(solution)/shard_map/ppermute | solution.py:542
  123.1 45.1 %all-gather.14.cloned.1.call-start = ((), (), s32[]{:S(2)}) async-start(), calls=%async_computation.8 | async-start | bytes 1310720 | tf_op jit(solution)/shard_map/all_gather | solution.py:567
  142.0 55.7 %all-gather.16.cloned.1.call-start = ((), (), s32[]{:S(2)}) async-start(), calls=%async_computation.9 | async-start | bytes 1310720 | tf_op jit(solution)/shard_map/all_gather | solution.py:567
  168.2 29.5 %collective-permute-start.14 = (bf16[512,1024]{1,0:T(8,128)(2,1)}, bf16[512,1024]{1,0:T(8,128)(2,1)S(1)}, u32[]{:S(2)}, u32[]{:S(2)}) collective-permute-start(bf16[512,1024]{1,0:T(8,128)(2,1)} %all-gather.14.cloned.1.call-done.refs_0_), channel_id=1, source_target_pairs={{0,16},{8,24},{16,0},{24,8},{1,17},{9,25},{17,1},{25,9},{2,18},{10... | collective-permute-start | bytes 3145736 | tf_op jit(solution)/shard_map/ppermute | solution.py:333
  169.7 28.0 %collective-permute-start.15 = (bf16[512,1024]{1,0:T(8,128)(2,1)}, bf16[512,1024]{1,0:T(8,128)(2,1)S(1)}, u32[]{:S(2)}, u32[]{:S(2)}) collective-permute-start(bf16[512,1024]{1,0:T(8,128)(2,1)} %all-gather.14.cloned.1.call-done.refs_0_), channel_id=1, source_target_pairs={{0,4},{4,0},{1,5},{5,1},{2,6},{6,2},{3,7},{7,3},{8,12},{12,8},{9,1... | collective-permute-start | bytes 3145736 | tf_op jit(solution)/shard_map/ppermute | solution.py:336
  171.2 37.7 %collective-permute-start.16 = (bf16[512,1024]{1,0:T(8,128)(2,1)}, bf16[512,1024]{1,0:T(8,128)(2,1)}, u32[]{:S(2)}, u32[]{:S(2)}) collective-permute-start(bf16[512,1024]{1,0:T(8,128)(2,1)} %all-gather.14.cloned.1.call-done.refs_0_), channel_id=1, source_target_pairs={{0,8},{8,0},{16,24},{24,16},{1,9},{9,1},{17,25},{25,17},{2,10},{10... | collective-permute-start | bytes 3145736 | tf_op jit(solution)/shard_map/ppermute | solution.py:330
  202.8 236.6 %reduce-scatter.4.cloned.1.call-start = ((), (), s32[]{:S(2)}) async-start(), calls=%async_computation.10 | async-start | bytes 2621440 | tf_op jit(solution)/shard_map/reduce_scatter | solution.py:579
  208.0 37.3 %collective-permute-start.23 = (bf16[512,1024]{1,0:T(8,128)(2,1)}, bf16[512,1024]{1,0:T(8,128)(2,1)}, u32[]{:S(2)}, u32[]{:S(2)}) collective-permute-start(bf16[512,1024]{1,0:T(8,128)(2,1)} %all-gather.16.cloned.1.call-done.refs_1_), channel_id=1, source_target_pairs={{0,16},{8,24},{16,0},{24,8},{1,17},{9,25},{17,1},{25,9},{2,18},{10... | collective-permute-start | bytes 3145736 | tf_op jit(solution)/shard_map/ppermute | solution.py:333
  208.8 37.2 %collective-permute-start.24 = (bf16[512,1024]{1,0:T(8,128)(2,1)}, bf16[512,1024]{1,0:T(8,128)(2,1)}, u32[]{:S(2)}, u32[]{:S(2)}) collective-permute-start(bf16[512,1024]{1,0:T(8,128)(2,1)} %all-gather.16.cloned.1.call-done.refs_1_), channel_id=1, source_target_pairs={{0,4},{4,0},{1,5},{5,1},{2,6},{6,2},{3,7},{7,3},{8,12},{12,8},{9,1... | collective-permute-start | bytes 3145736 | tf_op jit(solution)/shard_map/ppermute | solution.py:336
  211.6 33.7 %collective-permute-start.20 = (bf16[512,512]{1,0:T(8,128)(2,1)S(1)}, bf16[512,512]{1,0:T(8,128)(2,1)S(1)}, u32[]{:S(2)}, u32[]{:S(2)}) collective-permute-start(bf16[512,512]{1,0:T(8,128)(2,1)S(1)} %slice.502), channel_id=1, source_target_pairs={{0,4},{4,0},{1,5},{5,1},{2,6},{6,2},{3,7},{7,3},{8,12},{12,8},{9,1... | collective-permute-start | bytes 1572872 | tf_op jit(solution)/shard_map/ppermute | solution.py:336
  212.7 32.5 %collective-permute-start.21 = (bf16[512,512]{1,0:T(8,128)(2,1)S(1)}, bf16[512,512]{1,0:T(8,128)(2,1)S(1)}, u32[]{:S(2)}, u32[]{:S(2)}) collective-permute-start(bf16[512,512]{1,0:T(8,128)(2,1)S(1)} %slice.503), channel_id=1, source_target_pairs={{0,16},{8,24},{16,0},{24,8},{1,17},{9,25},{17,1},{25,9},{2,18},{10... | collective-permute-start | bytes 1572872 | tf_op jit(solution)/shard_map/ppermute | solution.py:333
  396.5 73.4 %all-gather.20.cloned.1.call-start = ((), (), s32[]{:S(2)}) async-start(), calls=%async_computation.12 | async-start | bytes 1310720 | tf_op jit(solution)/shard_map/all_gather | solution.py:567
  442.5 57.1 %all-gather.22.cloned.1.call-start = ((), (), s32[]{:S(2)}) async-start(), calls=%async_computation.13 | async-start | bytes 1310720 | tf_op jit(solution)/shard_map/all_gather | solution.py:567
  443.2 123.7 %all-gather.18.cloned.1.call-start = ((), (), s32[]{:S(2)}) async-start(), calls=%async_computation.11 | async-start | bytes 2621440 | tf_op jit(solution)/shard_map/all_gather | solution.py:596
  469.9 29.7 %collective-permute-start.48 = (bf16[512,1024]{1,0:T(8,128)(2,1)}, bf16[512,1024]{1,0:T(8,128)(2,1)}, u32[]{:S(2)}, u32[]{:S(2)}) collective-permute-start(bf16[512,1024]{1,0:T(8,128)(2,1)} %all-gather.20.cloned.1.call-done.refs_0_), channel_id=1, source_target_pairs={{0,16},{8,24},{16,0},{24,8},{1,17},{9,25},{17,1},{25,9},{2,18},{10... | collective-permute-start | bytes 3145736 | tf_op jit(solution)/shard_map/ppermute | solution.py:333
  471.4 28.2 %collective-permute-start.49 = (bf16[512,1024]{1,0:T(8,128)(2,1)}, bf16[512,1024]{1,0:T(8,128)(2,1)S(1)}, u32[]{:S(2)}, u32[]{:S(2)}) collective-permute-start(bf16[512,1024]{1,0:T(8,128)(2,1)} %all-gather.20.cloned.1.call-done.refs_0_), channel_id=1, source_target_pairs={{0,4},{4,0},{1,5},{5,1},{2,6},{6,2},{3,7},{7,3},{8,12},{12,8},{9,1... | collective-permute-start | bytes 3145736 | tf_op jit(solution)/shard_map/ppermute | solution.py:336
  472.8 29.0 %collective-permute-start.50 = (bf16[512,1024]{1,0:T(8,128)(2,1)}, bf16[512,1024]{1,0:T(8,128)(2,1)}, u32[]{:S(2)}, u32[]{:S(2)}) collective-permute-start(bf16[512,1024]{1,0:T(8,128)(2,1)} %all-gather.20.cloned.1.call-done.refs_0_), channel_id=1, source_target_pairs={{0,8},{8,0},{16,24},{24,16},{1,9},{9,1},{17,25},{25,17},{2,10},{10... | collective-permute-start | bytes 3145736 | tf_op jit(solution)/shard_map/ppermute | solution.py:330
  500.3 232.5 %reduce-scatter.6.cloned.1.call-start = ((), (), s32[]{:S(2)}) async-start(), calls=%async_computation.14 | async-start | bytes 2621440 | tf_op jit(solution)/shard_map/reduce_scatter | solution.py:579
  500.3 38.3 %collective-permute-start.57 = (bf16[512,1024]{1,0:T(8,128)(2,1)}, bf16[512,1024]{1,0:T(8,128)(2,1)S(1)}, u32[]{:S(2)}, u32[]{:S(2)}) collective-permute-start(bf16[512,1024]{1,0:T(8,128)(2,1)} %all-gather.22.cloned.1.call-done.refs_1_), channel_id=1, source_target_pairs={{0,16},{8,24},{16,0},{24,8},{1,17},{9,25},{17,1},{25,9},{2,18},{10... | collective-permute-start | bytes 3145736 | tf_op jit(solution)/shard_map/ppermute | solution.py:333
  501.8 36.8 %collective-permute-start.58 = (bf16[512,1024]{1,0:T(8,128)(2,1)}, bf16[512,1024]{1,0:T(8,128)(2,1)S(1)}, u32[]{:S(2)}, u32[]{:S(2)}) collective-permute-start(bf16[512,1024]{1,0:T(8,128)(2,1)} %all-gather.22.cloned.1.call-done.refs_1_), channel_id=1, source_target_pairs={{0,4},{4,0},{1,5},{5,1},{2,6},{6,2},{3,7},{7,3},{8,12},{12,8},{9,1... | collective-permute-start | bytes 3145736 | tf_op jit(solution)/shard_map/ppermute | solution.py:336
  504.4 34.2 %collective-permute-start.54 = (bf16[512,512]{1,0:T(8,128)(2,1)S(1)}, bf16[512,512]{1,0:T(8,128)(2,1)}, u32[]{:S(2)}, u32[]{:S(2)}) collective-permute-start(bf16[512,512]{1,0:T(8,128)(2,1)S(1)} %slice.523), channel_id=1, source_target_pairs={{0,4},{4,0},{1,5},{5,1},{2,6},{6,2},{3,7},{7,3},{8,12},{12,8},{9,1... | collective-permute-start | bytes 1572872 | tf_op jit(solution)/shard_map/ppermute | solution.py:336
  505.6 33.0 %collective-permute-start.55 = (bf16[512,512]{1,0:T(8,128)(2,1)S(1)}, bf16[512,512]{1,0:T(8,128)(2,1)}, u32[]{:S(2)}, u32[]{:S(2)}) collective-permute-start(bf16[512,512]{1,0:T(8,128)(2,1)S(1)} %slice.524), channel_id=1, source_target_pairs={{0,16},{8,24},{16,0},{24,8},{1,17},{9,25},{17,1},{25,9},{2,18},{10... | collective-permute-start | bytes 1572872 | tf_op jit(solution)/shard_map/ppermute | solution.py:333
  538.7 28.3 %collective-permute-start.64 = (bf16[512,1024]{1,0:T(8,128)(2,1)S(1)}, bf16[512,1024]{1,0:T(8,128)(2,1)S(1)}, u32[]{:S(2)}, u32[]{:S(2)}) collective-permute-start(bf16[512,1024]{1,0:T(8,128)(2,1)S(1)} %collective-permute-done.58.refs_1_), channel_id=1, source_target_pairs={{0,8},{8,0},{16,24},{24,16},{1,9},{9,1},{17,25},{25,17},{2,10},{10... | collective-permute-start | bytes 3145736 | tf_op jit(solution)/shard_map/ppermute | solution.py:330
  539.3 27.7 %collective-permute-start.63 = (bf16[512,512]{1,0:T(8,128)(2,1)}, bf16[512,512]{1,0:T(8,128)(2,1)}, u32[]{:S(2)}, u32[]{:S(2)}) collective-permute-start(bf16[512,512]{1,0:T(8,128)(2,1)} %collective-permute-done.55.refs_1_), channel_id=1, source_target_pairs={{0,8},{8,0},{16,24},{24,16},{1,9},{9,1},{17,25},{25,17},{2,10},{10... | collective-permute-start | bytes 1572872 | tf_op jit(solution)/shard_map/ppermute | solution.py:330
  594.3 28.3 %collective-permute-start.66 = (bf16[512,512]{1,0:T(8,128)(2,1)}, bf16[512,512]{1,0:T(8,128)(2,1)}, u32[]{:S(2)}, u32[]{:S(2)}) collective-permute-start(bf16[512,512]{1,0:T(8,128)(2,1)} %get-tuple-element.294), channel_id=1, source_target_pairs={{0,16},{8,24},{16,0},{24,8},{1,17},{9,25},{17,1},{25,9},{2,18},{10... | collective-permute-start | bytes 1572872 | tf_op jit(solution)/shard_map/ppermute | solution.py:333
  748.8 79.2 %all-gather.26.cloned.1.call-start = ((), (), s32[]{:S(2)}) async-start(), calls=%async_computation.17 | async-start | bytes 2621440 | tf_op jit(solution)/shard_map/all_gather | solution.py:640
  783.8 89.7 %reduce-scatter.8.cloned.1.call-start = ((), (), s32[]{:S(2)}) async-start(), calls=%async_computation.15 | async-start | bytes 2621440 | tf_op jit(solution)/shard_map/reduce_scatter | solution.py:659
  818.4 105.6 %all-gather.24.cloned.1.call-start = ((), (), s32[]{:S(2)}) async-start(), calls=%async_computation.16 | async-start | bytes 2621440 | tf_op jit(solution)/shard_map/all_gather | solution.py:668
  848.8 37.7 %collective-permute-start.95 = (bf16[256,1024]{0,1:T(8,128)(2,1)}, bf16[256,1024]{0,1:T(8,128)(2,1)}, u32[]{:S(2)}, u32[]{:S(2)}) collective-permute-start(bf16[256,1024]{0,1:T(8,128)(2,1)} %get-tuple-element.328), channel_id=1, source_target_pairs={{0,4},{4,0},{1,5},{5,1},{2,6},{6,2},{3,7},{7,3},{8,12},{12,8},{9,1... | collective-permute-start | bytes 1572872 | tf_op jit(solution)/shard_map/ppermute | solution.py:336
  850.3 39.9 %collective-permute-start.93 = (bf16[256,1024]{0,1:T(8,128)(2,1)}, bf16[256,1024]{0,1:T(8,128)(2,1)}, u32[]{:S(2)}, u32[]{:S(2)}) collective-permute-start(bf16[256,1024]{0,1:T(8,128)(2,1)} %get-tuple-element.327), channel_id=1, source_target_pairs={{0,16},{8,24},{16,0},{24,8},{1,17},{9,25},{17,1},{25,9},{2,18},{10... | collective-permute-start | bytes 1572872 | tf_op jit(solution)/shard_map/ppermute | solution.py:333
  (167 other events, 2435.6 us)
Sparse Core Ops, SparseCore 0:
  10.5 49.4 all-gather.9
  62.4 69.1 all-gather.11
  142.1 26.0 all-gather.13
  170.2 27.4 all-gather.15
  396.6 42.7 reduce-scatter.3
  442.6 27.2 all-gather.19
  472.1 27.4 all-gather.21
  501.8 45.4 all-gather.17
  688.5 41.9 reduce-scatter.5
  783.9 44.0 all-gather.25
  830.8 42.5 reduce-scatter.7
  877.9 46.0 all-gather.23

commit v5 on v4

--- a/solution.py
+++ b/solution.py
@@ -57,9 +57,9 @@
     return (queries, key_states, projected[:, 2])
 
 
-def attend_sequence(query_seq, kv_seq, valid_seq, score_scale):
+def attend_sequence(query_seq, key_seq, value_seq, valid_seq, score_scale):
     scores = (
-        jnp.einsum("qhd,khd->hqk", query_seq, kv_seq[:, 0], preferred_element_type=wide)
+        jnp.einsum("qhd,khd->hqk", query_seq, key_seq, preferred_element_type=wide)
         * score_scale
     )
     scores = jnp.where(valid_seq[None, None, :], scores, masked_score)
@@ -67,23 +67,23 @@
     exponent = jnp.exp(scores - peak_score)
     row_total = jnp.sum(exponent, axis=-1, keepdims=True)
     probability = (exponent / row_total).astype(low)
-    output = jnp.einsum("hqk,khd->qhd", probability, kv_seq[:, 1], preferred_element_type=wide)
+    output = jnp.einsum("hqk,khd->qhd", probability, value_seq, preferred_element_type=wide)
     return (output, (peak_score + jnp.log(row_total))[..., 0])
 
 
-def back_sequence(query_seq, kv_seq, valid_seq, log_seq, grad_seq, score_scale):
+def back_sequence(query_seq, key_seq, value_seq, valid_seq, log_seq, grad_seq, score_scale):
     scores = (
-        jnp.einsum("qhd,khd->hqk", query_seq, kv_seq[:, 0], preferred_element_type=wide)
+        jnp.einsum("qhd,khd->hqk", query_seq, key_seq, preferred_element_type=wide)
         * score_scale
     )
     scores = jnp.where(valid_seq[None, None, :], scores, masked_score)
     probability = jnp.exp(scores - log_seq[..., None])
-    grad_prob = jnp.einsum("qhd,khd->hqk", grad_seq, kv_seq[:, 1], preferred_element_type=wide)
+    grad_prob = jnp.einsum("qhd,khd->hqk", grad_seq, value_seq, preferred_element_type=wide)
     grad_scores = (
         probability * (grad_prob - jnp.sum(probability * grad_prob, axis=-1, keepdims=True))
     ).astype(low)
     grad_query = (
-        jnp.einsum("hqk,khd->qhd", grad_scores, kv_seq[:, 0], preferred_element_type=wide)
+        jnp.einsum("hqk,khd->qhd", grad_scores, key_seq, preferred_element_type=wide)
         * score_scale
     )
     grad_key = (
@@ -93,7 +93,7 @@
     grad_value = jnp.einsum(
         "hqk,qhd->khd", probability.astype(low), grad_seq, preferred_element_type=wide
     )
-    return (grad_query, jnp.stack([grad_key, grad_value], axis=1))
+    return (grad_query, grad_key, grad_value)
 
 
 def route_tables(route_rows, gate_rows, experts):
@@ -380,7 +380,7 @@
         from_x, from_y = self.along_x(near_x.astype(low)), self.along_y(near_y.astype(low))
         return own + from_x.astype(wide) + from_y.astype(wide)
 
-    def experts(self, first, second, call, filler, ready=()):
+    def experts(self, first, second, call, filler):
         if not self.tree:
             split = lambda a: jnp.split(lax.all_gather(a, plane, axis=0, tiled=True), self.shards)
             halves, made = list(zip(split(first), split(second), strict=True)), []
@@ -389,56 +389,44 @@
             return lax.psum_scatter(
                 jnp.concatenate(made, axis=0), plane, scatter_dimension=0, tiled=True
             )
-        parts, step = 4, first.shape[1] // 2
-        middle = step
+        step = first.shape[1]
         pre = lambda made, other: [
             added(made[:, k * step : (k + 1) * step], other[:, k * step : (k + 1) * step])
-            for k in range(parts)
+            for k in range(2)
         ]
         narrow = lambda a: a.astype(low)
-
-        def beyond(x_half, y_half):
-            return self.along_y(x_half[:, :middle]), self.along_x(y_half[:, middle:])
-
         x_first, y_first = self.along_x(first), self.along_y(first)
-        second = tie(second, x_first, y_first, ready)
+        second = tie(second, x_first, y_first)
         own_pieces = [first, second, self.core(first), self.core(second)]
-        far_first = beyond(x_first, y_first)
         x_second, y_second = self.along_x(second), self.along_y(second)
         over_x, over_y = self.core(x_first), self.core(y_first)
-        own = tie(call(0, tie(own_pieces, over_x, over_y)), far_first)
+        own = call(0, tie(own_pieces, over_x, over_y))
         x_second, y_second = tie((x_second, y_second), own[0])
-        far_second = beyond(x_second, y_second)
-        far_pieces = [self.core(piece) for piece in far_first]
+        far = [self.along_y(x_first), self.along_x(y_second)]
         over_y = [over_y, self.core(y_second)]
         near_x = call(2, [x_first, x_second, over_x, self.core(x_second)])
-        near_x = tie(near_x, far_second, far_pieces, over_y)
+        near_x = tie(near_x, far, over_y)
         other_own, other_x = self.core(own[1]), self.core(near_x[1])
-        far_pieces += [self.core(piece) for piece in far_second]
-        near_y = tie(call(4, [y_first, y_second, *over_y]), other_own, other_x, far_pieces)
+        far += [self.core(piece) for piece in far]
+        near_y = tie(call(4, [y_first, y_second, *over_y]), other_own, other_x, far)
         other_y = self.core(near_y[1])
         sum_x, sum_y = pre(near_x[0], other_x), pre(near_y[0], other_y)
-        early_x = [narrow(sum_x[k]) for k in (0, 2)]
-        early_y = [narrow(sum_y[k]) for k in (1, 3)]
-        last = call(6, tie([*far_first, *far_second, *far_pieces], early_x, early_y))
-        sent_x = [self.along_x(a) for a in early_x]
-        sent_y = [self.along_y(a) for a in early_y]
-        last = tie(last, sent_x, sent_y)
+        early_x, early_y = narrow(sum_x[0]), narrow(sum_y[1])
+        last = call(6, tie(far, early_x, early_y))
+        sent = [self.along_x(early_x), self.along_y(early_y)]
+        last = tie(last, sent)
         sum_far = pre(last[0], self.core(last[1]))
         sum_own = pre(own[0], other_own)
         fillers = iter(filler())
-        far = [(self.along_y if k % 2 else self.along_x)(narrow(sum_far[k])) for k in range(parts)]
+        far = [self.along_x(narrow(sum_far[0])), self.along_y(narrow(sum_far[1]))]
         far = tie(far, next(fillers))
         near = [
-            self.along_x(narrow(added(sum_x[k], far[k])))
-            if k % 2
-            else self.along_y(narrow(added(sum_y[k], far[k])))
-            for k in range(parts)
+            self.along_y(narrow(added(sum_y[0], far[0]))),
+            self.along_x(narrow(added(sum_x[1], far[1]))),
         ]
         near = tie(near, next(fillers))
-        sent = [sent_x[0], sent_y[0], sent_x[1], sent_y[1]]
         return jnp.concatenate(
-            [added(sum_own[k], sent[k]) + near[k].astype(wide) for k in range(parts)], axis=1
+            [added(sum_own[k], sent[k]) + near[k].astype(wide) for k in range(2)], axis=1
         ).astype(low)
 
 
@@ -534,18 +522,19 @@
     queries, query_back = jax.vjp(prepare_query, projected[:, 0], qk_float[0])
     key_states, key_back = jax.vjp(prepare_query, projected[:, 1], qk_float[1])
     query_low = queries.astype(low).reshape(seq_count, slot_count, heads_local, head_dim)
-    key_value = (
-        jnp.stack([key_states, projected[:, 2]], axis=1)
-        .astype(low)
-        .reshape(seq_count, slot_count, 2, heads_local, head_dim)
-    )
-    other_kv = lax.ppermute(key_value, "ctx", mirror)
-    gathered = jnp.concatenate([key_value, other_kv], axis=1)
+    by_head = lambda a: a.astype(low).reshape(seq_count, slot_count, heads_local, head_dim)
+    value_low, key_low = by_head(projected[:, 2]), by_head(key_states)
+    other_value = lax.ppermute(value_low, "ctx", mirror)
+    other_key = lax.ppermute(key_low, "ctx", mirror)
+    gathered_value = jnp.concatenate([value_low, other_value], axis=1)
+    gathered_key = jnp.concatenate([key_low, other_key], axis=1)
     other_position = (1 - ctx_index) * slot_count + own_slots
     key_position = jnp.concatenate([position, other_position])
     key_valid = key_position[None, :] < lengths[:, None]
     pieces = [
-        attend_sequence(query_low[i], gathered[i], key_valid[i], score_scale)
+        attend_sequence(
+            query_low[i], gathered_key[i], gathered_value[i], key_valid[i], score_scale
+        )
         for i in range(seq_count)
     ]
     attended_low = (
@@ -581,11 +570,14 @@
     teacher_own = own(teacher.reshape(tokens, width)).astype(wide)
     valid_own = own(row_valid)
     grad_scale = (2.0 * loss_scale / valid_count * valid_own)[:, None]
+    second_own, table, place = lax.optimization_barrier((normed_own[:, cols[1]], table, place))
+    first_block, second_block = spread(normed_own[:, cols[0]], second_own)
+    second_block, w_up = lax.optimization_barrier((second_block, w_up))
     mixture = places.experts(
-        *spread(normed_own[:, cols[0]], normed_own[:, cols[1]]),
+        first_block,
+        second_block,
         forward,
         lambda: ((), ()),
-        (w_up, table, place),
     )
     rows_in, gate_up, hidden = saved[0]
     final_own = middle_own + finish(mixture)
@@ -637,22 +629,30 @@
     grad_attended = lax.all_to_all(
         nt_dot(grad_branch, full_out).astype(low), "tp", split_axis=1, concat_axis=0, tiled=True
     )
-    branch_block = lax.all_gather(grad_branch, "tp", axis=0, tiled=True)
-    grad_w_out = jnp.einsum("nd,nf->df", branch_block, attended_low, preferred_element_type=wide)
     grad_heads = grad_attended.reshape(seq_count, slot_count, heads_local, head_dim)
     backs = [
         back_sequence(
-            query_low[i], gathered[i], key_valid[i], pieces[i][1], grad_heads[i], score_scale
+            query_low[i],
+            gathered_key[i],
+            gathered_value[i],
+            key_valid[i],
+            pieces[i][1],
+            grad_heads[i],
+            score_scale,
         )
         for i in range(seq_count)
     ]
-    grad_query = jnp.stack([b[0] for b in backs])
-    grad_kv = jnp.stack([b[1] for b in backs])
-    sent_kv = grad_kv[:, slot_count:].astype(low)
-    own_kv = grad_kv[:, :slot_count] + lax.ppermute(sent_kv, "ctx", mirror).astype(wide)
+    grad_query, grad_key, grad_value = [jnp.stack(parts) for parts in zip(*backs, strict=True)]
+
+    def returned(grad):
+        coming = lax.ppermute(grad[:, slot_count:].astype(low), "ctx", mirror)
+        return added(grad[:, :slot_count], coming).reshape(tokens, heads_local, head_dim)
+
+    grad_v, own_key = returned(grad_value), returned(grad_key)
+    branch_block = line_gather(grad_branch)
+    grad_w_out = jnp.einsum("nd,nf->df", branch_block, attended_low, preferred_element_type=wide)
     grad_q, grad_q_gain = query_back(grad_query.reshape(tokens, heads_local, head_dim))
-    grad_k, grad_k_gain = key_back(own_kv[:, :, 0].reshape(tokens, heads_local, head_dim))
-    grad_v = own_kv[:, :, 1].reshape(tokens, heads_local, head_dim)
+    grad_k, grad_k_gain = key_back(own_key)
     flat = lambda a: a.astype(low).reshape(tokens, -1)
     grad_proj_low = jnp.concatenate([flat(grad_q), flat(grad_k), flat(grad_v)], axis=1)
     grad_qk = jnp.stack([grad_q_gain, grad_k_gain])

time: 950 us -> 924 us (0.973)
    ppermute x25 -> x17, waiting for transfers between devices: 34.1 us -> 17.6 us  [along_y(): return lax.ppermute(a, 'ctx', [(i, i ^ 1) for i in range(self.ctx)])]
    ppermute x24 -> x16, waiting for transfers between devices: 63.4 us -> 78.8 us  [along_x(): return lax.ppermute(a, 'fsdp', [(i, i ^ 2) for i in range(self.fsdp)])]
    ppermute x2 -> x4, waiting for transfers between devices: 57.5 us -> 45.2 us  [the longest x1 23.4 us: per_device(): other_key = lax.ppermute(key_low, 'ctx', mirror)]
    ppermute x6 -> x12, starting transfers between devices: 14.6 us -> 26.6 us  [line_gather(): lax.ppermute(shard, 'tp', [(i, i + d) for i in range(size) if 0 <= i + d...]
    ppermute x6 -> x12, waiting for transfers between devices: 22.1 us -> 33.8 us  [line_gather(): lax.ppermute(shard, 'tp', [(i, i + d) for i in range(size) if 0 <= i + d...]
    ppermute x25 -> x17, starting transfers between devices: 27.5 us -> 18.7 us  [along_y(): return lax.ppermute(a, 'ctx', [(i, i ^ 1) for i in range(self.ctx)])]
    ppermute x24 -> x16, starting transfers between devices: 27.6 us -> 19.4 us  [along_x(): return lax.ppermute(a, 'fsdp', [(i, i ^ 2) for i in range(self.fsdp)])]
    unnamed x185 -> x210, local copies, waits for them, and re-layouts: 17.3 us -> 22.7 us
  transfers between devices with their start and end apart: 113 -> 100, of which waited for: 46 -> 51; matrix products, arithmetic and copies ran while one was open for 19% -> 21% of each run, Pallas kernels for 18% -> 19%
where the time goes in v5:
time: 924 us; the launch traced here: 914 us
  waiting for transfers between devices  392 us (42%)
  Pallas kernels  174 us (19%)
  starting transfers between devices  91.8 us (10%)
  matrix products  81.7 us (9%)
  local copies, waits for them, and re-layouts  81.6 us (9%)
  other arithmetic  72.2 us (8%)
  between operations  20.6 us (2%)
    pallas_call x8, Pallas kernels, expert_call(): pl.pallas_call(body, grid=(experts,), in_specs=in_specs + [pl.BlockSpec(m...  174 us
    all_gather x4, waiting for transfers between devices, spread(): lax.all_gather(half.astype(low), 'tp', axis=0, tiled=True)  92.6 us
    ppermute x16, waiting for transfers between devices, along_x(): return lax.ppermute(a, 'fsdp', [(i, i ^ 2) for i in range(self.fsdp)])  78.8 us
    reduce_scatter x2, waiting for transfers between devices, finish(): lax.psum_scatter(half, 'tp', scatter_dimension=0, tiled=True).astype(wide)  40.2 us
    ppermute x12, waiting for transfers between devices, line_gather(): lax.ppermute(shard, 'tp', [(i, i + d) for i in range(size) if 0 <= i + d...  33.8 us
    reduce_scatter x1, waiting for transfers between devices, per_device(): lax.psum_scatter(nt_dot(grad_proj_low, full_qkv).astype(low), 'tp', scatt...  27.2 us
    ppermute x12, starting transfers between devices, line_gather(): lax.ppermute(shard, 'tp', [(i, i + d) for i in range(size) if 0 <= i + d...  26.6 us
    reshape x1, local copies, waits for them, and re-layouts, per_device(): grad_up.reshape(shard_experts, width, 2, hidden_local)  25.1 us
  transfers between devices with their start and end apart: 100, of which 51 were waited for; matrix products, arithmetic and copies ran while one was open for 21% of the time, Pallas kernels for 19%

profile of v5, /device:TPU:0, one launch (start us, length us, event | category | flops | bytes accessed | tf_op | source)
XLA Modules:
  0.0 913.7 jit_solution(17120177539913784613)
XLA Ops:
  9.6 7.0 collective-permute-start.9
  33.6 12.8 %collective-permute-done.13 = bf16[512,256]{1,0:T(8,128)(2,1)S(1)} collective-permute-done((bf16[512,256]{1,0:T(8,128)(2,1)S(1)}, bf16[512,256]{1,0:T(8,128)(2,1)S(1)}, u32[]{:S(2)}, u32[]{:S(2)}) %collective-permute-start.13) | collective-permute-done | bytes 262176 | tf_op jit(solution)/shard_map/ppermute | solution.py:314
  60.0 6.4 fusion.11
  72.7 23.4 %collective-permute-done.8 = bf16[1,512,4,128]{1,3,2,0:T(8,128)(2,1)} collective-permute-done((bf16[1,512,4,128]{1,3,2,0:T(8,128)(2,1)}, bf16[1,512,4,128]{1,3,2,0:T(8,128)(2,1)}, u32[]{:S(2)}, u32[]{:S(2)}) %collective-permute-start.8) | collective-permute-done | bytes 524320 | tf_op jit(solution)/shard_map/ppermute | solution.py:528
  100.9 9.9 %collective-permute-done.7 = bf16[1,512,4,128]{1,3,2,0:T(8,128)(2,1)S(1)} collective-permute-done((bf16[1,512,4,128]{1,3,2,0:T(8,128)(2,1)S(1)}, bf16[1,512,4,128]{1,3,2,0:T(8,128)(2,1)S(1)}, u32[]{:S(2)}, u32[]{:S(2)}) %collective-permute-start.7) | collective-permute-done | bytes 524320 | tf_op jit(solution)/shard_map/ppermute | solution.py:527
  123.5 10.8 %all-to-all-done = bf16[4,128,512]{1,2,0:T(8,128)(2,1)S(1)} async-done(((bf16[4,128,512]{1,2,0:T(8,128)(2,1)}), bf16[4,128,512]{1,2,0:T(8,128)(2,1)S(1)}, u32[]{:S(2)}, u32[]{:S(2)}) %all-to-all-start) | async-done | bytes 524320 | tf_op jit(solution)/shard_map/all_to_all | solution.py:545
  144.8 26.8 %all-gather.13.cloned.1.call-done.refs_0_ = bf16[512,1024]{1,0:T(8,128)(2,1)} async-done(((bf16[128,1024]{1,0:T(8,128)(2,1)}), bf16[512,1024]{1,0:T(8,128)(2,1)}) %all-gather.13.cloned.1.call-update) | async-done | bytes 1048592 | tf_op jit(solution)/shard_map/all_gather | solution.py:556
  174.5 14.1 %reshape.364.refs_6_ = bf16[4,2048,512]{2,1,0:T(8,128)(2,1)} reshape(bf16[4,2048,2,256]{3,2,1,0:T(2,128)(2,1)} %param.20) | data formatting | bytes 16777216 | tf_op jit(solution)/shard_map/reshape | solution.py:497
  188.6 12.4 %all-gather.15.cloned.1.call-done.refs_1_ = bf16[512,1024]{1,0:T(8,128)(2,1)} async-done(((bf16[128,1024]{1,0:T(8,128)(2,1)}), bf16[512,1024]{1,0:T(8,128)(2,1)}) %all-gather.15.cloned.1.call-update) | async-done | bytes 1048592 | tf_op jit(solution)/shard_map/all_gather | solution.py:556
  207.8 20.3 %shard_map.186 = (bf16[512,2048]{1,0:T(8,128)(2,1)}, bf16[512,2048]{1,0:T(8,128)(2,1)}, bf16[4,8,160,2048]{3,2,1,0:T(8,128)(2,1)}, f32[4,8,160,512]{3,2,1,0:T(8,128)}, bf16[4,8,160,256]{3,2,1,0:T(8,128)(2,1)}) custom-call(bf16[512,1024]{1,0:T(8,128)(2,1)} %all-gather.13.cloned.1.call-done.refs_0_, bf16[512,1024]{1,0:T(8,128)(2,1)} %all-gather.15.cloned.1.call-done.refs_1_, ...), custom_call_target="tpu_custom_call" | custom-call | flops 9395240960 | bytes 17563648 | tf_op jit(solution)/shard_map/pallas_call | solution.py:268
  234.5 20.5 %shard_map.187 = (bf16[512,2048]{1,0:T(8,128)(2,1)}, bf16[512,2048]{1,0:T(8,128)(2,1)}, bf16[4,8,160,2048]{3,2,1,0:T(8,128)(2,1)}, f32[4,8,160,512]{3,2,1,0:T(8,128)}, bf16[4,8,160,256]{3,2,1,0:T(8,128)(2,1)}) custom-call(bf16[512,1024]{1,0:T(8,128)(2,1)} %collective-permute-done.15.refs_0_, ...), custom_call_target="tpu_custom_call", output_to_operand_aliasing={{2}: (8, {}), {3}: (9, {}), {4}: (10, {})} | custom-call | flops 9395240960 | bytes 17563648 | tf_op jit(solution)/shard_map/pallas_call | solution.py:268
  258.5 20.5 %shard_map.188 = (bf16[512,2048]{1,0:T(8,128)(2,1)}, bf16[512,2048]{1,0:T(8,128)(2,1)}, bf16[4,8,160,2048]{3,2,1,0:T(8,128)(2,1)}, f32[4,8,160,512]{3,2,1,0:T(8,128)}, bf16[4,8,160,256]{3,2,1,0:T(8,128)(2,1)}) custom-call(bf16[512,1024]{1,0:T(8,128)(2,1)} %collective-permute-done.16.refs_0_, ...), custom_call_target="tpu_custom_call", output_to_operand_aliasing={{2}: (8, {}), {3}: (9, {}), {4}: (10, {})} | custom-call | flops 9395240960 | bytes 17563648 | tf_op jit(solution)/shard_map/pallas_call | solution.py:268
  285.8 20.7 %shard_map.189 = (bf16[512,2048]{1,0:T(8,128)(2,1)}, bf16[512,2048]{1,0:T(8,128)(2,1)}, bf16[4,8,160,2048]{3,2,1,0:T(8,128)(2,1)}, f32[4,8,160,512]{3,2,1,0:T(8,128)}, bf16[4,8,160,256]{3,2,1,0:T(8,128)(2,1)}) custom-call(bf16[512,1024]{1,0:T(8,128)(2,1)} %collective-permute-done.25.refs_0_, ...), custom_call_target="tpu_custom_call", output_to_operand_aliasing={{2}: (8, {}), {3}: (9, {}), {4}: (10, {})} | custom-call | flops 9395240960 | bytes 17563648 | tf_op jit(solution)/shard_map/pallas_call | solution.py:268
  319.0 24.1 %collective-permute-done.35 = bf16[512,1024]{1,0:T(8,128)(2,1)S(1)} collective-permute-done((bf16[512,1024]{1,0:T(8,128)(2,1)S(1)}, bf16[512,1024]{1,0:T(8,128)(2,1)S(1)}, u32[]{:S(2)}, u32[]{:S(2)}) %collective-permute-start.35) | collective-permute-done | bytes 1048608 | tf_op jit(solution)/shard_map/ppermute | solution.py:333
  346.9 21.4 %collective-permute-done.38 = bf16[512,1024]{1,0:T(8,128)(2,1)S(1)} collective-permute-done((bf16[512,1024]{1,0:T(8,128)(2,1)S(1)}, bf16[512,1024]{1,0:T(8,128)(2,1)S(1)}, u32[]{:S(2)}, u32[]{:S(2)}) %collective-permute-start.38) | collective-permute-done | bytes 1048608 | tf_op jit(solution)/shard_map/ppermute | solution.py:333
  376.7 40.2 %reduce-scatter.4.cloned.1.call-done = bf16[128,2048]{1,0:T(8,128)(2,1)} async-done(((bf16[512,2048]{1,0:T(8,128)(2,1)}), bf16[128,2048]{1,0:T(8,128)(2,1)}) %reduce-scatter.4.cloned.1.call-update) | async-done | bytes 524304 | tf_op jit(solution)/shard_map/reduce_scatter | solution.py:568
  420.8 26.6 %all-gather.19.cloned.1.call-done.refs_0_ = bf16[512,1024]{1,0:T(8,128)(2,1)} async-done(((bf16[128,1024]{1,0:T(8,128)(2,1)}), bf16[512,1024]{1,0:T(8,128)(2,1)}) %all-gather.19.cloned.1.call-update) | async-done | bytes 1048592 | tf_op jit(solution)/shard_map/all_gather | solution.py:556
  450.4 26.7 %all-gather.21.cloned.1.call-done.refs_1_ = bf16[512,1024]{1,0:T(8,128)(2,1)} async-done(((bf16[128,1024]{1,0:T(8,128)(2,1)}), bf16[512,1024]{1,0:T(8,128)(2,1)}) %all-gather.21.cloned.1.call-update) | async-done | bytes 1048592 | tf_op jit(solution)/shard_map/all_gather | solution.py:556
  483.2 23.4 %shard_map.190 = (bf16[512,2048]{1,0:T(8,128)(2,1)}, bf16[512,2048]{1,0:T(8,128)(2,1)}, bf16[4,8,160,2048]{3,2,1,0:T(8,128)(2,1)}, bf16[4,8,160,512]{3,2,1,0:T(8,128)(2,1)}) custom-call(bf16[512,1024]{1,0:T(8,128)(2,1)} %all-gather.19.cloned.1.call-done.refs_0_, bf16[512,1024]{1,0:T(8,128)(2,1)} %all-gather.21.cloned.1.call-done.refs_1_, ...), custom_call_target="tpu_custom_call" | custom-call | flops 9395240960 | bytes 17563648 | tf_op jit(solution)/shard_map/pallas_call | solution.py:268
  511.1 22.7 %shard_map.191 = (bf16[512,2048]{1,0:T(8,128)(2,1)}, bf16[512,2048]{1,0:T(8,128)(2,1)}, bf16[4,8,160,2048]{3,2,1,0:T(8,128)(2,1)}, bf16[4,8,160,512]{3,2,1,0:T(8,128)(2,1)}) custom-call(bf16[512,1024]{1,0:T(8,128)(2,1)} %collective-permute-done.39.refs_0_, bf16[512,1024]{1,0:T(8,128)(2,1)} %copy-done.39, ...), custom_call_target="tpu_custom_call", output_to_operand_aliasing={{2}: (9, {}), {3}: (10, {})} | custom-call | flops 9395240960 | bytes 17563648 | tf_op jit(solution)/shard_map/pallas_call | solution.py:268
  534.8 22.8 %shard_map.192 = (bf16[512,2048]{1,0:T(8,128)(2,1)}, bf16[512,2048]{1,0:T(8,128)(2,1)}, bf16[4,8,160,2048]{3,2,1,0:T(8,128)(2,1)}, bf16[4,8,160,512]{3,2,1,0:T(8,128)(2,1)}) custom-call(bf16[512,1024]{1,0:T(8,128)(2,1)} %copy-done.33, bf16[512,1024]{1,0:T(8,128)(2,1)} %collective-permute-done.47.refs_1_, ...), custom_call_target="tpu_custom_call", output_to_operand_aliasing={{2}: (9, {}), {3}: (10, {})} | custom-call | flops 9395240960 | bytes 17563648 | tf_op jit(solution)/shard_map/pallas_call | solution.py:268
  564.4 23.0 %shard_map.193 = (bf16[512,2048]{1,0:T(8,128)(2,1)}, bf16[512,2048]{1,0:T(8,128)(2,1)}, bf16[4,8,160,2048]{3,2,1,0:T(8,128)(2,1)}, bf16[4,8,160,512]{3,2,1,0:T(8,128)(2,1)}) custom-call(bf16[512,1024]{1,0:T(8,128)(2,1)} %collective-permute-done.49.refs_0_, ...), custom_call_target="tpu_custom_call", output_to_operand_aliasing={{2}: (9, {}), {3}: (10, {})} | custom-call | flops 9395240960 | bytes 17563648 | tf_op jit(solution)/shard_map/pallas_call | solution.py:268
  598.6 15.2 %convolution_bitcast_fusion = f32[4,256,2048]{2,1,0:T(8,128)} fusion(bf16[4,8,160,256]{3,2,1,0:T(8,128)(2,1)S(1)} %copy-done.4, bf16[4,8,160,2048]{3,2,1,0:T(8,128)(2,1)} %get-tuple-element.174), kind=kOutput, calls=%fused_computation.25 | convolution fusion | flops 5368709120 | bytes 31981568 | tf_op jit(solution)/shard_map/ebcf,ebcd->efd/dot_general | solution.py:606
  613.8 7.9 collective-permute-done.59
  625.5 22.2 %collective-permute-done.62 = bf16[512,1024]{1,0:T(8,128)(2,1)S(1)} collective-permute-done((bf16[512,1024]{1,0:T(8,128)(2,1)S(1)}, bf16[512,1024]{1,0:T(8,128)(2,1)S(1)}, u32[]{:S(2)}, u32[]{:S(2)}) %collective-permute-start.62) | collective-permute-done | bytes 1048608 | tf_op jit(solution)/shard_map/ppermute | solution.py:333
  653.8 19.3 %fusion.86 = f32[4,2048,512,1]{1,2,3,0:T(8,128)} fusion(bf16[4,8,160,2048]{3,2,1,0:T(8,128)(2,1)} %get-tuple-element.177, bf16[4,8,160,512]{3,2,1,0:T(8,128)(2,1)} %get-tuple-element.178), kind=kOutput, calls=%fused_computation.263 | convolution fusion | flops 10737418240 | bytes 42991616 | tf_op jit(solution)/shard_map/ebcd,ebcf->edf/dot_general | solution.py:609
  673.1 25.1 %copy.120 = f32[4,2048,2,256]{3,2,1,0:T(2,128)} copy(f32[4,2048,2,256]{1,3,2,0:T(8,128)} %bitcast.198) | data formatting | bytes 33554432 | tf_op jit(solution)/shard_map/reshape | solution.py:620
  710.6 6.3 convolution_convert_fusion.3
  731.5 9.4 %collective-permute-done.72 = bf16[128,2048]{1,0:T(8,128)(2,1)S(1)} collective-permute-done((bf16[128,2048]{1,0:T(8,128)(2,1)S(1)}, bf16[128,2048]{1,0:T(8,128)(2,1)S(1)}, u32[]{:S(2)}, u32[]{:S(2)}) %collective-permute-start.72) | collective-permute-done | bytes 524320 | tf_op jit(solution)/shard_map/ppermute | solution.py:314
  765.9 7.6 collective-permute-done.63
  821.2 27.2 %reduce-scatter.8.cloned.1.call-done = bf16[128,2048]{1,0:T(8,128)(2,1)} async-done(((bf16[512,2048]{1,0:T(8,128)(2,1)}), bf16[128,2048]{1,0:T(8,128)(2,1)}) %reduce-scatter.8.cloned.1.call-update) | async-done | bytes 524304 | tf_op jit(solution)/shard_map/reduce_scatter | solution.py:659
  868.9 12.9 %collective-permute-done.66 = f32[1,4353]{1,0:T(1,128)S(1)} collective-permute-done((f32[1,4353]{1,0:T(1,128)S(1)}, f32[1,4353]{1,0:T(1,128)S(1)}, u32[]{:S(2)}, u32[]{:S(2)}) %collective-permute-start.66) | collective-permute-done | bytes 17444 | tf_op jit(solution)/shard_map/ppermute | solution.py:305
  (546 shorter events, 303.6 us)
Async XLA Ops:
  7.2 52.8 %all-gather.9.cloned.1.call-start = ((), (), s32[]{:S(2)}) async-start(), calls=%async_computation.6 | async-start | bytes 7077888 | tf_op jit(solution)/shard_map/all_gather | solution.py:508
  9.6 128.3 %all-gather.11.cloned.1.call-start = ((), (), s32[]{:S(2)}) async-start(), calls=%async_computation.7 | async-start | bytes 9437184 | tf_op jit(solution)/shard_map/all_gather | solution.py:512
  71.0 39.8 %collective-permute-start.7 = (bf16[1,512,4,128]{1,3,2,0:T(8,128)(2,1)S(1)}, bf16[1,512,4,128]{1,3,2,0:T(8,128)(2,1)S(1)}, u32[]{:S(2)}, u32[]{:S(2)}) collective-permute-start(bf16[1,512,4,128]{1,3,2,0:T(8,128)(2,1)S(1)} %fusion.51), channel_id=1, source_target_pairs={{0,4},{4,0},{1,5},{5,1},{2,6},{6,2},{3,7},{7,3},{8,12},{12,8},{9,1... | collective-permute-start | bytes 1572872 | tf_op jit(solution)/shard_map/ppermute | solution.py:527
  137.6 33.9 %all-gather.13.cloned.1.call-start = ((), (), s32[]{:S(2)}) async-start(), calls=%async_computation.8 | async-start | bytes 1310720 | tf_op jit(solution)/shard_map/all_gather | solution.py:556
  144.0 57.0 %all-gather.15.cloned.1.call-start = ((), (), s32[]{:S(2)}) async-start(), calls=%async_computation.9 | async-start | bytes 1310720 | tf_op jit(solution)/shard_map/all_gather | solution.py:556
  144.7 272.2 %reduce-scatter.4.cloned.1.call-start = ((), (), s32[]{:S(2)}) async-start(), calls=%async_computation.10 | async-start | bytes 2621440 | tf_op jit(solution)/shard_map/reduce_scatter | solution.py:568
  171.6 29.5 %collective-permute-start.15 = (bf16[512,1024]{1,0:T(8,128)(2,1)}, bf16[512,1024]{1,0:T(8,128)(2,1)}, u32[]{:S(2)}, u32[]{:S(2)}) collective-permute-start(bf16[512,1024]{1,0:T(8,128)(2,1)} %all-gather.13.cloned.1.call-done.refs_0_), channel_id=1, source_target_pairs={{0,16},{8,24},{16,0},{24,8},{1,17},{9,25},{17,1},{25,9},{2,18},{10... | collective-permute-start | bytes 3145736 | tf_op jit(solution)/shard_map/ppermute | solution.py:333
  173.0 28.0 %collective-permute-start.16 = (bf16[512,1024]{1,0:T(8,128)(2,1)}, bf16[512,1024]{1,0:T(8,128)(2,1)}, u32[]{:S(2)}, u32[]{:S(2)}) collective-permute-start(bf16[512,1024]{1,0:T(8,128)(2,1)} %all-gather.13.cloned.1.call-done.refs_0_), channel_id=1, source_target_pairs={{0,4},{4,0},{1,5},{5,1},{2,6},{6,2},{3,7},{7,3},{8,12},{12,8},{9,1... | collective-permute-start | bytes 3145736 | tf_op jit(solution)/shard_map/ppermute | solution.py:336
  174.5 31.1 %collective-permute-start.17 = (bf16[512,1024]{1,0:T(8,128)(2,1)}, bf16[512,1024]{1,0:T(8,128)(2,1)}, u32[]{:S(2)}, u32[]{:S(2)}) collective-permute-start(bf16[512,1024]{1,0:T(8,128)(2,1)} %all-gather.13.cloned.1.call-done.refs_0_), channel_id=1, source_target_pairs={{0,8},{8,0},{16,24},{24,16},{1,9},{9,1},{17,25},{25,17},{2,10},{10... | collective-permute-start | bytes 3145736 | tf_op jit(solution)/shard_map/ppermute | solution.py:330
  233.1 45.9 %collective-permute-start.21 = (bf16[512,2048]{1,0:T(8,128)(2,1)}, bf16[512,2048]{1,0:T(8,128)(2,1)S(1)}, u32[]{:S(2)}, u32[]{:S(2)}) collective-permute-start(bf16[512,2048]{1,0:T(8,128)(2,1)} %get-tuple-element.107), channel_id=1, source_target_pairs={{0,8},{8,0},{16,24},{24,16},{1,9},{9,1},{17,25},{25,17},{2,10},{10... | collective-permute-start | bytes 6291464 | tf_op jit(solution)/shard_map/ppermute | solution.py:330
  375.1 72.3 %all-gather.19.cloned.1.call-start = ((), (), s32[]{:S(2)}) async-start(), calls=%async_computation.12 | async-start | bytes 1310720 | tf_op jit(solution)/shard_map/all_gather | solution.py:556
  420.0 57.1 %all-gather.21.cloned.1.call-start = ((), (), s32[]{:S(2)}) async-start(), calls=%async_computation.13 | async-start | bytes 1310720 | tf_op jit(solution)/shard_map/all_gather | solution.py:556
  420.8 113.0 %all-gather.17.cloned.1.call-start = ((), (), s32[]{:S(2)}) async-start(), calls=%async_computation.11 | async-start | bytes 2621440 | tf_op jit(solution)/shard_map/all_gather | solution.py:588
  447.4 29.7 %collective-permute-start.39 = (bf16[512,1024]{1,0:T(8,128)(2,1)}, bf16[512,1024]{1,0:T(8,128)(2,1)}, u32[]{:S(2)}, u32[]{:S(2)}) collective-permute-start(bf16[512,1024]{1,0:T(8,128)(2,1)} %all-gather.19.cloned.1.call-done.refs_0_), channel_id=1, source_target_pairs={{0,16},{8,24},{16,0},{24,8},{1,17},{9,25},{17,1},{25,9},{2,18},{10... | collective-permute-start | bytes 3145736 | tf_op jit(solution)/shard_map/ppermute | solution.py:333
  448.9 28.2 %collective-permute-start.40 = (bf16[512,1024]{1,0:T(8,128)(2,1)}, bf16[512,1024]{1,0:T(8,128)(2,1)S(1)}, u32[]{:S(2)}, u32[]{:S(2)}) collective-permute-start(bf16[512,1024]{1,0:T(8,128)(2,1)} %all-gather.19.cloned.1.call-done.refs_0_), channel_id=1, source_target_pairs={{0,4},{4,0},{1,5},{5,1},{2,6},{6,2},{3,7},{7,3},{8,12},{12,8},{9,1... | collective-permute-start | bytes 3145736 | tf_op jit(solution)/shard_map/ppermute | solution.py:336
  450.4 29.0 %collective-permute-start.41 = (bf16[512,1024]{1,0:T(8,128)(2,1)}, bf16[512,1024]{1,0:T(8,128)(2,1)}, u32[]{:S(2)}, u32[]{:S(2)}) collective-permute-start(bf16[512,1024]{1,0:T(8,128)(2,1)} %all-gather.19.cloned.1.call-done.refs_0_), channel_id=1, source_target_pairs={{0,8},{8,0},{16,24},{24,16},{1,9},{9,1},{17,25},{25,17},{2,10},{10... | collective-permute-start | bytes 3145736 | tf_op jit(solution)/shard_map/ppermute | solution.py:330
  477.8 220.4 %reduce-scatter.6.cloned.1.call-start = ((), (), s32[]{:S(2)}) async-start(), calls=%async_computation.14 | async-start | bytes 2621440 | tf_op jit(solution)/shard_map/reduce_scatter | solution.py:568
  477.8 28.8 %collective-permute-start.46 = (bf16[512,1024]{1,0:T(8,128)(2,1)}, bf16[512,1024]{1,0:T(8,128)(2,1)S(1)}, u32[]{:S(2)}, u32[]{:S(2)}) collective-permute-start(bf16[512,1024]{1,0:T(8,128)(2,1)} %all-gather.21.cloned.1.call-done.refs_1_), channel_id=1, source_target_pairs={{0,16},{8,24},{16,0},{24,8},{1,17},{9,25},{17,1},{25,9},{2,18},{10... | collective-permute-start | bytes 3145736 | tf_op jit(solution)/shard_map/ppermute | solution.py:333
  479.4 27.3 %collective-permute-start.47 = (bf16[512,1024]{1,0:T(8,128)(2,1)}, bf16[512,1024]{1,0:T(8,128)(2,1)}, u32[]{:S(2)}, u32[]{:S(2)}) collective-permute-start(bf16[512,1024]{1,0:T(8,128)(2,1)} %all-gather.21.cloned.1.call-done.refs_1_), channel_id=1, source_target_pairs={{0,4},{4,0},{1,5},{5,1},{2,6},{6,2},{3,7},{7,3},{8,12},{12,8},{9,1... | collective-permute-start | bytes 3145736 | tf_op jit(solution)/shard_map/ppermute | solution.py:336
  506.9 27.0 %collective-permute-start.49 = (bf16[512,1024]{1,0:T(8,128)(2,1)}, bf16[512,1024]{1,0:T(8,128)(2,1)}, u32[]{:S(2)}, u32[]{:S(2)}) collective-permute-start(bf16[512,1024]{1,0:T(8,128)(2,1)} %collective-permute-done.39.refs_0_), channel_id=1, source_target_pairs={{0,4},{4,0},{1,5},{5,1},{2,6},{6,2},{3,7},{7,3},{8,12},{12,8},{9,1... | collective-permute-start | bytes 3145736 | tf_op jit(solution)/shard_map/ppermute | solution.py:336
  509.9 47.7 %collective-permute-start.45 = (bf16[512,2048]{1,0:T(8,128)(2,1)}, bf16[512,2048]{1,0:T(8,128)(2,1)S(1)}, u32[]{:S(2)}, u32[]{:S(2)}) collective-permute-start(bf16[512,2048]{1,0:T(8,128)(2,1)} %get-tuple-element.146), channel_id=1, source_target_pairs={{0,8},{8,0},{16,24},{24,16},{1,9},{9,1},{17,25},{25,17},{2,10},{10... | collective-permute-start | bytes 6291464 | tf_op jit(solution)/shard_map/ppermute | solution.py:330
  559.6 27.9 %collective-permute-start.53 = (bf16[512,1024]{1,0:T(8,128)(2,1)}, bf16[512,1024]{1,0:T(8,128)(2,1)}, u32[]{:S(2)}, u32[]{:S(2)}) collective-permute-start(bf16[512,1024]{1,0:T(8,128)(2,1)} %add_convert_fusion.8), channel_id=1, source_target_pairs={{0,16},{8,24},{16,0},{24,8},{1,17},{9,25},{17,1},{25,9},{2,18},{10... | collective-permute-start | bytes 3145736 | tf_op jit(solution)/shard_map/ppermute | solution.py:333
  708.9 32.0 %collective-permute-start.72 = (bf16[128,2048]{1,0:T(8,128)(2,1)S(1)}, bf16[128,2048]{1,0:T(8,128)(2,1)S(1)}, u32[]{:S(2)}, u32[]{:S(2)}) collective-permute-start(bf16[128,2048]{1,0:T(8,128)(2,1)S(1)} %get-tuple-element.239), channel_id=1, source_target_pairs={{0,1},{1,2},{2,3},{4,5},{5,6},{6,7},{8,9},{9,10},{10,11},{12,13},{... | collective-permute-start | bytes 1572872 | tf_op jit(solution)/shard_map/ppermute | solution.py:314
  717.8 28.7 %all-to-all-start.2 = ((bf16[128,4,512]{2,0,1:T(8,128)(2,1)}), bf16[128,4,512]{2,0,1:T(8,128)(2,1)S(1)}, u32[]{:S(2)}, u32[]{:S(2)}) async-start(bf16[128,4,512]{2,0,1:T(8,128)(2,1)} %bitcast.192), calls=%async_computation.4 | async-start | bytes 1048576 | tf_op jit(solution)/shard_map/all_to_all | solution.py:629
  721.3 127.1 %reduce-scatter.8.cloned.1.call-start = ((), (), s32[]{:S(2)}) async-start(), calls=%async_computation.15 | async-start | bytes 2621440 | tf_op jit(solution)/shard_map/reduce_scatter | solution.py:659
  721.3 65.8 %collective-permute-start.73 = (bf16[128,2048]{1,0:T(8,128)(2,1)S(1)}, bf16[128,2048]{1,0:T(8,128)(2,1)}, u32[]{:S(2)}, u32[]{:S(2)}) collective-permute-start(bf16[128,2048]{1,0:T(8,128)(2,1)S(1)} %get-tuple-element.239), channel_id=1, source_target_pairs={{1,0},{2,1},{3,2},{5,4},{6,5},{7,6},{9,8},{10,9},{11,10},{13,12},{... | collective-permute-start | bytes 1572872 | tf_op jit(solution)/shard_map/ppermute | solution.py:314
  722.6 66.4 %collective-permute-start.74 = (bf16[128,2048]{1,0:T(8,128)(2,1)S(1)}, bf16[128,2048]{1,0:T(8,128)(2,1)}, u32[]{:S(2)}, u32[]{:S(2)}) collective-permute-start(bf16[128,2048]{1,0:T(8,128)(2,1)S(1)} %get-tuple-element.239), channel_id=1, source_target_pairs={{2,0},{3,1},{6,4},{7,5},{10,8},{11,9},{14,12},{15,13},{18,16},{19,... | collective-permute-start | bytes 1572872 | tf_op jit(solution)/shard_map/ppermute | solution.py:314
  724.0 67.0 %collective-permute-start.75 = (bf16[128,2048]{1,0:T(8,128)(2,1)S(1)}, bf16[128,2048]{1,0:T(8,128)(2,1)}, u32[]{:S(2)}, u32[]{:S(2)}) collective-permute-start(bf16[128,2048]{1,0:T(8,128)(2,1)S(1)} %get-tuple-element.239), channel_id=1, source_target_pairs={{3,0},{7,4},{11,8},{15,12},{19,16},{23,20},{27,24},{31,28}} | collective-permute-start | bytes 1572872 | tf_op jit(solution)/shard_map/ppermute | solution.py:314
  786.2 112.6 %all-gather.23.cloned.1.call-start = ((), (), s32[]{:S(2)}) async-start(), calls=%async_computation.16 | async-start | bytes 2621440 | tf_op jit(solution)/shard_map/all_gather | solution.py:668
  817.9 43.5 %collective-permute-start.83 = (bf16[256,1024]{0,1:T(8,128)(2,1)}, bf16[256,1024]{0,1:T(8,128)(2,1)}, u32[]{:S(2)}, u32[]{:S(2)}) collective-permute-start(bf16[256,1024]{0,1:T(8,128)(2,1)} %get-tuple-element.278), channel_id=1, source_target_pairs={{0,4},{4,0},{1,5},{5,1},{2,6},{6,2},{3,7},{7,3},{8,12},{12,8},{9,1... | collective-permute-start | bytes 1572872 | tf_op jit(solution)/shard_map/ppermute | solution.py:336
  819.6 45.1 %collective-permute-start.81 = (bf16[256,1024]{0,1:T(8,128)(2,1)}, bf16[256,1024]{0,1:T(8,128)(2,1)}, u32[]{:S(2)}, u32[]{:S(2)}) collective-permute-start(bf16[256,1024]{0,1:T(8,128)(2,1)} %get-tuple-element.277), channel_id=1, source_target_pairs={{0,16},{8,24},{16,0},{24,8},{1,17},{9,25},{17,1},{25,9},{2,18},{10... | collective-permute-start | bytes 1572872 | tf_op jit(solution)/shard_map/ppermute | solution.py:333
  856.4 26.9 %collective-permute-start.78 = (bf16[256,1024]{0,1:T(8,128)(2,1)}, bf16[256,1024]{0,1:T(8,128)(2,1)S(1)}, u32[]{:S(2)}, u32[]{:S(2)}) collective-permute-start(bf16[256,1024]{0,1:T(8,128)(2,1)} %slice.488), channel_id=1, source_target_pairs={{0,16},{8,24},{16,0},{24,8},{1,17},{9,25},{17,1},{25,9},{2,18},{10... | collective-permute-start | bytes 1572872 | tf_op jit(solution)/shard_map/ppermute | solution.py:333
  (160 other events, 2040.1 us)
Sparse Core Ops, SparseCore 0:
  10.5 49.4 all-gather.8
  62.4 70.8 all-gather.10
  144.1 27.3 all-gather.12
  173.6 27.4 all-gather.14
  375.3 41.5 reduce-scatter.3
  420.1 27.2 all-gather.18
  449.7 27.4 all-gather.20
  478.8 45.4 all-gather.16
  653.9 42.2 reduce-scatter.5
  786.4 61.9 reduce-scatter.7
  852.8 46.0 all-gather.22

commit v6 on v5

--- a/solution.py
+++ b/solution.py
@@ -179,7 +179,7 @@
 
     half = down_ref.shape[1]
     rows, weight = take_rows(x_refs, table_ref, rows_ref)
-    gate_up = jnp.dot(rows, up_ref[0], preferred_element_type=wide)
+    gate_up = jnp.dot(rows, up_ref[expert], preferred_element_type=wide)
     gate_up_ref[0] = gate_up.reshape(blocks, capacity, 2 * half)
     gate_part = gate_up[:, :half]
     up_part = gate_up[:, half:]
@@ -188,7 +188,7 @@
     begin = pl.multiple_of(expert * capacity, 16)
     for cut in tiles_of(width):
         y_ref[:, pl.ds(begin, capacity), cut] = (
-            jnp.dot(hidden, down_ref[0, :, cut], preferred_element_type=wide)
+            jnp.dot(hidden, down_ref[expert, :, cut], preferred_element_type=wide)
             .astype(low)
             .reshape(blocks, capacity, -1)
         )
@@ -212,7 +212,7 @@
 
     half = down_ref.shape[1]
     rows, weight = take_rows(x_refs, table_ref, rows_ref)
-    grad_hidden = nt_dot(rows, down_ref[0]) * weight
+    grad_hidden = nt_dot(rows, down_ref[expert]) * weight
     gate_up = gate_up_ref[0].reshape(blocks * capacity, 2 * half)
     gate_part = gate_up[:, :half]
     up_part = gate_up[:, half:]
@@ -224,7 +224,7 @@
     begin = pl.multiple_of(expert * capacity, 16)
     for cut in tiles_of(width):
         y_ref[:, pl.ds(begin, capacity), cut] = (
-            nt_dot(grad_rows, up_ref[0, cut, :]).astype(low).reshape(blocks, capacity, -1)
+            nt_dot(grad_rows, up_ref[expert, cut, :]).astype(low).reshape(blocks, capacity, -1)
         )
 
     @pl.when(expert == experts - 1)
@@ -241,13 +241,13 @@
     row_spec = lambda last: pl.BlockSpec(
         (1, blocks, capacity, last), lambda e: (e, begin // blocks, 0, 0)
     )
-    row_shape = lambda last, kind: jax.ShapeDtypeStruct((experts, total, capacity, last), kind)
+    row_shape = lambda last, kind: pltpu.HBM((experts, total, capacity, last), kind)
     whole = lambda shape: pl.BlockSpec(shape, lambda e: (0,) * len(shape), pipeline_mode=once)
     in_specs = [whole(p.shape) for p in pieces] + [
         pl.BlockSpec((blocks, 1, 2, slots), lambda e: (0, e, 0, 0)),
         whole((blocks, slots, experts)),
-        pl.BlockSpec((1, width, double), lambda e: (e, 0, 0)),
-        pl.BlockSpec((1, half, width), lambda e: (e, 0, 0)),
+        pl.BlockSpec(memory_space=pltpu.VMEM),
+        pl.BlockSpec(memory_space=pltpu.VMEM),
     ]
     operands = [*pieces, table, place, w_up, w_down]
     n_out = blocks
@@ -255,7 +255,7 @@
     out_shape = [jax.ShapeDtypeStruct((slots, width), low)] * n_out + [row_shape(width, low)]
     if backward:
         in_specs.append(row_spec(double))
-        operands.append(gate_up)
+        operands.append(pltpu.with_memory_space_constraint(gate_up, pltpu.HBM))
         out_shape.append(row_shape(double, low))
     else:
         out_specs.append(row_spec(half))
@@ -277,7 +277,7 @@
             pltpu.VMEM((blocks, slots, experts * capacity), low),
         ],
         compiler_params=pltpu.CompilerParams(
-            dimension_semantics=("arbitrary",), vmem_limit_bytes=56 << 20
+            dimension_semantics=("arbitrary",), vmem_limit_bytes=(28 if backward else 28) << 20
         ),
         cost_estimate=pl.CostEstimate(
             flops=2 * rows * width * (2 * slots + double + half),
@@ -286,6 +286,29 @@
         ),
     )(*operands, *kept)
     return (made[:n_out], made[n_out:])
+
+
+def on_chip(*arrays):
+    count = len(arrays)
+
+    def body(*refs):
+        sources, targets, sems = refs[:count], refs[count : 2 * count], refs[-1]
+        copies = [
+            pltpu.make_async_copy(sources[i], targets[i], sems.at[i]) for i in range(count)
+        ]
+        for copy in copies:
+            copy.start()
+        for copy in copies:
+            copy.wait()
+
+    return pl.pallas_call(
+        body,
+        in_specs=[pl.BlockSpec(memory_space=pltpu.HBM)] * count,
+        out_specs=[pl.BlockSpec(memory_space=pltpu.VMEM)] * count,
+        out_shape=[pltpu.VMEM(a.shape, a.dtype) for a in arrays],
+        scratch_shapes=[pltpu.SemaphoreType.DMA((count,))],
+        compiler_params=pltpu.CompilerParams(vmem_limit_bytes=24 << 20),
+    )(*[pltpu.with_memory_space_constraint(a, pltpu.HBM) for a in arrays])
 
 
 def added(left, right):
@@ -405,7 +428,7 @@
         far = [self.along_y(x_first), self.along_x(y_second)]
         over_y = [over_y, self.core(y_second)]
         near_x = call(2, [x_first, x_second, over_x, self.core(x_second)])
-        near_x = tie(near_x, far, over_y)
+        near_x = tie(near_x, over_y)
         other_own, other_x = self.core(own[1]), self.core(near_x[1])
         far += [self.core(piece) for piece in far]
         near_y = tie(call(4, [y_first, y_second, *over_y]), other_own, other_x, far)
@@ -559,7 +582,7 @@
 
     def forward(begin, pieces):
         made, saved[0] = expert_call(
-            begin, pieces, some(table, begin, pieces), some(place, begin, pieces), w_up, w_down,
+            begin, pieces, some(table, begin, pieces), some(place, begin, pieces), *near_weights,
             None, saved[0], capacity, shards,
         )
         return made
@@ -573,6 +596,7 @@
     second_own, table, place = lax.optimization_barrier((normed_own[:, cols[1]], table, place))
     first_block, second_block = spread(normed_own[:, cols[0]], second_own)
     second_block, w_up = lax.optimization_barrier((second_block, w_up))
+    near_weights = on_chip(w_up, w_down)
     mixture = places.experts(
         first_block,
         second_block,
@@ -593,11 +617,9 @@
 
     def backward(begin, pieces):
         made, saved[0] = expert_call(
-            begin, pieces, some(table, begin, pieces), some(place, begin, pieces), w_up, w_down,
+            begin, pieces, some(table, begin, pieces), some(place, begin, pieces), *back_weights,
             gate_up, saved[0], capacity, shards,
         )
-        if begin == 2:
-            made = tie(made, activations)
         return made
 
     def weight_grads():
@@ -608,10 +630,13 @@
         yield [made[0]]
         grad_up = jnp.einsum("ebcd,ebcf->edf", rows_in, grad_rows, preferred_element_type=wide)
         made.append(grad_up)
-        yield [grad_up]
+        yield [grad_up, activations]
 
     made = []
-    total_in = places.experts(*spread_halves, backward, weight_grads)
+    first_block, second_block = spread_halves
+    second_block, w_up = lax.optimization_barrier((second_block, w_up))
+    back_weights = on_chip(w_up, w_down)
+    total_in = places.experts(first_block, second_block, backward, weight_grads)
     if not made:
         for _ in weight_grads():
             pass

time: 924 us -> 913 us (0.988)
  Pallas kernels: 174 us -> 147 us
  waiting for transfers between devices: 392 us -> 404 us
    pallas_call x8, Pallas kernels: 174 us -> 138 us  [expert_call(): pl.pallas_call(body, grid=(experts,), in_specs=in_specs + [pl.BlockSpec(m...]
    pallas_call x0 -> x2, Pallas kernels: none -> 9.27 us  [on_chip(): pl.pallas_call(body, in_specs=[pl.BlockSpec(memory_space=pltpu.HBM)] * co...]
    unnamed x210 -> x194, local copies, waits for them, and re-layouts: 22.7 us -> 22.8 us
  transfers between devices with their start and end apart: 100 -> 100, of which waited for: 51 -> 55; matrix products, arithmetic and copies ran while one was open for 21% -> 22% of each run, Pallas kernels for 19% -> 16%
where the time goes in v6:
time: 913 us; the launch traced here: 903 us
  waiting for transfers between devices  404 us (44%)
  Pallas kernels  147 us (16%)
  starting transfers between devices  92.3 us (10%)
  local copies, waits for them, and re-layouts  82.8 us (9%)
  matrix products  81.6 us (9%)
  other arithmetic  74.8 us (8%)
  between operations  20.3 us (2%)
    pallas_call x8, Pallas kernels, expert_call(): pl.pallas_call(body, grid=(experts,), in_specs=in_specs + [pl.BlockSpec(m...  138 us
    all_gather x4, waiting for transfers between devices, spread(): lax.all_gather(half.astype(low), 'tp', axis=0, tiled=True)  92.6 us
    ppermute x16, waiting for transfers between devices, along_x(): return lax.ppermute(a, 'fsdp', [(i, i ^ 2) for i in range(self.fsdp)])  80.9 us
    reduce_scatter x2, waiting for transfers between devices, finish(): lax.psum_scatter(half, 'tp', scatter_dimension=0, tiled=True).astype(wide)  40.3 us
    ppermute x12, waiting for transfers between devices, line_gather(): lax.ppermute(shard, 'tp', [(i, i + d) for i in range(size) if 0 <= i + d...  33.6 us
    reduce_scatter x1, waiting for transfers between devices, per_device(): lax.psum_scatter(nt_dot(grad_proj_low, full_qkv).astype(low), 'tp', scatt...  27.5 us
    ppermute x12, starting transfers between devices, line_gather(): lax.ppermute(shard, 'tp', [(i, i + d) for i in range(size) if 0 <= i + d...  26.9 us
    ppermute x17, waiting for transfers between devices, along_y(): return lax.ppermute(a, 'ctx', [(i, i ^ 1) for i in range(self.ctx)])  25.4 us
  transfers between devices with their start and end apart: 100, of which 55 were waited for; matrix products, arithmetic and copies ran while one was open for 22% of the time, Pallas kernels for 16%

profile of v6, /device:TPU:0, one launch (start us, length us, event | category | flops | bytes accessed | tf_op | source)
XLA Modules:
  0.0 902.9 jit_solution(7629258286445739347)
XLA Ops:
  9.6 7.0 collective-permute-start.9
  33.6 12.8 %collective-permute-done.13 = bf16[512,256]{1,0:T(8,128)(2,1)S(1)} collective-permute-done((bf16[512,256]{1,0:T(8,128)(2,1)S(1)}, bf16[512,256]{1,0:T(8,128)(2,1)S(1)}, u32[]{:S(2)}, u32[]{:S(2)}) %collective-permute-start.13) | collective-permute-done | bytes 262176 | tf_op jit(solution)/shard_map/ppermute | solution.py:337
  60.0 6.4 fusion.11
  72.8 23.4 %collective-permute-done.8 = bf16[1,512,4,128]{1,3,2,0:T(8,128)(2,1)} collective-permute-done((bf16[1,512,4,128]{1,3,2,0:T(8,128)(2,1)}, bf16[1,512,4,128]{1,3,2,0:T(8,128)(2,1)}, u32[]{:S(2)}, u32[]{:S(2)}) %collective-permute-start.8) | collective-permute-done | bytes 524320 | tf_op jit(solution)/shard_map/ppermute | solution.py:551
  101.0 10.0 %collective-permute-done.7 = bf16[1,512,4,128]{1,3,2,0:T(8,128)(2,1)S(1)} collective-permute-done((bf16[1,512,4,128]{1,3,2,0:T(8,128)(2,1)S(1)}, bf16[1,512,4,128]{1,3,2,0:T(8,128)(2,1)S(1)}, u32[]{:S(2)}, u32[]{:S(2)}) %collective-permute-start.7) | collective-permute-done | bytes 524320 | tf_op jit(solution)/shard_map/ppermute | solution.py:550
  123.6 10.7 %all-to-all-done = bf16[4,128,512]{1,2,0:T(8,128)(2,1)S(1)} async-done(((bf16[4,128,512]{1,2,0:T(8,128)(2,1)}), bf16[4,128,512]{1,2,0:T(8,128)(2,1)S(1)}, u32[]{:S(2)}, u32[]{:S(2)}) %all-to-all-start) | async-done | bytes 524320 | tf_op jit(solution)/shard_map/all_to_all | solution.py:568
  145.7 26.8 %all-gather.13.cloned.1.call-done.refs_0_ = bf16[512,1024]{1,0:T(8,128)(2,1)} async-done(((bf16[128,1024]{1,0:T(8,128)(2,1)}), bf16[512,1024]{1,0:T(8,128)(2,1)}) %all-gather.13.cloned.1.call-update) | async-done | bytes 1048592 | tf_op jit(solution)/shard_map/all_gather | solution.py:579
  175.4 14.1 %reshape.364.refs_0_ = bf16[4,2048,512]{2,1,0:T(8,128)(2,1)} reshape(bf16[4,2048,2,256]{3,2,1,0:T(2,128)(2,1)} %param.20) | data formatting | bytes 16777216 | tf_op jit(solution)/shard_map/reshape | solution.py:520
  189.5 12.4 %all-gather.15.cloned.1.call-done.refs_1_ = bf16[512,1024]{1,0:T(8,128)(2,1)} async-done(((bf16[128,1024]{1,0:T(8,128)(2,1)}), bf16[512,1024]{1,0:T(8,128)(2,1)}) %all-gather.15.cloned.1.call-update) | async-done | bytes 1048592 | tf_op jit(solution)/shard_map/all_gather | solution.py:579
  214.1 15.9 %shard_map.187 = (bf16[512,2048]{1,0:T(8,128)(2,1)S(1)}, bf16[512,2048]{1,0:T(8,128)(2,1)S(1)}, bf16[4,8,160,2048]{3,2,1,0:T(8,128)(2,1)}, f32[4,8,160,512]{3,2,1,0:T(8,128)}, bf16[4,8,160,256]{3,2,1,0:T(8,128)(2,1)}) custom-call(bf16[512,1024]{1,0:T(8,128)(2,1)S(1)} %copy-done.6, bf16[512,1024]{1,0:T(8,128)(2,1)S(1)} %copy-done.7, ...), custom_call_target="tpu_custom_call" | custom-call | flops 9395240960 | bytes 17563648 | tf_op jit(solution)/shard_map/pallas_call | solution.py:268
  235.7 17.0 %shard_map.188 = (bf16[512,2048]{1,0:T(8,128)(2,1)S(1)}, bf16[512,2048]{1,0:T(8,128)(2,1)}, bf16[4,8,160,2048]{3,2,1,0:T(8,128)(2,1)}, f32[4,8,160,512]{3,2,1,0:T(8,128)}, bf16[4,8,160,256]{3,2,1,0:T(8,128)(2,1)}) custom-call(bf16[512,1024]{1,0:T(8,128)(2,1)} %collective-permute-done.15.refs_0_, ...), custom_call_target="tpu_custom_call", output_to_operand_aliasing={{2}: (8, {}), {3}: (9, {}), {4}: (10, {})} | custom-call | flops 9395240960 | bytes 17563648 | tf_op jit(solution)/shard_map/pallas_call | solution.py:268
  259.8 15.6 %shard_map.189 = (bf16[512,2048]{1,0:T(8,128)(2,1)S(1)}, bf16[512,2048]{1,0:T(8,128)(2,1)S(1)}, bf16[4,8,160,2048]{3,2,1,0:T(8,128)(2,1)}, f32[4,8,160,512]{3,2,1,0:T(8,128)}, bf16[4,8,160,256]{3,2,1,0:T(8,128)(2,1)}) custom-call(bf16[512,1024]{1,0:T(8,128)(2,1)S(1)} %collective-permute-done.16.refs_0_, ...), custom_call_target="tpu_custom_call", output_to_operand_aliasing={{2}: (8, {}), {3}: (9, {}), {4}: (10, {})} | custom-call | flops 9395240960 | bytes 17563648 | tf_op jit(solution)/shard_map/pallas_call | solution.py:268
  281.2 14.5 %shard_map.190 = (bf16[512,2048]{1,0:T(8,128)(2,1)S(1)}, bf16[512,2048]{1,0:T(8,128)(2,1)S(1)}, bf16[4,8,160,2048]{3,2,1,0:T(8,128)(2,1)}, f32[4,8,160,512]{3,2,1,0:T(8,128)}, bf16[4,8,160,256]{3,2,1,0:T(8,128)(2,1)}) custom-call(bf16[512,1024]{1,0:T(8,128)(2,1)S(1)} %collective-permute-done.28.refs_0_, ...), custom_call_target="tpu_custom_call", output_to_operand_aliasing={{2}: (8, {}), {3}: (9, {}), {4}: (10, {})} | custom-call | flops 9395240960 | bytes 17563648 | tf_op jit(solution)/shard_map/pallas_call | solution.py:268
  295.7 7.1 collective-permute-done.27
  312.2 24.0 %collective-permute-done.35 = bf16[512,1024]{1,0:T(8,128)(2,1)S(1)} collective-permute-done((bf16[512,1024]{1,0:T(8,128)(2,1)S(1)}, bf16[512,1024]{1,0:T(8,128)(2,1)S(1)}, u32[]{:S(2)}, u32[]{:S(2)}) %collective-permute-start.35) | collective-permute-done | bytes 1048608 | tf_op jit(solution)/shard_map/ppermute | solution.py:356
  341.2 21.3 %collective-permute-done.38 = bf16[512,1024]{1,0:T(8,128)(2,1)S(1)} collective-permute-done((bf16[512,1024]{1,0:T(8,128)(2,1)S(1)}, bf16[512,1024]{1,0:T(8,128)(2,1)S(1)}, u32[]{:S(2)}, u32[]{:S(2)}) %collective-permute-start.38) | collective-permute-done | bytes 1048608 | tf_op jit(solution)/shard_map/ppermute | solution.py:356
  370.9 40.3 %reduce-scatter.4.cloned.1.call-done = bf16[128,2048]{1,0:T(8,128)(2,1)} async-done(((bf16[512,2048]{1,0:T(8,128)(2,1)}), bf16[128,2048]{1,0:T(8,128)(2,1)}) %reduce-scatter.4.cloned.1.call-update) | async-done | bytes 524304 | tf_op jit(solution)/shard_map/reduce_scatter | solution.py:591
  415.1 26.6 %all-gather.19.cloned.1.call-done.refs_0_ = bf16[512,1024]{1,0:T(8,128)(2,1)} async-done(((bf16[128,1024]{1,0:T(8,128)(2,1)}), bf16[512,1024]{1,0:T(8,128)(2,1)}) %all-gather.19.cloned.1.call-update) | async-done | bytes 1048592 | tf_op jit(solution)/shard_map/all_gather | solution.py:579
  444.6 26.7 %all-gather.21.cloned.1.call-done.refs_1_ = bf16[512,1024]{1,0:T(8,128)(2,1)} async-done(((bf16[128,1024]{1,0:T(8,128)(2,1)}), bf16[512,1024]{1,0:T(8,128)(2,1)}) %all-gather.21.cloned.1.call-update) | async-done | bytes 1048592 | tf_op jit(solution)/shard_map/all_gather | solution.py:579
  479.6 19.0 %shard_map.192 = (bf16[512,2048]{1,0:T(8,128)(2,1)S(1)}, bf16[512,2048]{1,0:T(8,128)(2,1)S(1)}, bf16[4,8,160,2048]{3,2,1,0:T(8,128)(2,1)}, bf16[4,8,160,512]{3,2,1,0:T(8,128)(2,1)}) custom-call(bf16[512,1024]{1,0:T(8,128)(2,1)S(1)} %copy-done.8, bf16[512,1024]{1,0:T(8,128)(2,1)S(1)} %copy-done.9, bf16[512,1024]{1,0:T(8,128)(2,1)} %collective-permute-done.41.refs_2_, ...), custom_call_target="tpu_custom_call" | custom-call | flops 9395240960 | bytes 17563648 | tf_op jit(solution)/shard_map/pallas_call | solution.py:268
  502.6 18.7 %shard_map.193 = (bf16[512,2048]{1,0:T(8,128)(2,1)S(1)}, bf16[512,2048]{1,0:T(8,128)(2,1)S(1)}, bf16[4,8,160,2048]{3,2,1,0:T(8,128)(2,1)}, bf16[4,8,160,512]{3,2,1,0:T(8,128)(2,1)}) custom-call(bf16[512,1024]{1,0:T(8,128)(2,1)} %collective-permute-done.39.refs_0_, ...), custom_call_target="tpu_custom_call", output_to_operand_aliasing={{2}: (9, {}), {3}: (10, {})} | custom-call | flops 9395240960 | bytes 17563648 | tf_op jit(solution)/shard_map/pallas_call | solution.py:268
  526.3 18.1 %shard_map.194 = (bf16[512,2048]{1,0:T(8,128)(2,1)S(1)}, bf16[512,2048]{1,0:T(8,128)(2,1)S(1)}, bf16[4,8,160,2048]{3,2,1,0:T(8,128)(2,1)}, bf16[4,8,160,512]{3,2,1,0:T(8,128)(2,1)}) custom-call(bf16[512,1024]{1,0:T(8,128)(2,1)S(1)} %collective-permute-done.40.refs_0_, ...), custom_call_target="tpu_custom_call", output_to_operand_aliasing={{2}: (9, {}), {3}: (10, {})} | custom-call | flops 9395240960 | bytes 17563648 | tf_op jit(solution)/shard_map/pallas_call | solution.py:268
  550.4 18.8 %shard_map.195 = (bf16[512,2048]{1,0:T(8,128)(2,1)S(1)}, bf16[512,2048]{1,0:T(8,128)(2,1)}, bf16[4,8,160,2048]{3,2,1,0:T(8,128)(2,1)}, bf16[4,8,160,512]{3,2,1,0:T(8,128)(2,1)}) custom-call(bf16[512,1024]{1,0:T(8,128)(2,1)S(1)} %collective-permute-done.52.refs_0_, ...), custom_call_target="tpu_custom_call", output_to_operand_aliasing={{2}: (9, {}), {3}: (10, {})} | custom-call | flops 9395240960 | bytes 17563648 | tf_op jit(solution)/shard_map/pallas_call | solution.py:268
  583.5 15.7 %convolution_bitcast_fusion = f32[4,256,2048]{2,1,0:T(8,128)} fusion(bf16[4,8,160,256]{3,2,1,0:T(8,128)(2,1)S(1)} %copy-done.17, bf16[4,8,160,2048]{3,2,1,0:T(8,128)(2,1)} %get-tuple-element.182), kind=kOutput, calls=%fused_computation.25 | convolution fusion | flops 5368709120 | bytes 31981568 | tf_op jit(solution)/shard_map/ebcf,ebcd->efd/dot_general | solution.py:628
  599.3 7.6 collective-permute-done.59
  619.3 15.1 %collective-permute-done.62 = bf16[512,1024]{1,0:T(8,128)(2,1)S(1)} collective-permute-done((bf16[512,1024]{1,0:T(8,128)(2,1)}, bf16[512,1024]{1,0:T(8,128)(2,1)S(1)}, u32[]{:S(2)}, u32[]{:S(2)}) %collective-permute-start.62) | collective-permute-done | bytes 1048608 | tf_op jit(solution)/shard_map/ppermute | solution.py:356
  643.3 19.2 %fusion.86 = f32[4,2048,512,1]{1,2,3,0:T(8,128)} fusion(bf16[4,8,160,2048]{3,2,1,0:T(8,128)(2,1)} %get-tuple-element.185, bf16[4,8,160,512]{3,2,1,0:T(8,128)(2,1)} %get-tuple-element.186), kind=kOutput, calls=%fused_computation.263 | convolution fusion | flops 10737418240 | bytes 42991616 | tf_op jit(solution)/shard_map/ebcd,ebcf->edf/dot_general | solution.py:631
  662.5 25.1 %copy.120 = f32[4,2048,2,256]{3,2,1,0:T(2,128)} copy(f32[4,2048,2,256]{1,3,2,0:T(8,128)} %bitcast.198) | data formatting | bytes 33554432 | tf_op jit(solution)/shard_map/reshape | solution.py:645
  721.3 9.3 %collective-permute-done.72 = bf16[128,2048]{1,0:T(8,128)(2,1)S(1)} collective-permute-done((bf16[128,2048]{1,0:T(8,128)(2,1)S(1)}, bf16[128,2048]{1,0:T(8,128)(2,1)S(1)}, u32[]{:S(2)}, u32[]{:S(2)}) %collective-permute-start.72) | collective-permute-done | bytes 524320 | tf_op jit(solution)/shard_map/ppermute | solution.py:337
  755.5 7.6 collective-permute-done.63
  810.3 27.5 %reduce-scatter.8.cloned.1.call-done = bf16[128,2048]{1,0:T(8,128)(2,1)} async-done(((bf16[512,2048]{1,0:T(8,128)(2,1)}), bf16[128,2048]{1,0:T(8,128)(2,1)}) %reduce-scatter.8.cloned.1.call-update) | async-done | bytes 524304 | tf_op jit(solution)/shard_map/reduce_scatter | solution.py:684
  858.3 12.8 %collective-permute-done.66 = f32[1,4353]{1,0:T(1,128)S(1)} collective-permute-done((f32[1,4353]{1,0:T(1,128)S(1)}, f32[1,4353]{1,0:T(1,128)S(1)}, u32[]{:S(2)}, u32[]{:S(2)}) %collective-permute-start.66) | collective-permute-done | bytes 17444 | tf_op jit(solution)/shard_map/ppermute | solution.py:328
  (532 shorter events, 335.3 us)
Async XLA Ops:
  7.2 52.8 %all-gather.9.cloned.1.call-start = ((), (), s32[]{:S(2)}) async-start(), calls=%async_computation.6 | async-start | bytes 7077888 | tf_op jit(solution)/shard_map/all_gather | solution.py:531
  9.6 128.3 %all-gather.11.cloned.1.call-start = ((), (), s32[]{:S(2)}) async-start(), calls=%async_computation.7 | async-start | bytes 9437184 | tf_op jit(solution)/shard_map/all_gather | solution.py:535
  70.6 25.6 %collective-permute-start.8 = (bf16[1,512,4,128]{1,3,2,0:T(8,128)(2,1)}, bf16[1,512,4,128]{1,3,2,0:T(8,128)(2,1)}, u32[]{:S(2)}, u32[]{:S(2)}) collective-permute-start(bf16[1,512,4,128]{1,3,2,0:T(8,128)(2,1)} %pad_maximum_fusion.7), channel_id=1, source_target_pairs={{0,4},{4,0},{1,5},{5,1},{2,6},{6,2},{3,7},{7,3},{8,12},{12,8},{9,1... | collective-permute-start | bytes 1572872 | tf_op jit(solution)/shard_map/ppermute | solution.py:551
  71.1 39.8 %collective-permute-start.7 = (bf16[1,512,4,128]{1,3,2,0:T(8,128)(2,1)S(1)}, bf16[1,512,4,128]{1,3,2,0:T(8,128)(2,1)S(1)}, u32[]{:S(2)}, u32[]{:S(2)}) collective-permute-start(bf16[1,512,4,128]{1,3,2,0:T(8,128)(2,1)S(1)} %fusion.51), channel_id=1, source_target_pairs={{0,4},{4,0},{1,5},{5,1},{2,6},{6,2},{3,7},{7,3},{8,12},{12,8},{9,1... | collective-permute-start | bytes 1572872 | tf_op jit(solution)/shard_map/ppermute | solution.py:550
  137.6 34.9 %all-gather.13.cloned.1.call-start = ((), (), s32[]{:S(2)}) async-start(), calls=%async_computation.8 | async-start | bytes 1310720 | tf_op jit(solution)/shard_map/all_gather | solution.py:579
  144.9 57.0 %all-gather.15.cloned.1.call-start = ((), (), s32[]{:S(2)}) async-start(), calls=%async_computation.9 | async-start | bytes 1310720 | tf_op jit(solution)/shard_map/all_gather | solution.py:579
  145.6 265.6 %reduce-scatter.4.cloned.1.call-start = ((), (), s32[]{:S(2)}) async-start(), calls=%async_computation.10 | async-start | bytes 2621440 | tf_op jit(solution)/shard_map/reduce_scatter | solution.py:591
  172.5 29.5 %collective-permute-start.15 = (bf16[512,1024]{1,0:T(8,128)(2,1)}, bf16[512,1024]{1,0:T(8,128)(2,1)}, u32[]{:S(2)}, u32[]{:S(2)}) collective-permute-start(bf16[512,1024]{1,0:T(8,128)(2,1)} %all-gather.13.cloned.1.call-done.refs_0_), channel_id=1, source_target_pairs={{0,16},{8,24},{16,0},{24,8},{1,17},{9,25},{17,1},{25,9},{2,18},{10... | collective-permute-start | bytes 3145736 | tf_op jit(solution)/shard_map/ppermute | solution.py:356
  174.0 28.0 %collective-permute-start.16 = (bf16[512,1024]{1,0:T(8,128)(2,1)}, bf16[512,1024]{1,0:T(8,128)(2,1)S(1)}, u32[]{:S(2)}, u32[]{:S(2)}) collective-permute-start(bf16[512,1024]{1,0:T(8,128)(2,1)} %all-gather.13.cloned.1.call-done.refs_0_), channel_id=1, source_target_pairs={{0,4},{4,0},{1,5},{5,1},{2,6},{6,2},{3,7},{7,3},{8,12},{12,8},{9,1... | collective-permute-start | bytes 3145736 | tf_op jit(solution)/shard_map/ppermute | solution.py:359
  175.4 32.4 %collective-permute-start.17 = (bf16[512,1024]{1,0:T(8,128)(2,1)}, bf16[512,1024]{1,0:T(8,128)(2,1)}, u32[]{:S(2)}, u32[]{:S(2)}) collective-permute-start(bf16[512,1024]{1,0:T(8,128)(2,1)} %all-gather.13.cloned.1.call-done.refs_0_), channel_id=1, source_target_pairs={{0,8},{8,0},{16,24},{24,16},{1,9},{9,1},{17,25},{25,17},{2,10},{10... | collective-permute-start | bytes 3145736 | tf_op jit(solution)/shard_map/ppermute | solution.py:353
  235.6 39.9 %collective-permute-start.21 = (bf16[512,2048]{1,0:T(8,128)(2,1)S(1)}, bf16[512,2048]{1,0:T(8,128)(2,1)}, u32[]{:S(2)}, u32[]{:S(2)}) collective-permute-start(bf16[512,2048]{1,0:T(8,128)(2,1)S(1)} %get-tuple-element.113), channel_id=1, source_target_pairs={{0,8},{8,0},{16,24},{24,16},{1,9},{9,1},{17,25},{25,17},{2,10},{10... | collective-permute-start | bytes 6291464 | tf_op jit(solution)/shard_map/ppermute | solution.py:353
  280.2 25.5 %collective-permute-start.33 = (bf16[512,1024]{1,0:T(8,128)(2,1)S(1)}, bf16[512,1024]{1,0:T(8,128)(2,1)S(1)}, u32[]{:S(2)}, u32[]{:S(2)}) collective-permute-start(bf16[512,1024]{1,0:T(8,128)(2,1)S(1)} %add_convert_fusion.15), channel_id=1, source_target_pairs={{0,4},{4,0},{1,5},{5,1},{2,6},{6,2},{3,7},{7,3},{8,12},{12,8},{9,1... | collective-permute-start | bytes 3145736 | tf_op jit(solution)/shard_map/ppermute | solution.py:359
  369.4 72.3 %all-gather.19.cloned.1.call-start = ((), (), s32[]{:S(2)}) async-start(), calls=%async_computation.12 | async-start | bytes 1310720 | tf_op jit(solution)/shard_map/all_gather | solution.py:579
  414.3 57.1 %all-gather.21.cloned.1.call-start = ((), (), s32[]{:S(2)}) async-start(), calls=%async_computation.13 | async-start | bytes 1310720 | tf_op jit(solution)/shard_map/all_gather | solution.py:579
  415.1 204.2 %all-gather.17.cloned.1.call-start = ((), (), s32[]{:S(2)}) async-start(), calls=%async_computation.11 | async-start | bytes 2621440 | tf_op jit(solution)/shard_map/all_gather | solution.py:612
  441.7 29.7 %collective-permute-start.39 = (bf16[512,1024]{1,0:T(8,128)(2,1)}, bf16[512,1024]{1,0:T(8,128)(2,1)}, u32[]{:S(2)}, u32[]{:S(2)}) collective-permute-start(bf16[512,1024]{1,0:T(8,128)(2,1)} %all-gather.19.cloned.1.call-done.refs_0_), channel_id=1, source_target_pairs={{0,16},{8,24},{16,0},{24,8},{1,17},{9,25},{17,1},{25,9},{2,18},{10... | collective-permute-start | bytes 3145736 | tf_op jit(solution)/shard_map/ppermute | solution.py:356
  443.2 28.2 %collective-permute-start.40 = (bf16[512,1024]{1,0:T(8,128)(2,1)}, bf16[512,1024]{1,0:T(8,128)(2,1)S(1)}, u32[]{:S(2)}, u32[]{:S(2)}) collective-permute-start(bf16[512,1024]{1,0:T(8,128)(2,1)} %all-gather.19.cloned.1.call-done.refs_0_), channel_id=1, source_target_pairs={{0,4},{4,0},{1,5},{5,1},{2,6},{6,2},{3,7},{7,3},{8,12},{12,8},{9,1... | collective-permute-start | bytes 3145736 | tf_op jit(solution)/shard_map/ppermute | solution.py:359
  444.6 28.9 %collective-permute-start.41 = (bf16[512,1024]{1,0:T(8,128)(2,1)}, bf16[512,1024]{1,0:T(8,128)(2,1)}, u32[]{:S(2)}, u32[]{:S(2)}) collective-permute-start(bf16[512,1024]{1,0:T(8,128)(2,1)} %all-gather.19.cloned.1.call-done.refs_0_), channel_id=1, source_target_pairs={{0,8},{8,0},{16,24},{24,16},{1,9},{9,1},{17,25},{25,17},{2,10},{10... | collective-permute-start | bytes 3145736 | tf_op jit(solution)/shard_map/ppermute | solution.py:353
  472.0 27.9 %collective-permute-start.46 = (bf16[512,1024]{1,0:T(8,128)(2,1)}, bf16[512,1024]{1,0:T(8,128)(2,1)S(1)}, u32[]{:S(2)}, u32[]{:S(2)}) collective-permute-start(bf16[512,1024]{1,0:T(8,128)(2,1)} %all-gather.21.cloned.1.call-done.refs_1_), channel_id=1, source_target_pairs={{0,16},{8,24},{16,0},{24,8},{1,17},{9,25},{17,1},{25,9},{2,18},{10... | collective-permute-start | bytes 3145736 | tf_op jit(solution)/shard_map/ppermute | solution.py:356
  473.5 26.4 %collective-permute-start.47 = (bf16[512,1024]{1,0:T(8,128)(2,1)}, bf16[512,1024]{1,0:T(8,128)(2,1)S(1)}, u32[]{:S(2)}, u32[]{:S(2)}) collective-permute-start(bf16[512,1024]{1,0:T(8,128)(2,1)} %all-gather.21.cloned.1.call-done.refs_1_), channel_id=1, source_target_pairs={{0,4},{4,0},{1,5},{5,1},{2,6},{6,2},{3,7},{7,3},{8,12},{12,8},{9,1... | collective-permute-start | bytes 3145736 | tf_op jit(solution)/shard_map/ppermute | solution.py:359
  501.6 42.9 %collective-permute-start.45 = (bf16[512,2048]{1,0:T(8,128)(2,1)S(1)}, bf16[512,2048]{1,0:T(8,128)(2,1)}, u32[]{:S(2)}, u32[]{:S(2)}) collective-permute-start(bf16[512,2048]{1,0:T(8,128)(2,1)S(1)} %get-tuple-element.156), channel_id=1, source_target_pairs={{0,8},{8,0},{16,24},{24,16},{1,9},{9,1},{17,25},{25,17},{2,10},{10... | collective-permute-start | bytes 6291464 | tf_op jit(solution)/shard_map/ppermute | solution.py:353
  574.5 113.1 %reduce-scatter.6.cloned.1.call-start = ((), (), s32[]{:S(2)}) async-start(), calls=%async_computation.14 | async-start | bytes 2621440 | tf_op jit(solution)/shard_map/reduce_scatter | solution.py:591
  698.7 32.0 %collective-permute-start.72 = (bf16[128,2048]{1,0:T(8,128)(2,1)S(1)}, bf16[128,2048]{1,0:T(8,128)(2,1)S(1)}, u32[]{:S(2)}, u32[]{:S(2)}) collective-permute-start(bf16[128,2048]{1,0:T(8,128)(2,1)S(1)} %get-tuple-element.247), channel_id=1, source_target_pairs={{0,1},{1,2},{2,3},{4,5},{5,6},{6,7},{8,9},{9,10},{10,11},{12,13},{... | collective-permute-start | bytes 1572872 | tf_op jit(solution)/shard_map/ppermute | solution.py:337
  707.7 28.6 %all-to-all-start.2 = ((bf16[128,4,512]{2,0,1:T(8,128)(2,1)}), bf16[128,4,512]{2,0,1:T(8,128)(2,1)S(1)}, u32[]{:S(2)}, u32[]{:S(2)}) async-start(bf16[128,4,512]{2,0,1:T(8,128)(2,1)} %bitcast.192), calls=%async_computation.4 | async-start | bytes 1048576 | tf_op jit(solution)/shard_map/all_to_all | solution.py:654
  711.2 126.6 %reduce-scatter.8.cloned.1.call-start = ((), (), s32[]{:S(2)}) async-start(), calls=%async_computation.15 | async-start | bytes 2621440 | tf_op jit(solution)/shard_map/reduce_scatter | solution.py:684
  711.3 65.3 %collective-permute-start.73 = (bf16[128,2048]{1,0:T(8,128)(2,1)S(1)}, bf16[128,2048]{1,0:T(8,128)(2,1)}, u32[]{:S(2)}, u32[]{:S(2)}) collective-permute-start(bf16[128,2048]{1,0:T(8,128)(2,1)S(1)} %get-tuple-element.247), channel_id=1, source_target_pairs={{1,0},{2,1},{3,2},{5,4},{6,5},{7,6},{9,8},{10,9},{11,10},{13,12},{... | collective-permute-start | bytes 1572872 | tf_op jit(solution)/shard_map/ppermute | solution.py:337
  712.6 65.9 %collective-permute-start.74 = (bf16[128,2048]{1,0:T(8,128)(2,1)S(1)}, bf16[128,2048]{1,0:T(8,128)(2,1)}, u32[]{:S(2)}, u32[]{:S(2)}) collective-permute-start(bf16[128,2048]{1,0:T(8,128)(2,1)S(1)} %get-tuple-element.247), channel_id=1, source_target_pairs={{2,0},{3,1},{6,4},{7,5},{10,8},{11,9},{14,12},{15,13},{18,16},{19,... | collective-permute-start | bytes 1572872 | tf_op jit(solution)/shard_map/ppermute | solution.py:337
  713.9 66.5 %collective-permute-start.75 = (bf16[128,2048]{1,0:T(8,128)(2,1)S(1)}, bf16[128,2048]{1,0:T(8,128)(2,1)}, u32[]{:S(2)}, u32[]{:S(2)}) collective-permute-start(bf16[128,2048]{1,0:T(8,128)(2,1)S(1)} %get-tuple-element.247), channel_id=1, source_target_pairs={{3,0},{7,4},{11,8},{15,12},{19,16},{23,20},{27,24},{31,28}} | collective-permute-start | bytes 1572872 | tf_op jit(solution)/shard_map/ppermute | solution.py:337
  775.5 112.8 %all-gather.23.cloned.1.call-start = ((), (), s32[]{:S(2)}) async-start(), calls=%async_computation.16 | async-start | bytes 2621440 | tf_op jit(solution)/shard_map/all_gather | solution.py:693
  807.2 43.7 %collective-permute-start.83 = (bf16[256,1024]{0,1:T(8,128)(2,1)}, bf16[256,1024]{0,1:T(8,128)(2,1)}, u32[]{:S(2)}, u32[]{:S(2)}) collective-permute-start(bf16[256,1024]{0,1:T(8,128)(2,1)} %get-tuple-element.286), channel_id=1, source_target_pairs={{0,4},{4,0},{1,5},{5,1},{2,6},{6,2},{3,7},{7,3},{8,12},{12,8},{9,1... | collective-permute-start | bytes 1572872 | tf_op jit(solution)/shard_map/ppermute | solution.py:359
  808.5 45.6 %collective-permute-start.81 = (bf16[256,1024]{0,1:T(8,128)(2,1)}, bf16[256,1024]{0,1:T(8,128)(2,1)}, u32[]{:S(2)}, u32[]{:S(2)}) collective-permute-start(bf16[256,1024]{0,1:T(8,128)(2,1)} %get-tuple-element.285), channel_id=1, source_target_pairs={{0,16},{8,24},{16,0},{24,8},{1,17},{9,25},{17,1},{25,9},{2,18},{10... | collective-permute-start | bytes 1572872 | tf_op jit(solution)/shard_map/ppermute | solution.py:356
  845.8 26.9 %collective-permute-start.78 = (bf16[256,1024]{0,1:T(8,128)(2,1)}, bf16[256,1024]{0,1:T(8,128)(2,1)S(1)}, u32[]{:S(2)}, u32[]{:S(2)}) collective-permute-start(bf16[256,1024]{0,1:T(8,128)(2,1)} %slice.488), channel_id=1, source_target_pairs={{0,16},{8,24},{16,0},{24,8},{1,17},{9,25},{17,1},{25,9},{2,18},{10... | collective-permute-start | bytes 1572872 | tf_op jit(solution)/shard_map/ppermute | solution.py:356
  (152 other events, 1852.9 us)
Sparse Core Ops, SparseCore 0:
  10.5 49.4 all-gather.8
  62.4 70.8 all-gather.10
  145.1 27.3 all-gather.12
  174.5 27.4 all-gather.14
  369.5 41.6 reduce-scatter.3
  414.4 27.2 all-gather.18
  443.9 27.4 all-gather.20
  574.7 44.5 all-gather.16
  643.4 42.2 reduce-scatter.5
  775.6 62.1 reduce-scatter.7
  842.2 46.0 all-gather.22

commit v7 on v6

--- a/solution.py
+++ b/solution.py
@@ -565,6 +565,7 @@
     )
     begin = tp_index * part
     own = lambda a: lax.dynamic_slice_in_dim(a, begin, part, 0)
+    attended_low, table, place = lax.optimization_barrier((attended_low, table, place))
     attended_own = lax.all_to_all(
         attended_low, "tp", split_axis=0, concat_axis=1, tiled=True
     )
@@ -593,7 +594,7 @@
     teacher_own = own(teacher.reshape(tokens, width)).astype(wide)
     valid_own = own(row_valid)
     grad_scale = (2.0 * loss_scale / valid_count * valid_own)[:, None]
-    second_own, table, place = lax.optimization_barrier((normed_own[:, cols[1]], table, place))
+    second_own = normed_own[:, cols[1]]
     first_block, second_block = spread(normed_own[:, cols[0]], second_own)
     second_block, w_up = lax.optimization_barrier((second_block, w_up))
     near_weights = on_chip(w_up, w_down)
@@ -673,8 +674,9 @@
         coming = lax.ppermute(grad[:, slot_count:].astype(low), "ctx", mirror)
         return added(grad[:, :slot_count], coming).reshape(tokens, heads_local, head_dim)
 
+    branch_block = lax.all_gather(grad_branch, "tp", axis=0, tiled=True)
     grad_v, own_key = returned(grad_value), returned(grad_key)
-    branch_block = line_gather(grad_branch)
+    grad_v, branch_block = lax.optimization_barrier((grad_v, branch_block))
     grad_w_out = jnp.einsum("nd,nf->df", branch_block, attended_low, preferred_element_type=wide)
     grad_q, grad_q_gain = query_back(grad_query.reshape(tokens, heads_local, head_dim))
     grad_k, grad_k_gain = key_back(own_key)

time: 913 us -> 877 us (0.961)
  waiting for transfers between devices: 404 us -> 369 us
  starting transfers between devices: 92.3 us -> 80.5 us
    ppermute x1, waiting for transfers between devices: 23.4 us -> 7.48 us  [per_device(): other_key = lax.ppermute(key_low, 'ctx', mirror)]
    reduce_scatter x1, waiting for transfers between devices: 27.5 us -> 13.6 us  [per_device(): lax.psum_scatter(nt_dot(grad_proj_low, full_qkv).astype(low), 'tp', scatt...]
    ppermute x12 -> x6, starting transfers between devices: 26.9 us -> 14.6 us  [line_gather(): lax.ppermute(shard, 'tp', [(i, i + d) for i in range(size) if 0 <= i + d...]
    ppermute x12 -> x6, waiting for transfers between devices: 33.6 us -> 21.9 us  [line_gather(): lax.ppermute(shard, 'tp', [(i, i + d) for i in range(size) if 0 <= i + d...]
    unnamed x194 -> x202, local copies, waits for them, and re-layouts: 22.8 us -> 19.3 us
  transfers between devices with their start and end apart: 100 -> 95, of which waited for: 55 -> 52; matrix products, arithmetic and copies ran while one was open for 22% -> 22% of each run, Pallas kernels for 16% -> 17%
where the time goes in v7:
time: 877 us; the launch traced here: 866 us
  waiting for transfers between devices  369 us (42%)
  Pallas kernels  147 us (17%)
  local copies, waits for them, and re-layouts  86.3 us (10%)
  matrix products  85.9 us (10%)
  starting transfers between devices  80.5 us (9%)
  other arithmetic  76.8 us (9%)
  between operations  20.5 us (2%)
    pallas_call x8, Pallas kernels, expert_call(): pl.pallas_call(body, grid=(experts,), in_specs=in_specs + [pl.BlockSpec(m...  138 us
    all_gather x4, waiting for transfers between devices, spread(): lax.all_gather(half.astype(low), 'tp', axis=0, tiled=True)  92.2 us
    ppermute x16, waiting for transfers between devices, along_x(): return lax.ppermute(a, 'fsdp', [(i, i ^ 2) for i in range(self.fsdp)])  80.2 us
    reduce_scatter x2, waiting for transfers between devices, finish(): lax.psum_scatter(half, 'tp', scatter_dimension=0, tiled=True).astype(wide)  39.6 us
    reshape x1, local copies, waits for them, and re-layouts, per_device(): grad_up.reshape(shard_experts, width, 2, hidden_local)  25.1 us
    ppermute x17, waiting for transfers between devices, along_y(): return lax.ppermute(a, 'ctx', [(i, i ^ 1) for i in range(self.ctx)])  24.3 us
    ppermute x6, waiting for transfers between devices, line_gather(): lax.ppermute(shard, 'tp', [(i, i + d) for i in range(size) if 0 <= i + d...  21.9 us
    ppermute x17, starting transfers between devices, along_y(): return lax.ppermute(a, 'ctx', [(i, i ^ 1) for i in range(self.ctx)])  21 us
  transfers between devices with their start and end apart: 95, of which 52 were waited for; matrix products, arithmetic and copies ran while one was open for 22% of the time, Pallas kernels for 17%

profile of v7, /device:TPU:0, one launch (start us, length us, event | category | flops | bytes accessed | tf_op | source)
XLA Modules:
  0.0 865.8 jit_solution(10631003803733496780)
XLA Ops:
  33.6 12.8 %collective-permute-done.13 = bf16[512,256]{1,0:T(8,128)(2,1)S(1)} collective-permute-done((bf16[512,256]{1,0:T(8,128)(2,1)S(1)}, bf16[512,256]{1,0:T(8,128)(2,1)S(1)}, u32[]{:S(2)}, u32[]{:S(2)}) %collective-permute-start.13) | collective-permute-done | bytes 262176 | tf_op jit(solution)/shard_map/ppermute | solution.py:337
  69.1 7.0 fusion.11
  90.2 7.5 collective-permute-done.8
  102.5 9.9 %collective-permute-done.7 = bf16[1,512,4,128]{1,3,2,0:T(8,128)(2,1)S(1)} collective-permute-done((bf16[1,512,4,128]{1,3,2,0:T(8,128)(2,1)S(1)}, bf16[1,512,4,128]{1,3,2,0:T(8,128)(2,1)S(1)}, u32[]{:S(2)}, u32[]{:S(2)}) %collective-permute-start.7) | collective-permute-done | bytes 524320 | tf_op jit(solution)/shard_map/ppermute | solution.py:550
  123.8 11.6 %all-to-all-done.1 = bf16[4,128,512]{2,1,0:T(8,128)(2,1)S(1)} async-done(((bf16[4,128,512]{2,1,0:T(8,128)(2,1)}), bf16[4,128,512]{2,1,0:T(8,128)(2,1)S(1)}, u32[]{:S(2)}, u32[]{:S(2)}) %all-to-all-start.1) | async-done | bytes 524320 | tf_op jit(solution)/shard_map/all_to_all | solution.py:569
  143.4 26.4 %all-gather.14.cloned.1.call-done.refs_0_ = bf16[512,1024]{1,0:T(8,128)(2,1)} async-done(((bf16[128,1024]{1,0:T(8,128)(2,1)}), bf16[512,1024]{1,0:T(8,128)(2,1)}) %all-gather.14.cloned.1.call-update) | async-done | bytes 1048592 | tf_op jit(solution)/shard_map/all_gather | solution.py:580
  172.8 14.1 %reshape.366.refs_0_ = bf16[4,2048,512]{2,1,0:T(8,128)(2,1)} reshape(bf16[4,2048,2,256]{3,2,1,0:T(2,128)(2,1)} %param.20) | data formatting | bytes 16777216 | tf_op jit(solution)/shard_map/reshape | solution.py:520
  186.9 12.4 %all-gather.16.cloned.1.call-done.refs_1_ = bf16[512,1024]{1,0:T(8,128)(2,1)} async-done(((bf16[128,1024]{1,0:T(8,128)(2,1)}), bf16[512,1024]{1,0:T(8,128)(2,1)}) %all-gather.16.cloned.1.call-update) | async-done | bytes 1048592 | tf_op jit(solution)/shard_map/all_gather | solution.py:580
  212.3 15.9 %shard_map.187 = (bf16[512,2048]{1,0:T(8,128)(2,1)S(1)}, bf16[512,2048]{1,0:T(8,128)(2,1)S(1)}, bf16[4,8,160,2048]{3,2,1,0:T(8,128)(2,1)}, f32[4,8,160,512]{3,2,1,0:T(8,128)}, bf16[4,8,160,256]{3,2,1,0:T(8,128)(2,1)}) custom-call(bf16[512,1024]{1,0:T(8,128)(2,1)S(1)} %copy-done.6, bf16[512,1024]{1,0:T(8,128)(2,1)S(1)} %copy-done.7, ...), custom_call_target="tpu_custom_call" | custom-call | flops 9395240960 | bytes 17563648 | tf_op jit(solution)/shard_map/pallas_call | solution.py:268
  233.1 17.0 %shard_map.188 = (bf16[512,2048]{1,0:T(8,128)(2,1)S(1)}, bf16[512,2048]{1,0:T(8,128)(2,1)}, bf16[4,8,160,2048]{3,2,1,0:T(8,128)(2,1)}, f32[4,8,160,512]{3,2,1,0:T(8,128)}, bf16[4,8,160,256]{3,2,1,0:T(8,128)(2,1)}) custom-call(bf16[512,1024]{1,0:T(8,128)(2,1)} %collective-permute-done.15.refs_0_, ...), custom_call_target="tpu_custom_call", output_to_operand_aliasing={{2}: (8, {}), {3}: (9, {}), {4}: (10, {})} | custom-call | flops 9395240960 | bytes 17563648 | tf_op jit(solution)/shard_map/pallas_call | solution.py:268
  257.2 15.6 %shard_map.189 = (bf16[512,2048]{1,0:T(8,128)(2,1)S(1)}, bf16[512,2048]{1,0:T(8,128)(2,1)S(1)}, bf16[4,8,160,2048]{3,2,1,0:T(8,128)(2,1)}, f32[4,8,160,512]{3,2,1,0:T(8,128)}, bf16[4,8,160,256]{3,2,1,0:T(8,128)(2,1)}) custom-call(bf16[512,1024]{1,0:T(8,128)(2,1)S(1)} %collective-permute-done.16.refs_0_, ...), custom_call_target="tpu_custom_call", output_to_operand_aliasing={{2}: (8, {}), {3}: (9, {}), {4}: (10, {})} | custom-call | flops 9395240960 | bytes 17563648 | tf_op jit(solution)/shard_map/pallas_call | solution.py:268
  278.5 14.5 %shard_map.190 = (bf16[512,2048]{1,0:T(8,128)(2,1)S(1)}, bf16[512,2048]{1,0:T(8,128)(2,1)S(1)}, bf16[4,8,160,2048]{3,2,1,0:T(8,128)(2,1)}, f32[4,8,160,512]{3,2,1,0:T(8,128)}, bf16[4,8,160,256]{3,2,1,0:T(8,128)(2,1)}) custom-call(bf16[512,1024]{1,0:T(8,128)(2,1)S(1)} %collective-permute-done.28.refs_0_, ...), custom_call_target="tpu_custom_call", output_to_operand_aliasing={{2}: (8, {}), {3}: (9, {}), {4}: (10, {})} | custom-call | flops 9395240960 | bytes 17563648 | tf_op jit(solution)/shard_map/pallas_call | solution.py:268
  293.1 7.1 collective-permute-done.27
  309.5 24.0 %collective-permute-done.35 = bf16[512,1024]{1,0:T(8,128)(2,1)S(1)} collective-permute-done((bf16[512,1024]{1,0:T(8,128)(2,1)S(1)}, bf16[512,1024]{1,0:T(8,128)(2,1)S(1)}, u32[]{:S(2)}, u32[]{:S(2)}) %collective-permute-start.35) | collective-permute-done | bytes 1048608 | tf_op jit(solution)/shard_map/ppermute | solution.py:356
  338.5 21.3 %collective-permute-done.38 = bf16[512,1024]{1,0:T(8,128)(2,1)S(1)} collective-permute-done((bf16[512,1024]{1,0:T(8,128)(2,1)S(1)}, bf16[512,1024]{1,0:T(8,128)(2,1)S(1)}, u32[]{:S(2)}, u32[]{:S(2)}) %collective-permute-start.38) | collective-permute-done | bytes 1048608 | tf_op jit(solution)/shard_map/ppermute | solution.py:356
  369.0 39.6 %reduce-scatter.4.cloned.1.call-done = bf16[128,2048]{1,0:T(8,128)(2,1)} async-done(((bf16[512,2048]{1,0:T(8,128)(2,1)}), bf16[128,2048]{1,0:T(8,128)(2,1)}) %reduce-scatter.4.cloned.1.call-update) | async-done | bytes 524304 | tf_op jit(solution)/shard_map/reduce_scatter | solution.py:592
  412.5 26.6 %all-gather.20.cloned.1.call-done.refs_0_ = bf16[512,1024]{1,0:T(8,128)(2,1)} async-done(((bf16[128,1024]{1,0:T(8,128)(2,1)}), bf16[512,1024]{1,0:T(8,128)(2,1)}) %all-gather.20.cloned.1.call-update) | async-done | bytes 1048592 | tf_op jit(solution)/shard_map/all_gather | solution.py:580
  442.1 26.7 %all-gather.22.cloned.1.call-done.refs_1_ = bf16[512,1024]{1,0:T(8,128)(2,1)} async-done(((bf16[128,1024]{1,0:T(8,128)(2,1)}), bf16[512,1024]{1,0:T(8,128)(2,1)}) %all-gather.22.cloned.1.call-update) | async-done | bytes 1048592 | tf_op jit(solution)/shard_map/all_gather | solution.py:580
  477.0 19.0 %shard_map.192 = (bf16[512,2048]{1,0:T(8,128)(2,1)S(1)}, bf16[512,2048]{1,0:T(8,128)(2,1)S(1)}, bf16[4,8,160,2048]{3,2,1,0:T(8,128)(2,1)}, bf16[4,8,160,512]{3,2,1,0:T(8,128)(2,1)}) custom-call(bf16[512,1024]{1,0:T(8,128)(2,1)S(1)} %copy-done.8, bf16[512,1024]{1,0:T(8,128)(2,1)S(1)} %copy-done.9, bf16[512,1024]{1,0:T(8,128)(2,1)} %collective-permute-done.41.refs_2_, ...), custom_call_target="tpu_custom_call" | custom-call | flops 9395240960 | bytes 17563648 | tf_op jit(solution)/shard_map/pallas_call | solution.py:268
  500.0 18.7 %shard_map.193 = (bf16[512,2048]{1,0:T(8,128)(2,1)S(1)}, bf16[512,2048]{1,0:T(8,128)(2,1)S(1)}, bf16[4,8,160,2048]{3,2,1,0:T(8,128)(2,1)}, bf16[4,8,160,512]{3,2,1,0:T(8,128)(2,1)}) custom-call(bf16[512,1024]{1,0:T(8,128)(2,1)} %collective-permute-done.39.refs_0_, ...), custom_call_target="tpu_custom_call", output_to_operand_aliasing={{2}: (9, {}), {3}: (10, {})} | custom-call | flops 9395240960 | bytes 17563648 | tf_op jit(solution)/shard_map/pallas_call | solution.py:268
  523.7 18.1 %shard_map.194 = (bf16[512,2048]{1,0:T(8,128)(2,1)S(1)}, bf16[512,2048]{1,0:T(8,128)(2,1)S(1)}, bf16[4,8,160,2048]{3,2,1,0:T(8,128)(2,1)}, bf16[4,8,160,512]{3,2,1,0:T(8,128)(2,1)}) custom-call(bf16[512,1024]{1,0:T(8,128)(2,1)S(1)} %collective-permute-done.40.refs_0_, ...), custom_call_target="tpu_custom_call", output_to_operand_aliasing={{2}: (9, {}), {3}: (10, {})} | custom-call | flops 9395240960 | bytes 17563648 | tf_op jit(solution)/shard_map/pallas_call | solution.py:268
  547.8 18.8 %shard_map.195 = (bf16[512,2048]{1,0:T(8,128)(2,1)S(1)}, bf16[512,2048]{1,0:T(8,128)(2,1)}, bf16[4,8,160,2048]{3,2,1,0:T(8,128)(2,1)}, bf16[4,8,160,512]{3,2,1,0:T(8,128)(2,1)}) custom-call(bf16[512,1024]{1,0:T(8,128)(2,1)S(1)} %collective-permute-done.52.refs_0_, ...), custom_call_target="tpu_custom_call", output_to_operand_aliasing={{2}: (9, {}), {3}: (10, {})} | custom-call | flops 9395240960 | bytes 17563648 | tf_op jit(solution)/shard_map/pallas_call | solution.py:268
  581.0 15.7 %convolution_bitcast_fusion = f32[4,256,2048]{2,1,0:T(8,128)} fusion(bf16[4,8,160,256]{3,2,1,0:T(8,128)(2,1)S(1)} %copy-done.17, bf16[4,8,160,2048]{3,2,1,0:T(8,128)(2,1)} %get-tuple-element.184), kind=kOutput, calls=%fused_computation.25 | convolution fusion | flops 5368709120 | bytes 31981568 | tf_op jit(solution)/shard_map/ebcf,ebcd->efd/dot_general | solution.py:629
  596.7 7.6 collective-permute-done.59
  616.7 15.2 %collective-permute-done.62 = bf16[512,1024]{1,0:T(8,128)(2,1)S(1)} collective-permute-done((bf16[512,1024]{1,0:T(8,128)(2,1)}, bf16[512,1024]{1,0:T(8,128)(2,1)S(1)}, u32[]{:S(2)}, u32[]{:S(2)}) %collective-permute-start.62) | collective-permute-done | bytes 1048608 | tf_op jit(solution)/shard_map/ppermute | solution.py:356
  640.7 19.5 %fusion.84 = f32[4,2048,512,1]{1,2,3,0:T(8,128)} fusion(bf16[4,8,160,2048]{3,2,1,0:T(8,128)(2,1)} %get-tuple-element.187, bf16[4,8,160,512]{3,2,1,0:T(8,128)(2,1)} %get-tuple-element.188), kind=kOutput, calls=%fused_computation.254 | convolution fusion | flops 10737418240 | bytes 42991616 | tf_op jit(solution)/shard_map/ebcd,ebcf->edf/dot_general | solution.py:632
  660.2 25.1 %copy.136 = f32[4,2048,2,256]{3,2,1,0:T(2,128)} copy(f32[4,2048,2,256]{1,3,2,0:T(8,128)} %bitcast.199) | data formatting | bytes 33554432 | tf_op jit(solution)/shard_map/reshape | solution.py:646
  701.4 12.2 %all-to-all-done.2 = bf16[128,4,512]{2,0,1:T(8,128)(2,1)S(1)} async-done(((bf16[128,4,512]{2,0,1:T(8,128)(2,1)}), bf16[128,4,512]{2,0,1:T(8,128)(2,1)S(1)}, u32[]{:S(2)}, u32[]{:S(2)}) %all-to-all-start.2) | async-done | bytes 524320 | tf_op jit(solution)/shard_map/all_to_all | solution.py:655
  733.1 8.0 collective-permute-done.63
  750.2 7.4 convolution_convert_fusion.2
  786.8 13.6 %reduce-scatter.8.cloned.1.call-done = bf16[128,2048]{1,0:T(8,128)(2,1)} async-done(((bf16[512,2048]{1,0:T(8,128)(2,1)}), bf16[128,2048]{1,0:T(8,128)(2,1)}) %reduce-scatter.8.cloned.1.call-update) | async-done | bytes 524304 | tf_op jit(solution)/shard_map/reduce_scatter | solution.py:686
  820.9 12.9 %collective-permute-done.66 = f32[1,4353]{1,0:T(1,128)S(1)} collective-permute-done((f32[1,4353]{1,0:T(1,128)S(1)}, f32[1,4353]{1,0:T(1,128)S(1)}, u32[]{:S(2)}, u32[]{:S(2)}) %collective-permute-start.66) | collective-permute-done | bytes 17444 | tf_op jit(solution)/shard_map/ppermute | solution.py:328
  (529 shorter events, 323.4 us)
Async XLA Ops:
  7.2 61.9 %all-gather.10.cloned.1.call-start = ((), (), s32[]{:S(2)}) async-start(), calls=%async_computation.6 | async-start | bytes 7077888 | tf_op jit(solution)/shard_map/all_gather | solution.py:531
  9.6 126.2 %all-gather.12.cloned.1.call-start = ((), (), s32[]{:S(2)}) async-start(), calls=%async_computation.7 | async-start | bytes 9437184 | tf_op jit(solution)/shard_map/all_gather | solution.py:535
  121.0 48.8 %all-gather.14.cloned.1.call-start = ((), (), s32[]{:S(2)}) async-start(), calls=%async_computation.8 | async-start | bytes 1310720 | tf_op jit(solution)/shard_map/all_gather | solution.py:580
  142.8 56.5 %all-gather.16.cloned.1.call-start = ((), (), s32[]{:S(2)}) async-start(), calls=%async_computation.9 | async-start | bytes 1310720 | tf_op jit(solution)/shard_map/all_gather | solution.py:580
  143.4 265.2 %reduce-scatter.4.cloned.1.call-start = ((), (), s32[]{:S(2)}) async-start(), calls=%async_computation.10 | async-start | bytes 2621440 | tf_op jit(solution)/shard_map/reduce_scatter | solution.py:592
  169.8 29.5 %collective-permute-start.15 = (bf16[512,1024]{1,0:T(8,128)(2,1)}, bf16[512,1024]{1,0:T(8,128)(2,1)}, u32[]{:S(2)}, u32[]{:S(2)}) collective-permute-start(bf16[512,1024]{1,0:T(8,128)(2,1)} %all-gather.14.cloned.1.call-done.refs_0_), channel_id=1, source_target_pairs={{0,16},{8,24},{16,0},{24,8},{1,17},{9,25},{17,1},{25,9},{2,18},{10... | collective-permute-start | bytes 3145736 | tf_op jit(solution)/shard_map/ppermute | solution.py:356
  171.3 28.0 %collective-permute-start.16 = (bf16[512,1024]{1,0:T(8,128)(2,1)}, bf16[512,1024]{1,0:T(8,128)(2,1)S(1)}, u32[]{:S(2)}, u32[]{:S(2)}) collective-permute-start(bf16[512,1024]{1,0:T(8,128)(2,1)} %all-gather.14.cloned.1.call-done.refs_0_), channel_id=1, source_target_pairs={{0,4},{4,0},{1,5},{5,1},{2,6},{6,2},{3,7},{7,3},{8,12},{12,8},{9,1... | collective-permute-start | bytes 3145736 | tf_op jit(solution)/shard_map/ppermute | solution.py:359
  172.8 32.4 %collective-permute-start.17 = (bf16[512,1024]{1,0:T(8,128)(2,1)}, bf16[512,1024]{1,0:T(8,128)(2,1)}, u32[]{:S(2)}, u32[]{:S(2)}) collective-permute-start(bf16[512,1024]{1,0:T(8,128)(2,1)} %all-gather.14.cloned.1.call-done.refs_0_), channel_id=1, source_target_pairs={{0,8},{8,0},{16,24},{24,16},{1,9},{9,1},{17,25},{25,17},{2,10},{10... | collective-permute-start | bytes 3145736 | tf_op jit(solution)/shard_map/ppermute | solution.py:353
  203.7 25.5 %collective-permute-start.22 = (bf16[512,1024]{1,0:T(8,128)(2,1)S(1)}, bf16[512,1024]{1,0:T(8,128)(2,1)S(1)}, u32[]{:S(2)}, u32[]{:S(2)}) collective-permute-start(bf16[512,1024]{1,0:T(8,128)(2,1)S(1)} %copy-done.7), channel_id=1, source_target_pairs={{0,16},{8,24},{16,0},{24,8},{1,17},{9,25},{17,1},{25,9},{2,18},{10... | collective-permute-start | bytes 3145736 | tf_op jit(solution)/shard_map/ppermute | solution.py:356
  230.9 25.3 %collective-permute-start.28 = (bf16[512,1024]{1,0:T(8,128)(2,1)}, bf16[512,1024]{1,0:T(8,128)(2,1)S(1)}, u32[]{:S(2)}, u32[]{:S(2)}) collective-permute-start(bf16[512,1024]{1,0:T(8,128)(2,1)} %collective-permute-done.15.refs_0_), channel_id=1, source_target_pairs={{0,4},{4,0},{1,5},{5,1},{2,6},{6,2},{3,7},{7,3},{8,12},{12,8},{9,1... | collective-permute-start | bytes 3145736 | tf_op jit(solution)/shard_map/ppermute | solution.py:359
  233.0 39.9 %collective-permute-start.21 = (bf16[512,2048]{1,0:T(8,128)(2,1)S(1)}, bf16[512,2048]{1,0:T(8,128)(2,1)}, u32[]{:S(2)}, u32[]{:S(2)}) collective-permute-start(bf16[512,2048]{1,0:T(8,128)(2,1)S(1)} %get-tuple-element.115), channel_id=1, source_target_pairs={{0,8},{8,0},{16,24},{24,16},{1,9},{9,1},{17,25},{25,17},{2,10},{10... | collective-permute-start | bytes 6291464 | tf_op jit(solution)/shard_map/ppermute | solution.py:353
  277.6 25.5 %collective-permute-start.33 = (bf16[512,1024]{1,0:T(8,128)(2,1)S(1)}, bf16[512,1024]{1,0:T(8,128)(2,1)S(1)}, u32[]{:S(2)}, u32[]{:S(2)}) collective-permute-start(bf16[512,1024]{1,0:T(8,128)(2,1)S(1)} %add_convert_fusion.15), channel_id=1, source_target_pairs={{0,4},{4,0},{1,5},{5,1},{2,6},{6,2},{3,7},{7,3},{8,12},{12,8},{9,1... | collective-permute-start | bytes 3145736 | tf_op jit(solution)/shard_map/ppermute | solution.py:359
  308.3 25.3 %collective-permute-start.35 = (bf16[512,1024]{1,0:T(8,128)(2,1)S(1)}, bf16[512,1024]{1,0:T(8,128)(2,1)S(1)}, u32[]{:S(2)}, u32[]{:S(2)}) collective-permute-start(bf16[512,1024]{1,0:T(8,128)(2,1)S(1)} %get-tuple-element.278), channel_id=1, source_target_pairs={{0,16},{8,24},{16,0},{24,8},{1,17},{9,25},{17,1},{25,9},{2,18},{10... | collective-permute-start | bytes 3145736 | tf_op jit(solution)/shard_map/ppermute | solution.py:356
  366.7 72.4 %all-gather.20.cloned.1.call-start = ((), (), s32[]{:S(2)}) async-start(), calls=%async_computation.12 | async-start | bytes 1310720 | tf_op jit(solution)/shard_map/all_gather | solution.py:580
  411.7 57.1 %all-gather.22.cloned.1.call-start = ((), (), s32[]{:S(2)}) async-start(), calls=%async_computation.13 | async-start | bytes 1310720 | tf_op jit(solution)/shard_map/all_gather | solution.py:580
  412.4 204.3 %all-gather.18.cloned.1.call-start = ((), (), s32[]{:S(2)}) async-start(), calls=%async_computation.11 | async-start | bytes 2621440 | tf_op jit(solution)/shard_map/all_gather | solution.py:613
  439.1 29.7 %collective-permute-start.39 = (bf16[512,1024]{1,0:T(8,128)(2,1)}, bf16[512,1024]{1,0:T(8,128)(2,1)}, u32[]{:S(2)}, u32[]{:S(2)}) collective-permute-start(bf16[512,1024]{1,0:T(8,128)(2,1)} %all-gather.20.cloned.1.call-done.refs_0_), channel_id=1, source_target_pairs={{0,16},{8,24},{16,0},{24,8},{1,17},{9,25},{17,1},{25,9},{2,18},{10... | collective-permute-start | bytes 3145736 | tf_op jit(solution)/shard_map/ppermute | solution.py:356
  440.6 28.2 %collective-permute-start.40 = (bf16[512,1024]{1,0:T(8,128)(2,1)}, bf16[512,1024]{1,0:T(8,128)(2,1)S(1)}, u32[]{:S(2)}, u32[]{:S(2)}) collective-permute-start(bf16[512,1024]{1,0:T(8,128)(2,1)} %all-gather.20.cloned.1.call-done.refs_0_), channel_id=1, source_target_pairs={{0,4},{4,0},{1,5},{5,1},{2,6},{6,2},{3,7},{7,3},{8,12},{12,8},{9,1... | collective-permute-start | bytes 3145736 | tf_op jit(solution)/shard_map/ppermute | solution.py:359
  442.0 28.9 %collective-permute-start.41 = (bf16[512,1024]{1,0:T(8,128)(2,1)}, bf16[512,1024]{1,0:T(8,128)(2,1)}, u32[]{:S(2)}, u32[]{:S(2)}) collective-permute-start(bf16[512,1024]{1,0:T(8,128)(2,1)} %all-gather.20.cloned.1.call-done.refs_0_), channel_id=1, source_target_pairs={{0,8},{8,0},{16,24},{24,16},{1,9},{9,1},{17,25},{25,17},{2,10},{10... | collective-permute-start | bytes 3145736 | tf_op jit(solution)/shard_map/ppermute | solution.py:353
  469.4 27.9 %collective-permute-start.46 = (bf16[512,1024]{1,0:T(8,128)(2,1)}, bf16[512,1024]{1,0:T(8,128)(2,1)S(1)}, u32[]{:S(2)}, u32[]{:S(2)}) collective-permute-start(bf16[512,1024]{1,0:T(8,128)(2,1)} %all-gather.22.cloned.1.call-done.refs_1_), channel_id=1, source_target_pairs={{0,16},{8,24},{16,0},{24,8},{1,17},{9,25},{17,1},{25,9},{2,18},{10... | collective-permute-start | bytes 3145736 | tf_op jit(solution)/shard_map/ppermute | solution.py:356
  470.9 26.4 %collective-permute-start.47 = (bf16[512,1024]{1,0:T(8,128)(2,1)}, bf16[512,1024]{1,0:T(8,128)(2,1)S(1)}, u32[]{:S(2)}, u32[]{:S(2)}) collective-permute-start(bf16[512,1024]{1,0:T(8,128)(2,1)} %all-gather.22.cloned.1.call-done.refs_1_), channel_id=1, source_target_pairs={{0,4},{4,0},{1,5},{5,1},{2,6},{6,2},{3,7},{7,3},{8,12},{12,8},{9,1... | collective-permute-start | bytes 3145736 | tf_op jit(solution)/shard_map/ppermute | solution.py:359
  497.9 25.3 %collective-permute-start.52 = (bf16[512,1024]{1,0:T(8,128)(2,1)}, bf16[512,1024]{1,0:T(8,128)(2,1)S(1)}, u32[]{:S(2)}, u32[]{:S(2)}) collective-permute-start(bf16[512,1024]{1,0:T(8,128)(2,1)} %collective-permute-done.39.refs_0_), channel_id=1, source_target_pairs={{0,4},{4,0},{1,5},{5,1},{2,6},{6,2},{3,7},{7,3},{8,12},{12,8},{9,1... | collective-permute-start | bytes 3145736 | tf_op jit(solution)/shard_map/ppermute | solution.py:359
  499.0 42.9 %collective-permute-start.45 = (bf16[512,2048]{1,0:T(8,128)(2,1)S(1)}, bf16[512,2048]{1,0:T(8,128)(2,1)}, u32[]{:S(2)}, u32[]{:S(2)}) collective-permute-start(bf16[512,2048]{1,0:T(8,128)(2,1)S(1)} %get-tuple-element.158), channel_id=1, source_target_pairs={{0,8},{8,0},{16,24},{24,16},{1,9},{9,1},{17,25},{25,17},{2,10},{10... | collective-permute-start | bytes 6291464 | tf_op jit(solution)/shard_map/ppermute | solution.py:353
  546.6 25.4 %collective-permute-start.57 = (bf16[512,1024]{1,0:T(8,128)(2,1)S(1)}, bf16[512,1024]{1,0:T(8,128)(2,1)}, u32[]{:S(2)}, u32[]{:S(2)}) collective-permute-start(bf16[512,1024]{1,0:T(8,128)(2,1)S(1)} %add_convert_fusion.7), channel_id=1, source_target_pairs={{0,4},{4,0},{1,5},{5,1},{2,6},{6,2},{3,7},{7,3},{8,12},{12,8},{9,1... | collective-permute-start | bytes 3145736 | tf_op jit(solution)/shard_map/ppermute | solution.py:359
  572.0 113.3 %reduce-scatter.6.cloned.1.call-start = ((), (), s32[]{:S(2)}) async-start(), calls=%async_computation.14 | async-start | bytes 2621440 | tf_op jit(solution)/shard_map/reduce_scatter | solution.py:592
  579.1 25.3 %collective-permute-start.59 = (bf16[512,1024]{1,0:T(8,128)(2,1)S(1)}, bf16[512,1024]{1,0:T(8,128)(2,1)S(1)}, u32[]{:S(2)}, u32[]{:S(2)}) collective-permute-start(bf16[512,1024]{1,0:T(8,128)(2,1)S(1)} %get-tuple-element.274), channel_id=1, source_target_pairs={{0,16},{8,24},{16,0},{24,8},{1,17},{9,25},{17,1},{25,9},{2,18},{10... | collective-permute-start | bytes 3145736 | tf_op jit(solution)/shard_map/ppermute | solution.py:356
  700.7 49.5 %all-gather.24.cloned.1.call-start = ((), (), s32[]{:S(2)}) async-start(), calls=%async_computation.15 | async-start | bytes 2621440 | tf_op jit(solution)/shard_map/all_gather | solution.py:677
  701.3 99.1 %reduce-scatter.8.cloned.1.call-start = ((), (), s32[]{:S(2)}) async-start(), calls=%async_computation.16 | async-start | bytes 2621440 | tf_op jit(solution)/shard_map/reduce_scatter | solution.py:686
  757.7 93.2 %all-gather.26.cloned.1.call-start = ((), (), s32[]{:S(2)}) async-start(), calls=%async_computation.17 | async-start | bytes 2621440 | tf_op jit(solution)/shard_map/all_gather | solution.py:695
  783.7 29.7 %collective-permute-start.77 = (bf16[256,1024]{0,1:T(8,128)(2,1)}, bf16[256,1024]{0,1:T(8,128)(2,1)}, u32[]{:S(2)}, u32[]{:S(2)}) collective-permute-start(bf16[256,1024]{0,1:T(8,128)(2,1)} %get-tuple-element.300), channel_id=1, source_target_pairs={{0,4},{4,0},{1,5},{5,1},{2,6},{6,2},{3,7},{7,3},{8,12},{12,8},{9,1... | collective-permute-start | bytes 1572872 | tf_op jit(solution)/shard_map/ppermute | solution.py:359
  785.1 31.6 %collective-permute-start.75 = (bf16[256,1024]{0,1:T(8,128)(2,1)}, bf16[256,1024]{0,1:T(8,128)(2,1)}, u32[]{:S(2)}, u32[]{:S(2)}) collective-permute-start(bf16[256,1024]{0,1:T(8,128)(2,1)} %get-tuple-element.299), channel_id=1, source_target_pairs={{0,16},{8,24},{16,0},{24,8},{1,17},{9,25},{17,1},{25,9},{2,18},{10... | collective-permute-start | bytes 1572872 | tf_op jit(solution)/shard_map/ppermute | solution.py:356
  808.4 26.9 %collective-permute-start.72 = (bf16[256,1024]{0,1:T(8,128)(2,1)}, bf16[256,1024]{0,1:T(8,128)(2,1)S(1)}, u32[]{:S(2)}, u32[]{:S(2)}) collective-permute-start(bf16[256,1024]{0,1:T(8,128)(2,1)} %slice.488), channel_id=1, source_target_pairs={{0,16},{8,24},{16,0},{24,8},{1,17},{9,25},{17,1},{25,9},{2,18},{10... | collective-permute-start | bytes 1572872 | tf_op jit(solution)/shard_map/ppermute | solution.py:356
  (154 other events, 1755.9 us)
Sparse Core Ops, SparseCore 0:
  10.5 49.4 all-gather.9
  62.4 72.3 all-gather.11
  142.9 26.8 all-gather.13
  171.8 27.4 all-gather.15
  366.9 41.6 reduce-scatter.3
  411.8 27.2 all-gather.19
  441.3 27.4 all-gather.21
  572.1 44.5 all-gather.17
  640.8 42.2 reduce-scatter.5
  703.4 46.2 all-gather.23
  757.8 42.5 reduce-scatter.7
  804.8 46.0 all-gather.25

commit v8 on v7

--- a/solution.py
+++ b/solution.py
@@ -243,16 +243,17 @@
     )
     row_shape = lambda last, kind: pltpu.HBM((experts, total, capacity, last), kind)
     whole = lambda shape: pl.BlockSpec(shape, lambda e: (0,) * len(shape), pipeline_mode=once)
-    in_specs = [whole(p.shape) for p in pieces] + [
+    in_specs = [pl.BlockSpec(memory_space=pltpu.VMEM)] * len(pieces) + [
         pl.BlockSpec((blocks, 1, 2, slots), lambda e: (0, e, 0, 0)),
         whole((blocks, slots, experts)),
         pl.BlockSpec(memory_space=pltpu.VMEM),
         pl.BlockSpec(memory_space=pltpu.VMEM),
     ]
-    operands = [*pieces, table, place, w_up, w_down]
+    held = [pltpu.with_memory_space_constraint(p, pltpu.VMEM) for p in pieces]
+    operands = [*held, table, place, w_up, w_down]
     n_out = blocks
-    out_specs = [whole((slots, width))] * n_out + [row_spec(width), row_spec(double)]
-    out_shape = [jax.ShapeDtypeStruct((slots, width), low)] * n_out + [row_shape(width, low)]
+    out_specs = [pl.BlockSpec(memory_space=pltpu.VMEM)] * n_out + [row_spec(width), row_spec(double)]
+    out_shape = [pltpu.VMEM((slots, width), low)] * n_out + [row_shape(width, low)]
     if backward:
         in_specs.append(row_spec(double))
         operands.append(pltpu.with_memory_space_constraint(gate_up, pltpu.HBM))
@@ -277,7 +278,7 @@
             pltpu.VMEM((blocks, slots, experts * capacity), low),
         ],
         compiler_params=pltpu.CompilerParams(
-            dimension_semantics=("arbitrary",), vmem_limit_bytes=(28 if backward else 28) << 20
+            dimension_semantics=("arbitrary",), vmem_limit_bytes=20 << 20
         ),
         cost_estimate=pl.CostEstimate(
             flops=2 * rows * width * (2 * slots + double + half),

time: 877 us -> 872 us (level)
    unnamed x202 -> x208, local copies, waits for them, and re-layouts: 19.3 us -> 19.3 us
where the time goes in v8:
time: 872 us; the launch traced here: 862 us
  waiting for transfers between devices  372 us (43%)
  Pallas kernels  146 us (17%)
  local copies, waits for them, and re-layouts  86.2 us (10%)
  matrix products  85.7 us (10%)
  starting transfers between devices  81.4 us (9%)
  other arithmetic  69.8 us (8%)
  between operations  20.6 us (2%)
    pallas_call x8, Pallas kernels, expert_call(): pl.pallas_call(body, grid=(experts,), in_specs=in_specs + [pl.BlockSpec(m...  137 us
    all_gather x4, waiting for transfers between devices, spread(): lax.all_gather(half.astype(low), 'tp', axis=0, tiled=True)  92.2 us
    ppermute x16, waiting for transfers between devices, along_x(): return lax.ppermute(a, 'fsdp', [(i, i ^ 2) for i in range(self.fsdp)])  76.3 us
    reduce_scatter x2, waiting for transfers between devices, finish(): lax.psum_scatter(half, 'tp', scatter_dimension=0, tiled=True).astype(wide)  39.6 us
    ppermute x17, waiting for transfers between devices, along_y(): return lax.ppermute(a, 'ctx', [(i, i ^ 1) for i in range(self.ctx)])  27.7 us
    reshape x1, local copies, waits for them, and re-layouts, per_device(): grad_up.reshape(shard_experts, width, 2, hidden_local)  25.1 us
    ppermute x6, waiting for transfers between devices, line_gather(): lax.ppermute(shard, 'tp', [(i, i + d) for i in range(size) if 0 <= i + d...  21.9 us
    ppermute x17, starting transfers between devices, along_y(): return lax.ppermute(a, 'ctx', [(i, i ^ 1) for i in range(self.ctx)])  21.1 us
  transfers between devices with their start and end apart: 95, of which 52 were waited for; matrix products, arithmetic and copies ran while one was open for 22% of the time, Pallas kernels for 17%

profile of v8, /device:TPU:0, one launch (start us, length us, event | category | flops | bytes accessed | tf_op | source)
XLA Modules:
  0.0 862.0 jit_solution(9308466934080178659)
XLA Ops:
  9.6 7.0 collective-permute-start.9
  33.6 12.8 %collective-permute-done.13 = bf16[512,256]{1,0:T(8,128)(2,1)S(1)} collective-permute-done((bf16[512,256]{1,0:T(8,128)(2,1)S(1)}, bf16[512,256]{1,0:T(8,128)(2,1)S(1)}, u32[]{:S(2)}, u32[]{:S(2)}) %collective-permute-start.13) | collective-permute-done | bytes 262176 | tf_op jit(solution)/shard_map/ppermute | solution.py:338
  69.0 6.9 fusion.11
  90.0 7.7 collective-permute-done.8
  102.5 9.9 %collective-permute-done.7 = bf16[1,512,4,128]{1,3,2,0:T(8,128)(2,1)S(1)} collective-permute-done((bf16[1,512,4,128]{1,3,2,0:T(8,128)(2,1)S(1)}, bf16[1,512,4,128]{1,3,2,0:T(8,128)(2,1)S(1)}, u32[]{:S(2)}, u32[]{:S(2)}) %collective-permute-start.7) | collective-permute-done | bytes 524320 | tf_op jit(solution)/shard_map/ppermute | solution.py:551
  123.8 11.6 %all-to-all-done.1 = bf16[4,128,512]{2,1,0:T(8,128)(2,1)S(1)} async-done(((bf16[4,128,512]{2,1,0:T(8,128)(2,1)}), bf16[4,128,512]{2,1,0:T(8,128)(2,1)S(1)}, u32[]{:S(2)}, u32[]{:S(2)}) %all-to-all-start.1) | async-done | bytes 524320 | tf_op jit(solution)/shard_map/all_to_all | solution.py:570
  143.5 26.4 %all-gather.14.cloned.1.call-done.refs_0_ = bf16[512,1024]{1,0:T(8,128)(2,1)} async-done(((bf16[128,1024]{1,0:T(8,128)(2,1)}), bf16[512,1024]{1,0:T(8,128)(2,1)}) %all-gather.14.cloned.1.call-update) | async-done | bytes 1048592 | tf_op jit(solution)/shard_map/all_gather | solution.py:581
  172.8 14.1 %reshape.366.refs_0_ = bf16[4,2048,512]{2,1,0:T(8,128)(2,1)} reshape(bf16[4,2048,2,256]{3,2,1,0:T(2,128)(2,1)} %param.20) | data formatting | bytes 16777216 | tf_op jit(solution)/shard_map/reshape | solution.py:521
  186.9 12.4 %all-gather.16.cloned.1.call-done.refs_1_ = bf16[512,1024]{1,0:T(8,128)(2,1)} async-done(((bf16[128,1024]{1,0:T(8,128)(2,1)}), bf16[512,1024]{1,0:T(8,128)(2,1)}) %all-gather.16.cloned.1.call-update) | async-done | bytes 1048592 | tf_op jit(solution)/shard_map/all_gather | solution.py:581
  212.3 15.9 %shard_map.187 = (bf16[512,2048]{1,0:T(8,128)(2,1)S(1)}, bf16[512,2048]{1,0:T(8,128)(2,1)S(1)}, bf16[4,8,160,2048]{3,2,1,0:T(8,128)(2,1)}, f32[4,8,160,512]{3,2,1,0:T(8,128)}, bf16[4,8,160,256]{3,2,1,0:T(8,128)(2,1)}) custom-call(bf16[512,1024]{1,0:T(8,128)(2,1)S(1)} %copy-done.6, bf16[512,1024]{1,0:T(8,128)(2,1)S(1)} %copy-done.7, ...), custom_call_target="tpu_custom_call" | custom-call | flops 9395240960 | bytes 17563648 | tf_op jit(solution)/shard_map/pallas_call | solution.py:269
  233.1 16.3 %shard_map.188 = (bf16[512,2048]{1,0:T(8,128)(2,1)S(1)}, bf16[512,2048]{1,0:T(8,128)(2,1)S(1)}, bf16[4,8,160,2048]{3,2,1,0:T(8,128)(2,1)}, f32[4,8,160,512]{3,2,1,0:T(8,128)}, bf16[4,8,160,256]{3,2,1,0:T(8,128)(2,1)}) custom-call(bf16[512,1024]{1,0:T(8,128)(2,1)} %collective-permute-done.15.refs_0_, ...), custom_call_target="tpu_custom_call", output_to_operand_aliasing={{2}: (8, {}), {3}: (9, {}), {4}: (10, {})} | custom-call | flops 9395240960 | bytes 17563648 | tf_op jit(solution)/shard_map/pallas_call | solution.py:269
  257.2 15.6 %shard_map.189 = (bf16[512,2048]{1,0:T(8,128)(2,1)S(1)}, bf16[512,2048]{1,0:T(8,128)(2,1)S(1)}, bf16[4,8,160,2048]{3,2,1,0:T(8,128)(2,1)}, f32[4,8,160,512]{3,2,1,0:T(8,128)}, bf16[4,8,160,256]{3,2,1,0:T(8,128)(2,1)}) custom-call(bf16[512,1024]{1,0:T(8,128)(2,1)S(1)} %collective-permute-done.16.refs_0_, ...), custom_call_target="tpu_custom_call", output_to_operand_aliasing={{2}: (8, {}), {3}: (9, {}), {4}: (10, {})} | custom-call | flops 9395240960 | bytes 17563648 | tf_op jit(solution)/shard_map/pallas_call | solution.py:269
  278.6 14.5 %shard_map.190 = (bf16[512,2048]{1,0:T(8,128)(2,1)S(1)}, bf16[512,2048]{1,0:T(8,128)(2,1)S(1)}, bf16[4,8,160,2048]{3,2,1,0:T(8,128)(2,1)}, f32[4,8,160,512]{3,2,1,0:T(8,128)}, bf16[4,8,160,256]{3,2,1,0:T(8,128)(2,1)}) custom-call(bf16[512,1024]{1,0:T(8,128)(2,1)S(1)} %collective-permute-done.28.refs_0_, ...), custom_call_target="tpu_custom_call", output_to_operand_aliasing={{2}: (8, {}), {3}: (9, {}), {4}: (10, {})} | custom-call | flops 9395240960 | bytes 17563648 | tf_op jit(solution)/shard_map/pallas_call | solution.py:269
  309.6 24.0 %collective-permute-done.35 = bf16[512,1024]{1,0:T(8,128)(2,1)S(1)} collective-permute-done((bf16[512,1024]{1,0:T(8,128)(2,1)S(1)}, bf16[512,1024]{1,0:T(8,128)(2,1)S(1)}, u32[]{:S(2)}, u32[]{:S(2)}) %collective-permute-start.35) | collective-permute-done | bytes 1048608 | tf_op jit(solution)/shard_map/ppermute | solution.py:357
  337.3 21.3 %collective-permute-done.38 = bf16[512,1024]{1,0:T(8,128)(2,1)S(1)} collective-permute-done((bf16[512,1024]{1,0:T(8,128)(2,1)S(1)}, bf16[512,1024]{1,0:T(8,128)(2,1)S(1)}, u32[]{:S(2)}, u32[]{:S(2)}) %collective-permute-start.38) | collective-permute-done | bytes 1048608 | tf_op jit(solution)/shard_map/ppermute | solution.py:357
  366.3 39.6 %reduce-scatter.4.cloned.1.call-done = bf16[128,2048]{1,0:T(8,128)(2,1)} async-done(((bf16[512,2048]{1,0:T(8,128)(2,1)}), bf16[128,2048]{1,0:T(8,128)(2,1)}) %reduce-scatter.4.cloned.1.call-update) | async-done | bytes 524304 | tf_op jit(solution)/shard_map/reduce_scatter | solution.py:593
  409.7 26.6 %all-gather.20.cloned.1.call-done.refs_0_ = bf16[512,1024]{1,0:T(8,128)(2,1)} async-done(((bf16[128,1024]{1,0:T(8,128)(2,1)}), bf16[512,1024]{1,0:T(8,128)(2,1)}) %all-gather.20.cloned.1.call-update) | async-done | bytes 1048592 | tf_op jit(solution)/shard_map/all_gather | solution.py:581
  439.3 26.7 %all-gather.22.cloned.1.call-done.refs_1_ = bf16[512,1024]{1,0:T(8,128)(2,1)} async-done(((bf16[128,1024]{1,0:T(8,128)(2,1)}), bf16[512,1024]{1,0:T(8,128)(2,1)}) %all-gather.22.cloned.1.call-update) | async-done | bytes 1048592 | tf_op jit(solution)/shard_map/all_gather | solution.py:581
  474.3 19.0 %shard_map.192 = (bf16[512,2048]{1,0:T(8,128)(2,1)S(1)}, bf16[512,2048]{1,0:T(8,128)(2,1)S(1)}, bf16[4,8,160,2048]{3,2,1,0:T(8,128)(2,1)}, bf16[4,8,160,512]{3,2,1,0:T(8,128)(2,1)}) custom-call(bf16[512,1024]{1,0:T(8,128)(2,1)S(1)} %copy-done.8, bf16[512,1024]{1,0:T(8,128)(2,1)S(1)} %copy-done.9, bf16[512,1024]{1,0:T(8,128)(2,1)} %collective-permute-done.41.refs_2_, ...), custom_call_target="tpu_custom_call" | custom-call | flops 9395240960 | bytes 17563648 | tf_op jit(solution)/shard_map/pallas_call | solution.py:269
  497.3 18.7 %shard_map.193 = (bf16[512,2048]{1,0:T(8,128)(2,1)S(1)}, bf16[512,2048]{1,0:T(8,128)(2,1)S(1)}, bf16[4,8,160,2048]{3,2,1,0:T(8,128)(2,1)}, bf16[4,8,160,512]{3,2,1,0:T(8,128)(2,1)}) custom-call(bf16[512,1024]{1,0:T(8,128)(2,1)} %collective-permute-done.39.refs_0_, ...), custom_call_target="tpu_custom_call", output_to_operand_aliasing={{2}: (9, {}), {3}: (10, {})} | custom-call | flops 9395240960 | bytes 17563648 | tf_op jit(solution)/shard_map/pallas_call | solution.py:269
  521.0 18.1 %shard_map.194 = (bf16[512,2048]{1,0:T(8,128)(2,1)S(1)}, bf16[512,2048]{1,0:T(8,128)(2,1)S(1)}, bf16[4,8,160,2048]{3,2,1,0:T(8,128)(2,1)}, bf16[4,8,160,512]{3,2,1,0:T(8,128)(2,1)}) custom-call(bf16[512,1024]{1,0:T(8,128)(2,1)S(1)} %collective-permute-done.40.refs_0_, ...), custom_call_target="tpu_custom_call", output_to_operand_aliasing={{2}: (9, {}), {3}: (10, {})} | custom-call | flops 9395240960 | bytes 17563648 | tf_op jit(solution)/shard_map/pallas_call | solution.py:269
  545.1 18.8 %shard_map.195 = (bf16[512,2048]{1,0:T(8,128)(2,1)S(1)}, bf16[512,2048]{1,0:T(8,128)(2,1)}, bf16[4,8,160,2048]{3,2,1,0:T(8,128)(2,1)}, bf16[4,8,160,512]{3,2,1,0:T(8,128)(2,1)}) custom-call(bf16[512,1024]{1,0:T(8,128)(2,1)S(1)} %collective-permute-done.52.refs_0_, ...), custom_call_target="tpu_custom_call", output_to_operand_aliasing={{2}: (9, {}), {3}: (10, {})} | custom-call | flops 9395240960 | bytes 17563648 | tf_op jit(solution)/shard_map/pallas_call | solution.py:269
  578.2 15.8 %convolution_bitcast_fusion = f32[4,256,2048]{2,1,0:T(8,128)} fusion(bf16[4,8,160,256]{3,2,1,0:T(8,128)(2,1)S(1)} %copy-done.17, bf16[4,8,160,2048]{3,2,1,0:T(8,128)(2,1)} %get-tuple-element.184), kind=kOutput, calls=%fused_computation.25 | convolution fusion | flops 5368709120 | bytes 31981568 | tf_op jit(solution)/shard_map/ebcf,ebcd->efd/dot_general | solution.py:630
  594.0 7.6 collective-permute-done.59
  614.0 13.9 %collective-permute-done.62 = bf16[512,1024]{1,0:T(8,128)(2,1)S(1)} collective-permute-done((bf16[512,1024]{1,0:T(8,128)(2,1)}, bf16[512,1024]{1,0:T(8,128)(2,1)S(1)}, u32[]{:S(2)}, u32[]{:S(2)}) %collective-permute-start.62) | collective-permute-done | bytes 1048608 | tf_op jit(solution)/shard_map/ppermute | solution.py:357
  636.8 19.3 %fusion.84 = f32[4,2048,512,1]{1,2,3,0:T(8,128)} fusion(bf16[4,8,160,2048]{3,2,1,0:T(8,128)(2,1)} %get-tuple-element.187, bf16[4,8,160,512]{3,2,1,0:T(8,128)(2,1)} %get-tuple-element.188), kind=kOutput, calls=%fused_computation.254 | convolution fusion | flops 10737418240 | bytes 42991616 | tf_op jit(solution)/shard_map/ebcd,ebcf->edf/dot_general | solution.py:633
  656.0 25.1 %copy.136 = f32[4,2048,2,256]{3,2,1,0:T(2,128)} copy(f32[4,2048,2,256]{1,3,2,0:T(8,128)} %bitcast.199) | data formatting | bytes 33554432 | tf_op jit(solution)/shard_map/reshape | solution.py:647
  697.2 12.2 %all-to-all-done.2 = bf16[128,4,512]{2,0,1:T(8,128)(2,1)S(1)} async-done(((bf16[128,4,512]{2,0,1:T(8,128)(2,1)}), bf16[128,4,512]{2,0,1:T(8,128)(2,1)S(1)}, u32[]{:S(2)}, u32[]{:S(2)}) %all-to-all-start.2) | async-done | bytes 524320 | tf_op jit(solution)/shard_map/all_to_all | solution.py:656
  728.9 8.0 collective-permute-done.63
  745.6 7.4 convolution_convert_fusion.2
  783.1 13.4 %reduce-scatter.8.cloned.1.call-done = bf16[128,2048]{1,0:T(8,128)(2,1)} async-done(((bf16[512,2048]{1,0:T(8,128)(2,1)}), bf16[128,2048]{1,0:T(8,128)(2,1)}) %reduce-scatter.8.cloned.1.call-update) | async-done | bytes 524304 | tf_op jit(solution)/shard_map/reduce_scatter | solution.py:687
  817.0 12.8 %collective-permute-done.66 = f32[1,4353]{1,0:T(1,128)S(1)} collective-permute-done((f32[1,4353]{1,0:T(1,128)S(1)}, f32[1,4353]{1,0:T(1,128)S(1)}, u32[]{:S(2)}, u32[]{:S(2)}) %collective-permute-start.66) | collective-permute-done | bytes 17444 | tf_op jit(solution)/shard_map/ppermute | solution.py:329
  (535 shorter events, 321.9 us)
Async XLA Ops:
  7.2 61.8 %all-gather.10.cloned.1.call-start = ((), (), s32[]{:S(2)}) async-start(), calls=%async_computation.6 | async-start | bytes 7077888 | tf_op jit(solution)/shard_map/all_gather | solution.py:532
  9.6 126.2 %all-gather.12.cloned.1.call-start = ((), (), s32[]{:S(2)}) async-start(), calls=%async_computation.7 | async-start | bytes 9437184 | tf_op jit(solution)/shard_map/all_gather | solution.py:536
  121.0 48.8 %all-gather.14.cloned.1.call-start = ((), (), s32[]{:S(2)}) async-start(), calls=%async_computation.8 | async-start | bytes 1310720 | tf_op jit(solution)/shard_map/all_gather | solution.py:581
  142.8 56.5 %all-gather.16.cloned.1.call-start = ((), (), s32[]{:S(2)}) async-start(), calls=%async_computation.9 | async-start | bytes 1310720 | tf_op jit(solution)/shard_map/all_gather | solution.py:581
  143.4 262.5 %reduce-scatter.4.cloned.1.call-start = ((), (), s32[]{:S(2)}) async-start(), calls=%async_computation.10 | async-start | bytes 2621440 | tf_op jit(solution)/shard_map/reduce_scatter | solution.py:593
  169.9 29.5 %collective-permute-start.15 = (bf16[512,1024]{1,0:T(8,128)(2,1)}, bf16[512,1024]{1,0:T(8,128)(2,1)}, u32[]{:S(2)}, u32[]{:S(2)}) collective-permute-start(bf16[512,1024]{1,0:T(8,128)(2,1)} %all-gather.14.cloned.1.call-done.refs_0_), channel_id=1, source_target_pairs={{0,16},{8,24},{16,0},{24,8},{1,17},{9,25},{17,1},{25,9},{2,18},{10... | collective-permute-start | bytes 3145736 | tf_op jit(solution)/shard_map/ppermute | solution.py:357
  171.3 28.0 %collective-permute-start.16 = (bf16[512,1024]{1,0:T(8,128)(2,1)}, bf16[512,1024]{1,0:T(8,128)(2,1)S(1)}, u32[]{:S(2)}, u32[]{:S(2)}) collective-permute-start(bf16[512,1024]{1,0:T(8,128)(2,1)} %all-gather.14.cloned.1.call-done.refs_0_), channel_id=1, source_target_pairs={{0,4},{4,0},{1,5},{5,1},{2,6},{6,2},{3,7},{7,3},{8,12},{12,8},{9,1... | collective-permute-start | bytes 3145736 | tf_op jit(solution)/shard_map/ppermute | solution.py:360
  172.8 32.4 %collective-permute-start.17 = (bf16[512,1024]{1,0:T(8,128)(2,1)}, bf16[512,1024]{1,0:T(8,128)(2,1)}, u32[]{:S(2)}, u32[]{:S(2)}) collective-permute-start(bf16[512,1024]{1,0:T(8,128)(2,1)} %all-gather.14.cloned.1.call-done.refs_0_), channel_id=1, source_target_pairs={{0,8},{8,0},{16,24},{24,16},{1,9},{9,1},{17,25},{25,17},{2,10},{10... | collective-permute-start | bytes 3145736 | tf_op jit(solution)/shard_map/ppermute | solution.py:354
  203.7 25.5 %collective-permute-start.22 = (bf16[512,1024]{1,0:T(8,128)(2,1)S(1)}, bf16[512,1024]{1,0:T(8,128)(2,1)S(1)}, u32[]{:S(2)}, u32[]{:S(2)}) collective-permute-start(bf16[512,1024]{1,0:T(8,128)(2,1)S(1)} %copy-done.7), channel_id=1, source_target_pairs={{0,16},{8,24},{16,0},{24,8},{1,17},{9,25},{17,1},{25,9},{2,18},{10... | collective-permute-start | bytes 3145736 | tf_op jit(solution)/shard_map/ppermute | solution.py:357
  230.9 25.3 %collective-permute-start.28 = (bf16[512,1024]{1,0:T(8,128)(2,1)}, bf16[512,1024]{1,0:T(8,128)(2,1)S(1)}, u32[]{:S(2)}, u32[]{:S(2)}) collective-permute-start(bf16[512,1024]{1,0:T(8,128)(2,1)} %collective-permute-done.15.refs_0_), channel_id=1, source_target_pairs={{0,4},{4,0},{1,5},{5,1},{2,6},{6,2},{3,7},{7,3},{8,12},{12,8},{9,1... | collective-permute-start | bytes 3145736 | tf_op jit(solution)/shard_map/ppermute | solution.py:360
  233.0 39.9 %collective-permute-start.21 = (bf16[512,2048]{1,0:T(8,128)(2,1)S(1)}, bf16[512,2048]{1,0:T(8,128)(2,1)S(1)}, u32[]{:S(2)}, u32[]{:S(2)}) collective-permute-start(bf16[512,2048]{1,0:T(8,128)(2,1)S(1)} %get-tuple-element.115), channel_id=1, source_target_pairs={{0,8},{8,0},{16,24},{24,16},{1,9},{9,1},{17,25},{25,17},{2,10},{10... | collective-permute-start | bytes 6291464 | tf_op jit(solution)/shard_map/ppermute | solution.py:354
  277.6 25.5 %collective-permute-start.33 = (bf16[512,1024]{1,0:T(8,128)(2,1)S(1)}, bf16[512,1024]{1,0:T(8,128)(2,1)S(1)}, u32[]{:S(2)}, u32[]{:S(2)}) collective-permute-start(bf16[512,1024]{1,0:T(8,128)(2,1)S(1)} %add_convert_fusion.15), channel_id=1, source_target_pairs={{0,4},{4,0},{1,5},{5,1},{2,6},{6,2},{3,7},{7,3},{8,12},{12,8},{9,1... | collective-permute-start | bytes 3145736 | tf_op jit(solution)/shard_map/ppermute | solution.py:360
  364.0 72.3 %all-gather.20.cloned.1.call-start = ((), (), s32[]{:S(2)}) async-start(), calls=%async_computation.12 | async-start | bytes 1310720 | tf_op jit(solution)/shard_map/all_gather | solution.py:581
  408.9 57.1 %all-gather.22.cloned.1.call-start = ((), (), s32[]{:S(2)}) async-start(), calls=%async_computation.13 | async-start | bytes 1310720 | tf_op jit(solution)/shard_map/all_gather | solution.py:581
  409.7 204.3 %all-gather.18.cloned.1.call-start = ((), (), s32[]{:S(2)}) async-start(), calls=%async_computation.11 | async-start | bytes 2621440 | tf_op jit(solution)/shard_map/all_gather | solution.py:614
  436.4 29.7 %collective-permute-start.39 = (bf16[512,1024]{1,0:T(8,128)(2,1)}, bf16[512,1024]{1,0:T(8,128)(2,1)}, u32[]{:S(2)}, u32[]{:S(2)}) collective-permute-start(bf16[512,1024]{1,0:T(8,128)(2,1)} %all-gather.20.cloned.1.call-done.refs_0_), channel_id=1, source_target_pairs={{0,16},{8,24},{16,0},{24,8},{1,17},{9,25},{17,1},{25,9},{2,18},{10... | collective-permute-start | bytes 3145736 | tf_op jit(solution)/shard_map/ppermute | solution.py:357
  437.8 28.2 %collective-permute-start.40 = (bf16[512,1024]{1,0:T(8,128)(2,1)}, bf16[512,1024]{1,0:T(8,128)(2,1)S(1)}, u32[]{:S(2)}, u32[]{:S(2)}) collective-permute-start(bf16[512,1024]{1,0:T(8,128)(2,1)} %all-gather.20.cloned.1.call-done.refs_0_), channel_id=1, source_target_pairs={{0,4},{4,0},{1,5},{5,1},{2,6},{6,2},{3,7},{7,3},{8,12},{12,8},{9,1... | collective-permute-start | bytes 3145736 | tf_op jit(solution)/shard_map/ppermute | solution.py:360
  439.3 28.9 %collective-permute-start.41 = (bf16[512,1024]{1,0:T(8,128)(2,1)}, bf16[512,1024]{1,0:T(8,128)(2,1)}, u32[]{:S(2)}, u32[]{:S(2)}) collective-permute-start(bf16[512,1024]{1,0:T(8,128)(2,1)} %all-gather.20.cloned.1.call-done.refs_0_), channel_id=1, source_target_pairs={{0,8},{8,0},{16,24},{24,16},{1,9},{9,1},{17,25},{25,17},{2,10},{10... | collective-permute-start | bytes 3145736 | tf_op jit(solution)/shard_map/ppermute | solution.py:354
  466.7 27.9 %collective-permute-start.46 = (bf16[512,1024]{1,0:T(8,128)(2,1)}, bf16[512,1024]{1,0:T(8,128)(2,1)S(1)}, u32[]{:S(2)}, u32[]{:S(2)}) collective-permute-start(bf16[512,1024]{1,0:T(8,128)(2,1)} %all-gather.22.cloned.1.call-done.refs_1_), channel_id=1, source_target_pairs={{0,16},{8,24},{16,0},{24,8},{1,17},{9,25},{17,1},{25,9},{2,18},{10... | collective-permute-start | bytes 3145736 | tf_op jit(solution)/shard_map/ppermute | solution.py:357
  468.2 26.4 %collective-permute-start.47 = (bf16[512,1024]{1,0:T(8,128)(2,1)}, bf16[512,1024]{1,0:T(8,128)(2,1)S(1)}, u32[]{:S(2)}, u32[]{:S(2)}) collective-permute-start(bf16[512,1024]{1,0:T(8,128)(2,1)} %all-gather.22.cloned.1.call-done.refs_1_), channel_id=1, source_target_pairs={{0,4},{4,0},{1,5},{5,1},{2,6},{6,2},{3,7},{7,3},{8,12},{12,8},{9,1... | collective-permute-start | bytes 3145736 | tf_op jit(solution)/shard_map/ppermute | solution.py:360
  495.1 25.3 %collective-permute-start.52 = (bf16[512,1024]{1,0:T(8,128)(2,1)}, bf16[512,1024]{1,0:T(8,128)(2,1)S(1)}, u32[]{:S(2)}, u32[]{:S(2)}) collective-permute-start(bf16[512,1024]{1,0:T(8,128)(2,1)} %collective-permute-done.39.refs_0_), channel_id=1, source_target_pairs={{0,4},{4,0},{1,5},{5,1},{2,6},{6,2},{3,7},{7,3},{8,12},{12,8},{9,1... | collective-permute-start | bytes 3145736 | tf_op jit(solution)/shard_map/ppermute | solution.py:360
  496.2 42.9 %collective-permute-start.45 = (bf16[512,2048]{1,0:T(8,128)(2,1)S(1)}, bf16[512,2048]{1,0:T(8,128)(2,1)S(1)}, u32[]{:S(2)}, u32[]{:S(2)}) collective-permute-start(bf16[512,2048]{1,0:T(8,128)(2,1)S(1)} %get-tuple-element.158), channel_id=1, source_target_pairs={{0,8},{8,0},{16,24},{24,16},{1,9},{9,1},{17,25},{25,17},{2,10},{10... | collective-permute-start | bytes 6291464 | tf_op jit(solution)/shard_map/ppermute | solution.py:354
  539.7 25.7 %collective-permute-start.51 = (bf16[512,1024]{1,0:T(8,128)(2,1)S(1)}, bf16[512,1024]{1,0:T(8,128)(2,1)}, u32[]{:S(2)}, u32[]{:S(2)}) collective-permute-start(bf16[512,1024]{1,0:T(8,128)(2,1)S(1)} %add_convert_fusion.8), channel_id=1, source_target_pairs={{0,16},{8,24},{16,0},{24,8},{1,17},{9,25},{17,1},{25,9},{2,18},{10... | collective-permute-start | bytes 3145736 | tf_op jit(solution)/shard_map/ppermute | solution.py:357
  543.8 25.4 %collective-permute-start.57 = (bf16[512,1024]{1,0:T(8,128)(2,1)S(1)}, bf16[512,1024]{1,0:T(8,128)(2,1)}, u32[]{:S(2)}, u32[]{:S(2)}) collective-permute-start(bf16[512,1024]{1,0:T(8,128)(2,1)S(1)} %add_convert_fusion.7), channel_id=1, source_target_pairs={{0,4},{4,0},{1,5},{5,1},{2,6},{6,2},{3,7},{7,3},{8,12},{12,8},{9,1... | collective-permute-start | bytes 3145736 | tf_op jit(solution)/shard_map/ppermute | solution.py:360
  569.2 111.9 %reduce-scatter.6.cloned.1.call-start = ((), (), s32[]{:S(2)}) async-start(), calls=%async_computation.14 | async-start | bytes 2621440 | tf_op jit(solution)/shard_map/reduce_scatter | solution.py:593
  576.3 25.3 %collective-permute-start.59 = (bf16[512,1024]{1,0:T(8,128)(2,1)S(1)}, bf16[512,1024]{1,0:T(8,128)(2,1)S(1)}, u32[]{:S(2)}, u32[]{:S(2)}) collective-permute-start(bf16[512,1024]{1,0:T(8,128)(2,1)S(1)} %get-tuple-element.274), channel_id=1, source_target_pairs={{0,16},{8,24},{16,0},{24,8},{1,17},{9,25},{17,1},{25,9},{2,18},{10... | collective-permute-start | bytes 3145736 | tf_op jit(solution)/shard_map/ppermute | solution.py:357
  696.6 49.0 %all-gather.24.cloned.1.call-start = ((), (), s32[]{:S(2)}) async-start(), calls=%async_computation.15 | async-start | bytes 2621440 | tf_op jit(solution)/shard_map/all_gather | solution.py:678
  697.2 99.3 %reduce-scatter.8.cloned.1.call-start = ((), (), s32[]{:S(2)}) async-start(), calls=%async_computation.16 | async-start | bytes 2621440 | tf_op jit(solution)/shard_map/reduce_scatter | solution.py:687
  753.0 94.0 %all-gather.26.cloned.1.call-start = ((), (), s32[]{:S(2)}) async-start(), calls=%async_computation.17 | async-start | bytes 2621440 | tf_op jit(solution)/shard_map/all_gather | solution.py:696
  779.1 30.5 %collective-permute-start.77 = (bf16[256,1024]{0,1:T(8,128)(2,1)}, bf16[256,1024]{0,1:T(8,128)(2,1)}, u32[]{:S(2)}, u32[]{:S(2)}) collective-permute-start(bf16[256,1024]{0,1:T(8,128)(2,1)} %get-tuple-element.300), channel_id=1, source_target_pairs={{0,4},{4,0},{1,5},{5,1},{2,6},{6,2},{3,7},{7,3},{8,12},{12,8},{9,1... | collective-permute-start | bytes 1572872 | tf_op jit(solution)/shard_map/ppermute | solution.py:360
  780.6 32.3 %collective-permute-start.75 = (bf16[256,1024]{0,1:T(8,128)(2,1)}, bf16[256,1024]{0,1:T(8,128)(2,1)}, u32[]{:S(2)}, u32[]{:S(2)}) collective-permute-start(bf16[256,1024]{0,1:T(8,128)(2,1)} %get-tuple-element.299), channel_id=1, source_target_pairs={{0,16},{8,24},{16,0},{24,8},{1,17},{9,25},{17,1},{25,9},{2,18},{10... | collective-permute-start | bytes 1572872 | tf_op jit(solution)/shard_map/ppermute | solution.py:357
  804.5 26.9 %collective-permute-start.72 = (bf16[256,1024]{0,1:T(8,128)(2,1)}, bf16[256,1024]{0,1:T(8,128)(2,1)S(1)}, u32[]{:S(2)}, u32[]{:S(2)}) collective-permute-start(bf16[256,1024]{0,1:T(8,128)(2,1)} %slice.488), channel_id=1, source_target_pairs={{0,16},{8,24},{16,0},{24,8},{1,17},{9,25},{17,1},{25,9},{2,18},{10... | collective-permute-start | bytes 1572872 | tf_op jit(solution)/shard_map/ppermute | solution.py:357
  (157 other events, 1784.8 us)
Sparse Core Ops, SparseCore 0:
  10.5 49.4 all-gather.9
  62.4 72.3 all-gather.11
  142.9 26.8 all-gather.13
  171.9 27.4 all-gather.15
  364.1 41.6 reduce-scatter.3
  409.1 27.2 all-gather.19
  438.6 27.4 all-gather.21
  569.4 44.5 all-gather.17
  636.9 42.2 reduce-scatter.5
  699.3 46.2 all-gather.23
  753.1 43.3 reduce-scatter.7
  800.9 46.0 all-gather.25

commit v9 on v8

--- a/solution.py
+++ b/solution.py
@@ -180,7 +180,7 @@
     half = down_ref.shape[1]
     rows, weight = take_rows(x_refs, table_ref, rows_ref)
     gate_up = jnp.dot(rows, up_ref[expert], preferred_element_type=wide)
-    gate_up_ref[0] = gate_up.reshape(blocks, capacity, 2 * half)
+    gate_up_ref[0] = gate_up.astype(low).reshape(blocks, capacity, 2 * half)
     gate_part = gate_up[:, :half]
     up_part = gate_up[:, half:]
     hidden = (gate_part * jax.nn.sigmoid(gate_part) * up_part * weight).astype(low)
@@ -213,7 +213,7 @@
     half = down_ref.shape[1]
     rows, weight = take_rows(x_refs, table_ref, rows_ref)
     grad_hidden = nt_dot(rows, down_ref[expert]) * weight
-    gate_up = gate_up_ref[0].reshape(blocks * capacity, 2 * half)
+    gate_up = gate_up_ref[0].astype(wide).reshape(blocks * capacity, 2 * half)
     gate_part = gate_up[:, :half]
     up_part = gate_up[:, half:]
     sigmoid = jax.nn.sigmoid(gate_part)
@@ -260,7 +260,7 @@
         out_shape.append(row_shape(double, low))
     else:
         out_specs.append(row_spec(half))
-        out_shape += [row_shape(double, wide), row_shape(half, low)]
+        out_shape += [row_shape(double, low), row_shape(half, low)]
     aliases = {len(operands) + i: n_out + i for i in range(len(kept))}
     rows = experts * blocks * capacity
     body = functools.partial(

time: 872 us -> 872 us (level)
  transfers between devices with their start and end apart: 95 -> 95, of which waited for: 52 -> 53; matrix products, arithmetic and copies ran while one was open for 22% -> 22% of each run, Pallas kernels for 17% -> 17%
where the time goes in v9:
time: 872 us; the launch traced here: 862 us
  waiting for transfers between devices  372 us (43%)
  Pallas kernels  146 us (17%)
  local copies, waits for them, and re-layouts  86.2 us (10%)
  matrix products  85.7 us (10%)
  starting transfers between devices  81.5 us (9%)
  other arithmetic  69.8 us (8%)
  between operations  20.6 us (2%)
    pallas_call x8, Pallas kernels, expert_call(): pl.pallas_call(body, grid=(experts,), in_specs=in_specs + [pl.BlockSpec(m...  136 us
    all_gather x4, waiting for transfers between devices, spread(): lax.all_gather(half.astype(low), 'tp', axis=0, tiled=True)  92.2 us
    ppermute x16, waiting for transfers between devices, along_x(): return lax.ppermute(a, 'fsdp', [(i, i ^ 2) for i in range(self.fsdp)])  76.7 us
    reduce_scatter x2, waiting for transfers between devices, finish(): lax.psum_scatter(half, 'tp', scatter_dimension=0, tiled=True).astype(wide)  39.6 us
    ppermute x17, waiting for transfers between devices, along_y(): return lax.ppermute(a, 'ctx', [(i, i ^ 1) for i in range(self.ctx)])  27.8 us
    reshape x1, local copies, waits for them, and re-layouts, per_device(): grad_up.reshape(shard_experts, width, 2, hidden_local)  25.1 us
    ppermute x6, waiting for transfers between devices, line_gather(): lax.ppermute(shard, 'tp', [(i, i + d) for i in range(size) if 0 <= i + d...  21.9 us
    ppermute x17, starting transfers between devices, along_y(): return lax.ppermute(a, 'ctx', [(i, i ^ 1) for i in range(self.ctx)])  21 us
  transfers between devices with their start and end apart: 95, of which 53 were waited for; matrix products, arithmetic and copies ran while one was open for 22% of the time, Pallas kernels for 17%

profile of v9, /device:TPU:0, one launch (start us, length us, event | category | flops | bytes accessed | tf_op | source)
XLA Modules:
  0.0 861.8 jit_solution(3200221866116543681)
XLA Ops:
  9.6 7.0 collective-permute-start.9
  33.6 12.8 %collective-permute-done.13 = bf16[512,256]{1,0:T(8,128)(2,1)S(1)} collective-permute-done((bf16[512,256]{1,0:T(8,128)(2,1)S(1)}, bf16[512,256]{1,0:T(8,128)(2,1)S(1)}, u32[]{:S(2)}, u32[]{:S(2)}) %collective-permute-start.13) | collective-permute-done | bytes 262176 | tf_op jit(solution)/shard_map/ppermute | solution.py:338
  69.0 6.9 fusion.11
  90.0 7.7 collective-permute-done.8
  102.5 9.9 %collective-permute-done.7 = bf16[1,512,4,128]{1,3,2,0:T(8,128)(2,1)S(1)} collective-permute-done((bf16[1,512,4,128]{1,3,2,0:T(8,128)(2,1)S(1)}, bf16[1,512,4,128]{1,3,2,0:T(8,128)(2,1)S(1)}, u32[]{:S(2)}, u32[]{:S(2)}) %collective-permute-start.7) | collective-permute-done | bytes 524320 | tf_op jit(solution)/shard_map/ppermute | solution.py:551
  123.8 11.6 %all-to-all-done.1 = bf16[4,128,512]{2,1,0:T(8,128)(2,1)S(1)} async-done(((bf16[4,128,512]{2,1,0:T(8,128)(2,1)}), bf16[4,128,512]{2,1,0:T(8,128)(2,1)S(1)}, u32[]{:S(2)}, u32[]{:S(2)}) %all-to-all-start.1) | async-done | bytes 524320 | tf_op jit(solution)/shard_map/all_to_all | solution.py:570
  143.5 26.4 %all-gather.14.cloned.1.call-done.refs_0_ = bf16[512,1024]{1,0:T(8,128)(2,1)} async-done(((bf16[128,1024]{1,0:T(8,128)(2,1)}), bf16[512,1024]{1,0:T(8,128)(2,1)}) %all-gather.14.cloned.1.call-update) | async-done | bytes 1048592 | tf_op jit(solution)/shard_map/all_gather | solution.py:581
  172.8 14.1 %reshape.366.refs_0_ = bf16[4,2048,512]{2,1,0:T(8,128)(2,1)} reshape(bf16[4,2048,2,256]{3,2,1,0:T(2,128)(2,1)} %param.20) | data formatting | bytes 16777216 | tf_op jit(solution)/shard_map/reshape | solution.py:521
  186.9 12.4 %all-gather.16.cloned.1.call-done.refs_1_ = bf16[512,1024]{1,0:T(8,128)(2,1)} async-done(((bf16[128,1024]{1,0:T(8,128)(2,1)}), bf16[512,1024]{1,0:T(8,128)(2,1)}) %all-gather.16.cloned.1.call-update) | async-done | bytes 1048592 | tf_op jit(solution)/shard_map/all_gather | solution.py:581
  212.3 15.8 %shard_map.187 = (bf16[512,2048]{1,0:T(8,128)(2,1)S(1)}, bf16[512,2048]{1,0:T(8,128)(2,1)S(1)}, bf16[4,8,160,2048]{3,2,1,0:T(8,128)(2,1)}, bf16[4,8,160,512]{3,2,1,0:T(8,128)(2,1)}, bf16[4,8,160,256]{3,2,1,0:T(8,128)(2,1)}) custom-call(bf16[512,1024]{1,0:T(8,128)(2,1)S(1)} %copy-done.6, bf16[512,1024]{1,0:T(8,128)(2,1)S(1)} %copy-done.7, ...), custom_call_target="tpu_custom_call" | custom-call | flops 9395240960 | bytes 17563648 | tf_op jit(solution)/shard_map/pallas_call | solution.py:269
  233.1 16.2 %shard_map.188 = (bf16[512,2048]{1,0:T(8,128)(2,1)S(1)}, bf16[512,2048]{1,0:T(8,128)(2,1)S(1)}, bf16[4,8,160,2048]{3,2,1,0:T(8,128)(2,1)}, bf16[4,8,160,512]{3,2,1,0:T(8,128)(2,1)}, bf16[4,8,160,256]{3,2,1,0:T(8,128)(2,1)}) custom-call(bf16[512,1024]{1,0:T(8,128)(2,1)} %collective-permute-done.15.refs_0_,, ...), custom_call_target="tpu_custom_call", output_to_operand_aliasing={{2}: (8, {}), {3}: (9, {}), {4}: (10, {})} | custom-call | flops 9395240960 | bytes 17563648 | tf_op jit(solution)/shard_map/pallas_call | solution.py:269
  257.2 15.5 %shard_map.189 = (bf16[512,2048]{1,0:T(8,128)(2,1)S(1)}, bf16[512,2048]{1,0:T(8,128)(2,1)S(1)}, bf16[4,8,160,2048]{3,2,1,0:T(8,128)(2,1)}, bf16[4,8,160,512]{3,2,1,0:T(8,128)(2,1)}, bf16[4,8,160,256]{3,2,1,0:T(8,128)(2,1)}) custom-call(bf16[512,1024]{1,0:T(8,128)(2,1)S(1)} %collective-permute-done.16.refs, ...), custom_call_target="tpu_custom_call", output_to_operand_aliasing={{2}: (8, {}), {3}: (9, {}), {4}: (10, {})} | custom-call | flops 9395240960 | bytes 17563648 | tf_op jit(solution)/shard_map/pallas_call | solution.py:269
  278.5 14.4 %shard_map.190 = (bf16[512,2048]{1,0:T(8,128)(2,1)S(1)}, bf16[512,2048]{1,0:T(8,128)(2,1)S(1)}, bf16[4,8,160,2048]{3,2,1,0:T(8,128)(2,1)}, bf16[4,8,160,512]{3,2,1,0:T(8,128)(2,1)}, bf16[4,8,160,256]{3,2,1,0:T(8,128)(2,1)}) custom-call(bf16[512,1024]{1,0:T(8,128)(2,1)S(1)} %collective-permute-done.28.refs, ...), custom_call_target="tpu_custom_call", output_to_operand_aliasing={{2}: (8, {}), {3}: (9, {}), {4}: (10, {})} | custom-call | flops 9395240960 | bytes 17563648 | tf_op jit(solution)/shard_map/pallas_call | solution.py:269
  309.4 24.0 %collective-permute-done.35 = bf16[512,1024]{1,0:T(8,128)(2,1)S(1)} collective-permute-done((bf16[512,1024]{1,0:T(8,128)(2,1)S(1)}, bf16[512,1024]{1,0:T(8,128)(2,1)S(1)}, u32[]{:S(2)}, u32[]{:S(2)}) %collective-permute-start.35) | collective-permute-done | bytes 1048608 | tf_op jit(solution)/shard_map/ppermute | solution.py:357
  337.2 21.3 %collective-permute-done.38 = bf16[512,1024]{1,0:T(8,128)(2,1)S(1)} collective-permute-done((bf16[512,1024]{1,0:T(8,128)(2,1)S(1)}, bf16[512,1024]{1,0:T(8,128)(2,1)S(1)}, u32[]{:S(2)}, u32[]{:S(2)}) %collective-permute-start.38) | collective-permute-done | bytes 1048608 | tf_op jit(solution)/shard_map/ppermute | solution.py:357
  366.2 39.6 %reduce-scatter.4.cloned.1.call-done = bf16[128,2048]{1,0:T(8,128)(2,1)} async-done(((bf16[512,2048]{1,0:T(8,128)(2,1)}), bf16[128,2048]{1,0:T(8,128)(2,1)}) %reduce-scatter.4.cloned.1.call-update) | async-done | bytes 524304 | tf_op jit(solution)/shard_map/reduce_scatter | solution.py:593
  409.6 26.6 %all-gather.20.cloned.1.call-done.refs_0_ = bf16[512,1024]{1,0:T(8,128)(2,1)} async-done(((bf16[128,1024]{1,0:T(8,128)(2,1)}), bf16[512,1024]{1,0:T(8,128)(2,1)}) %all-gather.20.cloned.1.call-update) | async-done | bytes 1048592 | tf_op jit(solution)/shard_map/all_gather | solution.py:581
  439.2 26.7 %all-gather.22.cloned.1.call-done.refs_1_ = bf16[512,1024]{1,0:T(8,128)(2,1)} async-done(((bf16[128,1024]{1,0:T(8,128)(2,1)}), bf16[512,1024]{1,0:T(8,128)(2,1)}) %all-gather.22.cloned.1.call-update) | async-done | bytes 1048592 | tf_op jit(solution)/shard_map/all_gather | solution.py:581
  474.2 18.9 %shard_map.192 = (bf16[512,2048]{1,0:T(8,128)(2,1)S(1)}, bf16[512,2048]{1,0:T(8,128)(2,1)S(1)}, bf16[4,8,160,2048]{3,2,1,0:T(8,128)(2,1)}, bf16[4,8,160,512]{3,2,1,0:T(8,128)(2,1)}) custom-call(bf16[512,1024]{1,0:T(8,128)(2,1)S(1)} %copy-done.8, bf16[512,1024]{1,0:T(8,128)(2,1)S(1)} %copy-done.9, bf16[512,1024]{1,0:T(8,128)(2,1)} %collective-permute-done.41.refs_2_, ...), custom_call_target="tpu_custom_call" | custom-call | flops 9395240960 | bytes 17563648 | tf_op jit(solution)/shard_map/pallas_call | solution.py:269
  497.1 18.7 %shard_map.193 = (bf16[512,2048]{1,0:T(8,128)(2,1)S(1)}, bf16[512,2048]{1,0:T(8,128)(2,1)S(1)}, bf16[4,8,160,2048]{3,2,1,0:T(8,128)(2,1)}, bf16[4,8,160,512]{3,2,1,0:T(8,128)(2,1)}) custom-call(bf16[512,1024]{1,0:T(8,128)(2,1)} %collective-permute-done.39.refs_0_, ...), custom_call_target="tpu_custom_call", output_to_operand_aliasing={{2}: (9, {}), {3}: (10, {})} | custom-call | flops 9395240960 | bytes 17563648 | tf_op jit(solution)/shard_map/pallas_call | solution.py:269
  520.8 18.1 %shard_map.194 = (bf16[512,2048]{1,0:T(8,128)(2,1)S(1)}, bf16[512,2048]{1,0:T(8,128)(2,1)S(1)}, bf16[4,8,160,2048]{3,2,1,0:T(8,128)(2,1)}, bf16[4,8,160,512]{3,2,1,0:T(8,128)(2,1)}) custom-call(bf16[512,1024]{1,0:T(8,128)(2,1)S(1)} %collective-permute-done.40.refs_0_, ...), custom_call_target="tpu_custom_call", output_to_operand_aliasing={{2}: (9, {}), {3}: (10, {})} | custom-call | flops 9395240960 | bytes 17563648 | tf_op jit(solution)/shard_map/pallas_call | solution.py:269
  544.9 18.8 %shard_map.195 = (bf16[512,2048]{1,0:T(8,128)(2,1)S(1)}, bf16[512,2048]{1,0:T(8,128)(2,1)}, bf16[4,8,160,2048]{3,2,1,0:T(8,128)(2,1)}, bf16[4,8,160,512]{3,2,1,0:T(8,128)(2,1)}) custom-call(bf16[512,1024]{1,0:T(8,128)(2,1)S(1)} %collective-permute-done.52.refs_0_, ...), custom_call_target="tpu_custom_call", output_to_operand_aliasing={{2}: (9, {}), {3}: (10, {})} | custom-call | flops 9395240960 | bytes 17563648 | tf_op jit(solution)/shard_map/pallas_call | solution.py:269
  578.1 15.8 %convolution_bitcast_fusion = f32[4,256,2048]{2,1,0:T(8,128)} fusion(bf16[4,8,160,256]{3,2,1,0:T(8,128)(2,1)S(1)} %copy-done.17, bf16[4,8,160,2048]{3,2,1,0:T(8,128)(2,1)} %get-tuple-element.184), kind=kOutput, calls=%fused_computation.25 | convolution fusion | flops 5368709120 | bytes 31981568 | tf_op jit(solution)/shard_map/ebcf,ebcd->efd/dot_general | solution.py:630
  593.8 7.6 collective-permute-done.59
  613.8 13.9 %collective-permute-done.62 = bf16[512,1024]{1,0:T(8,128)(2,1)S(1)} collective-permute-done((bf16[512,1024]{1,0:T(8,128)(2,1)}, bf16[512,1024]{1,0:T(8,128)(2,1)S(1)}, u32[]{:S(2)}, u32[]{:S(2)}) %collective-permute-start.62) | collective-permute-done | bytes 1048608 | tf_op jit(solution)/shard_map/ppermute | solution.py:357
  636.6 19.3 %fusion.84 = f32[4,2048,512,1]{1,2,3,0:T(8,128)} fusion(bf16[4,8,160,2048]{3,2,1,0:T(8,128)(2,1)} %get-tuple-element.187, bf16[4,8,160,512]{3,2,1,0:T(8,128)(2,1)} %get-tuple-element.188), kind=kOutput, calls=%fused_computation.254 | convolution fusion | flops 10737418240 | bytes 42991616 | tf_op jit(solution)/shard_map/ebcd,ebcf->edf/dot_general | solution.py:633
  655.8 25.1 %copy.136 = f32[4,2048,2,256]{3,2,1,0:T(2,128)} copy(f32[4,2048,2,256]{1,3,2,0:T(8,128)} %bitcast.199) | data formatting | bytes 33554432 | tf_op jit(solution)/shard_map/reshape | solution.py:647
  697.0 12.2 %all-to-all-done.2 = bf16[128,4,512]{2,0,1:T(8,128)(2,1)S(1)} async-done(((bf16[128,4,512]{2,0,1:T(8,128)(2,1)}), bf16[128,4,512]{2,0,1:T(8,128)(2,1)S(1)}, u32[]{:S(2)}, u32[]{:S(2)}) %all-to-all-start.2) | async-done | bytes 524320 | tf_op jit(solution)/shard_map/all_to_all | solution.py:656
  728.7 8.0 collective-permute-done.63
  745.4 7.4 convolution_convert_fusion.2
  782.9 13.4 %reduce-scatter.8.cloned.1.call-done = bf16[128,2048]{1,0:T(8,128)(2,1)} async-done(((bf16[512,2048]{1,0:T(8,128)(2,1)}), bf16[128,2048]{1,0:T(8,128)(2,1)}) %reduce-scatter.8.cloned.1.call-update) | async-done | bytes 524304 | tf_op jit(solution)/shard_map/reduce_scatter | solution.py:687
  816.8 12.8 %collective-permute-done.66 = f32[1,4353]{1,0:T(1,128)S(1)} collective-permute-done((f32[1,4353]{1,0:T(1,128)S(1)}, f32[1,4353]{1,0:T(1,128)S(1)}, u32[]{:S(2)}, u32[]{:S(2)}) %collective-permute-start.66) | collective-permute-done | bytes 17444 | tf_op jit(solution)/shard_map/ppermute | solution.py:329
  (535 shorter events, 322.3 us)
Async XLA Ops:
  7.2 61.8 %all-gather.10.cloned.1.call-start = ((), (), s32[]{:S(2)}) async-start(), calls=%async_computation.6 | async-start | bytes 7077888 | tf_op jit(solution)/shard_map/all_gather | solution.py:532
  9.6 126.2 %all-gather.12.cloned.1.call-start = ((), (), s32[]{:S(2)}) async-start(), calls=%async_computation.7 | async-start | bytes 9437184 | tf_op jit(solution)/shard_map/all_gather | solution.py:536
  121.0 48.8 %all-gather.14.cloned.1.call-start = ((), (), s32[]{:S(2)}) async-start(), calls=%async_computation.8 | async-start | bytes 1310720 | tf_op jit(solution)/shard_map/all_gather | solution.py:581
  142.8 56.5 %all-gather.16.cloned.1.call-start = ((), (), s32[]{:S(2)}) async-start(), calls=%async_computation.9 | async-start | bytes 1310720 | tf_op jit(solution)/shard_map/all_gather | solution.py:581
  143.4 262.3 %reduce-scatter.4.cloned.1.call-start = ((), (), s32[]{:S(2)}) async-start(), calls=%async_computation.10 | async-start | bytes 2621440 | tf_op jit(solution)/shard_map/reduce_scatter | solution.py:593
  169.9 29.5 %collective-permute-start.15 = (bf16[512,1024]{1,0:T(8,128)(2,1)}, bf16[512,1024]{1,0:T(8,128)(2,1)}, u32[]{:S(2)}, u32[]{:S(2)}) collective-permute-start(bf16[512,1024]{1,0:T(8,128)(2,1)} %all-gather.14.cloned.1.call-done.refs_0_), channel_id=1, source_target_pairs={{0,16},{8,24},{16,0},{24,8},{1,17},{9,25},{17,1},{25,9},{2,18},{10... | collective-permute-start | bytes 3145736 | tf_op jit(solution)/shard_map/ppermute | solution.py:357
  171.3 28.0 %collective-permute-start.16 = (bf16[512,1024]{1,0:T(8,128)(2,1)}, bf16[512,1024]{1,0:T(8,128)(2,1)S(1)}, u32[]{:S(2)}, u32[]{:S(2)}) collective-permute-start(bf16[512,1024]{1,0:T(8,128)(2,1)} %all-gather.14.cloned.1.call-done.refs_0_), channel_id=1, source_target_pairs={{0,4},{4,0},{1,5},{5,1},{2,6},{6,2},{3,7},{7,3},{8,12},{12,8},{9,1... | collective-permute-start | bytes 3145736 | tf_op jit(solution)/shard_map/ppermute | solution.py:360
  172.8 32.4 %collective-permute-start.17 = (bf16[512,1024]{1,0:T(8,128)(2,1)}, bf16[512,1024]{1,0:T(8,128)(2,1)}, u32[]{:S(2)}, u32[]{:S(2)}) collective-permute-start(bf16[512,1024]{1,0:T(8,128)(2,1)} %all-gather.14.cloned.1.call-done.refs_0_), channel_id=1, source_target_pairs={{0,8},{8,0},{16,24},{24,16},{1,9},{9,1},{17,25},{25,17},{2,10},{10... | collective-permute-start | bytes 3145736 | tf_op jit(solution)/shard_map/ppermute | solution.py:354
  203.7 25.5 %collective-permute-start.22 = (bf16[512,1024]{1,0:T(8,128)(2,1)S(1)}, bf16[512,1024]{1,0:T(8,128)(2,1)S(1)}, u32[]{:S(2)}, u32[]{:S(2)}) collective-permute-start(bf16[512,1024]{1,0:T(8,128)(2,1)S(1)} %copy-done.7), channel_id=1, source_target_pairs={{0,16},{8,24},{16,0},{24,8},{1,17},{9,25},{17,1},{25,9},{2,18},{10... | collective-permute-start | bytes 3145736 | tf_op jit(solution)/shard_map/ppermute | solution.py:357
  230.9 25.3 %collective-permute-start.28 = (bf16[512,1024]{1,0:T(8,128)(2,1)}, bf16[512,1024]{1,0:T(8,128)(2,1)S(1)}, u32[]{:S(2)}, u32[]{:S(2)}) collective-permute-start(bf16[512,1024]{1,0:T(8,128)(2,1)} %collective-permute-done.15.refs_0_), channel_id=1, source_target_pairs={{0,4},{4,0},{1,5},{5,1},{2,6},{6,2},{3,7},{7,3},{8,12},{12,8},{9,1... | collective-permute-start | bytes 3145736 | tf_op jit(solution)/shard_map/ppermute | solution.py:360
  233.0 39.8 %collective-permute-start.21 = (bf16[512,2048]{1,0:T(8,128)(2,1)S(1)}, bf16[512,2048]{1,0:T(8,128)(2,1)S(1)}, u32[]{:S(2)}, u32[]{:S(2)}) collective-permute-start(bf16[512,2048]{1,0:T(8,128)(2,1)S(1)} %get-tuple-element.115), channel_id=1, source_target_pairs={{0,8},{8,0},{16,24},{24,16},{1,9},{9,1},{17,25},{25,17},{2,10},{10... | collective-permute-start | bytes 6291464 | tf_op jit(solution)/shard_map/ppermute | solution.py:354
  277.5 25.5 %collective-permute-start.33 = (bf16[512,1024]{1,0:T(8,128)(2,1)S(1)}, bf16[512,1024]{1,0:T(8,128)(2,1)S(1)}, u32[]{:S(2)}, u32[]{:S(2)}) collective-permute-start(bf16[512,1024]{1,0:T(8,128)(2,1)S(1)} %add_convert_fusion.15), channel_id=1, source_target_pairs={{0,4},{4,0},{1,5},{5,1},{2,6},{6,2},{3,7},{7,3},{8,12},{12,8},{9,1... | collective-permute-start | bytes 3145736 | tf_op jit(solution)/shard_map/ppermute | solution.py:360
  308.2 25.3 %collective-permute-start.35 = (bf16[512,1024]{1,0:T(8,128)(2,1)S(1)}, bf16[512,1024]{1,0:T(8,128)(2,1)S(1)}, u32[]{:S(2)}, u32[]{:S(2)}) collective-permute-start(bf16[512,1024]{1,0:T(8,128)(2,1)S(1)} %get-tuple-element.278), channel_id=1, source_target_pairs={{0,16},{8,24},{16,0},{24,8},{1,17},{9,25},{17,1},{25,9},{2,18},{10... | collective-permute-start | bytes 3145736 | tf_op jit(solution)/shard_map/ppermute | solution.py:357
  363.9 72.3 %all-gather.20.cloned.1.call-start = ((), (), s32[]{:S(2)}) async-start(), calls=%async_computation.12 | async-start | bytes 1310720 | tf_op jit(solution)/shard_map/all_gather | solution.py:581
  408.8 57.1 %all-gather.22.cloned.1.call-start = ((), (), s32[]{:S(2)}) async-start(), calls=%async_computation.13 | async-start | bytes 1310720 | tf_op jit(solution)/shard_map/all_gather | solution.py:581
  409.6 204.2 %all-gather.18.cloned.1.call-start = ((), (), s32[]{:S(2)}) async-start(), calls=%async_computation.11 | async-start | bytes 2621440 | tf_op jit(solution)/shard_map/all_gather | solution.py:614
  436.3 29.7 %collective-permute-start.39 = (bf16[512,1024]{1,0:T(8,128)(2,1)}, bf16[512,1024]{1,0:T(8,128)(2,1)}, u32[]{:S(2)}, u32[]{:S(2)}) collective-permute-start(bf16[512,1024]{1,0:T(8,128)(2,1)} %all-gather.20.cloned.1.call-done.refs_0_), channel_id=1, source_target_pairs={{0,16},{8,24},{16,0},{24,8},{1,17},{9,25},{17,1},{25,9},{2,18},{10... | collective-permute-start | bytes 3145736 | tf_op jit(solution)/shard_map/ppermute | solution.py:357
  437.7 28.2 %collective-permute-start.40 = (bf16[512,1024]{1,0:T(8,128)(2,1)}, bf16[512,1024]{1,0:T(8,128)(2,1)S(1)}, u32[]{:S(2)}, u32[]{:S(2)}) collective-permute-start(bf16[512,1024]{1,0:T(8,128)(2,1)} %all-gather.20.cloned.1.call-done.refs_0_), channel_id=1, source_target_pairs={{0,4},{4,0},{1,5},{5,1},{2,6},{6,2},{3,7},{7,3},{8,12},{12,8},{9,1... | collective-permute-start | bytes 3145736 | tf_op jit(solution)/shard_map/ppermute | solution.py:360
  439.2 28.9 %collective-permute-start.41 = (bf16[512,1024]{1,0:T(8,128)(2,1)}, bf16[512,1024]{1,0:T(8,128)(2,1)}, u32[]{:S(2)}, u32[]{:S(2)}) collective-permute-start(bf16[512,1024]{1,0:T(8,128)(2,1)} %all-gather.20.cloned.1.call-done.refs_0_), channel_id=1, source_target_pairs={{0,8},{8,0},{16,24},{24,16},{1,9},{9,1},{17,25},{25,17},{2,10},{10... | collective-permute-start | bytes 3145736 | tf_op jit(solution)/shard_map/ppermute | solution.py:354
  466.6 27.9 %collective-permute-start.46 = (bf16[512,1024]{1,0:T(8,128)(2,1)}, bf16[512,1024]{1,0:T(8,128)(2,1)S(1)}, u32[]{:S(2)}, u32[]{:S(2)}) collective-permute-start(bf16[512,1024]{1,0:T(8,128)(2,1)} %all-gather.22.cloned.1.call-done.refs_1_), channel_id=1, source_target_pairs={{0,16},{8,24},{16,0},{24,8},{1,17},{9,25},{17,1},{25,9},{2,18},{10... | collective-permute-start | bytes 3145736 | tf_op jit(solution)/shard_map/ppermute | solution.py:357
  468.1 26.4 %collective-permute-start.47 = (bf16[512,1024]{1,0:T(8,128)(2,1)}, bf16[512,1024]{1,0:T(8,128)(2,1)S(1)}, u32[]{:S(2)}, u32[]{:S(2)}) collective-permute-start(bf16[512,1024]{1,0:T(8,128)(2,1)} %all-gather.22.cloned.1.call-done.refs_1_), channel_id=1, source_target_pairs={{0,4},{4,0},{1,5},{5,1},{2,6},{6,2},{3,7},{7,3},{8,12},{12,8},{9,1... | collective-permute-start | bytes 3145736 | tf_op jit(solution)/shard_map/ppermute | solution.py:360
  495.0 25.3 %collective-permute-start.52 = (bf16[512,1024]{1,0:T(8,128)(2,1)}, bf16[512,1024]{1,0:T(8,128)(2,1)S(1)}, u32[]{:S(2)}, u32[]{:S(2)}) collective-permute-start(bf16[512,1024]{1,0:T(8,128)(2,1)} %collective-permute-done.39.refs_0_), channel_id=1, source_target_pairs={{0,4},{4,0},{1,5},{5,1},{2,6},{6,2},{3,7},{7,3},{8,12},{12,8},{9,1... | collective-permute-start | bytes 3145736 | tf_op jit(solution)/shard_map/ppermute | solution.py:360
  496.1 42.9 %collective-permute-start.45 = (bf16[512,2048]{1,0:T(8,128)(2,1)S(1)}, bf16[512,2048]{1,0:T(8,128)(2,1)S(1)}, u32[]{:S(2)}, u32[]{:S(2)}) collective-permute-start(bf16[512,2048]{1,0:T(8,128)(2,1)S(1)} %get-tuple-element.158), channel_id=1, source_target_pairs={{0,8},{8,0},{16,24},{24,16},{1,9},{9,1},{17,25},{25,17},{2,10},{10... | collective-permute-start | bytes 6291464 | tf_op jit(solution)/shard_map/ppermute | solution.py:354
  539.6 25.7 %collective-permute-start.51 = (bf16[512,1024]{1,0:T(8,128)(2,1)S(1)}, bf16[512,1024]{1,0:T(8,128)(2,1)}, u32[]{:S(2)}, u32[]{:S(2)}) collective-permute-start(bf16[512,1024]{1,0:T(8,128)(2,1)S(1)} %add_convert_fusion.8), channel_id=1, source_target_pairs={{0,16},{8,24},{16,0},{24,8},{1,17},{9,25},{17,1},{25,9},{2,18},{10... | collective-permute-start | bytes 3145736 | tf_op jit(solution)/shard_map/ppermute | solution.py:357
  543.7 25.4 %collective-permute-start.57 = (bf16[512,1024]{1,0:T(8,128)(2,1)S(1)}, bf16[512,1024]{1,0:T(8,128)(2,1)}, u32[]{:S(2)}, u32[]{:S(2)}) collective-permute-start(bf16[512,1024]{1,0:T(8,128)(2,1)S(1)} %add_convert_fusion.7), channel_id=1, source_target_pairs={{0,4},{4,0},{1,5},{5,1},{2,6},{6,2},{3,7},{7,3},{8,12},{12,8},{9,1... | collective-permute-start | bytes 3145736 | tf_op jit(solution)/shard_map/ppermute | solution.py:360
  569.1 111.9 %reduce-scatter.6.cloned.1.call-start = ((), (), s32[]{:S(2)}) async-start(), calls=%async_computation.14 | async-start | bytes 2621440 | tf_op jit(solution)/shard_map/reduce_scatter | solution.py:593
  696.4 49.0 %all-gather.24.cloned.1.call-start = ((), (), s32[]{:S(2)}) async-start(), calls=%async_computation.15 | async-start | bytes 2621440 | tf_op jit(solution)/shard_map/all_gather | solution.py:678
  697.0 99.4 %reduce-scatter.8.cloned.1.call-start = ((), (), s32[]{:S(2)}) async-start(), calls=%async_computation.16 | async-start | bytes 2621440 | tf_op jit(solution)/shard_map/reduce_scatter | solution.py:687
  752.8 94.0 %all-gather.26.cloned.1.call-start = ((), (), s32[]{:S(2)}) async-start(), calls=%async_computation.17 | async-start | bytes 2621440 | tf_op jit(solution)/shard_map/all_gather | solution.py:696
  778.9 30.5 %collective-permute-start.77 = (bf16[256,1024]{0,1:T(8,128)(2,1)}, bf16[256,1024]{0,1:T(8,128)(2,1)}, u32[]{:S(2)}, u32[]{:S(2)}) collective-permute-start(bf16[256,1024]{0,1:T(8,128)(2,1)} %get-tuple-element.300), channel_id=1, source_target_pairs={{0,4},{4,0},{1,5},{5,1},{2,6},{6,2},{3,7},{7,3},{8,12},{12,8},{9,1... | collective-permute-start | bytes 1572872 | tf_op jit(solution)/shard_map/ppermute | solution.py:360
  780.4 32.3 %collective-permute-start.75 = (bf16[256,1024]{0,1:T(8,128)(2,1)}, bf16[256,1024]{0,1:T(8,128)(2,1)}, u32[]{:S(2)}, u32[]{:S(2)}) collective-permute-start(bf16[256,1024]{0,1:T(8,128)(2,1)} %get-tuple-element.299), channel_id=1, source_target_pairs={{0,16},{8,24},{16,0},{24,8},{1,17},{9,25},{17,1},{25,9},{2,18},{10... | collective-permute-start | bytes 1572872 | tf_op jit(solution)/shard_map/ppermute | solution.py:357
  804.3 26.9 %collective-permute-start.72 = (bf16[256,1024]{0,1:T(8,128)(2,1)}, bf16[256,1024]{0,1:T(8,128)(2,1)S(1)}, u32[]{:S(2)}, u32[]{:S(2)}) collective-permute-start(bf16[256,1024]{0,1:T(8,128)(2,1)} %slice.488), channel_id=1, source_target_pairs={{0,16},{8,24},{16,0},{24,8},{1,17},{9,25},{17,1},{25,9},{2,18},{10... | collective-permute-start | bytes 1572872 | tf_op jit(solution)/shard_map/ppermute | solution.py:357
  (157 other events, 1784.3 us)
Sparse Core Ops, SparseCore 0:
  10.5 49.4 all-gather.9
  62.4 72.3 all-gather.11
  142.9 26.8 all-gather.13
  171.9 27.4 all-gather.15
  364.0 41.6 reduce-scatter.3
  409.0 27.2 all-gather.19
  438.5 27.4 all-gather.21
  569.2 44.5 all-gather.17
  636.7 42.2 reduce-scatter.5
  699.0 46.2 all-gather.23
  752.9 43.3 reduce-scatter.7
  800.8 46.0 all-gather.25

commit v10 on v9

--- a/solution.py
+++ b/solution.py
@@ -626,13 +626,13 @@
 
     def weight_grads():
         rows_back, grad_rows = saved[0]
+        grad_up = jnp.einsum("ebcd,ebcf->edf", rows_in, grad_rows, preferred_element_type=wide)
+        made.append(grad_up)
+        yield [grad_up]
         made.append(
             jnp.einsum("ebcf,ebcd->efd", hidden, rows_back, preferred_element_type=wide)
         )
-        yield [made[0]]
-        grad_up = jnp.einsum("ebcd,ebcf->edf", rows_in, grad_rows, preferred_element_type=wide)
-        made.append(grad_up)
-        yield [grad_up, activations]
+        yield [made[1], activations]
 
     made = []
     first_block, second_block = spread_halves
@@ -642,7 +642,7 @@
     if not made:
         for _ in weight_grads():
             pass
-    grad_down, grad_up = made
+    grad_up, grad_down = made
     grad_gate_up = with_layout_constraint(
         grad_up.reshape(shard_experts, width, 2, hidden_local),
         Layout(major_to_minor=(0, 1, 2, 3)),

time: 872 us -> 875 us (level)
  transfers between devices with their start and end apart: 95 -> 95, of which waited for: 53 -> 51; matrix products, arithmetic and copies ran while one was open for 22% -> 21% of each run, Pallas kernels for 17% -> 17%
where the time goes in v10:
time: 875 us; the launch traced here: 864 us
  waiting for transfers between devices  374 us (43%)
  Pallas kernels  145 us (17%)
  local copies, waits for them, and re-layouts  85.9 us (10%)
  matrix products  85 us (10%)
  starting transfers between devices  81.4 us (9%)
  other arithmetic  72.4 us (8%)
  between operations  20.8 us (2%)
    pallas_call x8, Pallas kernels, expert_call(): pl.pallas_call(body, grid=(experts,), in_specs=in_specs + [pl.BlockSpec(m...  136 us
    all_gather x4, waiting for transfers between devices, spread(): lax.all_gather(half.astype(low), 'tp', axis=0, tiled=True)  92.3 us
    ppermute x16, waiting for transfers between devices, along_x(): return lax.ppermute(a, 'fsdp', [(i, i ^ 2) for i in range(self.fsdp)])  82 us
    reduce_scatter x2, waiting for transfers between devices, finish(): lax.psum_scatter(half, 'tp', scatter_dimension=0, tiled=True).astype(wide)  39.6 us
    ppermute x17, waiting for transfers between devices, along_y(): return lax.ppermute(a, 'ctx', [(i, i ^ 1) for i in range(self.ctx)])  29.3 us
    reshape x1, local copies, waits for them, and re-layouts, per_device(): grad_up.reshape(shard_experts, width, 2, hidden_local)  25.1 us
    ppermute x6, waiting for transfers between devices, line_gather(): lax.ppermute(shard, 'tp', [(i, i + d) for i in range(size) if 0 <= i + d...  21.9 us
    ppermute x17, starting transfers between devices, along_y(): return lax.ppermute(a, 'ctx', [(i, i ^ 1) for i in range(self.ctx)])  21.4 us
  transfers between devices with their start and end apart: 95, of which 51 were waited for; matrix products, arithmetic and copies ran while one was open for 21% of the time, Pallas kernels for 17%

profile of v10, /device:TPU:0, one launch (start us, length us, event | category | flops | bytes accessed | tf_op | source)
XLA Modules:
  0.0 864.3 jit_solution(4130529358174970840)
XLA Ops:
  9.6 7.0 collective-permute-start.9
  33.6 12.8 %collective-permute-done.13 = bf16[512,256]{1,0:T(8,128)(2,1)S(1)} collective-permute-done((bf16[512,256]{1,0:T(8,128)(2,1)S(1)}, bf16[512,256]{1,0:T(8,128)(2,1)S(1)}, u32[]{:S(2)}, u32[]{:S(2)}) %collective-permute-start.13) | collective-permute-done | bytes 262176 | tf_op jit(solution)/shard_map/ppermute | solution.py:338
  69.0 6.9 fusion.11
  90.0 7.7 collective-permute-done.8
  102.5 9.9 %collective-permute-done.7 = bf16[1,512,4,128]{1,3,2,0:T(8,128)(2,1)S(1)} collective-permute-done((bf16[1,512,4,128]{1,3,2,0:T(8,128)(2,1)S(1)}, bf16[1,512,4,128]{1,3,2,0:T(8,128)(2,1)S(1)}, u32[]{:S(2)}, u32[]{:S(2)}) %collective-permute-start.7) | collective-permute-done | bytes 524320 | tf_op jit(solution)/shard_map/ppermute | solution.py:551
  123.8 11.7 %all-to-all-done.1 = bf16[4,128,512]{2,1,0:T(8,128)(2,1)S(1)} async-done(((bf16[4,128,512]{2,1,0:T(8,128)(2,1)}), bf16[4,128,512]{2,1,0:T(8,128)(2,1)S(1)}, u32[]{:S(2)}, u32[]{:S(2)}) %all-to-all-start.1) | async-done | bytes 524320 | tf_op jit(solution)/shard_map/all_to_all | solution.py:570
  143.5 26.5 %all-gather.14.cloned.1.call-done.refs_0_ = bf16[512,1024]{1,0:T(8,128)(2,1)} async-done(((bf16[128,1024]{1,0:T(8,128)(2,1)}), bf16[512,1024]{1,0:T(8,128)(2,1)}) %all-gather.14.cloned.1.call-update) | async-done | bytes 1048592 | tf_op jit(solution)/shard_map/all_gather | solution.py:581
  173.0 14.1 %reshape.366.refs_0_ = bf16[4,2048,512]{2,1,0:T(8,128)(2,1)} reshape(bf16[4,2048,2,256]{3,2,1,0:T(2,128)(2,1)} %param.20) | data formatting | bytes 16777216 | tf_op jit(solution)/shard_map/reshape | solution.py:521
  187.1 12.4 %all-gather.16.cloned.1.call-done.refs_1_ = bf16[512,1024]{1,0:T(8,128)(2,1)} async-done(((bf16[128,1024]{1,0:T(8,128)(2,1)}), bf16[512,1024]{1,0:T(8,128)(2,1)}) %all-gather.16.cloned.1.call-update) | async-done | bytes 1048592 | tf_op jit(solution)/shard_map/all_gather | solution.py:581
  212.5 15.8 %shard_map.187 = (bf16[512,2048]{1,0:T(8,128)(2,1)S(1)}, bf16[512,2048]{1,0:T(8,128)(2,1)S(1)}, bf16[4,8,160,2048]{3,2,1,0:T(8,128)(2,1)}, bf16[4,8,160,512]{3,2,1,0:T(8,128)(2,1)}, bf16[4,8,160,256]{3,2,1,0:T(8,128)(2,1)}) custom-call(bf16[512,1024]{1,0:T(8,128)(2,1)S(1)} %copy-done.6, bf16[512,1024]{1,0:T(8,128)(2,1)S(1)} %copy-done.7, ...), custom_call_target="tpu_custom_call" | custom-call | flops 9395240960 | bytes 17563648 | tf_op jit(solution)/shard_map/pallas_call | solution.py:269
  233.2 16.0 %shard_map.188 = (bf16[512,2048]{1,0:T(8,128)(2,1)S(1)}, bf16[512,2048]{1,0:T(8,128)(2,1)S(1)}, bf16[4,8,160,2048]{3,2,1,0:T(8,128)(2,1)}, bf16[4,8,160,512]{3,2,1,0:T(8,128)(2,1)}, bf16[4,8,160,256]{3,2,1,0:T(8,128)(2,1)}) custom-call(bf16[512,1024]{1,0:T(8,128)(2,1)} %collective-permute-done.15.refs_0_,, ...), custom_call_target="tpu_custom_call", output_to_operand_aliasing={{2}: (8, {}), {3}: (9, {}), {4}: (10, {})} | custom-call | flops 9395240960 | bytes 17563648 | tf_op jit(solution)/shard_map/pallas_call | solution.py:269
  249.7 6.7 collective-permute-done.28.refs_0_
  257.4 15.5 %shard_map.189 = (bf16[512,2048]{1,0:T(8,128)(2,1)S(1)}, bf16[512,2048]{1,0:T(8,128)(2,1)S(1)}, bf16[4,8,160,2048]{3,2,1,0:T(8,128)(2,1)}, bf16[4,8,160,512]{3,2,1,0:T(8,128)(2,1)}, bf16[4,8,160,256]{3,2,1,0:T(8,128)(2,1)}) custom-call(bf16[512,1024]{1,0:T(8,128)(2,1)S(1)} %collective-permute-done.16.refs, ...), custom_call_target="tpu_custom_call", output_to_operand_aliasing={{2}: (8, {}), {3}: (9, {}), {4}: (10, {})} | custom-call | flops 9395240960 | bytes 17563648 | tf_op jit(solution)/shard_map/pallas_call | solution.py:269
  278.6 14.7 %shard_map.190 = (bf16[512,2048]{1,0:T(8,128)(2,1)S(1)}, bf16[512,2048]{1,0:T(8,128)(2,1)S(1)}, bf16[4,8,160,2048]{3,2,1,0:T(8,128)(2,1)}, bf16[4,8,160,512]{3,2,1,0:T(8,128)(2,1)}, bf16[4,8,160,256]{3,2,1,0:T(8,128)(2,1)}) custom-call(bf16[512,1024]{1,0:T(8,128)(2,1)S(1)} %collective-permute-done.28.refs, ...), custom_call_target="tpu_custom_call", output_to_operand_aliasing={{2}: (8, {}), {3}: (9, {}), {4}: (10, {})} | custom-call | flops 9395240960 | bytes 17563648 | tf_op jit(solution)/shard_map/pallas_call | solution.py:269
  309.6 24.0 %collective-permute-done.35 = bf16[512,1024]{1,0:T(8,128)(2,1)S(1)} collective-permute-done((bf16[512,1024]{1,0:T(8,128)(2,1)S(1)}, bf16[512,1024]{1,0:T(8,128)(2,1)S(1)}, u32[]{:S(2)}, u32[]{:S(2)}) %collective-permute-start.35) | collective-permute-done | bytes 1048608 | tf_op jit(solution)/shard_map/ppermute | solution.py:357
  337.4 21.3 %collective-permute-done.38 = bf16[512,1024]{1,0:T(8,128)(2,1)S(1)} collective-permute-done((bf16[512,1024]{1,0:T(8,128)(2,1)S(1)}, bf16[512,1024]{1,0:T(8,128)(2,1)S(1)}, u32[]{:S(2)}, u32[]{:S(2)}) %collective-permute-start.38) | collective-permute-done | bytes 1048608 | tf_op jit(solution)/shard_map/ppermute | solution.py:357
  366.4 39.6 %reduce-scatter.4.cloned.1.call-done = bf16[128,2048]{1,0:T(8,128)(2,1)} async-done(((bf16[512,2048]{1,0:T(8,128)(2,1)}), bf16[128,2048]{1,0:T(8,128)(2,1)}) %reduce-scatter.4.cloned.1.call-update) | async-done | bytes 524304 | tf_op jit(solution)/shard_map/reduce_scatter | solution.py:593
  409.9 26.6 %all-gather.20.cloned.1.call-done.refs_0_ = bf16[512,1024]{1,0:T(8,128)(2,1)} async-done(((bf16[128,1024]{1,0:T(8,128)(2,1)}), bf16[512,1024]{1,0:T(8,128)(2,1)}) %all-gather.20.cloned.1.call-update) | async-done | bytes 1048592 | tf_op jit(solution)/shard_map/all_gather | solution.py:581
  439.4 26.7 %all-gather.22.cloned.1.call-done.refs_1_ = bf16[512,1024]{1,0:T(8,128)(2,1)} async-done(((bf16[128,1024]{1,0:T(8,128)(2,1)}), bf16[512,1024]{1,0:T(8,128)(2,1)}) %all-gather.22.cloned.1.call-update) | async-done | bytes 1048592 | tf_op jit(solution)/shard_map/all_gather | solution.py:581
  474.4 18.7 %shard_map.192 = (bf16[512,2048]{1,0:T(8,128)(2,1)S(1)}, bf16[512,2048]{1,0:T(8,128)(2,1)S(1)}, bf16[4,8,160,2048]{3,2,1,0:T(8,128)(2,1)}, bf16[4,8,160,512]{3,2,1,0:T(8,128)(2,1)}) custom-call(bf16[512,1024]{1,0:T(8,128)(2,1)S(1)} %copy-done.8, bf16[512,1024]{1,0:T(8,128)(2,1)S(1)} %copy-done.9, bf16[512,1024]{1,0:T(8,128)(2,1)} %collective-permute-done.41.refs_2_, ...), custom_call_target="tpu_custom_call" | custom-call | flops 9395240960 | bytes 17563648 | tf_op jit(solution)/shard_map/pallas_call | solution.py:269
  497.1 18.7 %shard_map.193 = (bf16[512,2048]{1,0:T(8,128)(2,1)S(1)}, bf16[512,2048]{1,0:T(8,128)(2,1)S(1)}, bf16[4,8,160,2048]{3,2,1,0:T(8,128)(2,1)}, bf16[4,8,160,512]{3,2,1,0:T(8,128)(2,1)}) custom-call(bf16[512,1024]{1,0:T(8,128)(2,1)} %collective-permute-done.39.refs_0_, ...), custom_call_target="tpu_custom_call", output_to_operand_aliasing={{2}: (9, {}), {3}: (10, {})} | custom-call | flops 9395240960 | bytes 17563648 | tf_op jit(solution)/shard_map/pallas_call | solution.py:269
  520.8 18.1 %shard_map.194 = (bf16[512,2048]{1,0:T(8,128)(2,1)S(1)}, bf16[512,2048]{1,0:T(8,128)(2,1)S(1)}, bf16[4,8,160,2048]{3,2,1,0:T(8,128)(2,1)}, bf16[4,8,160,512]{3,2,1,0:T(8,128)(2,1)}) custom-call(bf16[512,1024]{1,0:T(8,128)(2,1)S(1)} %collective-permute-done.40.refs_0_, ...), custom_call_target="tpu_custom_call", output_to_operand_aliasing={{2}: (9, {}), {3}: (10, {})} | custom-call | flops 9395240960 | bytes 17563648 | tf_op jit(solution)/shard_map/pallas_call | solution.py:269
  544.9 18.5 %shard_map.195 = (bf16[512,2048]{1,0:T(8,128)(2,1)S(1)}, bf16[512,2048]{1,0:T(8,128)(2,1)S(1)}, bf16[4,8,160,2048]{3,2,1,0:T(8,128)(2,1)}, bf16[4,8,160,512]{3,2,1,0:T(8,128)(2,1)}) custom-call(bf16[512,1024]{1,0:T(8,128)(2,1)S(1)} %collective-permute-done.52.refs_0_, ...), custom_call_target="tpu_custom_call", output_to_operand_aliasing={{2}: (9, {}), {3}: (10, {})} | custom-call | flops 9395240960 | bytes 17563648 | tf_op jit(solution)/shard_map/pallas_call | solution.py:269
  577.5 23.5 %collective-permute-done.59 = bf16[512,1024]{1,0:T(8,128)(2,1)} collective-permute-done((bf16[512,1024]{1,0:T(8,128)(2,1)}, bf16[512,1024]{1,0:T(8,128)(2,1)}, u32[]{:S(2)}, u32[]{:S(2)}) %collective-permute-start.59) | collective-permute-done | bytes 1048608 | tf_op jit(solution)/shard_map/ppermute | solution.py:357
  610.1 15.4 %convolution_bitcast_fusion = f32[4,256,2048]{2,1,0:T(8,128)} fusion(bf16[4,8,160,256]{3,2,1,0:T(8,128)(2,1)S(1)} %copy-done.17, bf16[4,8,160,2048]{3,2,1,0:T(8,128)(2,1)} %get-tuple-element.188), kind=kOutput, calls=%fused_computation.25 | convolution fusion | flops 5368709120 | bytes 31981568 | tf_op jit(solution)/shard_map/ebcf,ebcd->efd/dot_general | solution.py:633
  638.8 19.3 %fusion.84 = f32[4,2048,512,1]{1,2,3,0:T(8,128)} fusion(bf16[4,8,160,2048]{3,2,1,0:T(8,128)(2,1)} %get-tuple-element.183, bf16[4,8,160,512]{3,2,1,0:T(8,128)(2,1)} %get-tuple-element.184), kind=kOutput, calls=%fused_computation.254 | convolution fusion | flops 10737418240 | bytes 42991616 | tf_op jit(solution)/shard_map/ebcd,ebcf->edf/dot_general | solution.py:629
  658.1 25.1 %copy.136 = f32[4,2048,2,256]{3,2,1,0:T(2,128)} copy(f32[4,2048,2,256]{1,3,2,0:T(8,128)} %bitcast.199) | data formatting | bytes 33554432 | tf_op jit(solution)/shard_map/reshape | solution.py:647
  699.5 12.0 %all-to-all-done.2 = bf16[128,4,512]{2,0,1:T(8,128)(2,1)S(1)} async-done(((bf16[128,4,512]{2,0,1:T(8,128)(2,1)}), bf16[128,4,512]{2,0,1:T(8,128)(2,1)S(1)}, u32[]{:S(2)}, u32[]{:S(2)}) %all-to-all-start.2) | async-done | bytes 524320 | tf_op jit(solution)/shard_map/all_to_all | solution.py:656
  730.8 8.0 collective-permute-done.63
  748.0 7.4 convolution_convert_fusion.2
  785.1 13.6 %reduce-scatter.8.cloned.1.call-done = bf16[128,2048]{1,0:T(8,128)(2,1)} async-done(((bf16[512,2048]{1,0:T(8,128)(2,1)}), bf16[128,2048]{1,0:T(8,128)(2,1)}) %reduce-scatter.8.cloned.1.call-update) | async-done | bytes 524304 | tf_op jit(solution)/shard_map/reduce_scatter | solution.py:687
  819.2 12.9 %collective-permute-done.66 = f32[1,4353]{1,0:T(1,128)S(1)} collective-permute-done((f32[1,4353]{1,0:T(1,128)S(1)}, f32[1,4353]{1,0:T(1,128)S(1)}, u32[]{:S(2)}, u32[]{:S(2)}) %collective-permute-start.66) | collective-permute-done | bytes 17444 | tf_op jit(solution)/shard_map/ppermute | solution.py:329
  (535 shorter events, 316.5 us)
Async XLA Ops:
  7.2 61.8 %all-gather.10.cloned.1.call-start = ((), (), s32[]{:S(2)}) async-start(), calls=%async_computation.6 | async-start | bytes 7077888 | tf_op jit(solution)/shard_map/all_gather | solution.py:532
  9.6 126.2 %all-gather.12.cloned.1.call-start = ((), (), s32[]{:S(2)}) async-start(), calls=%async_computation.7 | async-start | bytes 9437184 | tf_op jit(solution)/shard_map/all_gather | solution.py:536
  121.0 49.0 %all-gather.14.cloned.1.call-start = ((), (), s32[]{:S(2)}) async-start(), calls=%async_computation.8 | async-start | bytes 1310720 | tf_op jit(solution)/shard_map/all_gather | solution.py:581
  142.9 56.6 %all-gather.16.cloned.1.call-start = ((), (), s32[]{:S(2)}) async-start(), calls=%async_computation.9 | async-start | bytes 1310720 | tf_op jit(solution)/shard_map/all_gather | solution.py:581
  143.4 262.5 %reduce-scatter.4.cloned.1.call-start = ((), (), s32[]{:S(2)}) async-start(), calls=%async_computation.10 | async-start | bytes 2621440 | tf_op jit(solution)/shard_map/reduce_scatter | solution.py:593
  170.0 29.5 %collective-permute-start.15 = (bf16[512,1024]{1,0:T(8,128)(2,1)}, bf16[512,1024]{1,0:T(8,128)(2,1)}, u32[]{:S(2)}, u32[]{:S(2)}) collective-permute-start(bf16[512,1024]{1,0:T(8,128)(2,1)} %all-gather.14.cloned.1.call-done.refs_0_), channel_id=1, source_target_pairs={{0,16},{8,24},{16,0},{24,8},{1,17},{9,25},{17,1},{25,9},{2,18},{10... | collective-permute-start | bytes 3145736 | tf_op jit(solution)/shard_map/ppermute | solution.py:357
  171.5 28.0 %collective-permute-start.16 = (bf16[512,1024]{1,0:T(8,128)(2,1)}, bf16[512,1024]{1,0:T(8,128)(2,1)S(1)}, u32[]{:S(2)}, u32[]{:S(2)}) collective-permute-start(bf16[512,1024]{1,0:T(8,128)(2,1)} %all-gather.14.cloned.1.call-done.refs_0_), channel_id=1, source_target_pairs={{0,4},{4,0},{1,5},{5,1},{2,6},{6,2},{3,7},{7,3},{8,12},{12,8},{9,1... | collective-permute-start | bytes 3145736 | tf_op jit(solution)/shard_map/ppermute | solution.py:360
  173.0 32.4 %collective-permute-start.17 = (bf16[512,1024]{1,0:T(8,128)(2,1)}, bf16[512,1024]{1,0:T(8,128)(2,1)}, u32[]{:S(2)}, u32[]{:S(2)}) collective-permute-start(bf16[512,1024]{1,0:T(8,128)(2,1)} %all-gather.14.cloned.1.call-done.refs_0_), channel_id=1, source_target_pairs={{0,8},{8,0},{16,24},{24,16},{1,9},{9,1},{17,25},{25,17},{2,10},{10... | collective-permute-start | bytes 3145736 | tf_op jit(solution)/shard_map/ppermute | solution.py:354
  203.9 25.5 %collective-permute-start.22 = (bf16[512,1024]{1,0:T(8,128)(2,1)S(1)}, bf16[512,1024]{1,0:T(8,128)(2,1)S(1)}, u32[]{:S(2)}, u32[]{:S(2)}) collective-permute-start(bf16[512,1024]{1,0:T(8,128)(2,1)S(1)} %copy-done.7), channel_id=1, source_target_pairs={{0,16},{8,24},{16,0},{24,8},{1,17},{9,25},{17,1},{25,9},{2,18},{10... | collective-permute-start | bytes 3145736 | tf_op jit(solution)/shard_map/ppermute | solution.py:357
  231.1 25.3 %collective-permute-start.28 = (bf16[512,1024]{1,0:T(8,128)(2,1)}, bf16[512,1024]{1,0:T(8,128)(2,1)S(1)}, u32[]{:S(2)}, u32[]{:S(2)}) collective-permute-start(bf16[512,1024]{1,0:T(8,128)(2,1)} %collective-permute-done.15.refs_0_), channel_id=1, source_target_pairs={{0,4},{4,0},{1,5},{5,1},{2,6},{6,2},{3,7},{7,3},{8,12},{12,8},{9,1... | collective-permute-start | bytes 3145736 | tf_op jit(solution)/shard_map/ppermute | solution.py:360
  233.1 39.8 %collective-permute-start.21 = (bf16[512,2048]{1,0:T(8,128)(2,1)S(1)}, bf16[512,2048]{1,0:T(8,128)(2,1)S(1)}, u32[]{:S(2)}, u32[]{:S(2)}) collective-permute-start(bf16[512,2048]{1,0:T(8,128)(2,1)S(1)} %get-tuple-element.115), channel_id=1, source_target_pairs={{0,8},{8,0},{16,24},{24,16},{1,9},{9,1},{17,25},{25,17},{2,10},{10... | collective-permute-start | bytes 6291464 | tf_op jit(solution)/shard_map/ppermute | solution.py:354
  277.7 25.5 %collective-permute-start.33 = (bf16[512,1024]{1,0:T(8,128)(2,1)S(1)}, bf16[512,1024]{1,0:T(8,128)(2,1)S(1)}, u32[]{:S(2)}, u32[]{:S(2)}) collective-permute-start(bf16[512,1024]{1,0:T(8,128)(2,1)S(1)} %add_convert_fusion.15), channel_id=1, source_target_pairs={{0,4},{4,0},{1,5},{5,1},{2,6},{6,2},{3,7},{7,3},{8,12},{12,8},{9,1... | collective-permute-start | bytes 3145736 | tf_op jit(solution)/shard_map/ppermute | solution.py:360
  364.1 72.4 %all-gather.20.cloned.1.call-start = ((), (), s32[]{:S(2)}) async-start(), calls=%async_computation.12 | async-start | bytes 1310720 | tf_op jit(solution)/shard_map/all_gather | solution.py:581
  409.1 57.1 %all-gather.22.cloned.1.call-start = ((), (), s32[]{:S(2)}) async-start(), calls=%async_computation.13 | async-start | bytes 1310720 | tf_op jit(solution)/shard_map/all_gather | solution.py:581
  409.8 215.7 %all-gather.18.cloned.1.call-start = ((), (), s32[]{:S(2)}) async-start(), calls=%async_computation.11 | async-start | bytes 2621440 | tf_op jit(solution)/shard_map/all_gather | solution.py:614
  436.5 29.7 %collective-permute-start.39 = (bf16[512,1024]{1,0:T(8,128)(2,1)}, bf16[512,1024]{1,0:T(8,128)(2,1)}, u32[]{:S(2)}, u32[]{:S(2)}) collective-permute-start(bf16[512,1024]{1,0:T(8,128)(2,1)} %all-gather.20.cloned.1.call-done.refs_0_), channel_id=1, source_target_pairs={{0,16},{8,24},{16,0},{24,8},{1,17},{9,25},{17,1},{25,9},{2,18},{10... | collective-permute-start | bytes 3145736 | tf_op jit(solution)/shard_map/ppermute | solution.py:357
  438.0 28.2 %collective-permute-start.40 = (bf16[512,1024]{1,0:T(8,128)(2,1)}, bf16[512,1024]{1,0:T(8,128)(2,1)S(1)}, u32[]{:S(2)}, u32[]{:S(2)}) collective-permute-start(bf16[512,1024]{1,0:T(8,128)(2,1)} %all-gather.20.cloned.1.call-done.refs_0_), channel_id=1, source_target_pairs={{0,4},{4,0},{1,5},{5,1},{2,6},{6,2},{3,7},{7,3},{8,12},{12,8},{9,1... | collective-permute-start | bytes 3145736 | tf_op jit(solution)/shard_map/ppermute | solution.py:360
  439.4 28.9 %collective-permute-start.41 = (bf16[512,1024]{1,0:T(8,128)(2,1)}, bf16[512,1024]{1,0:T(8,128)(2,1)}, u32[]{:S(2)}, u32[]{:S(2)}) collective-permute-start(bf16[512,1024]{1,0:T(8,128)(2,1)} %all-gather.20.cloned.1.call-done.refs_0_), channel_id=1, source_target_pairs={{0,8},{8,0},{16,24},{24,16},{1,9},{9,1},{17,25},{25,17},{2,10},{10... | collective-permute-start | bytes 3145736 | tf_op jit(solution)/shard_map/ppermute | solution.py:354
  466.8 27.6 %collective-permute-start.46 = (bf16[512,1024]{1,0:T(8,128)(2,1)}, bf16[512,1024]{1,0:T(8,128)(2,1)S(1)}, u32[]{:S(2)}, u32[]{:S(2)}) collective-permute-start(bf16[512,1024]{1,0:T(8,128)(2,1)} %all-gather.22.cloned.1.call-done.refs_1_), channel_id=1, source_target_pairs={{0,16},{8,24},{16,0},{24,8},{1,17},{9,25},{17,1},{25,9},{2,18},{10... | collective-permute-start | bytes 3145736 | tf_op jit(solution)/shard_map/ppermute | solution.py:357
  468.3 26.2 %collective-permute-start.47 = (bf16[512,1024]{1,0:T(8,128)(2,1)}, bf16[512,1024]{1,0:T(8,128)(2,1)S(1)}, u32[]{:S(2)}, u32[]{:S(2)}) collective-permute-start(bf16[512,1024]{1,0:T(8,128)(2,1)} %all-gather.22.cloned.1.call-done.refs_1_), channel_id=1, source_target_pairs={{0,4},{4,0},{1,5},{5,1},{2,6},{6,2},{3,7},{7,3},{8,12},{12,8},{9,1... | collective-permute-start | bytes 3145736 | tf_op jit(solution)/shard_map/ppermute | solution.py:360
  495.0 25.3 %collective-permute-start.52 = (bf16[512,1024]{1,0:T(8,128)(2,1)}, bf16[512,1024]{1,0:T(8,128)(2,1)S(1)}, u32[]{:S(2)}, u32[]{:S(2)}) collective-permute-start(bf16[512,1024]{1,0:T(8,128)(2,1)} %collective-permute-done.39.refs_0_), channel_id=1, source_target_pairs={{0,4},{4,0},{1,5},{5,1},{2,6},{6,2},{3,7},{7,3},{8,12},{12,8},{9,1... | collective-permute-start | bytes 3145736 | tf_op jit(solution)/shard_map/ppermute | solution.py:360
  496.3 42.7 %collective-permute-start.45 = (bf16[512,2048]{1,0:T(8,128)(2,1)S(1)}, bf16[512,2048]{1,0:T(8,128)(2,1)S(1)}, u32[]{:S(2)}, u32[]{:S(2)}) collective-permute-start(bf16[512,2048]{1,0:T(8,128)(2,1)S(1)} %get-tuple-element.158), channel_id=1, source_target_pairs={{0,8},{8,0},{16,24},{24,16},{1,9},{9,1},{17,25},{25,17},{2,10},{10... | collective-permute-start | bytes 6291464 | tf_op jit(solution)/shard_map/ppermute | solution.py:354
  539.7 25.4 %collective-permute-start.51 = (bf16[512,1024]{1,0:T(8,128)(2,1)S(1)}, bf16[512,1024]{1,0:T(8,128)(2,1)S(1)}, u32[]{:S(2)}, u32[]{:S(2)}) collective-permute-start(bf16[512,1024]{1,0:T(8,128)(2,1)S(1)} %add_convert_fusion.8), channel_id=1, source_target_pairs={{0,16},{8,24},{16,0},{24,8},{1,17},{9,25},{17,1},{25,9},{2,18},{10... | collective-permute-start | bytes 3145736 | tf_op jit(solution)/shard_map/ppermute | solution.py:357
  543.7 25.3 %collective-permute-start.57 = (bf16[512,1024]{1,0:T(8,128)(2,1)S(1)}, bf16[512,1024]{1,0:T(8,128)(2,1)S(1)}, u32[]{:S(2)}, u32[]{:S(2)}) collective-permute-start(bf16[512,1024]{1,0:T(8,128)(2,1)S(1)} %add_convert_fusion.7), channel_id=1, source_target_pairs={{0,4},{4,0},{1,5},{5,1},{2,6},{6,2},{3,7},{7,3},{8,12},{12,8},{9,1... | collective-permute-start | bytes 3145736 | tf_op jit(solution)/shard_map/ppermute | solution.py:360
  575.5 25.5 %collective-permute-start.59 = (bf16[512,1024]{1,0:T(8,128)(2,1)}, bf16[512,1024]{1,0:T(8,128)(2,1)}, u32[]{:S(2)}, u32[]{:S(2)}) collective-permute-start(bf16[512,1024]{1,0:T(8,128)(2,1)} %get-tuple-element.274), channel_id=1, source_target_pairs={{0,16},{8,24},{16,0},{24,8},{1,17},{9,25},{17,1},{25,9},{2,18},{10... | collective-permute-start | bytes 3145736 | tf_op jit(solution)/shard_map/ppermute | solution.py:357
  577.5 105.8 %reduce-scatter.6.cloned.1.call-start = ((), (), s32[]{:S(2)}) async-start(), calls=%async_computation.14 | async-start | bytes 2621440 | tf_op jit(solution)/shard_map/reduce_scatter | solution.py:593
  698.6 49.4 %all-gather.24.cloned.1.call-start = ((), (), s32[]{:S(2)}) async-start(), calls=%async_computation.15 | async-start | bytes 2621440 | tf_op jit(solution)/shard_map/all_gather | solution.py:678
  699.2 99.5 %reduce-scatter.8.cloned.1.call-start = ((), (), s32[]{:S(2)}) async-start(), calls=%async_computation.16 | async-start | bytes 2621440 | tf_op jit(solution)/shard_map/reduce_scatter | solution.py:687
  755.5 93.7 %all-gather.26.cloned.1.call-start = ((), (), s32[]{:S(2)}) async-start(), calls=%async_computation.17 | async-start | bytes 2621440 | tf_op jit(solution)/shard_map/all_gather | solution.py:696
  781.4 30.4 %collective-permute-start.77 = (bf16[256,1024]{0,1:T(8,128)(2,1)}, bf16[256,1024]{0,1:T(8,128)(2,1)}, u32[]{:S(2)}, u32[]{:S(2)}) collective-permute-start(bf16[256,1024]{0,1:T(8,128)(2,1)} %get-tuple-element.300), channel_id=1, source_target_pairs={{0,4},{4,0},{1,5},{5,1},{2,6},{6,2},{3,7},{7,3},{8,12},{12,8},{9,1... | collective-permute-start | bytes 1572872 | tf_op jit(solution)/shard_map/ppermute | solution.py:360
  782.9 32.1 %collective-permute-start.75 = (bf16[256,1024]{0,1:T(8,128)(2,1)}, bf16[256,1024]{0,1:T(8,128)(2,1)}, u32[]{:S(2)}, u32[]{:S(2)}) collective-permute-start(bf16[256,1024]{0,1:T(8,128)(2,1)} %get-tuple-element.299), channel_id=1, source_target_pairs={{0,16},{8,24},{16,0},{24,8},{1,17},{9,25},{17,1},{25,9},{2,18},{10... | collective-permute-start | bytes 1572872 | tf_op jit(solution)/shard_map/ppermute | solution.py:357
  806.8 26.8 %collective-permute-start.72 = (bf16[256,1024]{0,1:T(8,128)(2,1)}, bf16[256,1024]{0,1:T(8,128)(2,1)S(1)}, u32[]{:S(2)}, u32[]{:S(2)}) collective-permute-start(bf16[256,1024]{0,1:T(8,128)(2,1)} %slice.488), channel_id=1, source_target_pairs={{0,16},{8,24},{16,0},{24,8},{1,17},{9,25},{17,1},{25,9},{2,18},{10... | collective-permute-start | bytes 1572872 | tf_op jit(solution)/shard_map/ppermute | solution.py:357
  (157 other events, 1804.0 us)
Sparse Core Ops, SparseCore 0:
  10.5 49.4 all-gather.9
  62.4 72.3 all-gather.11
  143.0 27.0 all-gather.13
  172.0 27.4 all-gather.15
  364.2 41.6 reduce-scatter.3
  409.2 27.2 all-gather.19
  438.7 27.4 all-gather.21
  577.6 44.6 all-gather.17
  639.0 42.5 reduce-scatter.5
  701.3 46.4 all-gather.23
  755.6 43.0 reduce-scatter.7
  803.1 46.0 all-gather.25
